TPU v7x, 32 devices: a whole 2x2x4 slice. The times are simulated.
32 devices in a mesh: view: 4 (over z), gz: 2 (over x), gy: 4 (over y, core).
Axes of the slice: x: 2, y: 2, z: 4, core: 2. Of those that a mesh axis runs over, the one named last changes fastest.
Arguments:
- pieces: bfloat16 [4, 128, 8, 2048], P('view', ('gz', 'gy')), may hold values from 0.19921875 to 2
- piece_owner: int32 [4, 128, 1], P('view', ('gz', 'gy')), may hold values from 0 to 7; in each aligned block of 16 rows (0 to 15, 16 to 31, ..., all dimensions but the last counted through in order) at most 4 rows name the same one
- piece_row: int32 [4, 128], P('view', ('gz', 'gy')), may hold values from 0 to 3
- estimate: float32 [8, 32, 2048], P('gz', 'gy', 'view'), may hold values from 0.5 to 1.5
- psf_x: float32 [4, 257], P('view'), may hold values from 0.00097276265 to 0.0068093385
- stencil: float32 [4, 3, 3], P('view'), may hold values from 0.03 to 0.2
- background: float32 [4], P('view'), may hold values from 0.05 to 0.5
- bleach_table: float32 [4, 16], replicated, may hold values from 0.2 to 2
- bleach_index: int32 [4, 8], P(None, 'gz'), may hold values from 0 to 15
Outputs:
- joined: float32 [8, 32, 2048], P('gz', 'gy', 'view')
Inputs may be any that keep to these rules, and one draw needn't show every extreme that they name: `piece_owner`: among the 16 blocks of a view that one device holds (aligned blocks of rows), no owner is named more than 4 times, a bound that some block reaches.
All inputs are finite; a program needn't handle non-finite values.
Results may differ from a plain program's by a relative error of at most 0.00098.
Values may be sent and summed in bfloat16 or wider, within the bound.
No kernel may reach another device: no remote copies, remote signals or barrier semaphores. Data moves between devices by JAX's collectives and lax.ppermute only.
A program may use at most 64 MiB of HBM per device.

v0:
```python
import jax
import jax.numpy as jnp
from jax import lax
from jax.sharding import PartitionSpec as P

ITERS = 2


def extended(cells, sides, width):
    for axis, dim in sides:
        count = lax.axis_size(axis)
        ends = count - 1
        head = lax.slice_in_dim(cells, 0, width, axis=dim)
        tail = lax.slice_in_dim(cells, cells.shape[dim] - width, cells.shape[dim], axis=dim)
        cells = jnp.concatenate(
            [
                lax.ppermute(tail, axis, [(i, (i + 1) % count) for i in range(ends)]),
                cells,
                lax.ppermute(head, axis, [((i + 1) % count, i) for i in range(ends)]),
            ],
            axis=dim,
        )
    return cells


def partner_2(array, axis, bit):
    return lax.ppermute(array, axis, [(i, i ^ 1 << bit) for i in range(lax.axis_size(axis))])


def band_blocks(profile, tile):
    taps_n = profile.shape[0]
    half = (taps_n - 1) // 2
    row_ids = jnp.arange(tile)[:, None]
    col_ids = jnp.arange(tile)[None, :]
    blocks = []
    for shift_no in (-1, 0, 1):
        offsets = shift_no * tile + row_ids - col_ids + half
        inside = (offsets >= 0) & (offsets < taps_n)
        entries = jnp.take(profile, jnp.clip(offsets, 0, taps_n - 1))
        blocks.append(jnp.where(inside, entries, jnp.float32(0.0)).astype(jnp.bfloat16))
    return blocks


def band_apply(rows_2d, stacked, tile):
    row_count = rows_2d.shape[0]
    tiles_n = rows_2d.shape[1] // tile
    product = jnp.dot(
        rows_2d.reshape(row_count * tiles_n, tile), stacked, preferred_element_type=jnp.float32
    )
    product = product.reshape(row_count, tiles_n, 3, tile)
    zero_tile = jnp.zeros((row_count, 1, tile), jnp.float32)
    from_prev = jnp.concatenate([zero_tile, product[:, :-1, 0]], axis=1)
    from_next = jnp.concatenate([product[:, 1:, 2], zero_tile], axis=1)
    result = product[:, :, 1] + from_prev + from_next
    return result.reshape(row_count, tiles_n * tile)


def smear(padded, taps, depth_n, height_n):
    result = jnp.zeros((depth_n, height_n, padded.shape[2]), jnp.float32)
    for tap_z in range(3):
        for tap_y in range(3):
            result = result + taps[tap_z, tap_y] * padded[
                tap_z : tap_z + depth_n, tap_y : tap_y + height_n
            ].astype(jnp.float32)
    return result


def spread(volume, taps):
    padded = extended(volume, (("gz", 0), ("gy", 1)), 1)
    return smear(padded, taps, volume.shape[0], volume.shape[1])


def shards(
    pieces, piece_owner, piece_row, estimate, psf_x, stencil, background, bleach_table, bleach_index
):
    depth_n = estimate.shape[0]
    height_n = estimate.shape[1]
    width = pieces.shape[3]
    per_dev = pieces.shape[1]
    gz_count = lax.axis_size("gz")
    gy_count = lax.axis_size("gy")
    blocks = gz_count * gy_count
    capacity = max(2, 2 * per_dev // blocks)
    tile = min(width, 256)
    owners = piece_owner[0, :, 0]
    piece_rows = piece_row[0]
    positions = jnp.arange(per_dev)
    same_owner = owners[:, None] == owners[None, :]
    earlier = positions[None, :] < positions[:, None]
    ranking = jnp.sum(same_owner & earlier, axis=1)
    slot_of = owners * capacity + ranking
    slot_ids = jnp.arange(blocks * capacity)
    picker = slot_ids[:, None] == slot_of[None, :]
    outgoing = jnp.dot(
        picker.astype(jnp.bfloat16),
        pieces[0].reshape(per_dev, height_n * width),
        preferred_element_type=jnp.float32,
    ).astype(jnp.bfloat16)
    send_rows = jnp.sum(jnp.where(picker, piece_rows[None, :] + 1, 0), axis=1) - 1
    incoming, incoming_rows = (
        lax.all_to_all(
            outgoing.reshape(blocks, capacity, height_n * width),
            ("gz", "gy"),
            split_axis=0,
            concat_axis=0,
            tiled=True,
        ),
        lax.all_to_all(
            send_rows.reshape(blocks, capacity),
            ("gz", "gy"),
            split_axis=0,
            concat_axis=0,
            tiled=True,
        ),
    )
    placer = jnp.arange(depth_n)[:, None] == incoming_rows.reshape(1, -1)
    measured = jnp.dot(
        placer.astype(jnp.bfloat16),
        incoming.reshape(-1, height_n * width),
        preferred_element_type=jnp.float32,
    ).reshape(depth_n, height_n, width)
    levels = jnp.arange(bleach_table.shape[1])
    matches = bleach_index[:, :, None] == levels[None, None, :]
    weight_all = jnp.sum(jnp.where(matches, bleach_table[:, None, :], jnp.float32(0.0)), axis=-1)
    total = jnp.sum(weight_all, axis=0)
    view_index = lax.axis_index("view")
    own_weight = lax.dynamic_index_in_dim(weight_all, view_index, 0, keepdims=False)
    lower, middle, upper = band_blocks(psf_x[0], tile)
    forward_stack = jnp.concatenate([lower, middle, upper], axis=1)
    backward_stack = jnp.concatenate([upper.T, middle.T, lower.T], axis=1)
    taps = stencil[0]
    flipped = taps[::-1, ::-1]
    bg_level = background[0]
    whole_est = lax.all_gather(estimate, "view", axis=2, tiled=True)
    for iteration in range(ITERS):
        blur_x = band_apply(whole_est.astype(jnp.bfloat16).reshape(-1, width), forward_stack, tile)
        blurred = spread(blur_x.astype(jnp.bfloat16).reshape(depth_n, height_n, width), taps)
        ratio = (measured / (blurred + bg_level)).astype(jnp.bfloat16)
        partner = partner_2(ratio, "view", 1)
        mixed = (
            0.5 * (ratio.astype(jnp.float32) + partner[:, :, ::-1].astype(jnp.float32))
        ).astype(jnp.bfloat16)
        back_x = band_apply(mixed.reshape(-1, width), backward_stack, tile)
        corrected = spread(back_x.astype(jnp.bfloat16).reshape(depth_n, height_n, width), flipped)
        weighted = own_weight[:, None, None] * corrected
        numerator = lax.psum(weighted, "view")
        whole_est = whole_est * numerator / total[:, None, None]
    columns = estimate.shape[2]
    return lax.dynamic_slice_in_dim(whole_est, view_index * columns, columns, 2)


def solution(mesh):
    placed = (
        P("view", ("gz", "gy"), None, None),
        P("view", ("gz", "gy"), None),
        P("view", ("gz", "gy")),
        P("gz", "gy", "view"),
        P("view", None),
        P("view", None, None),
        P("view"),
        P(),
        P(None, "gz"),
    )
    return jax.shard_map(
        shards, mesh=mesh, in_specs=placed, out_specs=P("gz", "gy", "view"), check_vma=False
    )
```

profile of v0, /device:TPU:1, one launch (start us, length us, event | category | flops | bytes accessed | tf_op | source)
XLA Modules:
  0.0 1435.6 jit_solution(8668029683732731288)
XLA Ops:
  7.2 402.0 %gather_fusion.2 = bf16[65536]{0:T(1024)(128)(2,1)S(1)} fusion(bf16[257]{0:T(512)(128)(2,1)S(1)} %reduce.2, s32[65536]{0:T(1024)S(1)} %broadcast_clamp_fusion), kind=kCustom, calls=%fused_computation.2.clone | custom fusion | bytes 524288 | tf_op jit(solution)/shard_map/jit(_take)/gather | solution.py:39
  409.5 402.1 %gather_fusion.1 = bf16[65536]{0:T(1024)(128)(2,1)S(1)} fusion(bf16[257]{0:T(512)(128)(2,1)S(1)} %reduce.2, s32[65536]{0:T(1024)S(1)} %broadcast_clamp_fusion.1), kind=kCustom, calls=%fused_computation.1.clone | custom fusion | bytes 524288 | tf_op jit(solution)/shard_map/jit(_take)/gather | solution.py:39
  812.0 402.1 %gather_fusion = bf16[65536]{0:T(1024)(128)(2,1)S(1)} fusion(bf16[257]{0:T(512)(128)(2,1)S(1)} %reduce.2, s32[65536]{0:T(1024)S(1)} %broadcast_clamp_fusion.2), kind=kCustom, calls=%fused_computation.clone | custom fusion | bytes 524288 | tf_op jit(solution)/shard_map/jit(_take)/gather | solution.py:39
  1214.4 13.3 all_gather.3
  1230.0 3.1 collective-permute-start
  1235.4 7.5 all-to-all-start
  1246.8 4.2 all-to-all-start.1
  1252.4 3.5 collective-permute-start.2
  1255.9 1.9 collective-permute-start.3
  1257.8 6.7 all-to-all-done.1
  1265.3 6.0 divide_convert_fusion.1
  1272.0 7.4 collective-permute-done.4
  1281.3 3.1 collective-permute-start.5
  1286.1 3.3 collective-permute-done.6
  1289.5 5.0 collective-permute-start.7
  1294.4 1.9 collective-permute-start.8
  1296.4 3.5 collective-permute-done.8
  1299.9 6.6 add_multiply_fusion.1
  1306.8 30.8 %all-reduce.11.cloned.1.call-done = f32[4,8,2048]{2,1,0:T(8,128)} async-done(((f32[4,8,2048]{2,1,0:T(8,128)}), f32[4,8,2048]{2,1,0:T(8,128)}) %all-reduce.11.cloned.1.call-update) | async-done | bytes 262160 | tf_op jit(solution)/shard_map/psum | solution.py:146
  1339.1 3.1 collective-permute-start.9
  1343.6 3.3 collective-permute-done.10
  1347.0 6.5 collective-permute-start.11
  1353.5 1.9 collective-permute-start.12
  1355.5 3.5 collective-permute-done.12
  1358.9 6.0 divide_convert_fusion
  1364.9 1.9 collective-permute-start.13
  1366.9 5.2 collective-permute-done.13
  1376.8 3.3 collective-permute-done.15
  1380.2 3.5 collective-permute-start.16
  1385.6 3.5 collective-permute-done.17
  1389.1 6.6 add_multiply_fusion
  1395.8 31.5 %all-reduce.13.cloned.1.call-done = f32[4,8,2048]{2,1,0:T(8,128)} async-done(((f32[4,8,2048]{2,1,0:T(8,128)}), f32[4,8,2048]{2,1,0:T(8,128)}) %all-reduce.13.cloned.1.call-update) | async-done | bytes 262160 | tf_op jit(solution)/shard_map/psum | solution.py:146
  (137 shorter events, 26.8 us)
Async XLA Ops:
  6.5 0.7 copy-start
  812.0 402.4 %copy-start.2 = (f32[4,8,512]{2,1,0:T(8,128)S(1)}, f32[4,8,512]{2,1,0:T(8,128)}, u32[]{:S(2)}) copy-start(f32[4,8,512]{2,1,0:T(8,128)} %param.14) | copy-start | bytes 196612
  1229.7 4.7 copy-start.6
  1229.7 4.9 copy-start.7
  1229.7 13.2 copy-start.5
  1229.7 13.2 copy-start.1
  1230.0 22.3 %collective-permute-start = (bf16[1,8,2048]{2,1,0:T(8,128)(2,1)S(1)}, bf16[1,8,2048]{2,1,0:T(8,128)(2,1)S(1)}, u32[]{:S(2)}, u32[]{:S(2)}) collective-permute-start(bf16[1,8,2048]{2,1,0:T(8,128)(2,1)S(1)} %slice.313), channel_id=1, source_target_pairs={{0,4},{1,5},{2,6},{3,7},{8,12},{9,13},{10,14},{11,15},{16,20},{17,... | collective-permute-start | bytes 98312 | tf_op jit(solution)/shard_map/ppermute | solution.py:17
  1233.1 19.1 %collective-permute-start.1 = (bf16[1,8,2048]{2,1,0:T(8,128)(2,1)S(1)}, bf16[1,8,2048]{2,1,0:T(8,128)(2,1)S(1)}, u32[]{:S(2)}, u32[]{:S(2)}) collective-permute-start(bf16[1,8,2048]{2,1,0:T(8,128)(2,1)S(1)} %slice.315), channel_id=1, source_target_pairs={{4,0},{5,1},{6,2},{7,3},{12,8},{13,9},{14,10},{15,11},{20,16},{21,... | collective-permute-start | bytes 98312 | tf_op jit(solution)/shard_map/ppermute | solution.py:19
  1235.4 11.4 all-to-all-start
  1246.8 17.8 %all-to-all-start.1 = ((bf16[8,4,16384]{2,1,0:T(4,128)(2,1)}), bf16[8,4,16384]{2,1,0:T(4,128)(2,1)S(1)}, u32[]{:S(2)}, u32[]{:S(2)}) async-start(bf16[8,4,16384]{2,1,0:T(4,128)(2,1)} %reshape.116), calls=%async_computation.1 | async-start | bytes 2097152 | tf_op jit(solution)/shard_map/all_to_all | solution.py:101
  1251.0 86.6 %all-reduce.11.cloned.1.call-start = ((), (), s32[]{:S(2)}) async-start(), calls=%async_computation.2 | async-start | bytes 524288 | tf_op jit(solution)/shard_map/psum | solution.py:146
  1252.4 12.8 collective-permute-start.2
  1255.9 9.4 collective-permute-start.3
  1271.3 8.1 collective-permute-start.4
  1281.1 3.3 copy-start.3
  1281.1 3.3 copy-start.4
  1281.3 4.8 collective-permute-start.5
  1284.8 4.7 collective-permute-start.6
  1289.5 6.9 collective-permute-start.7
  1294.4 5.4 collective-permute-start.8
  1306.5 120.7 %all-reduce.13.cloned.1.call-start = ((), (), s32[]{:S(2)}) async-start(), calls=%async_computation.3 | async-start | bytes 524288 | tf_op jit(solution)/shard_map/psum | solution.py:146
  1339.1 4.5 collective-permute-start.9
  1342.3 4.7 collective-permute-start.10
  1347.0 8.4 collective-permute-start.11
  1353.5 5.4 collective-permute-start.12
  1364.9 7.2 collective-permute-start.13
  1374.0 2.7 collective-permute-start.14
  1375.5 4.7 collective-permute-start.15
  1380.2 5.4 collective-permute-start.16
  1383.7 5.4 collective-permute-start.17
Sparse Core Ops, SparseCore 0:
  1306.6 30.8 all-reduce.10
  1395.9 31.3 all-reduce.12
where the time goes:
time: 1440 us
  local copies, waits for them, and re-layouts  1220 us (85%)
  waiting for transfers between devices  103 us (7%)
  starting transfers between devices  56.1 us (4%)
  other arithmetic  30.7 us (2%)
  between operations  15 us (1%)
    gather x6, local copies, waits for them, and re-layouts, band_blocks(): entries = jnp.take(profile, jnp.clip(offsets, 0, taps_n - 1))  1210 us
    psum x2, waiting for transfers between devices, shards(): numerator = lax.psum(weighted, 'view')  62.3 us
    ppermute x8, starting transfers between devices, extended(): lax.ppermute(tail, axis, [(i, (i + 1) % count) for i in range(ends)])  29.1 us
  transfers between devices with their start and end apart: 22, of which 13 were waited for; matrix products, arithmetic and copies ran while one was open for 0% of the time, Pallas kernels for 0%

commit v1 on v0

v1 whole, which is shorter than its diff:
```python
import functools

import jax
import jax.numpy as jnp
from jax import lax
from jax.experimental import pallas as pl
from jax.experimental.pallas import tpu as pltpu
from jax.sharding import PartitionSpec as P

BF = jnp.bfloat16
F32 = jnp.float32
TILE = 256
LIMIT = 56 << 20


def whole(*spaces):
    return [pl.BlockSpec(memory_space=space) for space in spaces]


def swap(array, axis, size, mask):
    return lax.ppermute(array, axis, [(i, i ^ mask) for i in range(size)])


def upward(array, axis, size):
    return lax.ppermute(array, axis, [(i, i + 1) for i in range(size - 1)])


def downward(array, axis, size):
    return lax.ppermute(array, axis, [(i + 1, i) for i in range(size - 1)])


class Frame:
    def __init__(self, slabs, depth):
        self.mirrored = slabs == 2
        self.depth = depth
        self.own = 0 if self.mirrored else depth
        self.size = 2 * depth if self.mirrored else 3 * depth

    def need(self, radius):
        return range(
            max(0, self.own - radius), min(self.size, self.own + self.depth + radius)
        )

    def source(self, f):
        k = f - self.own
        if 0 <= k < self.depth:
            return "own", k
        if self.mirrored:
            return "up", 2 * self.depth - 1 - k
        return ("dn", f) if k < 0 else ("up", k - self.depth)

    def sent(self, radius):
        if self.mirrored:
            return {"up": range(self.depth - radius, self.depth)}
        return {
            "dn": range(self.depth - radius, self.depth),
            "up": range(0, radius),
        }


def exchange_z(frame, make, slabs, radius):
    got = {}
    for side, slices in frame.sent(radius).items():
        payload = make(slices)
        if frame.mirrored:
            got[side] = swap(payload, "gz", slabs, 1)
        elif side == "dn":
            got[side] = upward(payload, "gz", slabs)
        else:
            got[side] = downward(payload, "gz", slabs)
    return got


def cells_kernel(pairs, cell_ref, pieces_ref, even_ref, odd_ref, acc):
    count = pieces_ref.shape[0]

    def clear(i, carry):
        acc[i] = jnp.zeros(acc.shape[1:], F32)
        return carry

    lax.fori_loop(0, acc.shape[0], clear, 0)

    def add(i, carry):
        c = cell_ref[i]
        acc[c] = acc[c] + pieces_ref[i].astype(F32)
        return carry

    lax.fori_loop(0, count, add, 0)
    depth = even_ref.shape[1]

    def put(i, carry):
        pair = i // depth
        f = i % depth
        even_ref[pair, f] = acc[pair * 2 * depth + f].astype(BF)
        odd_ref[pair, f] = acc[(pair * 2 + 1) * depth + f].astype(BF)
        return carry

    lax.fori_loop(0, pairs * depth, put, 0)


def reversal():
    rows = lax.broadcasted_iota(jnp.int32, (TILE, TILE), 0)
    cols = lax.broadcasted_iota(jnp.int32, (TILE, TILE), 1)
    return jnp.where(rows + cols == TILE - 1, F32(1.0), F32(0.0)).astype(BF)


def total_kernel(parts, *refs):
    ins, (out_ref, rev_ref) = refs[:parts], refs[parts:]
    tiles = out_ref.shape[0]
    flip = reversal()
    for t in range(tiles):
        cut = slice(t * TILE, (t + 1) * TILE)
        acc = ins[0][:, :, cut].astype(F32)
        for ref in ins[1:]:
            acc = acc + ref[:, :, cut].astype(F32)
        block = acc.reshape(out_ref.shape[1:]).astype(BF)
        out_ref[t] = block
        rev_ref[tiles - 1 - t] = jnp.dot(
            block, flip, preferred_element_type=F32
        ).astype(BF)


def band(base_row):
    wide = jnp.broadcast_to(base_row, (TILE, 3 * TILE))
    return pltpu.roll(wide, 0, 1, stride=1, stride_axis=0).astype(BF)


def conv(src, first, tiles, rows, blocks, dst, step):
    s = 0
    while s < tiles:
        n = min(step, tiles - s)
        lhs = jnp.concatenate(
            [
                src[pl.ds(first + s + k, n)].reshape(n * rows, TILE)
                for k in range(3)
            ],
            axis=1,
        )
        dst[s : s + n] = jnp.dot(lhs, blocks, preferred_element_type=F32).reshape(
            n, rows, TILE
        )
        s += n


def taps_sum(slices, zs, taps):
    result = {}
    for z in zs:
        sums = [None, None, None]
        for j in range(3):
            for i in range(3):
                at = z + i - 1
                if at in slices:
                    term = taps(z, i, j) * slices[at]
                    sums[j] = term if sums[j] is None else sums[j] + term
        result[z] = sums
    return result


def along_y(sums):
    n = sums[0].shape[0]
    return pltpu.roll(sums[0], 1, 0) + sums[1] + pltpu.roll(sums[2], n - 1, 0)


def forward_kernel(
    frame, tiles, sides, num_ref, base_ref, own_ref, *refs
):
    halo_ref = refs[len(sides)]
    side_refs = dict(zip(sides, refs[: len(sides)]))
    blocks_ref, recip_ref, frame_ref, u, c = refs[len(sides) + 1 :]
    size = frame.size
    rows = size * 16
    flip = reversal()
    for v in range(4):
        fwd = band(base_ref[v : v + 1, :])
        bwd = band(base_ref[4 + v : 5 + v, :])
        f3 = [fwd[:, 2 * TILE :], fwd[:, TILE : 2 * TILE], fwd[:, :TILE]]
        b3 = [bwd[:, 2 * TILE :], bwd[:, TILE : 2 * TILE], bwd[:, :TILE]]
        if v >= 2:
            f3 = [
                jnp.dot(x, flip, preferred_element_type=F32).astype(BF) for x in f3
            ]
            b3 = [
                jnp.dot(flip, x, preferred_element_type=F32).astype(BF)
                for x in b3[::-1]
            ]
        for k in range(3):
            blocks_ref[v, 0, k * TILE : (k + 1) * TILE, :] = f3[k]
            blocks_ref[v, 1, k * TILE : (k + 1) * TILE, :] = b3[k]
    u[0] = jnp.zeros((rows, TILE), BF)
    u[tiles + 1] = jnp.zeros((rows, TILE), BF)

    def fill(t, carry):
        for f in range(size):
            where, k = frame.source(f)
            src = own_ref if where == "own" else side_refs[where]
            both = jnp.concatenate(
                [
                    src[t, k * 8 : (k + 1) * 8, :].astype(F32),
                    halo_ref[t, f * 8 : (f + 1) * 8, :].astype(F32),
                ],
                axis=0,
            ).astype(BF)
            u[t + 1, f * 16 : (f + 1) * 16, :] = both
            frame_ref[t, f * 16 : (f + 1) * 16, :] = both
        return carry

    lax.fori_loop(0, tiles, fill, 0)
    zs = frame.need(3)
    for v in range(4):
        conv(u, 0, tiles, rows, blocks_ref[v, 0], c, 2)

        def divide(t, carry, v=v):
            from_t = t if v < 2 else tiles - 1 - t
            for h in range(TILE // 128):
                cut = slice(h * 128, (h + 1) * 128)
                slices = {
                    f: c[from_t, f * 16 : (f + 1) * 16, cut] for f in range(size)
                }
                sums = taps_sum(slices, zs, lambda z, i, j: num_ref[v * 9 + i * 3 + j])
                for n, z in enumerate(zs):
                    recip_ref[v, t, n * 16 : (n + 1) * 16, cut] = (
                        1.0 / (along_y(sums[z]) + num_ref[36 + v])
                    ).astype(BF)
            return carry

        lax.fori_loop(0, tiles, divide, 0)


def main_kernel(frame, tiles, sides, int_ref, num_ref, wt_ref, est_ref, *refs):
    own_refs = refs[:4]
    side_refs = dict(zip(sides, refs[4 : 4 + len(sides)]))
    halo_ref, blocks_ref, recip_ref, frame_ref, out_ref = refs[
        4 + len(sides) : 9 + len(sides)
    ]
    m1, u2, m2, c0, c1, c2, c3, kept = refs[9 + len(sides) :]
    c = [c0, c1, c2, c3]
    view, upside = int_ref[0], int_ref[1]
    depth = frame.depth
    z3, z2, z1, z0 = (frame.need(r) for r in (3, 2, 1, 0))
    skip = {
        side: min(slices) for side, slices in frame.sent(3).items()
    }
    meas_at = {z: n for n, z in enumerate(z3)}

    def measured(v, t, z, cut):
        where, k = frame.source(z)
        n = meas_at[z]
        if where == "own":
            own = own_refs[v][t, k * 8 : (k + 1) * 8, cut]
        else:
            k = k - skip[where]
            own = side_refs[where][v, t, k * 8 : (k + 1) * 8, cut]
        return jnp.concatenate(
            [
                own.astype(F32),
                halo_ref[v, t, n * 8 : (n + 1) * 8, cut].astype(F32),
            ],
            axis=0,
        )

    def mix(v, t, z, cut, recip_a, recip_b):
        a = (measured(v, t, z, cut) * recip_a).astype(BF).astype(F32)
        b = (measured(v + 2, t, z, cut) * recip_b).astype(BF).astype(F32)
        return (0.5 * (a + b)).astype(BF)

    def zero_ends(ref):
        for e in (0, ref.shape[0] - 1):
            ref[e] = jnp.zeros(ref.shape[1:], BF)

    for ref in (m1, u2, m2):
        zero_ends(ref)

    for v in range(2):

        def ratios(t, carry, v=v):
            for h in range(TILE // 128):
                cut = slice(h * 128, (h + 1) * 128)
                for n, z in enumerate(z3):
                    at = slice(n * 16, (n + 1) * 16)
                    m1[t + 1, at, cut] = mix(
                        v,
                        t,
                        z,
                        cut,
                        recip_ref[v, t, at, cut].astype(F32),
                        recip_ref[v + 2, t, at, cut].astype(F32),
                    )
            return carry

        lax.fori_loop(0, tiles, ratios, 0)
        for w in (v, v + 2):
            conv(m1, 0, tiles, m1.shape[1], blocks_ref[w, 1], c[w], 2)

    def numerator(slices_of, zs):
        totals = {z: [None, None, None] for z in zs}
        for v in range(4):
            slices = slices_of(v)
            sums = taps_sum(
                slices,
                zs,
                lambda z, i, j, v=v: wt_ref[(v * frame.size + z) * 9 + i * 3 + j],
            )
            for z in zs:
                for j in range(3):
                    old = totals[z][j]
                    totals[z][j] = sums[z][j] if old is None else old + sums[z][j]
        return totals

    def update(t, carry):
        for h in range(TILE // 128):
            cut = slice(h * 128, (h + 1) * 128)

            def slices_of(v):
                from_t = t if v < 2 else tiles - 1 - t
                return {
                    z: c[v][from_t, n * 16 : (n + 1) * 16, cut]
                    for n, z in enumerate(z3)
                }

            totals = numerator(slices_of, z2)
            for n, z in enumerate(z2):
                change = along_y(totals[z])
                before = frame_ref[t, z * 16 : (z + 1) * 16, cut].astype(F32)
                u2[t + 1, n * 16 : (n + 1) * 16, cut] = (before * change).astype(BF)
                if z in z0:
                    k = z - frame.own
                    kept[t, k * 8 : (k + 1) * 8, cut] = change[:8]
        return carry

    lax.fori_loop(0, tiles, update, 0)

    rows1 = m2.shape[1]
    n2 = u2.shape[1]
    for v in range(2):
        for w in (v, v + 2):
            conv(u2, 0, tiles, n2, blocks_ref[w, 0], c[w].at[:, :n2, :], 2)

        def ratios2(t, carry, v=v):
            for h in range(TILE // 128):
                cut = slice(h * 128, (h + 1) * 128)
                recips = []
                for w in (v, v + 2):
                    from_t = t if w < 2 else tiles - 1 - t
                    slices = {
                        z: c[w][from_t, n * 16 : (n + 1) * 16, cut]
                        for n, z in enumerate(z2)
                    }
                    sums = taps_sum(
                        slices, z1, lambda z, i, j, w=w: num_ref[w * 9 + i * 3 + j]
                    )
                    recips.append(
                        {z: 1.0 / (along_y(sums[z]) + num_ref[36 + w]) for z in z1}
                    )
                for n, z in enumerate(z1):
                    m2[t + 1, n * 16 : (n + 1) * 16, cut] = mix(
                        v, t, z, cut, recips[0][z], recips[1][z]
                    )
            return carry

        lax.fori_loop(0, tiles, ratios2, 0)
        mine = tiles // 4
        for w in (v, v + 2):
            first = view * mine if w < 2 else tiles - (view + 1) * mine
            conv(m2, first, mine, rows1, blocks_ref[w, 1], c[w].at[:, :rows1, :], 2)

    mine = tiles // 4
    for s in range(mine):
        for h in range(TILE // 128):
            cut = slice(h * 128, (h + 1) * 128)

            def slices_of(v):
                from_s = s if v < 2 else mine - 1 - s
                return {
                    z: c[v][from_s, n * 16 : (n + 1) * 16, cut]
                    for n, z in enumerate(z1)
                }

            totals = numerator(slices_of, z0)
            for z in z0:
                k = z - frame.own
                to = k + upside * (depth - 1 - 2 * k)
                lanes = slice(s * TILE + h * 128, s * TILE + (h + 1) * 128)
                first_change = kept[view * mine + s, k * 8 : (k + 1) * 8, cut]
                out_ref[to, :, lanes] = (
                    est_ref[to, :, lanes] * first_change * along_y(totals[z])[:8]
                )


def shards(
    pieces, piece_owner, piece_row, estimate, psf_x, stencil, background, bleach_table, bleach_index
):
    depth, height = estimate.shape[:2]
    chunk = estimate.shape[2]
    width = pieces.shape[3]
    tiles = width // TILE
    slabs = lax.axis_size("gz")
    bands = lax.axis_size("gy")
    blocks = slabs * bands
    frame = Frame(slabs, depth)
    view = lax.axis_index("view")
    slab = lax.axis_index("gz")
    me = slab * bands + lax.axis_index("gy")
    upside = (slab if frame.mirrored else 0 * slab).astype(jnp.int32)
    vmem, smem = pltpu.VMEM, pltpu.SMEM
    params = pltpu.CompilerParams(vmem_limit_bytes=LIMIT)

    turned = jnp.where(upside == 1, estimate[::-1], estimate).astype(BF)
    half = (psf_x.shape[1] - 1) // 2
    profile = psf_x[0].astype(BF)
    exact = jnp.concatenate(
        [
            jnp.where(upside == 1, stencil[0][::-1], stencil[0]).reshape(-1),
            background,
        ]
    )
    part0 = lax.reduce_precision(exact, 8, 7)
    part1 = lax.reduce_precision(exact - part0, 8, 7)
    part2 = lax.reduce_precision(exact - part0 - part1, 8, 7)

    def row(x):
        return jnp.pad(x, (0, chunk - x.shape[0]))[None]

    extra = jnp.concatenate(
        [row(profile), row(profile[::-1])]
        + [row(x.astype(BF)) for x in (part0, part1, part2)]
        + [jnp.zeros((3, chunk), BF)],
        axis=0,
    )
    payload = jnp.concatenate([turned.reshape(depth * height, chunk), extra], axis=0)
    heard = [payload] + [swap(payload, "view", 4, mask) for mask in (1, 2, 3)]
    heard = jnp.stack(heard)
    numbers = heard[:, depth * height :]
    parts = numbers[:, 2:5, :10].astype(F32)
    exacts = parts[:, 0] + parts[:, 1] + parts[:, 2]
    taps_all = exacts[:, :9]
    nums = jnp.concatenate([taps_all.reshape(-1), exacts[:, 9]])
    edge = TILE - half
    base = jnp.pad(
        jnp.concatenate([numbers[:, 1, : 2 * half + 1], numbers[:, 0, : 2 * half + 1]]),
        ((0, 0), (edge, 3 * TILE - edge - 2 * half - 1)),
    ).astype(F32)

    def ordered(x):
        a = jnp.where(view % 2 == 1, jnp.stack([x[1], x[0], x[3], x[2]]), x)
        return jnp.where(view // 2 == 1, jnp.concatenate([a[2:], a[:2]]), a)

    own_est = ordered(
        heard[:, : depth * height]
        .reshape(4, depth * height, chunk // TILE, TILE)
        .transpose(0, 2, 1, 3)
    ).reshape(tiles, depth * height, TILE)

    index_own = jnp.where(upside == 1, bleach_index[:, ::-1], bleach_index)
    index_far = exchange_z(
        frame, lambda s: index_own[:, s.start : s.stop], slabs, depth
    )

    def frame_index(f):
        where, k = frame.source(f)
        return (index_own if where == "own" else index_far[where])[:, k]

    indices = jnp.stack([frame_index(f) for f in range(frame.size)], axis=1)
    levels = jnp.arange(bleach_table.shape[1])
    matches = indices[:, :, None] == levels[None, None, :]
    weight = jnp.sum(jnp.where(matches, bleach_table[:, None, :], F32(0.0)), axis=-1)
    share = ordered(weight / jnp.sum(weight, axis=0))
    weighted = (share[:, :, None] * taps_all[:, ::-1][:, None, :]).reshape(-1)

    sides = tuple(frame.sent(1))
    far_est = exchange_z(
        frame,
        lambda s: own_est[:, s.start * height : s.stop * height],
        slabs,
        depth,
    )

    def z_list(own, far, radius):
        first = {side: min(s) for side, s in frame.sent(radius).items()}
        picked = []
        for f in frame.need(radius):
            where, k = frame.source(f)
            if where == "own":
                picked.append(own[..., k * height : (k + 1) * height, :])
            else:
                k = k - first[where]
                picked.append(far[where][..., k * height : (k + 1) * height, :])
        return jnp.stack(picked, axis=-3)

    def y_halo(stacked):
        hi = downward(stacked[..., : height // 2, :], "gy", bands)
        lo = upward(stacked[..., height // 2 :, :], "gy", bands)
        tile = jnp.concatenate([hi, lo], axis=-2)
        return tile.reshape(tile.shape[:-3] + (-1, TILE))

    halo_est = y_halo(z_list(own_est, far_est, depth))
    size = frame.size
    blocks_all, recip, est_frame = pl.pallas_call(
        functools.partial(forward_kernel, frame, tiles, sides),
        out_shape=(
            jax.ShapeDtypeStruct((4, 2, 3 * TILE, TILE), BF),
            jax.ShapeDtypeStruct((4, tiles, len(frame.need(3)) * 16, TILE), BF),
            jax.ShapeDtypeStruct((tiles, size * 16, TILE), BF),
        ),
        in_specs=whole(smem, *([vmem] * (3 + len(sides)))),
        out_specs=whole(vmem, vmem, vmem),
        scratch_shapes=[
            vmem((tiles + 2, size * 16, TILE), BF),
            vmem((tiles, size * 16, TILE), F32),
        ],
        compiler_params=params,
    )(nums, base, own_est, *[far_est[s] for s in sides], halo_est)

    owners = piece_owner[0, :, 0]
    rows = piece_row[0]
    if frame.mirrored:
        rows = jnp.where(owners // bands == 1, depth - 1 - rows, rows)
    cell = (owners ^ me) * depth + rows
    pairs = blocks // 2
    half_cells = jax.ShapeDtypeStruct((pairs, depth, height, width), BF)
    even, odd = pl.pallas_call(
        functools.partial(cells_kernel, pairs),
        out_shape=(half_cells, half_cells),
        in_specs=whole(smem, vmem),
        out_specs=whole(vmem, vmem),
        scratch_shapes=[vmem((blocks * depth, height, width), F32)],
        compiler_params=params,
    )(cell, pieces[0])
    other = swap(odd, "gy", bands, 1)
    kept = [even[k] + other[k] for k in range(pairs)]
    kept = kept[:1] + [
        swap(kept[k], ("gz", "gy"), blocks, 2 * k) for k in range(1, pairs)
    ]
    block = jax.ShapeDtypeStruct((tiles, depth * height, TILE), BF)
    plain, turned_x = pl.pallas_call(
        functools.partial(total_kernel, pairs),
        out_shape=(block, block),
        in_specs=whole(*([vmem] * pairs)),
        out_specs=whole(vmem, vmem),
        compiler_params=params,
    )(*kept)
    views = [
        plain,
        swap(plain, "view", 4, 1),
        swap(turned_x, "view", 4, 2),
        swap(turned_x, "view", 4, 3),
    ]
    far = exchange_z(
        frame,
        lambda s: jnp.stack([x[:, s.start * height : s.stop * height] for x in views]),
        slabs,
        3,
    )
    halo = y_halo(
        jnp.stack(
            [
                z_list(x, {s: far[s][v] for s in sides}, 3)
                for v, x in enumerate(views)
            ]
        )
    )
    ints = jnp.stack([view.astype(jnp.int32), upside])
    n3, n2, n1 = (len(frame.need(r)) * 16 for r in (3, 2, 1))
    return pl.pallas_call(
        functools.partial(main_kernel, frame, tiles, sides),
        out_shape=jax.ShapeDtypeStruct(estimate.shape, F32),
        in_specs=whole(smem, smem, smem, *([vmem] * (9 + len(sides)))),
        out_specs=pl.BlockSpec(memory_space=vmem),
        scratch_shapes=[
            vmem((tiles + 2, n3, TILE), BF),
            vmem((tiles + 2, n2, TILE), BF),
            vmem((tiles + 2, n1, TILE), BF),
        ]
        + [vmem((tiles, n3, TILE), F32)] * 4
        + [vmem((tiles, depth * height, TILE), F32)],
        compiler_params=params,
    )(
        ints,
        nums,
        weighted,
        estimate,
        *views,
        *[far[s] for s in sides],
        halo,
        blocks_all,
        recip,
        est_frame,
    )


def solution(mesh):
    placed = (
        P("view", ("gz", "gy"), None, None),
        P("view", ("gz", "gy"), None),
        P("view", ("gz", "gy")),
        P("gz", "gy", "view"),
        P("view", None),
        P("view", None, None),
        P("view"),
        P(),
        P(None, "gz"),
    )
    return jax.shard_map(
        shards, mesh=mesh, in_specs=placed, out_specs=P("gz", "gy", "view"), check_vma=False
    )
```

time: 1440 us -> 101 us (0.07)
  local copies, waits for them, and re-layouts: 1220 us -> 8.93 us
  waiting for transfers between devices: 103 us -> 23.2 us
  Pallas kernels: 0 us -> 27.9 us
  starting transfers between devices: 56.1 us -> 28.5 us
  other arithmetic: 30.7 us -> 10.8 us
    gather x6 -> x0, local copies, waits for them, and re-layouts: 1210 us -> none  [band_blocks(): entries = jnp.take(profile, jnp.clip(offsets, 0, taps_n - 1))]
    psum x2 -> x0, waiting for transfers between devices: 62.3 us -> none  [shards(): numerator = lax.psum(weighted, 'view')]
    pallas_call x0 -> x4, Pallas kernels: none -> 27.9 us  [the longest x1 13.5 us: shards(): pl.pallas_call(functools.partial(main_kernel, frame, tiles, sides), out_s...]
    ppermute x18 -> x17, starting transfers between devices: 44.3 us -> 28.5 us  [the longest x13 14.8 us: swap(): return lax.ppermute(array, axis, [(i, i ^ mask) for i in range(size)])]
    ppermute x18 -> x17, waiting for transfers between devices: 33.2 us -> 23.2 us  [the longest x13 23.2 us: swap(): return lax.ppermute(array, axis, [(i, i ^ mask) for i in range(size)])]
  transfers between devices with their start and end apart: 22 -> 17, of which waited for: 13 -> 6; matrix products, arithmetic and copies ran while one was open for 0% -> 13% of each run, Pallas kernels for 0% -> 12%
where the time goes in v1:
time: 101 us
  starting transfers between devices  28.5 us (28%)
  Pallas kernels  27.9 us (28%)
  waiting for transfers between devices  23.2 us (23%)
  other arithmetic  10.8 us (11%)
  local copies, waits for them, and re-layouts  8.93 us (9%)
  between operations  1.26 us (1%)
    ppermute x13, waiting for transfers between devices, swap(): return lax.ppermute(array, axis, [(i, i ^ mask) for i in range(size)])  23.2 us
    ppermute x13, starting transfers between devices, swap(): return lax.ppermute(array, axis, [(i, i ^ mask) for i in range(size)])  14.8 us
    pallas_call x1, Pallas kernels, shards(): pl.pallas_call(functools.partial(main_kernel, frame, tiles, sides), out_s...  13.5 us
    pallas_call x1, Pallas kernels, shards(): pl.pallas_call(functools.partial(forward_kernel, frame, tiles, sides), ou...  9.71 us
    ppermute x2, starting transfers between devices, upward(): return lax.ppermute(array, axis, [(i, i + 1) for i in range(size - 1)])  7.21 us
    ppermute x2, starting transfers between devices, downward(): return lax.ppermute(array, axis, [(i + 1, i) for i in range(size - 1)])  6.49 us
    unnamed x54, local copies, waits for them, and re-layouts  4.77 us
    pallas_call x1, Pallas kernels, shards(): pl.pallas_call(functools.partial(cells_kernel, pairs), out_shape=(half_ce...  2.64 us
  transfers between devices with their start and end apart: 17, of which 6 were waited for; matrix products, arithmetic and copies ran while one was open for 13% of the time, Pallas kernels for 12%

profile of v1, /device:TPU:1, one launch (start us, length us, event | category | flops | bytes accessed | tf_op | source)
XLA Modules:
  0.0 100.7 jit_solution(6683005267890475982)
XLA Ops:
  0.7 0.7 convert_reduce_fusion
  3.2 0.9 fusion.5
  4.2 4.2 %collective-permute-start.2 = (bf16[40,512]{1,0:T(8,128)(2,1)S(1)}, bf16[40,512]{1,0:T(8,128)(2,1)S(1)}, u32[]{:S(2)}, u32[]{:S(2)}) collective-permute-start(bf16[40,512]{1,0:T(8,128)(2,1)S(1)} %concatenate.33), channel_id=1, source_target_pairs={{0,24},{8,16},{16,8},{24,0},{1,25},{9,17},{17,9},{25,1},{2,26},{10... | collective-permute-start | bytes 122888 | tf_op jit(solution)/shard_map/ppermute | solution.py:21
  8.8 0.8 rev.18
  10.8 1.2 %fusion.14.cell_ref = s32[16]{0:T(128)} fusion(s32[1,16]{1,0:T(1,128)} %param.11, s32[1,16,1]{1,2,0:T(1,128)} %param.10, s32[]{:T(128)S(6)} %add.62), kind=kLoop, calls=%fused_computation.135 | loop fusion | flops 336 | bytes 196 | tf_op jit(solution)/shard_map/add | solution.py:517
  12.0 2.6 %shard_map.91 = (bf16[4,4,8,2048]{3,2,1,0:T(8,128)(2,1)}, bf16[4,4,8,2048]{3,2,1,0:T(8,128)(2,1)}) custom-call(s32[16]{0:T(128)} %fusion.14.cell_ref, bf16[16,8,2048]{2,1,0:T(8,128)(2,1)} %bitcast.223), custom_call_target="tpu_custom_call" | custom-call | tf_op jit(solution)/shard_map/pallas_call | solution.py:520
  14.7 1.7 %collective-permute-start.4 = (bf16[4,4,8,2048]{3,2,1,0:T(8,128)(2,1)}, bf16[4,4,8,2048]{3,2,1,0:T(8,128)(2,1)S(1)}, u32[]{:S(2)}, u32[]{:S(2)}) collective-permute-start(bf16[4,4,8,2048]{3,2,1,0:T(8,128)(2,1)} %get-tuple-element.13), channel_id=1, source_target_pairs={{0,1},{1,0},{2,3},{3,2},{4,5},{5,4},{6,7},{7,6},{8,9},{9,8},{10,11... | collective-permute-start | bytes 1572872 | tf_op jit(solution)/shard_map/ppermute | solution.py:21
  17.2 0.9 select_reduce_fusion
  19.1 0.8 collective-permute-start.14
  20.4 3.9 %collective-permute-done.14.refs_0_ = bf16[8,32,256]{2,1,0:T(8,128)(2,1)S(1)} collective-permute-done((bf16[8,32,256]{2,1,0:T(8,128)(2,1)S(1)}, bf16[8,32,256]{2,1,0:T(8,128)(2,1)S(1)}, u32[]{:S(2)}, u32[]{:S(2)}) %collective-permute-start.14) | collective-permute-done | bytes 131104 | tf_op jit(solution)/shard_map/ppermute | solution.py:21
  24.4 0.7 fusion
  25.0 1.8 %collective-permute-start.7 = (bf16[4,8,2048]{2,1,0:T(8,128)(2,1)S(1)}, bf16[4,8,2048]{2,1,0:T(8,128)(2,1)S(1)}, u32[]{:S(2)}, u32[]{:S(2)}) collective-permute-start(bf16[4,8,2048]{2,1,0:T(8,128)(2,1)S(1)} %get-tuple-element.23), channel_id=1, source_target_pairs={{0,6},{1,7},{2,4},{3,5},{4,2},{5,3},{6,0},{7,1},{8,14},{9,15},{10,... | collective-permute-start | bytes 393224 | tf_op jit(solution)/shard_map/ppermute | solution.py:21
  27.7 2.5 %collective-permute-done.7.refs_3_ = bf16[4,8,2048]{2,1,0:T(8,128)(2,1)S(1)} collective-permute-done((bf16[4,8,2048]{2,1,0:T(8,128)(2,1)S(1)}, bf16[4,8,2048]{2,1,0:T(8,128)(2,1)S(1)}, u32[]{:S(2)}, u32[]{:S(2)}) %collective-permute-start.7) | collective-permute-done | bytes 131104 | tf_op jit(solution)/shard_map/ppermute | solution.py:21
  30.2 2.9 %collective-permute-done.6.refs_2_ = bf16[4,8,2048]{2,1,0:T(8,128)(2,1)S(1)} collective-permute-done((bf16[4,8,2048]{2,1,0:T(8,128)(2,1)S(1)}, bf16[4,8,2048]{2,1,0:T(8,128)(2,1)S(1)}, u32[]{:S(2)}, u32[]{:S(2)}) %collective-permute-start.6) | collective-permute-done | bytes 131104 | tf_op jit(solution)/shard_map/ppermute | solution.py:21
  34.0 2.1 %shard_map.92 = (bf16[8,32,256]{2,1,0:T(8,128)(2,1)}, bf16[8,32,256]{2,1,0:T(8,128)(2,1)}) custom-call(bf16[4,8,2048]{2,1,0:T(8,128)(2,1)} %get-tuple-element.26.refs_0_, bf16[4,8,2048]{2,1,0:T(8,128)(2,1)} %copy-done.9, bf16[4,8,2048]{2,1,0:T(8,128)(2,1)} %copy-done.8, bf16[4,8,2048]{2,1,0:T(8,128)(2,1)} %copy-done.7), custom_call_target="tpu_custom_call" | custom-call | tf_op jit(solution)/shard_map/pallas_call | solution.py:534
  36.0 3.3 %collective-permute-start.10 = (bf16[8,32,256]{2,1,0:T(8,128)(2,1)}, bf16[8,32,256]{2,1,0:T(8,128)(2,1)S(1)}, u32[]{:S(2)}, u32[]{:S(2)}) collective-permute-start(bf16[8,32,256]{2,1,0:T(8,128)(2,1)} %get-tuple-element.15), channel_id=1, source_target_pairs={{0,24},{8,16},{16,8},{24,0},{1,25},{9,17},{17,9},{25,1},{2,26},{10... | collective-permute-start | bytes 393224 | tf_op jit(solution)/shard_map/ppermute | solution.py:21
  39.3 0.9 slice_bitcast_fusion.7
  40.5 0.8 constant_dynamic-update-slice_fusion.6
  41.3 0.8 constant_dynamic-update-slice_fusion.5
  42.1 0.8 constant_dynamic-update-slice_fusion.4
  42.8 0.8 constant_dynamic-update-slice_fusion.3
  43.6 5.9 %collective-permute-done.9.refs_2_ = bf16[8,32,256]{2,1,0:T(8,128)(2,1)S(1)} collective-permute-done((bf16[8,32,256]{2,1,0:T(8,128)(2,1)}, bf16[8,32,256]{2,1,0:T(8,128)(2,1)S(1)}, u32[]{:S(2)}, u32[]{:S(2)}) %collective-permute-start.9) | collective-permute-done | bytes 131104 | tf_op jit(solution)/shard_map/ppermute | solution.py:21
  49.6 0.9 collective-permute-start.11
  50.7 7.8 %collective-permute-done.11.refs_4_ = bf16[4,8,24,256]{3,2,1,0:T(8,128)(2,1)S(1)} collective-permute-done((bf16[4,8,24,256]{3,2,1,0:T(8,128)(2,1)S(1)}, bf16[4,8,24,256]{3,2,1,0:T(8,128)(2,1)S(1)}, u32[]{:S(2)}, u32[]{:S(2)}) %collective-permute-start.11) | collective-permute-done | bytes 393248 | tf_op jit(solution)/shard_map/ppermute | solution.py:21
  59.4 4.6 %collective-permute-start.12 = (bf16[4,8,7,4,256]{4,3,1,2,0:T(4,128)(2,1)S(1)}, bf16[4,8,7,4,256]{4,3,1,2,0:T(4,128)(2,1)S(1)}, u32[]{:S(2)}, u32[]{:S(2)}) collective-permute-start(bf16[4,8,7,4,256]{4,3,1,2,0:T(4,128)(2,1)S(1)} %get-tuple-element.27), channel_id=1, source_target_pairs={{1,0},{2,1},{3,2},{5,4},{6,5},{7,6},{9,8},{10,9},{11,10},{13,12},{... | collective-permute-start | bytes 1376264 | tf_op jit(solution)/shard_map/ppermute | solution.py:29
  64.0 3.6 %collective-permute-start.13 = (bf16[4,8,7,4,256]{4,3,1,2,0:T(4,128)(2,1)S(1)}, bf16[4,8,7,4,256]{4,3,1,2,0:T(4,128)(2,1)S(1)}, u32[]{:S(2)}, u32[]{:S(2)}) collective-permute-start(bf16[4,8,7,4,256]{4,3,1,2,0:T(4,128)(2,1)S(1)} %get-tuple-element.28), channel_id=1, source_target_pairs={{0,1},{1,2},{2,3},{4,5},{5,6},{6,7},{8,9},{9,10},{10,11},{12,13},{... | collective-permute-start | bytes 1376264 | tf_op jit(solution)/shard_map/ppermute | solution.py:25
  67.7 1.9 %collective-permute-start.15 = (bf16[8,8,4,256]{3,2,0,1:T(4,128)(2,1)S(1)}, bf16[8,8,4,256]{3,2,0,1:T(4,128)(2,1)S(1)}, u32[]{:S(2)}, u32[]{:S(2)}) collective-permute-start(bf16[8,8,4,256]{3,2,0,1:T(4,128)(2,1)S(1)} %get-tuple-element.35), channel_id=1, source_target_pairs={{1,0},{2,1},{3,2},{5,4},{6,5},{7,6},{9,8},{10,9},{11,10},{13,12},{... | collective-permute-start | bytes 393224 | tf_op jit(solution)/shard_map/ppermute | solution.py:29
  69.6 3.6 %collective-permute-start.16 = (bf16[8,8,4,256]{3,2,0,1:T(4,128)(2,1)S(1)}, bf16[8,8,4,256]{3,2,0,1:T(4,128)(2,1)S(1)}, u32[]{:S(2)}, u32[]{:S(2)}) collective-permute-start(bf16[8,8,4,256]{3,2,0,1:T(4,128)(2,1)S(1)} %get-tuple-element.36), channel_id=1, source_target_pairs={{0,1},{1,2},{2,3},{4,5},{5,6},{6,7},{8,9},{9,10},{10,11},{12,13},{... | collective-permute-start | bytes 393224 | tf_op jit(solution)/shard_map/ppermute | solution.py:25
  75.2 0.9 copy_bitcast_fusion.1.refs_1_
  76.1 9.7 %shard_map.93 = (bf16[4,2,768,256]{3,2,1,0:T(8,128)(2,1)}, bf16[4,8,112,256]{3,2,1,0:T(8,128)(2,1)}, bf16[8,128,256]{2,1,0:T(8,128)(2,1)}) custom-call(f32[40]{0:T(128)} %pad_maximum_fusion.8.num_ref, f32[8,768]{1,0:T(8,128)} %fusion.10.base_ref, bf16[8,32,256]{2,1,0:T(8,128)(2,1)} %bitcast.222, bf16[8,32,256]{2,1,0:T(8,128)(2,1)} %copy-done.6, ...), custom_call_target="tpu_custom_call" | custom-call | tf_op jit(solution)/shard_map/pallas_call | solution.py:497
  85.8 1.4 %copy_bitcast_fusion.refs_5_ = bf16[4,8,56,256]{3,2,1,0:T(8,128)(2,1)} fusion(bf16[4,8,7,4,256]{4,3,1,2,0:T(4,128)(2,1)S(1)} %collective-permute-done.13, bf16[4,8,7,4,256]{4,3,1,2,0:T(4,128)(2,1)S(1)} %collective-permute-done.12), kind=kLoop, calls=%fused_computation.2 | loop fusion | flops 1835008 | bytes 1835008 | tf_op jit(solution)/shard_map/reshape | solution.py:493
  87.2 13.5 %shard_map.94 = f32[4,8,512]{2,1,0:T(8,128)} custom-call(s32[2]{0:T(128)} %pad_add_fusion.int_ref, f32[40]{0:T(128)} %pad_maximum_fusion.8.num_ref, f32[288]{0:T(512)} %mul.26.wt_ref, f32[4,8,512]{2,1,0:T(8,128)} %est_ref.1, bf16[8,32,256]{2,1,0:T(8,128)(2,1)} %get-tuple-element.14.refs_0_, bf16[8,32,256]{2,1,0:T(8,128)(2,1)} %copy-done.4, ...), custom_call_target="tpu_custom_call" | custom-call | tf_op jit(solution)/shard_map/pallas_call | solution.py:563
  (127 shorter events, 10.6 us)
Async XLA Ops:
  4.2 14.1 %collective-permute-start.2 = (bf16[40,512]{1,0:T(8,128)(2,1)S(1)}, bf16[40,512]{1,0:T(8,128)(2,1)S(1)}, u32[]{:S(2)}, u32[]{:S(2)}) collective-permute-start(bf16[40,512]{1,0:T(8,128)(2,1)S(1)} %concatenate.33), channel_id=1, source_target_pairs={{0,24},{8,16},{16,8},{24,0},{1,25},{9,17},{17,9},{25,1},{2,26},{10... | collective-permute-start | bytes 122888 | tf_op jit(solution)/shard_map/ppermute | solution.py:21
  8.4 9.9 %collective-permute-start.1 = (bf16[40,512]{1,0:T(8,128)(2,1)S(1)}, bf16[40,512]{1,0:T(8,128)(2,1)S(1)}, u32[]{:S(2)}, u32[]{:S(2)}) collective-permute-start(bf16[40,512]{1,0:T(8,128)(2,1)S(1)} %concatenate.33), channel_id=1, source_target_pairs={{0,16},{8,24},{16,0},{24,8},{1,17},{9,25},{17,1},{25,9},{2,18},{10... | collective-permute-start | bytes 122888 | tf_op jit(solution)/shard_map/ppermute | solution.py:21
  8.4 10.0 %collective-permute-start = (bf16[40,512]{1,0:T(8,128)(2,1)S(1)}, bf16[40,512]{1,0:T(8,128)(2,1)S(1)}, u32[]{:S(2)}, u32[]{:S(2)}) collective-permute-start(bf16[40,512]{1,0:T(8,128)(2,1)S(1)} %concatenate.33), channel_id=1, source_target_pairs={{0,8},{8,0},{16,24},{24,16},{1,9},{9,1},{17,25},{25,17},{2,10},{10... | collective-permute-start | bytes 122888 | tf_op jit(solution)/shard_map/ppermute | solution.py:21
  10.2 6.8 %collective-permute-start.3 = (s32[4,4]{1,0:T(4,128)S(1)}, s32[4,4]{1,0:T(4,128)S(1)}, u32[]{:S(2)}, u32[]{:S(2)}) collective-permute-start(s32[4,4]{1,0:T(4,128)S(1)} %broadcast_select_fusion), channel_id=1, source_target_pairs={{0,4},{4,0},{1,5},{5,1},{2,6},{6,2},{3,7},{7,3},{8,12},{12,8},{9,1... | collective-permute-start | bytes 200 | tf_op jit(solution)/shard_map/ppermute | solution.py:21
  14.7 9.7 %collective-permute-start.4 = (bf16[4,4,8,2048]{3,2,1,0:T(8,128)(2,1)}, bf16[4,4,8,2048]{3,2,1,0:T(8,128)(2,1)S(1)}, u32[]{:S(2)}, u32[]{:S(2)}) collective-permute-start(bf16[4,4,8,2048]{3,2,1,0:T(8,128)(2,1)} %get-tuple-element.13), channel_id=1, source_target_pairs={{0,1},{1,0},{2,3},{3,2},{4,5},{5,4},{6,7},{7,6},{8,9},{9,8},{10,11... | collective-permute-start | bytes 1572872 | tf_op jit(solution)/shard_map/ppermute | solution.py:21
  18.5 5.9 %copy-start.5 = (bf16[4,4,8,2048]{3,2,1,0:T(8,128)(2,1)S(1)}, bf16[4,4,8,2048]{3,2,1,0:T(8,128)(2,1)}, u32[]{:S(2)}) copy-start(bf16[4,4,8,2048]{3,2,1,0:T(8,128)(2,1)} %get-tuple-element.12) | copy-start | bytes 1572868
  19.1 30.4 %copy-start.1 = (bf16[4,2,32,256]{3,2,1,0:T(8,128)(2,1)}, bf16[4,2,32,256]{3,2,1,0:T(8,128)(2,1)S(1)}, u32[]{:S(2)}) copy-start(bf16[4,2,32,256]{3,2,1,0:T(8,128)(2,1)S(1)} %maximum_select_fusion.1) | copy-start | bytes 393220
  19.1 5.2 %collective-permute-start.14 = (bf16[8,32,256]{2,1,0:T(8,128)(2,1)S(1)}, bf16[8,32,256]{2,1,0:T(8,128)(2,1)S(1)}, u32[]{:S(2)}, u32[]{:S(2)}) collective-permute-start(bf16[8,32,256]{2,1,0:T(8,128)(2,1)S(1)} %bitcast.217), channel_id=1, source_target_pairs={{0,4},{4,0},{1,5},{5,1},{2,6},{6,2},{3,7},{7,3},{8,12},{12,8},{9,1... | collective-permute-start | bytes 393224 | tf_op jit(solution)/shard_map/ppermute | solution.py:21
  24.3 25.3 %copy-start.6 = (bf16[8,32,256]{2,1,0:T(8,128)(2,1)}, bf16[8,32,256]{2,1,0:T(8,128)(2,1)S(1)}, u32[]{:S(2)}) copy-start(bf16[8,32,256]{2,1,0:T(8,128)(2,1)S(1)} %collective-permute-done.14.refs_0_) | copy-start | bytes 393220
  25.0 5.1 %collective-permute-start.7 = (bf16[4,8,2048]{2,1,0:T(8,128)(2,1)S(1)}, bf16[4,8,2048]{2,1,0:T(8,128)(2,1)S(1)}, u32[]{:S(2)}, u32[]{:S(2)}) collective-permute-start(bf16[4,8,2048]{2,1,0:T(8,128)(2,1)S(1)} %get-tuple-element.23), channel_id=1, source_target_pairs={{0,6},{1,7},{2,4},{3,5},{4,2},{5,3},{6,0},{7,1},{8,14},{9,15},{10,... | collective-permute-start | bytes 393224 | tf_op jit(solution)/shard_map/ppermute | solution.py:21
  26.9 6.2 %collective-permute-start.6 = (bf16[4,8,2048]{2,1,0:T(8,128)(2,1)S(1)}, bf16[4,8,2048]{2,1,0:T(8,128)(2,1)S(1)}, u32[]{:S(2)}, u32[]{:S(2)}) collective-permute-start(bf16[4,8,2048]{2,1,0:T(8,128)(2,1)S(1)} %get-tuple-element.24), channel_id=1, source_target_pairs={{0,4},{1,5},{2,6},{3,7},{4,0},{5,1},{6,2},{7,3},{8,12},{9,13},{10,... | collective-permute-start | bytes 393224 | tf_op jit(solution)/shard_map/ppermute | solution.py:21
  27.5 5.8 %collective-permute-start.5 = (bf16[4,8,2048]{2,1,0:T(8,128)(2,1)S(1)}, bf16[4,8,2048]{2,1,0:T(8,128)(2,1)S(1)}, u32[]{:S(2)}, u32[]{:S(2)}) collective-permute-start(bf16[4,8,2048]{2,1,0:T(8,128)(2,1)S(1)} %get-tuple-element.25), channel_id=1, source_target_pairs={{0,2},{1,3},{2,0},{3,1},{4,6},{5,7},{6,4},{7,5},{8,10},{9,11},{10,... | collective-permute-start | bytes 393224 | tf_op jit(solution)/shard_map/ppermute | solution.py:21
  30.2 3.1 %copy-start.7 = (bf16[4,8,2048]{2,1,0:T(8,128)(2,1)}, bf16[4,8,2048]{2,1,0:T(8,128)(2,1)S(1)}, u32[]{:S(2)}) copy-start(bf16[4,8,2048]{2,1,0:T(8,128)(2,1)S(1)} %collective-permute-done.7.refs_3_) | copy-start | bytes 393220
  33.1 0.7 copy-start.8
  33.3 0.7 copy-start.9
  36.0 7.6 %collective-permute-start.10 = (bf16[8,32,256]{2,1,0:T(8,128)(2,1)}, bf16[8,32,256]{2,1,0:T(8,128)(2,1)S(1)}, u32[]{:S(2)}, u32[]{:S(2)}) collective-permute-start(bf16[8,32,256]{2,1,0:T(8,128)(2,1)} %get-tuple-element.15), channel_id=1, source_target_pairs={{0,24},{8,16},{16,8},{24,0},{1,25},{9,17},{17,9},{25,1},{2,26},{10... | collective-permute-start | bytes 393224 | tf_op jit(solution)/shard_map/ppermute | solution.py:21
  39.3 10.2 %collective-permute-start.9 = (bf16[8,32,256]{2,1,0:T(8,128)(2,1)}, bf16[8,32,256]{2,1,0:T(8,128)(2,1)S(1)}, u32[]{:S(2)}, u32[]{:S(2)}) collective-permute-start(bf16[8,32,256]{2,1,0:T(8,128)(2,1)} %get-tuple-element.15), channel_id=1, source_target_pairs={{0,16},{8,24},{16,0},{24,8},{1,17},{9,25},{17,1},{25,9},{2,18},{10... | collective-permute-start | bytes 393224 | tf_op jit(solution)/shard_map/ppermute | solution.py:21
  40.2 9.3 %collective-permute-start.8 = (bf16[8,32,256]{2,1,0:T(8,128)(2,1)}, bf16[8,32,256]{2,1,0:T(8,128)(2,1)S(1)}, u32[]{:S(2)}, u32[]{:S(2)}) collective-permute-start(bf16[8,32,256]{2,1,0:T(8,128)(2,1)} %get-tuple-element.14.refs_0_), channel_id=1, source_target_pairs={{0,8},{8,0},{16,24},{24,16},{1,9},{9,1},{17,25},{25,17},{2,10},{10... | collective-permute-start | bytes 393224 | tf_op jit(solution)/shard_map/ppermute | solution.py:21
  43.6 15.1 %copy-start.2 = (bf16[8,32,256]{2,1,0:T(8,128)(2,1)}, bf16[8,32,256]{2,1,0:T(8,128)(2,1)S(1)}, u32[]{:S(2)}) copy-start(bf16[8,32,256]{2,1,0:T(8,128)(2,1)S(1)} %collective-permute-done.10.refs_3_) | copy-start | bytes 393220
  49.5 9.4 %copy-start.3 = (bf16[8,32,256]{2,1,0:T(8,128)(2,1)}, bf16[8,32,256]{2,1,0:T(8,128)(2,1)S(1)}, u32[]{:S(2)}) copy-start(bf16[8,32,256]{2,1,0:T(8,128)(2,1)S(1)} %collective-permute-done.9.refs_2_) | copy-start | bytes 393220
  49.5 9.3 %copy-start.4 = (bf16[8,32,256]{2,1,0:T(8,128)(2,1)}, bf16[8,32,256]{2,1,0:T(8,128)(2,1)S(1)}, u32[]{:S(2)}) copy-start(bf16[8,32,256]{2,1,0:T(8,128)(2,1)S(1)} %collective-permute-done.8.refs_1_) | copy-start | bytes 393220
  49.6 8.9 %collective-permute-start.11 = (bf16[4,8,24,256]{3,2,1,0:T(8,128)(2,1)S(1)}, bf16[4,8,24,256]{3,2,1,0:T(8,128)(2,1)S(1)}, u32[]{:S(2)}, u32[]{:S(2)}) collective-permute-start(bf16[4,8,24,256]{3,2,1,0:T(8,128)(2,1)S(1)} %pad_maximum_fusion.2), channel_id=1, source_target_pairs={{0,4},{4,0},{1,5},{5,1},{2,6},{6,2},{3,7},{7,3},{8,12},{12,8},{9,1... | collective-permute-start | bytes 1179656 | tf_op jit(solution)/shard_map/ppermute | solution.py:21
  58.6 0.8 copy-start
  59.4 26.4 %collective-permute-start.12 = (bf16[4,8,7,4,256]{4,3,1,2,0:T(4,128)(2,1)S(1)}, bf16[4,8,7,4,256]{4,3,1,2,0:T(4,128)(2,1)S(1)}, u32[]{:S(2)}, u32[]{:S(2)}) collective-permute-start(bf16[4,8,7,4,256]{4,3,1,2,0:T(4,128)(2,1)S(1)} %get-tuple-element.27), channel_id=1, source_target_pairs={{1,0},{2,1},{3,2},{5,4},{6,5},{7,6},{9,8},{10,9},{11,10},{13,12},{... | collective-permute-start | bytes 1376264 | tf_op jit(solution)/shard_map/ppermute | solution.py:29
  64.0 21.8 %collective-permute-start.13 = (bf16[4,8,7,4,256]{4,3,1,2,0:T(4,128)(2,1)S(1)}, bf16[4,8,7,4,256]{4,3,1,2,0:T(4,128)(2,1)S(1)}, u32[]{:S(2)}, u32[]{:S(2)}) collective-permute-start(bf16[4,8,7,4,256]{4,3,1,2,0:T(4,128)(2,1)S(1)} %get-tuple-element.28), channel_id=1, source_target_pairs={{0,1},{1,2},{2,3},{4,5},{5,6},{6,7},{8,9},{9,10},{10,11},{12,13},{... | collective-permute-start | bytes 1376264 | tf_op jit(solution)/shard_map/ppermute | solution.py:25
  67.7 7.5 %collective-permute-start.15 = (bf16[8,8,4,256]{3,2,0,1:T(4,128)(2,1)S(1)}, bf16[8,8,4,256]{3,2,0,1:T(4,128)(2,1)S(1)}, u32[]{:S(2)}, u32[]{:S(2)}) collective-permute-start(bf16[8,8,4,256]{3,2,0,1:T(4,128)(2,1)S(1)} %get-tuple-element.35), channel_id=1, source_target_pairs={{1,0},{2,1},{3,2},{5,4},{6,5},{7,6},{9,8},{10,9},{11,10},{13,12},{... | collective-permute-start | bytes 393224 | tf_op jit(solution)/shard_map/ppermute | solution.py:29
  69.6 5.6 %collective-permute-start.16 = (bf16[8,8,4,256]{3,2,0,1:T(4,128)(2,1)S(1)}, bf16[8,8,4,256]{3,2,0,1:T(4,128)(2,1)S(1)}, u32[]{:S(2)}, u32[]{:S(2)}) collective-permute-start(bf16[8,8,4,256]{3,2,0,1:T(4,128)(2,1)S(1)} %get-tuple-element.36), channel_id=1, source_target_pairs={{0,1},{1,2},{2,3},{4,5},{5,6},{6,7},{8,9},{9,10},{10,11},{12,13},{... | collective-permute-start | bytes 393224 | tf_op jit(solution)/shard_map/ppermute | solution.py:25

commit v2 on v1

v2 whole, which is shorter than its diff:
```python
import functools

import jax
import jax.numpy as jnp
from jax import lax
from jax.experimental import pallas as pl
from jax.experimental.pallas import tpu as pltpu
from jax.sharding import PartitionSpec as P

BF = jnp.bfloat16
F32 = jnp.float32
TILE = 256
LIMIT = 56 << 20


def whole(*spaces):
    return [pl.BlockSpec(memory_space=space) for space in spaces]


def swap(array, axis, size, mask):
    return lax.ppermute(array, axis, [(i, i ^ mask) for i in range(size)])


def upward(array, axis, size):
    return lax.ppermute(array, axis, [(i, i + 1) for i in range(size - 1)])


def downward(array, axis, size):
    return lax.ppermute(array, axis, [(i + 1, i) for i in range(size - 1)])


class Frame:
    def __init__(self, slabs, depth):
        self.mirrored = slabs == 2
        self.depth = depth
        self.own = 0 if self.mirrored else depth
        self.size = 2 * depth if self.mirrored else 3 * depth

    def need(self, radius):
        return range(
            max(0, self.own - radius), min(self.size, self.own + self.depth + radius)
        )

    def source(self, f):
        k = f - self.own
        if 0 <= k < self.depth:
            return "own", k
        if self.mirrored:
            return "up", 2 * self.depth - 1 - k
        return ("dn", f) if k < 0 else ("up", k - self.depth)

    def place(self, f, radius):
        where, k = self.source(f)
        at = 0
        for name, slices in [("own", range(self.depth))] + list(self.sent(radius).items()):
            if name == where:
                return at + k - slices.start
            at += len(slices)

    def sent(self, radius):
        if self.mirrored:
            return {"up": range(self.depth - radius, self.depth)}
        return {
            "dn": range(self.depth - radius, self.depth),
            "up": range(0, radius),
        }


def exchange_z(frame, make, slabs, radius):
    got = {}
    for side, slices in frame.sent(radius).items():
        payload = make(slices)
        if frame.mirrored:
            got[side] = swap(payload, "gz", slabs, 1)
        elif side == "dn":
            got[side] = upward(payload, "gz", slabs)
        else:
            got[side] = downward(payload, "gz", slabs)
    return got


def place():
    return lax.axis_index("view"), lax.axis_index("gz")


def cells_kernel(pairs, bands, mirrored, owner_ref, row_ref, pieces_ref, even_ref, odd_ref, acc):
    count = pieces_ref.shape[0]
    depth = even_ref.shape[1]
    me = lax.axis_index("gz") * bands + lax.axis_index("gy")

    def clear(i, carry):
        acc[i] = jnp.zeros(acc.shape[1:], F32)
        return carry

    lax.fori_loop(0, acc.shape[0], clear, 0)

    def add(i, carry):
        owner = owner_ref[0, i, 0]
        row = row_ref[0, i]
        if mirrored:
            row = jnp.where(owner >= bands, depth - 1 - row, row)
        c = (owner ^ me) * depth + row
        acc[c] = acc[c] + pieces_ref[i].astype(F32)
        return carry

    lax.fori_loop(0, count, add, 0)

    def put(pair, carry):
        for f in range(depth):
            even_ref[pair, f] = acc[pair * 2 * depth + f].astype(BF)
            odd_ref[pair, f] = acc[(pair * 2 + 1) * depth + f].astype(BF)
        return carry

    lax.fori_loop(0, pairs, put, 0)


def payload_kernel(mirrored, taps_ref, bg_ref, est_ref, psf_ref, out_ref, tail):
    depth, height = est_ref.shape[:2]
    upside = lax.axis_index("gz") if mirrored else 0
    for k in range(depth):
        out_ref[k * height : (k + 1) * height, :] = est_ref[
            k + upside * (depth - 1 - 2 * k)
        ].astype(BF)
    tail[...] = jnp.zeros(tail.shape, F32)
    tail[0:1, : psf_ref.shape[1]] = psf_ref[...]
    lanes = lax.broadcasted_iota(jnp.int32, (1, 128), 1)
    exact = jnp.where(lanes == 9, bg_ref[0], F32(0.0))
    for i in range(3):
        for j in range(3):
            tap = taps_ref[0, i + upside * (2 - 2 * i), j]
            exact = jnp.where(lanes == i * 3 + j, tap, exact)
    for n in range(3):
        part = exact.astype(BF).astype(F32)
        tail[n + 1 : n + 2, :128] = part
        exact = exact - part
    out_ref[depth * height :, :] = tail[...].astype(BF)


def reversal():
    rows = lax.broadcasted_iota(jnp.int32, (TILE, TILE), 0)
    cols = lax.broadcasted_iota(jnp.int32, (TILE, TILE), 1)
    return jnp.where(rows + cols == TILE - 1, F32(1.0), F32(0.0)).astype(BF)


def total_kernel(parts, *refs):
    ins, (out_ref, rev_ref) = refs[:parts], refs[parts:]
    tiles, rows, _ = out_ref.shape
    for t in range(tiles):
        cut = slice(t * TILE, (t + 1) * TILE)
        acc = ins[0][:, :, cut].astype(F32)
        for ref in ins[1:]:
            acc = acc + ref[:, :, cut].astype(F32)
        out_ref[t] = acc.reshape(rows, TILE).astype(BF)
    back = jnp.dot(
        out_ref[...].reshape(tiles * rows, TILE), reversal(), preferred_element_type=F32
    ).astype(BF)
    for t in range(tiles):
        rev_ref[tiles - 1 - t] = back[t * rows : (t + 1) * rows]


def band_kernel(at, *refs):
    heard, out_ref = refs[:4], refs[4]
    flip = reversal()
    for v in range(4):
        row = heard[v][at : at + 8, : 3 * 128].astype(F32)[0:1]
        edge = TILE // 2
        base = jnp.concatenate(
            [jnp.zeros((1, edge), F32), row, jnp.zeros((1, 2 * edge), F32)], axis=1
        )
        wide = pltpu.roll(
            jnp.broadcast_to(base, (TILE, 3 * TILE)), 0, 1, stride=1, stride_axis=0
        ).astype(BF)
        turned = jnp.dot(flip, wide, preferred_element_type=F32).astype(BF)
        for k in range(3):
            cut = slice(k * TILE, (k + 1) * TILE)
            to = slice((2 - k) * TILE, (3 - k) * TILE)
            if v >= 2:
                out_ref[2 + v, cut, :] = turned[:, cut]
            else:
                out_ref[2 + v, to, :] = wide[:, cut]
                out_ref[v, cut, :] = jnp.dot(
                    turned[:, cut], flip, preferred_element_type=F32
                ).astype(BF)


def forward_block(v):
    return v if v < 2 else v + 2


def backward_block(v):
    return v + 2


def conv(src, first, tiles, rows, blocks, dst, step):
    s = 0
    while s < tiles:
        n = min(step, tiles - s)
        lhs = jnp.concatenate(
            [
                src[pl.ds(first + s + k, n)].reshape(n * rows, TILE)
                for k in range(3)
            ],
            axis=1,
        )
        out = jnp.dot(lhs, blocks, preferred_element_type=F32).astype(BF)
        dst[s : s + n] = out.reshape(n, rows, TILE)
        s += n


def taps_sum(slices, zs, taps):
    result = {}
    for z in zs:
        sums = [None, None, None]
        for j in range(3):
            for i in range(3):
                at = z + i - 1
                if at in slices:
                    term = taps(z, i, j) * slices[at]
                    sums[j] = term if sums[j] is None else sums[j] + term
        result[z] = sums
    return result


def along_y(sums):
    n = sums[0].shape[0]
    return pltpu.roll(sums[0], 1, 0) + sums[1] + pltpu.roll(sums[2], n - 1, 0)


def frame_kernel(frame, tiles, sides, *refs):
    own_refs, refs = refs[:4], refs[4:]
    side_refs = dict(zip(sides, refs[: len(sides)]))
    hi_ref, lo_ref, out_ref = refs[len(sides) :]
    view = lax.axis_index("view")
    for e in (0, tiles + 1):
        out_ref[e] = jnp.zeros(out_ref.shape[1:], BF)
    for v in range(4):
        for s in range(tiles // 4):
            t = (view ^ v) * (tiles // 4) + s + 1
            cut = slice(s * TILE, (s + 1) * TILE)
            for f in range(frame.size):
                where, k = frame.source(f)
                rows = slice(k * 8, (k + 1) * 8)
                if where == "own":
                    own = own_refs[v][rows, cut]
                else:
                    own = side_refs[where][v, rows, cut]
                n = frame.place(f, frame.depth)
                out_ref[t, f * 16 : (f + 1) * 16, :] = jnp.concatenate(
                    [
                        own.astype(F32),
                        hi_ref[v, n, :, cut].astype(F32),
                        lo_ref[v, n, :, cut].astype(F32),
                    ],
                    axis=0,
                ).astype(BF)


def forward_kernel(frame, tiles, views, num_ref, blocks_ref, frame_ref, recip_ref, c):
    size = frame.size
    zs = frame.need(3)
    for at, v in enumerate(views):
        conv(frame_ref, 0, tiles, size * 16, blocks_ref[forward_block(v)], c, 2)

        def divide(t, carry, v=v, at=at):
            from_t = t if v < 2 else tiles - 1 - t
            for h in range(TILE // 128):
                cut = slice(h * 128, (h + 1) * 128)
                slices = {
                    f: c[from_t, f * 16 : (f + 1) * 16, cut].astype(F32)
                    for f in range(size)
                }
                sums = taps_sum(slices, zs, lambda z, i, j: num_ref[v * 9 + i * 3 + j])
                for n, z in enumerate(zs):
                    recip_ref[at, t, n * 16 : (n + 1) * 16, cut] = (
                        1.0 / (along_y(sums[z]) + num_ref[36 + v])
                    ).astype(BF)
            return carry

        lax.fori_loop(0, tiles, divide, 0)


def main_kernel(frame, tiles, sides, num_ref, wt_ref, est_ref, *refs):
    own_refs, refs = refs[:4], refs[4:]
    count = len(sides)
    far_refs, refs = refs[: 2 * count], refs[2 * count :]
    hi_refs, lo_refs = refs[0:2], refs[2:4]
    recip_refs = refs[4:6]
    blocks_ref, frame_ref, out_ref = refs[6:9]
    m1, u2, m2, c0, c1, c2, c3, kept = refs[9:]
    c = [c0, c1, c2, c3]
    view = lax.axis_index("view")
    upside = lax.axis_index("gz") if frame.mirrored else 0
    depth = frame.depth
    z3, z2, z1, z0 = (frame.need(r) for r in (3, 2, 1, 0))
    sent = frame.sent(3)

    def measured(v, t, z, cut):
        where, k = frame.source(z)
        pair, w = v // 2, v % 2
        if where == "own":
            own = own_refs[v][t, k * 8 : (k + 1) * 8, cut]
        else:
            k = k - sent[where].start
            far = far_refs[pair * count + sides.index(where)]
            own = far[w, t, k * 8 : (k + 1) * 8, cut]
        n = frame.place(z, 3)
        return jnp.concatenate(
            [
                own.astype(F32),
                hi_refs[pair][w, t, n, :, cut].astype(F32),
                lo_refs[pair][w, t, n, :, cut].astype(F32),
            ],
            axis=0,
        )

    def mix(v, t, z, cut, recip_a, recip_b):
        a = (measured(v, t, z, cut) * recip_a).astype(BF).astype(F32)
        b = (measured(v + 2, t, z, cut) * recip_b).astype(BF).astype(F32)
        return (0.5 * (a + b)).astype(BF)

    def zero_ends(ref):
        for e in (0, ref.shape[0] - 1):
            ref[e] = jnp.zeros(ref.shape[1:], BF)

    for ref in (m1, u2, m2):
        zero_ends(ref)

    for v in range(2):

        def ratios(t, carry, v=v):
            for h in range(TILE // 128):
                cut = slice(h * 128, (h + 1) * 128)
                for n, z in enumerate(z3):
                    at = slice(n * 16, (n + 1) * 16)
                    m1[t + 1, at, cut] = mix(
                        v,
                        t,
                        z,
                        cut,
                        recip_refs[0][v, t, at, cut].astype(F32),
                        recip_refs[1][v, t, at, cut].astype(F32),
                    )
            return carry

        lax.fori_loop(0, tiles, ratios, 0)
        for w in (v, v + 2):
            conv(m1, 0, tiles, m1.shape[1], blocks_ref[backward_block(w)], c[w], 2)

    def numerator(slices_of, zs):
        totals = {z: [None, None, None] for z in zs}
        for v in range(4):
            slices = slices_of(v)
            sums = taps_sum(
                slices,
                zs,
                lambda z, i, j, v=v: wt_ref[(v * frame.size + z) * 9 + i * 3 + j],
            )
            for z in zs:
                for j in range(3):
                    old = totals[z][j]
                    totals[z][j] = sums[z][j] if old is None else old + sums[z][j]
        return totals

    def update(t, carry):
        for h in range(TILE // 128):
            cut = slice(h * 128, (h + 1) * 128)

            def slices_of(v):
                from_t = t if v < 2 else tiles - 1 - t
                return {
                    z: c[v][from_t, n * 16 : (n + 1) * 16, cut].astype(F32)
                    for n, z in enumerate(z3)
                }

            totals = numerator(slices_of, z2)
            for n, z in enumerate(z2):
                change = along_y(totals[z])
                before = frame_ref[t + 1, z * 16 : (z + 1) * 16, cut].astype(F32)
                u2[t + 1, n * 16 : (n + 1) * 16, cut] = (before * change).astype(BF)
                if z in z0:
                    k = z - frame.own
                    kept[t, k * 8 : (k + 1) * 8, cut] = change[:8]
        return carry

    lax.fori_loop(0, tiles, update, 0)

    rows1 = m2.shape[1]
    n2 = u2.shape[1]
    for v in range(2):
        for w in (v, v + 2):
            conv(u2, 0, tiles, n2, blocks_ref[forward_block(w)], c[w].at[:, :n2, :], 2)

        def ratios2(t, carry, v=v):
            for h in range(TILE // 128):
                cut = slice(h * 128, (h + 1) * 128)
                recips = []
                for w in (v, v + 2):
                    from_t = t if w < 2 else tiles - 1 - t
                    slices = {
                        z: c[w][from_t, n * 16 : (n + 1) * 16, cut].astype(F32)
                        for n, z in enumerate(z2)
                    }
                    sums = taps_sum(
                        slices, z1, lambda z, i, j, w=w: num_ref[w * 9 + i * 3 + j]
                    )
                    recips.append(
                        {z: 1.0 / (along_y(sums[z]) + num_ref[36 + w]) for z in z1}
                    )
                for n, z in enumerate(z1):
                    m2[t + 1, n * 16 : (n + 1) * 16, cut] = mix(
                        v, t, z, cut, recips[0][z], recips[1][z]
                    )
            return carry

        lax.fori_loop(0, tiles, ratios2, 0)
        mine = tiles // 4
        for w in (v, v + 2):
            first = view * mine if w < 2 else tiles - (view + 1) * mine
            conv(m2, first, mine, rows1, blocks_ref[backward_block(w)], c[w].at[:, :rows1, :], 2)

    mine = tiles // 4
    for s in range(mine):
        for h in range(TILE // 128):
            cut = slice(h * 128, (h + 1) * 128)

            def slices_of(v):
                from_s = s if v < 2 else mine - 1 - s
                return {
                    z: c[v][from_s, n * 16 : (n + 1) * 16, cut].astype(F32)
                    for n, z in enumerate(z1)
                }

            totals = numerator(slices_of, z0)
            for z in z0:
                k = z - frame.own
                to = k + upside * (depth - 1 - 2 * k)
                lanes = slice(s * TILE + h * 128, s * TILE + (h + 1) * 128)
                first_change = kept[view * mine + s, k * 8 : (k + 1) * 8, cut]
                out_ref[to, :, lanes] = (
                    est_ref[to, :, lanes] * first_change * along_y(totals[z])[:8]
                )


def after(token, *arrays):
    return lax.optimization_barrier((token,) + arrays)[1:]


def shards(
    pieces, piece_owner, piece_row, estimate, psf_x, stencil, background, bleach_table, bleach_index
):
    depth, height, chunk = estimate.shape
    width = pieces.shape[3]
    tiles = width // TILE
    slabs = lax.axis_size("gz")
    bands = lax.axis_size("gy")
    blocks = slabs * bands
    frame = Frame(slabs, depth)
    size = frame.size
    sides = tuple(frame.sent(1))
    view = lax.axis_index("view")
    vmem, smem = pltpu.VMEM, pltpu.SMEM
    params = pltpu.CompilerParams(vmem_limit_bytes=LIMIT)

    def call(kernel, shapes, ins, outs, *args, scratch=()):
        return pl.pallas_call(
            kernel,
            out_shape=shapes,
            in_specs=whole(*ins),
            out_specs=whole(*outs) if isinstance(shapes, tuple) else whole(*outs)[0],
            scratch_shapes=list(scratch),
            compiler_params=params,
        )(*args)

    def shape(*dims, dtype=BF):
        return jax.ShapeDtypeStruct(dims, dtype)

    pairs = blocks // 2
    half_cells = shape(pairs, depth, height, width)
    even, odd = call(
        functools.partial(cells_kernel, pairs, bands, frame.mirrored),
        (half_cells, half_cells),
        (smem, smem, vmem),
        (vmem, vmem),
        piece_owner,
        piece_row,
        pieces[0],
        scratch=[vmem((blocks * depth, height, width), F32)],
    )
    other = swap(odd, "gy", bands, 1)

    area = depth * height
    late = after(even[0, 0, 0, 0], stencil, background, estimate, psf_x, bleach_index)
    payload = call(
        functools.partial(payload_kernel, frame.mirrored),
        shape(area + 8, chunk),
        (smem, smem, vmem, vmem),
        (vmem,),
        *late[:4],
        scratch=[vmem((8, chunk), F32)],
    )
    heard = [payload] + [swap(payload, "view", 4, mask) for mask in (1, 2, 3)]

    kept = [even[k] + other[k] for k in range(pairs)]
    moved = [swap(kept[k], ("gz", "gy"), blocks, 2 * k) for k in range(1, pairs)]
    plain, turned = call(
        functools.partial(total_kernel, pairs),
        (shape(tiles, area, TILE), shape(tiles, area, TILE)),
        [vmem] * pairs,
        (vmem, vmem),
        kept[0],
        *moved,
    )

    heard = after(kept[1][0, 0, 0], *heard)
    own_est = jnp.stack([x[:area] for x in heard])
    far_est = exchange_z(
        frame, lambda s: own_est[:, s.start * height : s.stop * height], slabs, depth
    )

    def y_halo(own, far):
        def rows(cut):
            parts = [
                x.reshape(x.shape[:-2] + (-1, height, x.shape[-1]))[..., cut, :]
                for x in [own] + [far[s] for s in sides]
            ]
            return jnp.concatenate(parts, axis=-3)

        hi = downward(rows(slice(0, height // 2)), "gy", bands)
        lo = upward(rows(slice(height // 2, height)), "gy", bands)
        return hi, lo

    hi_est, lo_est = y_halo(own_est, far_est)
    table = call(
        functools.partial(band_kernel, area),
        shape(6, 3 * TILE, TILE),
        [vmem] * 4,
        (vmem,),
        *heard,
    )
    numbers = jnp.stack([x[area + 1 : area + 4, :10] for x in heard]).astype(F32)
    exacts = numbers[:, 0] + numbers[:, 1] + numbers[:, 2]
    taps_all = exacts[:, :9]
    nums = jnp.concatenate([taps_all.reshape(-1), exacts[:, 9]])

    def relative(x):
        a = jnp.where(view % 2 == 1, jnp.stack([x[1], x[0], x[3], x[2]]), x)
        return jnp.where(view // 2 == 1, jnp.concatenate([a[2:], a[:2]]), a)

    index_own = late[4]
    if frame.mirrored:
        index_own = jnp.where(lax.axis_index("gz") == 1, index_own[:, ::-1], index_own)
    index_far = exchange_z(frame, lambda s: index_own[:, s.start : s.stop], slabs, depth)

    def frame_index(f):
        where, k = frame.source(f)
        return (index_own if where == "own" else index_far[where])[:, k]

    indices = jnp.stack([frame_index(f) for f in range(size)], axis=1)
    levels = jnp.arange(bleach_table.shape[1])
    matches = indices[:, :, None] == levels[None, None, :]
    weight = jnp.sum(jnp.where(matches, bleach_table[:, None, :], F32(0.0)), axis=-1)
    share = relative(weight / jnp.sum(weight, axis=0))
    weighted = (share[:, :, None] * taps_all[:, ::-1][:, None, :]).reshape(-1)

    near = swap(plain, "view", 4, 1)
    opposite = swap(turned, "view", 4, 2)
    last = swap(opposite, "view", 4, 1)

    def halos(pair):
        own = jnp.stack(pair)
        far = exchange_z(
            frame, lambda s: own[:, :, s.start * height : s.stop * height], slabs, 3
        )
        hi, lo = y_halo(own, far)
        return [far[s] for s in sides], hi, lo

    far_a, hi_a, lo_a = halos((plain, near))
    far_b, hi_b, lo_b = halos((opposite, last))

    est_frame = call(
        functools.partial(frame_kernel, frame, tiles, sides),
        shape(tiles + 2, size * 16, TILE),
        [vmem] * (6 + len(sides)),
        (vmem,),
        *heard,
        *[far_est[s] for s in sides],
        hi_est,
        lo_est,
    )
    n3, n2, n1 = (len(frame.need(r)) * 16 for r in (3, 2, 1))

    def forward(views, nums):
        return call(
            functools.partial(forward_kernel, frame, tiles, views),
            shape(2, tiles, n3, TILE),
            (smem, vmem, vmem),
            (vmem,),
            nums,
            table,
            est_frame,
            scratch=[vmem((tiles, size * 16, TILE), BF)],
        )

    recip_a = forward((0, 1), *after(plain[0, 0, 0], nums))
    recip_b = forward((2, 3), *after(recip_a[0, 0, 0, 0], nums))
    return call(
        functools.partial(main_kernel, frame, tiles, sides),
        shape(*estimate.shape, dtype=F32),
        [smem, smem] + [vmem] * (13 + 2 * len(sides)),
        (vmem,),
        nums,
        weighted,
        estimate,
        plain,
        near,
        opposite,
        last,
        *far_a,
        *far_b,
        hi_a,
        hi_b,
        lo_a,
        lo_b,
        recip_a,
        recip_b,
        table,
        est_frame,
        scratch=[
            vmem((tiles + 2, n3, TILE), BF),
            vmem((tiles + 2, n2, TILE), BF),
            vmem((tiles + 2, n1, TILE), BF),
        ]
        + [vmem((tiles, n3, TILE), BF)] * 4
        + [vmem((tiles, area, TILE), F32)],
    )


def solution(mesh):
    placed = (
        P("view", ("gz", "gy"), None, None),
        P("view", ("gz", "gy"), None),
        P("view", ("gz", "gy")),
        P("gz", "gy", "view"),
        P("view", None),
        P("view", None, None),
        P("view"),
        P(),
        P(None, "gz"),
    )
    return jax.shard_map(
        shards, mesh=mesh, in_specs=placed, out_specs=P("gz", "gy", "view"), check_vma=False
    )
```

time: 101 us -> 104 us (1.030); the launches traced: 101 us -> 102 us
  waiting for transfers between devices: 23.2 us -> 14 us
  Pallas kernels: 27.9 us -> 36.3 us
  starting transfers between devices: 28.5 us -> 35.2 us
  other arithmetic: 10.8 us -> 5.86 us
  local copies, waits for them, and re-layouts: 8.93 us -> 9.99 us
    ppermute x13 -> x14, waiting for transfers between devices: 23.2 us -> 12.8 us  [swap(): return lax.ppermute(array, axis, [(i, i ^ mask) for i in range(size)])]
    pallas_call x4 -> x8, Pallas kernels: 27.9 us -> 36.3 us  [call(): pl.pallas_call(kernel, out_shape=shapes, in_specs=whole(*ins), out_specs=...]
    ppermute x2 -> x3, starting transfers between devices: 7.21 us -> 12.3 us  [upward(): return lax.ppermute(array, axis, [(i, i + 1) for i in range(size - 1)])]
    reshape x3 -> x0, other arithmetic: 3.18 us -> none  [the longest x2 2.25 us: y_halo(): return tile.reshape(tile.shape[:-3] + (-1, TILE))]
    convert_element_type x5 -> x0, other arithmetic: 1.42 us -> none  [the longest x1 0.7 us: shards(): profile = psf_x[0].astype(BF)]
    optimization_barrier x0 -> x1, local copies, waits for them, and re-layouts: none -> 1.27 us  [after(): return lax.optimization_barrier((token,) + arrays)[1:]]
    add x2 -> x1, other arithmetic: 1.22 us -> 0.01 us  [shards(): exacts = numbers[:, 0] + numbers[:, 1] + numbers[:, 2]]
    ppermute x13 -> x14, starting transfers between devices: 14.8 us -> 16 us  [swap(): return lax.ppermute(array, axis, [(i, i ^ mask) for i in range(size)])]
  transfers between devices with their start and end apart: 17 -> 20, of which waited for: 6 -> 7; matrix products, arithmetic and copies ran while one was open for 13% -> 11% of each run, Pallas kernels for 12% -> 20%
where the time goes in v2:
time: 104 us; the launch traced here: 102 us
  Pallas kernels  36.3 us (35%)
  starting transfers between devices  35.2 us (34%)
  waiting for transfers between devices  14 us (13%)
  local copies, waits for them, and re-layouts  9.99 us (10%)
  other arithmetic  5.86 us (6%)
  between operations  1.05 us (1%)
    pallas_call x8, Pallas kernels, call(): pl.pallas_call(kernel, out_shape=shapes, in_specs=whole(*ins), out_specs=...  36.3 us
    ppermute x14, starting transfers between devices, swap(): return lax.ppermute(array, axis, [(i, i ^ mask) for i in range(size)])  16 us
    ppermute x14, waiting for transfers between devices, swap(): return lax.ppermute(array, axis, [(i, i ^ mask) for i in range(size)])  12.8 us
    ppermute x3, starting transfers between devices, upward(): return lax.ppermute(array, axis, [(i, i + 1) for i in range(size - 1)])  12.3 us
    ppermute x3, starting transfers between devices, downward(): return lax.ppermute(array, axis, [(i + 1, i) for i in range(size - 1)])  6.85 us
    unnamed x41, local copies, waits for them, and re-layouts  4.24 us
  transfers between devices with their start and end apart: 20, of which 7 were waited for; matrix products, arithmetic and copies ran while one was open for 11% of the time, Pallas kernels for 20%

profile of v2, /device:TPU:1, one launch (start us, length us, event | category | flops | bytes accessed | tf_op | source)
XLA Modules:
  0.0 102.4 jit_solution(9712363211263055033)
XLA Ops:
  0.7 1.3 %copy.14.taps_ref = f32[1,3,3]{2,1,0:T(4,128)} copy(f32[1,3,3]{2,0,1:T(1,128)} %param.14) | data formatting | bytes 72 | tf_op jit(solution)/shard_map/optimization_barrier | solution.py:445
  1.9 1.5 %shard_map.91.refs_0_ = bf16[40,512]{1,0:T(8,128)(2,1)} custom-call(f32[1,3,3]{2,1,0:T(4,128)} %copy.14.taps_ref, f32[1]{0:T(128)S(6)} %copy.16.bg_ref, f32[4,8,512]{2,1,0:T(8,128)} %est_ref.2, f32[1,257]{1,0:T(1,128)} %psf_ref), custom_call_target="tpu_custom_call" | custom-call | tf_op jit(solution)/shard_map/pallas_call | solution.py:465
  3.4 4.2 %collective-permute-start.2 = (bf16[40,512]{1,0:T(8,128)(2,1)}, bf16[40,512]{1,0:T(8,128)(2,1)S(1)}, u32[]{:S(2)}, u32[]{:S(2)}) collective-permute-start(bf16[40,512]{1,0:T(8,128)(2,1)} %shard_map.91.refs_0_), channel_id=1, source_target_pairs={{0,24},{8,16},{16,8},{24,0},{1,25},{9,17},{17,9},{25,1},{2,26},{10... | collective-permute-start | bytes 122888 | tf_op jit(solution)/shard_map/ppermute | solution.py:21
  9.9 1.3 %copy.15.owner_ref = s32[1,16,1]{2,1,0:T(8,128)} copy(s32[1,16,1]{1,2,0:T(1,128)} %param.10) | data formatting | bytes 128 | tf_op args[1]
  11.2 2.6 %shard_map.92 = (bf16[4,4,8,2048]{3,2,1,0:T(8,128)(2,1)}, bf16[4,4,8,2048]{3,2,1,0:T(8,128)(2,1)}) custom-call(s32[1,16,1]{2,1,0:T(8,128)} %copy.15.owner_ref, s32[1,16]{1,0:T(1,128)} %row_ref.1, bf16[16,8,2048]{2,1,0:T(8,128)(2,1)} %bitcast.61), custom_call_target="tpu_custom_call" | custom-call | tf_op jit(solution)/shard_map/pallas_call | solution.py:465
  13.8 1.7 %collective-permute-start.4 = (bf16[4,4,8,2048]{3,2,1,0:T(8,128)(2,1)}, bf16[4,4,8,2048]{3,2,1,0:T(8,128)(2,1)S(1)}, u32[]{:S(2)}, u32[]{:S(2)}) collective-permute-start(bf16[4,4,8,2048]{3,2,1,0:T(8,128)(2,1)} %get-tuple-element.28), channel_id=1, source_target_pairs={{0,1},{1,0},{2,3},{3,2},{4,5},{5,4},{6,7},{7,6},{8,9},{9,8},{10,11... | collective-permute-start | bytes 1572872 | tf_op jit(solution)/shard_map/ppermute | solution.py:21
  15.7 0.9 select_reduce_fusion
  18.7 3.2 %shard_map.94.blocks_ref.refs_12_ = bf16[6,768,256]{2,1,0:T(8,128)(2,1)} custom-call(bf16[40,512]{1,0:T(8,128)(2,1)} %shard_map.91.refs_0_, bf16[40,512]{1,0:T(8,128)(2,1)} %copy-done.10, bf16[40,512]{1,0:T(8,128)(2,1)} %copy-done.9, bf16[40,512]{1,0:T(8,128)(2,1)} %copy-done.8), custom_call_target="tpu_custom_call" | custom-call | tf_op jit(solution)/shard_map/pallas_call | solution.py:465
  24.8 1.8 %collective-permute-start.7 = (bf16[4,8,2048]{2,1,0:T(8,128)(2,1)S(1)}, bf16[4,8,2048]{2,1,0:T(8,128)(2,1)S(1)}, u32[]{:S(2)}, u32[]{:S(2)}) collective-permute-start(bf16[4,8,2048]{2,1,0:T(8,128)(2,1)S(1)} %get-tuple-element.33), channel_id=1, source_target_pairs={{0,6},{1,7},{2,4},{3,5},{4,2},{5,3},{6,0},{7,1},{8,14},{9,15},{10,... | collective-permute-start | bytes 393224 | tf_op jit(solution)/shard_map/ppermute | solution.py:21
  26.6 0.9 collective-permute-start.6
  27.5 4.8 %collective-permute-done.7.refs_3_ = bf16[4,8,2048]{2,1,0:T(8,128)(2,1)S(1)} collective-permute-done((bf16[4,8,2048]{2,1,0:T(8,128)(2,1)S(1)}, bf16[4,8,2048]{2,1,0:T(8,128)(2,1)S(1)}, u32[]{:S(2)}, u32[]{:S(2)}) %collective-permute-start.7) | collective-permute-done | bytes 131104 | tf_op jit(solution)/shard_map/ppermute | solution.py:21
  32.4 1.7 %collective-permute-done.6.refs_2_ = bf16[4,8,2048]{2,1,0:T(8,128)(2,1)S(1)} collective-permute-done((bf16[4,8,2048]{2,1,0:T(8,128)(2,1)S(1)}, bf16[4,8,2048]{2,1,0:T(8,128)(2,1)S(1)}, u32[]{:S(2)}, u32[]{:S(2)}) %collective-permute-start.6) | collective-permute-done | bytes 131104 | tf_op jit(solution)/shard_map/ppermute | solution.py:21
  34.1 1.2 %collective-permute-done.5.refs_1_ = bf16[4,8,2048]{2,1,0:T(8,128)(2,1)S(1)} collective-permute-done((bf16[4,8,2048]{2,1,0:T(8,128)(2,1)S(1)}, bf16[4,8,2048]{2,1,0:T(8,128)(2,1)S(1)}, u32[]{:S(2)}, u32[]{:S(2)}) %collective-permute-start.5) | collective-permute-done | bytes 131104 | tf_op jit(solution)/shard_map/ppermute | solution.py:21
  36.0 2.0 %shard_map.93 = (bf16[8,32,256]{2,1,0:T(8,128)(2,1)}, bf16[8,32,256]{2,1,0:T(8,128)(2,1)}) custom-call(bf16[4,8,2048]{2,1,0:T(8,128)(2,1)} %get-tuple-element.36.refs_0_, bf16[4,8,2048]{2,1,0:T(8,128)(2,1)} %copy-done.19, bf16[4,8,2048]{2,1,0:T(8,128)(2,1)} %copy-done.18, bf16[4,8,2048]{2,1,0:T(8,128)(2,1)} %copy-done.17), custom_call_target="tpu_custom_call" | custom-call | tf_op jit(solution)/shard_map/pallas_call | solution.py:465
  38.0 1.9 %collective-permute-start.9 = (bf16[8,32,256]{2,1,0:T(8,128)(2,1)}, bf16[8,32,256]{2,1,0:T(8,128)(2,1)S(1)}, u32[]{:S(2)}, u32[]{:S(2)}) collective-permute-start(bf16[8,32,256]{2,1,0:T(8,128)(2,1)} %get-tuple-element.30), channel_id=1, source_target_pairs={{0,16},{8,24},{16,0},{24,8},{1,17},{9,25},{17,1},{25,9},{2,18},{10... | collective-permute-start | bytes 393224 | tf_op jit(solution)/shard_map/ppermute | solution.py:21
  39.8 1.8 %collective-permute-start.8 = (bf16[8,32,256]{2,1,0:T(8,128)(2,1)}, bf16[8,32,256]{2,1,0:T(8,128)(2,1)S(1)}, u32[]{:S(2)}, u32[]{:S(2)}) collective-permute-start(bf16[8,32,256]{2,1,0:T(8,128)(2,1)} %get-tuple-element.29.refs_0_), channel_id=1, source_target_pairs={{0,8},{8,0},{16,24},{24,16},{1,9},{9,1},{17,25},{25,17},{2,10},{10... | collective-permute-start | bytes 393224 | tf_op jit(solution)/shard_map/ppermute | solution.py:21
  41.7 3.0 %collective-permute-start.18 = (bf16[4,8,4,512]{3,2,1,0:T(4,128)(2,1)S(1)}, bf16[4,8,4,512]{3,2,1,0:T(4,128)(2,1)S(1)}, u32[]{:S(2)}, u32[]{:S(2)}) collective-permute-start(bf16[4,8,4,512]{3,2,1,0:T(4,128)(2,1)S(1)} %pad_maximum_fusion.8), channel_id=1, source_target_pairs={{1,0},{2,1},{3,2},{5,4},{6,5},{7,6},{9,8},{10,9},{11,10},{13,12},{... | collective-permute-start | bytes 393224 | tf_op jit(solution)/shard_map/ppermute | solution.py:29
  44.7 1.7 %collective-permute-done.9.refs_2_ = bf16[8,32,256]{2,1,0:T(8,128)(2,1)S(1)} collective-permute-done((bf16[8,32,256]{2,1,0:T(8,128)(2,1)}, bf16[8,32,256]{2,1,0:T(8,128)(2,1)S(1)}, u32[]{:S(2)}, u32[]{:S(2)}) %collective-permute-start.9) | collective-permute-done | bytes 131104 | tf_op jit(solution)/shard_map/ppermute | solution.py:21
  46.4 0.9 collective-permute-start.10
  47.3 1.0 pad_maximum_fusion.5
  49.0 1.0 fusion.3
  51.0 3.1 %collective-permute-done.11.refs_4_ = bf16[2,8,24,256]{3,2,1,0:T(8,128)(2,1)S(1)} collective-permute-done((bf16[2,8,24,256]{3,2,1,0:T(8,128)(2,1)S(1)}, bf16[2,8,24,256]{3,2,1,0:T(8,128)(2,1)S(1)}, u32[]{:S(2)}, u32[]{:S(2)}) %collective-permute-start.11) | collective-permute-done | bytes 196640 | tf_op jit(solution)/shard_map/ppermute | solution.py:21
  54.2 5.0 %collective-permute-start.15 = (bf16[2,8,7,4,256]{4,3,2,1,0:T(4,128)(2,1)S(1)}, bf16[2,8,7,4,256]{4,3,2,1,0:T(4,128)(2,1)S(1)}, u32[]{:S(2)}, u32[]{:S(2)}) collective-permute-start(bf16[2,8,7,4,256]{4,3,2,1,0:T(4,128)(2,1)S(1)} %fusion.1), channel_id=1, source_target_pairs={{0,1},{1,2},{2,3},{4,5},{5,6},{6,7},{8,9},{9,10},{10,11},{12,13},{... | collective-permute-start | bytes 688136 | tf_op jit(solution)/shard_map/ppermute | solution.py:25
  59.4 1.9 %collective-permute-start.13 = (bf16[2,8,7,4,256]{4,3,2,1,0:T(4,128)(2,1)S(1)}, bf16[2,8,7,4,256]{4,3,2,1,0:T(4,128)(2,1)S(1)}, u32[]{:S(2)}, u32[]{:S(2)}) collective-permute-start(bf16[2,8,7,4,256]{4,3,2,1,0:T(4,128)(2,1)S(1)} %pad_maximum_fusion.2), channel_id=1, source_target_pairs={{1,0},{2,1},{3,2},{5,4},{6,5},{7,6},{9,8},{10,9},{11,10},{13,12},{... | collective-permute-start | bytes 688136 | tf_op jit(solution)/shard_map/ppermute | solution.py:29
  61.6 3.6 %collective-permute-start.16 = (bf16[2,8,7,4,256]{4,3,2,1,0:T(4,128)(2,1)S(1)}, bf16[2,8,7,4,256]{4,3,2,1,0:T(4,128)(2,1)S(1)}, u32[]{:S(2)}, u32[]{:S(2)}) collective-permute-start(bf16[2,8,7,4,256]{4,3,2,1,0:T(4,128)(2,1)S(1)} %fusion), channel_id=1, source_target_pairs={{0,1},{1,2},{2,3},{4,5},{5,6},{6,7},{8,9},{9,10},{10,11},{12,13},{... | collective-permute-start | bytes 688136 | tf_op jit(solution)/shard_map/ppermute | solution.py:25
  65.4 1.9 %collective-permute-start.14 = (bf16[2,8,7,4,256]{4,3,2,1,0:T(4,128)(2,1)S(1)}, bf16[2,8,7,4,256]{4,3,2,1,0:T(4,128)(2,1)S(1)}, u32[]{:S(2)}, u32[]{:S(2)}) collective-permute-start(bf16[2,8,7,4,256]{4,3,2,1,0:T(4,128)(2,1)S(1)} %pad_maximum_fusion.3), channel_id=1, source_target_pairs={{1,0},{2,1},{3,2},{5,4},{6,5},{7,6},{9,8},{10,9},{11,10},{13,12},{... | collective-permute-start | bytes 688136 | tf_op jit(solution)/shard_map/ppermute | solution.py:29
  67.5 3.6 %collective-permute-start.19 = (bf16[4,8,4,512]{3,2,1,0:T(4,128)(2,1)S(1)}, bf16[4,8,4,512]{3,2,1,0:T(4,128)(2,1)S(1)}, u32[]{:S(2)}, u32[]{:S(2)}) collective-permute-start(bf16[4,8,4,512]{3,2,1,0:T(4,128)(2,1)S(1)} %pad_maximum_fusion.9), channel_id=1, source_target_pairs={{0,1},{1,2},{2,3},{4,5},{5,6},{6,7},{8,9},{9,10},{10,11},{12,13},{... | collective-permute-start | bytes 393224 | tf_op jit(solution)/shard_map/ppermute | solution.py:25
  71.9 1.2 %collective-permute-done.19.refs_6_ = bf16[4,8,4,512]{3,2,1,0:T(4,128)(2,1)S(1)} collective-permute-done((bf16[4,8,4,512]{3,2,1,0:T(4,128)(2,1)S(1)}, bf16[4,8,4,512]{3,2,1,0:T(4,128)(2,1)S(1)}, u32[]{:S(2)}, u32[]{:S(2)}) %collective-permute-start.19) | collective-permute-done | bytes 131104 | tf_op jit(solution)/shard_map/ppermute | solution.py:25
  73.7 2.0 %shard_map.95.frame_ref.refs_13_ = bf16[10,128,256]{2,1,0:T(8,128)(2,1)} custom-call(bf16[40,512]{1,0:T(8,128)(2,1)} %shard_map.91.refs_0_, bf16[40,512]{1,0:T(8,128)(2,1)} %copy-done.10, bf16[40,512]{1,0:T(8,128)(2,1)} %copy-done.9, bf16[40,512]{1,0:T(8,128)(2,1)} %copy-done.8, bf16[4,32,512]{2,1,0:T(8,128)(2,1)} %copy-done.7, ...), custom_call_target="tpu_custom_call" | custom-call | tf_op jit(solution)/shard_map/pallas_call | solution.py:465
  75.7 5.5 %shard_map.97.refs_11_ = bf16[2,8,112,256]{3,2,1,0:T(8,128)(2,1)} custom-call(f32[40]{0:T(128)} %pad_maximum_fusion.13.num_ref, bf16[6,768,256]{2,1,0:T(8,128)(2,1)} %shard_map.94.blocks_ref.refs_12_, bf16[10,128,256]{2,1,0:T(8,128)(2,1)} %shard_map.95.frame_ref.refs_13_), custom_call_target="tpu_custom_call" | custom-call | tf_op jit(solution)/shard_map/pallas_call | solution.py:465
  81.3 5.5 %shard_map.96.refs_10_ = bf16[2,8,112,256]{3,2,1,0:T(8,128)(2,1)} custom-call(f32[40]{0:T(128)} %pad_maximum_fusion.13.num_ref, bf16[6,768,256]{2,1,0:T(8,128)(2,1)} %shard_map.94.blocks_ref.refs_12_, bf16[10,128,256]{2,1,0:T(8,128)(2,1)} %shard_map.95.frame_ref.refs_13_), custom_call_target="tpu_custom_call" | custom-call | tf_op jit(solution)/shard_map/pallas_call | solution.py:465
  88.4 14.0 %shard_map.98 = f32[4,8,512]{2,1,0:T(8,128)} custom-call(f32[40]{0:T(128)} %pad_maximum_fusion.13.num_ref, f32[288]{0:T(512)} %mul.20.wt_ref, f32[4,8,512]{2,1,0:T(8,128)} %est_ref.2, bf16[8,32,256]{2,1,0:T(8,128)(2,1)} %get-tuple-element.29.refs_0_, bf16[8,32,256]{2,1,0:T(8,128)(2,1)} %copy-done.2, bf16[8,32,256]{2,1,0:T(8,128)(2,1)} %copy-done.1, ...), custom_call_target="tpu_custom_call" | custom-call | tf_op jit(solution)/shard_map/pallas_call | solution.py:465
  (96 shorter events, 13.6 us)
Async XLA Ops:
  3.4 13.3 %collective-permute-start.2 = (bf16[40,512]{1,0:T(8,128)(2,1)}, bf16[40,512]{1,0:T(8,128)(2,1)S(1)}, u32[]{:S(2)}, u32[]{:S(2)}) collective-permute-start(bf16[40,512]{1,0:T(8,128)(2,1)} %shard_map.91.refs_0_), channel_id=1, source_target_pairs={{0,24},{8,16},{16,8},{24,0},{1,25},{9,17},{17,9},{25,1},{2,26},{10... | collective-permute-start | bytes 122888 | tf_op jit(solution)/shard_map/ppermute | solution.py:21
  7.6 9.2 %collective-permute-start.1 = (bf16[40,512]{1,0:T(8,128)(2,1)}, bf16[40,512]{1,0:T(8,128)(2,1)S(1)}, u32[]{:S(2)}, u32[]{:S(2)}) collective-permute-start(bf16[40,512]{1,0:T(8,128)(2,1)} %shard_map.91.refs_0_), channel_id=1, source_target_pairs={{0,16},{8,24},{16,0},{24,8},{1,17},{9,25},{17,1},{25,9},{2,18},{10... | collective-permute-start | bytes 122888 | tf_op jit(solution)/shard_map/ppermute | solution.py:21
  7.6 9.2 %collective-permute-start = (bf16[40,512]{1,0:T(8,128)(2,1)}, bf16[40,512]{1,0:T(8,128)(2,1)S(1)}, u32[]{:S(2)}, u32[]{:S(2)}) collective-permute-start(bf16[40,512]{1,0:T(8,128)(2,1)} %shard_map.91.refs_0_), channel_id=1, source_target_pairs={{0,8},{8,0},{16,24},{24,16},{1,9},{9,1},{17,25},{25,17},{2,10},{10... | collective-permute-start | bytes 122888 | tf_op jit(solution)/shard_map/ppermute | solution.py:21
  9.3 6.2 %collective-permute-start.3 = (s32[4,4]{1,0:T(4,128)S(1)}, s32[4,4]{1,0:T(4,128)S(1)}, u32[]{:S(2)}, u32[]{:S(2)}) collective-permute-start(s32[4,4]{1,0:T(4,128)S(1)} %broadcast_select_fusion), channel_id=1, source_target_pairs={{0,4},{4,0},{1,5},{5,1},{2,6},{6,2},{3,7},{7,3},{8,12},{12,8},{9,1... | collective-permute-start | bytes 200 | tf_op jit(solution)/shard_map/ppermute | solution.py:21
  13.8 10.3 %copy-start.6 = (bf16[4,4,8,2048]{3,2,1,0:T(8,128)(2,1)S(1)}, bf16[4,4,8,2048]{3,2,1,0:T(8,128)(2,1)}, u32[]{:S(2)}) copy-start(bf16[4,4,8,2048]{3,2,1,0:T(8,128)(2,1)} %get-tuple-element.27) | copy-start | bytes 1572868
  13.8 10.3 %collective-permute-start.4 = (bf16[4,4,8,2048]{3,2,1,0:T(8,128)(2,1)}, bf16[4,4,8,2048]{3,2,1,0:T(8,128)(2,1)S(1)}, u32[]{:S(2)}, u32[]{:S(2)}) collective-permute-start(bf16[4,4,8,2048]{3,2,1,0:T(8,128)(2,1)} %get-tuple-element.28), channel_id=1, source_target_pairs={{0,1},{1,0},{2,3},{3,2},{4,5},{5,4},{6,7},{7,6},{8,9},{9,8},{10,11... | collective-permute-start | bytes 1572872 | tf_op jit(solution)/shard_map/ppermute | solution.py:21
  16.7 1.9 %copy-start.8 = (bf16[40,512]{1,0:T(8,128)(2,1)}, bf16[40,512]{1,0:T(8,128)(2,1)S(1)}, u32[]{:S(2)}) copy-start(bf16[40,512]{1,0:T(8,128)(2,1)S(1)} %collective-permute-done.2.refs_3_) | copy-start | bytes 122884
  16.8 1.9 %copy-start.9 = (bf16[40,512]{1,0:T(8,128)(2,1)}, bf16[40,512]{1,0:T(8,128)(2,1)S(1)}, u32[]{:S(2)}) copy-start(bf16[40,512]{1,0:T(8,128)(2,1)S(1)} %collective-permute-done.1.refs_2_) | copy-start | bytes 122884
  23.3 18.2 %collective-permute-start.17 = (bf16[4,32,512]{2,1,0:T(8,128)(2,1)S(1)}, bf16[4,32,512]{2,1,0:T(8,128)(2,1)S(1)}, u32[]{:S(2)}, u32[]{:S(2)}) collective-permute-start(bf16[4,32,512]{2,1,0:T(8,128)(2,1)S(1)} %pad_maximum_fusion.6), channel_id=1, source_target_pairs={{0,4},{4,0},{1,5},{5,1},{2,6},{6,2},{3,7},{7,3},{8,12},{12,8},{9,1... | collective-permute-start | bytes 393224 | tf_op jit(solution)/shard_map/ppermute | solution.py:21
  24.8 7.5 %collective-permute-start.7 = (bf16[4,8,2048]{2,1,0:T(8,128)(2,1)S(1)}, bf16[4,8,2048]{2,1,0:T(8,128)(2,1)S(1)}, u32[]{:S(2)}, u32[]{:S(2)}) collective-permute-start(bf16[4,8,2048]{2,1,0:T(8,128)(2,1)S(1)} %get-tuple-element.33), channel_id=1, source_target_pairs={{0,6},{1,7},{2,4},{3,5},{4,2},{5,3},{6,0},{7,1},{8,14},{9,15},{10,... | collective-permute-start | bytes 393224 | tf_op jit(solution)/shard_map/ppermute | solution.py:21
  26.6 7.5 %collective-permute-start.6 = (bf16[4,8,2048]{2,1,0:T(8,128)(2,1)S(1)}, bf16[4,8,2048]{2,1,0:T(8,128)(2,1)S(1)}, u32[]{:S(2)}, u32[]{:S(2)}) collective-permute-start(bf16[4,8,2048]{2,1,0:T(8,128)(2,1)S(1)} %get-tuple-element.34), channel_id=1, source_target_pairs={{0,4},{1,5},{2,6},{3,7},{4,0},{5,1},{6,2},{7,3},{8,12},{9,13},{10,... | collective-permute-start | bytes 393224 | tf_op jit(solution)/shard_map/ppermute | solution.py:21
  27.5 7.8 %collective-permute-start.5 = (bf16[4,8,2048]{2,1,0:T(8,128)(2,1)S(1)}, bf16[4,8,2048]{2,1,0:T(8,128)(2,1)S(1)}, u32[]{:S(2)}, u32[]{:S(2)}) collective-permute-start(bf16[4,8,2048]{2,1,0:T(8,128)(2,1)S(1)} %get-tuple-element.35), channel_id=1, source_target_pairs={{0,2},{1,3},{2,0},{3,1},{4,6},{5,7},{6,4},{7,5},{8,10},{9,11},{10,... | collective-permute-start | bytes 393224 | tf_op jit(solution)/shard_map/ppermute | solution.py:21
  32.4 3.0 %copy-start.17 = (bf16[4,8,2048]{2,1,0:T(8,128)(2,1)}, bf16[4,8,2048]{2,1,0:T(8,128)(2,1)S(1)}, u32[]{:S(2)}) copy-start(bf16[4,8,2048]{2,1,0:T(8,128)(2,1)S(1)} %collective-permute-done.7.refs_3_) | copy-start | bytes 393220
  38.0 16.1 %copy-start = (bf16[8,32,256]{2,1,0:T(8,128)(2,1)S(1)}, bf16[8,32,256]{2,1,0:T(8,128)(2,1)}, u32[]{:S(2)}) copy-start(bf16[8,32,256]{2,1,0:T(8,128)(2,1)} %get-tuple-element.29.refs_0_) | copy-start | bytes 393220
  38.0 8.4 %collective-permute-start.9 = (bf16[8,32,256]{2,1,0:T(8,128)(2,1)}, bf16[8,32,256]{2,1,0:T(8,128)(2,1)S(1)}, u32[]{:S(2)}, u32[]{:S(2)}) collective-permute-start(bf16[8,32,256]{2,1,0:T(8,128)(2,1)} %get-tuple-element.30), channel_id=1, source_target_pairs={{0,16},{8,24},{16,0},{24,8},{1,17},{9,25},{17,1},{25,9},{2,18},{10... | collective-permute-start | bytes 393224 | tf_op jit(solution)/shard_map/ppermute | solution.py:21
  39.8 7.5 %collective-permute-start.8 = (bf16[8,32,256]{2,1,0:T(8,128)(2,1)}, bf16[8,32,256]{2,1,0:T(8,128)(2,1)S(1)}, u32[]{:S(2)}, u32[]{:S(2)}) collective-permute-start(bf16[8,32,256]{2,1,0:T(8,128)(2,1)} %get-tuple-element.29.refs_0_), channel_id=1, source_target_pairs={{0,8},{8,0},{16,24},{24,16},{1,9},{9,1},{17,25},{25,17},{2,10},{10... | collective-permute-start | bytes 393224 | tf_op jit(solution)/shard_map/ppermute | solution.py:21
  41.6 23.8 %copy-start.7 = (bf16[4,32,512]{2,1,0:T(8,128)(2,1)}, bf16[4,32,512]{2,1,0:T(8,128)(2,1)S(1)}, u32[]{:S(2)}) copy-start(bf16[4,32,512]{2,1,0:T(8,128)(2,1)S(1)} %collective-permute-done.17.refs_4_) | copy-start | bytes 393220
  41.7 25.7 %collective-permute-start.18 = (bf16[4,8,4,512]{3,2,1,0:T(4,128)(2,1)S(1)}, bf16[4,8,4,512]{3,2,1,0:T(4,128)(2,1)S(1)}, u32[]{:S(2)}, u32[]{:S(2)}) collective-permute-start(bf16[4,8,4,512]{3,2,1,0:T(4,128)(2,1)S(1)} %pad_maximum_fusion.8), channel_id=1, source_target_pairs={{1,0},{2,1},{3,2},{5,4},{6,5},{7,6},{9,8},{10,9},{11,10},{13,12},{... | collective-permute-start | bytes 393224 | tf_op jit(solution)/shard_map/ppermute | solution.py:29
  46.4 21.0 %copy-start.1 = (bf16[8,32,256]{2,1,0:T(8,128)(2,1)}, bf16[8,32,256]{2,1,0:T(8,128)(2,1)S(1)}, u32[]{:S(2)}) copy-start(bf16[8,32,256]{2,1,0:T(8,128)(2,1)S(1)} %collective-permute-done.9.refs_2_) | copy-start | bytes 393220
  46.4 3.8 %collective-permute-start.10 = (bf16[8,32,256]{2,1,0:T(8,128)(2,1)S(1)}, bf16[8,32,256]{2,1,0:T(8,128)(2,1)S(1)}, u32[]{:S(2)}, u32[]{:S(2)}) collective-permute-start(bf16[8,32,256]{2,1,0:T(8,128)(2,1)S(1)} %collective-permute-done.9.refs_2_), channel_id=1, source_target_pairs={{0,8},{8,0},{16,24},{24,16},{1,9},{9,1},{17,25},{25,17},{2,10},{10... | collective-permute-start | bytes 393224 | tf_op jit(solution)/shard_map/ppermute | solution.py:21
  47.3 20.1 %copy-start.2 = (bf16[8,32,256]{2,1,0:T(8,128)(2,1)}, bf16[8,32,256]{2,1,0:T(8,128)(2,1)S(1)}, u32[]{:S(2)}) copy-start(bf16[8,32,256]{2,1,0:T(8,128)(2,1)S(1)} %collective-permute-done.8.refs_1_) | copy-start | bytes 393220
  48.3 5.7 %collective-permute-start.11 = (bf16[2,8,24,256]{3,2,1,0:T(8,128)(2,1)S(1)}, bf16[2,8,24,256]{3,2,1,0:T(8,128)(2,1)S(1)}, u32[]{:S(2)}, u32[]{:S(2)}) collective-permute-start(bf16[2,8,24,256]{3,2,1,0:T(8,128)(2,1)S(1)} %pad_maximum_fusion.5), channel_id=1, source_target_pairs={{0,4},{4,0},{1,5},{5,1},{2,6},{6,2},{3,7},{7,3},{8,12},{12,8},{9,1... | collective-permute-start | bytes 589832 | tf_op jit(solution)/shard_map/ppermute | solution.py:21
  50.2 25.5 %copy-start.3 = (bf16[8,32,256]{2,1,0:T(8,128)(2,1)}, bf16[8,32,256]{2,1,0:T(8,128)(2,1)S(1)}, u32[]{:S(2)}) copy-start(bf16[8,32,256]{2,1,0:T(8,128)(2,1)S(1)} %collective-permute-done.10.refs_3_) | copy-start | bytes 393220
  50.2 11.1 %collective-permute-start.12 = (bf16[2,8,24,256]{3,2,1,0:T(8,128)(2,1)S(1)}, bf16[2,8,24,256]{3,2,1,0:T(8,128)(2,1)S(1)}, u32[]{:S(2)}, u32[]{:S(2)}) collective-permute-start(bf16[2,8,24,256]{3,2,1,0:T(8,128)(2,1)S(1)} %pad_maximum_fusion.4), channel_id=1, source_target_pairs={{0,4},{4,0},{1,5},{5,1},{2,6},{6,2},{3,7},{7,3},{8,12},{12,8},{9,1... | collective-permute-start | bytes 589832 | tf_op jit(solution)/shard_map/ppermute | solution.py:21
  54.0 27.2 %copy-start.4 = (bf16[2,8,24,256]{3,2,1,0:T(8,128)(2,1)}, bf16[2,8,24,256]{3,2,1,0:T(8,128)(2,1)S(1)}, u32[]{:S(2)}) copy-start(bf16[2,8,24,256]{3,2,1,0:T(8,128)(2,1)S(1)} %collective-permute-done.11.refs_4_) | copy-start | bytes 589828
  54.2 32.6 %collective-permute-start.15 = (bf16[2,8,7,4,256]{4,3,2,1,0:T(4,128)(2,1)S(1)}, bf16[2,8,7,4,256]{4,3,2,1,0:T(4,128)(2,1)S(1)}, u32[]{:S(2)}, u32[]{:S(2)}) collective-permute-start(bf16[2,8,7,4,256]{4,3,2,1,0:T(4,128)(2,1)S(1)} %fusion.1), channel_id=1, source_target_pairs={{0,1},{1,2},{2,3},{4,5},{5,6},{6,7},{8,9},{9,10},{10,11},{12,13},{... | collective-permute-start | bytes 688136 | tf_op jit(solution)/shard_map/ppermute | solution.py:25
  59.4 27.4 %collective-permute-start.13 = (bf16[2,8,7,4,256]{4,3,2,1,0:T(4,128)(2,1)S(1)}, bf16[2,8,7,4,256]{4,3,2,1,0:T(4,128)(2,1)S(1)}, u32[]{:S(2)}, u32[]{:S(2)}) collective-permute-start(bf16[2,8,7,4,256]{4,3,2,1,0:T(4,128)(2,1)S(1)} %pad_maximum_fusion.2), channel_id=1, source_target_pairs={{1,0},{2,1},{3,2},{5,4},{6,5},{7,6},{9,8},{10,9},{11,10},{13,12},{... | collective-permute-start | bytes 688136 | tf_op jit(solution)/shard_map/ppermute | solution.py:29
  61.4 19.9 %copy-start.5 = (bf16[2,8,24,256]{3,2,1,0:T(8,128)(2,1)}, bf16[2,8,24,256]{3,2,1,0:T(8,128)(2,1)S(1)}, u32[]{:S(2)}) copy-start(bf16[2,8,24,256]{3,2,1,0:T(8,128)(2,1)S(1)} %collective-permute-done.12.refs_5_) | copy-start | bytes 589828
  61.6 25.2 %collective-permute-start.16 = (bf16[2,8,7,4,256]{4,3,2,1,0:T(4,128)(2,1)S(1)}, bf16[2,8,7,4,256]{4,3,2,1,0:T(4,128)(2,1)S(1)}, u32[]{:S(2)}, u32[]{:S(2)}) collective-permute-start(bf16[2,8,7,4,256]{4,3,2,1,0:T(4,128)(2,1)S(1)} %fusion), channel_id=1, source_target_pairs={{0,1},{1,2},{2,3},{4,5},{5,6},{6,7},{8,9},{9,10},{10,11},{12,13},{... | collective-permute-start | bytes 688136 | tf_op jit(solution)/shard_map/ppermute | solution.py:25
  65.4 21.4 %collective-permute-start.14 = (bf16[2,8,7,4,256]{4,3,2,1,0:T(4,128)(2,1)S(1)}, bf16[2,8,7,4,256]{4,3,2,1,0:T(4,128)(2,1)S(1)}, u32[]{:S(2)}, u32[]{:S(2)}) collective-permute-start(bf16[2,8,7,4,256]{4,3,2,1,0:T(4,128)(2,1)S(1)} %pad_maximum_fusion.3), channel_id=1, source_target_pairs={{1,0},{2,1},{3,2},{5,4},{6,5},{7,6},{9,8},{10,9},{11,10},{13,12},{... | collective-permute-start | bytes 688136 | tf_op jit(solution)/shard_map/ppermute | solution.py:29
  67.5 5.6 %copy-start.15 = (bf16[4,8,4,512]{3,2,1,0:T(4,128)(2,1)}, bf16[4,8,4,512]{3,2,1,0:T(4,128)(2,1)S(1)}, u32[]{:S(2)}) copy-start(bf16[4,8,4,512]{3,2,1,0:T(4,128)(2,1)S(1)} %collective-permute-done.18.refs_5_) | copy-start | bytes 393220
  67.5 5.6 %collective-permute-start.19 = (bf16[4,8,4,512]{3,2,1,0:T(4,128)(2,1)S(1)}, bf16[4,8,4,512]{3,2,1,0:T(4,128)(2,1)S(1)}, u32[]{:S(2)}, u32[]{:S(2)}) collective-permute-start(bf16[4,8,4,512]{3,2,1,0:T(4,128)(2,1)S(1)} %pad_maximum_fusion.9), channel_id=1, source_target_pairs={{0,1},{1,2},{2,3},{4,5},{5,6},{6,7},{8,9},{9,10},{10,11},{12,13},{... | collective-permute-start | bytes 393224 | tf_op jit(solution)/shard_map/ppermute | solution.py:25
  (8 other events, 7.5 us)

commit v3 on v2

--- a/solution.py
+++ b/solution.py
@@ -19,6 +19,11 @@
 
 def swap(array, axis, size, mask):
     return lax.ppermute(array, axis, [(i, i ^ mask) for i in range(size)])
+
+
+def core_side(own, bands):
+    first = swap(own[0], "gy", bands, 1)
+    return first, swap(own[1], "gy", bands, 3)
 
 
 def upward(array, axis, size):
@@ -114,7 +119,7 @@
     lax.fori_loop(0, pairs, put, 0)
 
 
-def payload_kernel(mirrored, taps_ref, bg_ref, est_ref, psf_ref, out_ref, tail):
+def payload_kernel(mirrored, bg_ref, taps_ref, est_ref, psf_ref, _, out_ref, tail):
     depth, height = est_ref.shape[:2]
     upside = lax.axis_index("gz") if mirrored else 0
     for k in range(depth):
@@ -122,18 +127,60 @@
             k + upside * (depth - 1 - 2 * k)
         ].astype(BF)
     tail[...] = jnp.zeros(tail.shape, F32)
-    tail[0:1, : psf_ref.shape[1]] = psf_ref[...]
+    for i in range(3):
+        tail[0:1, 3 * i : 3 * i + 3] = taps_ref[0, pl.ds(i + upside * (2 - 2 * i), 1), :]
     lanes = lax.broadcasted_iota(jnp.int32, (1, 128), 1)
-    exact = jnp.where(lanes == 9, bg_ref[0], F32(0.0))
-    for i in range(3):
-        for j in range(3):
-            tap = taps_ref[0, i + upside * (2 - 2 * i), j]
-            exact = jnp.where(lanes == i * 3 + j, tap, exact)
+    exact = jnp.where(lanes == 9, bg_ref[0], tail[0:1, :128])
     for n in range(3):
         part = exact.astype(BF).astype(F32)
         tail[n + 1 : n + 2, :128] = part
         exact = exact - part
+    tail[0:1, : psf_ref.shape[1]] = psf_ref[...]
     out_ref[depth * height :, :] = tail[...].astype(BF)
+
+
+def stack_kernel(rows, *refs):
+    ins, out_ref = refs[:-2], refs[-1]
+    for v, ref in enumerate(ins):
+        out_ref[v] = ref[..., rows, :]
+
+
+def edges_kernel(height, depth, groups, *refs):
+    out1, out2 = refs[-2:]
+    views, fars = refs[: groups[0]], refs[groups[0] : groups[0] + groups[1]]
+    half = height // 2
+    gy = lax.axis_index("gy")
+    even = gy % 2 == 0
+    inner = (gy == 1) | (gy == 2)
+    lead = out1.shape[1:-3]
+
+    def put(at, block):
+        turned = pltpu.roll(block, half, block.ndim - 2)
+        one = jnp.where(even, turned, block)
+        two = jnp.where(inner, jnp.where(even, block, turned), 0.0)
+        out1[at] = one[..., :half, :].astype(BF)
+        out2[at] = two[..., :half, :].astype(BF)
+
+    for v, own in enumerate(views):
+        n = 0
+        for number, source in [(depth, own)] + [
+            (far.shape[-2] // height, far.at[v]) for far in fars
+        ]:
+            for k in range(number):
+                rows = slice(k * height, (k + 1) * height)
+                if lead:
+                    for t in range(lead[0]):
+                        put((v, t, n), source[t, rows, :].astype(F32))
+                else:
+                    put((v, n), source[rows, :].astype(F32))
+                n += 1
+
+
+def beside(even, one, two):
+    one, two = one.astype(F32), two.astype(F32)
+    return jnp.where(
+        even, jnp.concatenate([one, two], axis=0), jnp.concatenate([two, one], axis=0)
+    )
 
 
 def reversal():
@@ -143,7 +190,7 @@
 
 
 def total_kernel(parts, *refs):
-    ins, (out_ref, rev_ref) = refs[:parts], refs[parts:]
+    ins, (out_ref, rev_ref) = refs[:parts], refs[parts + 1 :]
     tiles, rows, _ = out_ref.shape
     for t in range(tiles):
         cut = slice(t * TILE, (t + 1) * TILE)
@@ -159,7 +206,7 @@
 
 
 def band_kernel(at, *refs):
-    heard, out_ref = refs[:4], refs[4]
+    heard, out_ref = refs[:4], refs[5]
     flip = reversal()
     for v in range(4):
         row = heard[v][at : at + 8, : 3 * 128].astype(F32)[0:1]
@@ -229,8 +276,9 @@
 def frame_kernel(frame, tiles, sides, *refs):
     own_refs, refs = refs[:4], refs[4:]
     side_refs = dict(zip(sides, refs[: len(sides)]))
-    hi_ref, lo_ref, out_ref = refs[len(sides) :]
+    one_ref, two_ref, _, out_ref = refs[len(sides) :]
     view = lax.axis_index("view")
+    even = lax.axis_index("gy") % 2 == 0
     for e in (0, tiles + 1):
         out_ref[e] = jnp.zeros(out_ref.shape[1:], BF)
     for v in range(4):
@@ -248,14 +296,13 @@
                 out_ref[t, f * 16 : (f + 1) * 16, :] = jnp.concatenate(
                     [
                         own.astype(F32),
-                        hi_ref[v, n, :, cut].astype(F32),
-                        lo_ref[v, n, :, cut].astype(F32),
+                        beside(even, one_ref[v, n, :, cut], two_ref[v, n, :, cut]),
                     ],
                     axis=0,
                 ).astype(BF)
 
 
-def forward_kernel(frame, tiles, views, num_ref, blocks_ref, frame_ref, recip_ref, c):
+def forward_kernel(frame, tiles, views, num_ref, blocks_ref, frame_ref, _, recip_ref, c):
     size = frame.size
     zs = frame.need(3)
     for at, v in enumerate(views):
@@ -283,7 +330,8 @@
     own_refs, refs = refs[:4], refs[4:]
     count = len(sides)
     far_refs, refs = refs[: 2 * count], refs[2 * count :]
-    hi_refs, lo_refs = refs[0:2], refs[2:4]
+    one_refs, two_refs = refs[0:2], refs[2:4]
+    even = lax.axis_index("gy") % 2 == 0
     recip_refs = refs[4:6]
     blocks_ref, frame_ref, out_ref = refs[6:9]
     m1, u2, m2, c0, c1, c2, c3, kept = refs[9:]
@@ -307,8 +355,11 @@
         return jnp.concatenate(
             [
                 own.astype(F32),
-                hi_refs[pair][w, t, n, :, cut].astype(F32),
-                lo_refs[pair][w, t, n, :, cut].astype(F32),
+                beside(
+                    even,
+                    one_refs[pair][w, t, n, :, cut],
+                    two_refs[pair][w, t, n, :, cut],
+                ),
             ],
             axis=0,
         )
@@ -441,10 +492,6 @@
                 )
 
 
-def after(token, *arrays):
-    return lax.optimization_barrier((token,) + arrays)[1:]
-
-
 def shards(
     pieces, piece_owner, piece_row, estimate, psf_x, stencil, background, bleach_table, bleach_index
 ):
@@ -488,55 +535,73 @@
     )
     other = swap(odd, "gy", bands, 1)
 
+    free = pl.ANY
+
     area = depth * height
-    late = after(even[0, 0, 0, 0], stencil, background, estimate, psf_x, bleach_index)
     payload = call(
         functools.partial(payload_kernel, frame.mirrored),
         shape(area + 8, chunk),
-        (smem, smem, vmem, vmem),
+        (smem, vmem, vmem, vmem, free),
         (vmem,),
-        *late[:4],
+        background,
+        stencil,
+        estimate,
+        psf_x,
+        even,
         scratch=[vmem((8, chunk), F32)],
     )
     heard = [payload] + [swap(payload, "view", 4, mask) for mask in (1, 2, 3)]
 
     kept = [even[k] + other[k] for k in range(pairs)]
     moved = [swap(kept[k], ("gz", "gy"), blocks, 2 * k) for k in range(1, pairs)]
+
+    def stack(arrays, slices, token):
+        rows = slice(slices.start * height, slices.stop * height)
+        dims = (len(arrays),) + arrays[0].shape[:-2] + (len(slices) * height, arrays[0].shape[-1])
+        return call(
+            functools.partial(stack_kernel, rows),
+            shape(*dims),
+            [vmem] * len(arrays) + [free],
+            (vmem,),
+            *arrays,
+            token,
+        )
+
+    def edges(arrays, far, token, count):
+        dims = (len(arrays),) + arrays[0].shape[:-2] + (count, height // 2, arrays[0].shape[-1])
+        fars = [far[s] for s in sides]
+        return call(
+            functools.partial(edges_kernel, height, depth, (len(arrays), len(fars))),
+            (shape(*dims), shape(*dims)),
+            [vmem] * (len(arrays) + len(fars)) + [free],
+            (vmem, vmem),
+            *arrays,
+            *fars,
+            token,
+        )
+
+    far_est = exchange_z(frame, lambda s: stack(heard, s, kept[1]), slabs, depth)
+    table = call(
+        functools.partial(band_kernel, area),
+        shape(6, 3 * TILE, TILE),
+        [vmem] * 4 + [free],
+        (vmem,),
+        *heard,
+        kept[1],
+    )
+    est_edges = edges(heard, far_est, table, size)
+    one_est, two_est = core_side(est_edges, bands)
+
     plain, turned = call(
         functools.partial(total_kernel, pairs),
         (shape(tiles, area, TILE), shape(tiles, area, TILE)),
-        [vmem] * pairs,
+        [vmem] * pairs + [free],
         (vmem, vmem),
         kept[0],
         *moved,
-    )
-
-    heard = after(kept[1][0, 0, 0], *heard)
-    own_est = jnp.stack([x[:area] for x in heard])
-    far_est = exchange_z(
-        frame, lambda s: own_est[:, s.start * height : s.stop * height], slabs, depth
-    )
-
-    def y_halo(own, far):
-        def rows(cut):
-            parts = [
-                x.reshape(x.shape[:-2] + (-1, height, x.shape[-1]))[..., cut, :]
-                for x in [own] + [far[s] for s in sides]
-            ]
-            return jnp.concatenate(parts, axis=-3)
-
-        hi = downward(rows(slice(0, height // 2)), "gy", bands)
-        lo = upward(rows(slice(height // 2, height)), "gy", bands)
-        return hi, lo
-
-    hi_est, lo_est = y_halo(own_est, far_est)
-    table = call(
-        functools.partial(band_kernel, area),
-        shape(6, 3 * TILE, TILE),
-        [vmem] * 4,
-        (vmem,),
-        *heard,
-    )
+        est_edges[0],
+    )
+
     numbers = jnp.stack([x[area + 1 : area + 4, :10] for x in heard]).astype(F32)
     exacts = numbers[:, 0] + numbers[:, 1] + numbers[:, 2]
     taps_all = exacts[:, :9]
@@ -546,7 +611,7 @@
         a = jnp.where(view % 2 == 1, jnp.stack([x[1], x[0], x[3], x[2]]), x)
         return jnp.where(view // 2 == 1, jnp.concatenate([a[2:], a[:2]]), a)
 
-    index_own = late[4]
+    index_own = bleach_index
     if frame.mirrored:
         index_own = jnp.where(lax.axis_index("gz") == 1, index_own[:, ::-1], index_own)
     index_far = exchange_z(frame, lambda s: index_own[:, s.start : s.stop], slabs, depth)
@@ -566,43 +631,51 @@
     opposite = swap(turned, "view", 4, 2)
     last = swap(opposite, "view", 4, 1)
 
-    def halos(pair):
-        own = jnp.stack(pair)
-        far = exchange_z(
-            frame, lambda s: own[:, :, s.start * height : s.stop * height], slabs, 3
-        )
-        hi, lo = y_halo(own, far)
-        return [far[s] for s in sides], hi, lo
-
-    far_a, hi_a, lo_a = halos((plain, near))
-    far_b, hi_b, lo_b = halos((opposite, last))
+    n3, n2, n1 = (len(frame.need(r)) * 16 for r in (3, 2, 1))
 
     est_frame = call(
         functools.partial(frame_kernel, frame, tiles, sides),
         shape(tiles + 2, size * 16, TILE),
-        [vmem] * (6 + len(sides)),
+        [vmem] * (6 + len(sides)) + [free],
         (vmem,),
         *heard,
         *[far_est[s] for s in sides],
-        hi_est,
-        lo_est,
-    )
-    n3, n2, n1 = (len(frame.need(r)) * 16 for r in (3, 2, 1))
-
-    def forward(views, nums):
+        one_est,
+        two_est,
+        plain,
+    )
+
+    def far_rows(pair, token):
+        tokens = []
+
+        def make(slices):
+            tokens.append(stack(pair, slices, token))
+            return tokens[-1]
+
+        return exchange_z(frame, make, slabs, 3), tokens[-1]
+
+    def forward(views, token):
         return call(
             functools.partial(forward_kernel, frame, tiles, views),
             shape(2, tiles, n3, TILE),
-            (smem, vmem, vmem),
+            (smem, vmem, vmem, free),
             (vmem,),
             nums,
             table,
             est_frame,
+            token,
             scratch=[vmem((tiles, size * 16, TILE), BF)],
         )
 
-    recip_a = forward((0, 1), *after(plain[0, 0, 0], nums))
-    recip_b = forward((2, 3), *after(recip_a[0, 0, 0, 0], nums))
+    count3 = len(frame.need(3))
+    far_a, token = far_rows((plain, near), est_frame)
+    recip_a = forward((0, 1), token)
+    far_b, token = far_rows((opposite, last), recip_a)
+    edges_a = edges((plain, near), far_a, token, count3)
+    one_a, two_a = core_side(edges_a, bands)
+    edges_b = edges((opposite, last), far_b, edges_a[0], count3)
+    one_b, two_b = core_side(edges_b, bands)
+    recip_b = forward((2, 3), edges_b[0])
     return call(
         functools.partial(main_kernel, frame, tiles, sides),
         shape(*estimate.shape, dtype=F32),
@@ -615,12 +688,12 @@
         near,
         opposite,
         last,
-        *far_a,
-        *far_b,
-        hi_a,
-        hi_b,
-        lo_a,
-        lo_b,
+        *[far_a[s] for s in sides],
+        *[far_b[s] for s in sides],
+        one_a,
+        one_b,
+        two_a,
+        two_b,
         recip_a,
         recip_b,
         table,

time: 104 us -> 97.1 us (0.934)
  Pallas kernels: 36.3 us -> 47.4 us
  starting transfers between devices: 35.2 us -> 24.6 us
  waiting for transfers between devices: 14 us -> 4.31 us
  local copies, waits for them, and re-layouts: 9.99 us -> 14.6 us
  other arithmetic: 5.86 us -> 4.2 us
    ppermute x6 -> x0, starting transfers between devices: 19.2 us -> none  [the longest x3 12.3 us: upward(): return lax.ppermute(array, axis, [(i, i + 1) for i in range(size - 1)])]
    pallas_call x8 -> x14, Pallas kernels: 36.3 us -> 47.4 us  [call(): pl.pallas_call(kernel, out_shape=shapes, in_specs=whole(*ins), out_specs=...]
    ppermute x14 -> x20, starting transfers between devices: 16 us -> 24.6 us  [swap(): return lax.ppermute(array, axis, [(i, i ^ mask) for i in range(size)])]
    ppermute x14 -> x20, waiting for transfers between devices: 12.8 us -> 4.31 us  [swap(): return lax.ppermute(array, axis, [(i, i ^ mask) for i in range(size)])]
    unnamed x41 -> x40, local copies, waits for them, and re-layouts: 4.24 us -> 10.6 us
    another operation x6 -> x0, other arithmetic: 2.02 us -> none  [the longest x4 1.98 us: halos(): own = jnp.stack(pair)]
    another operation x2 -> x0, local copies, waits for them, and re-layouts: 1.55 us -> none  [shards(): own_est = jnp.stack([x[:area] for x in heard])]
    another operation x2 -> x4, local copies, waits for them, and re-layouts: 0.71 us -> 2.05 us  [shards(): numbers = jnp.stack([x[area + 1:area + 4, :10] for x in heard]).astype(F32)]
  transfers between devices with their start and end apart: 20 -> 20, of which waited for: 7 -> 3; matrix products, arithmetic and copies ran while one was open for 11% -> 9% of each run, Pallas kernels for 20% -> 28%
where the time goes in v3:
time: 97.1 us; the launch traced here: 96 us
  Pallas kernels  47.4 us (49%)
  starting transfers between devices  24.6 us (25%)
  local copies, waits for them, and re-layouts  14.6 us (15%)
  waiting for transfers between devices  4.31 us (4%)
  other arithmetic  4.2 us (4%)
    pallas_call x14, Pallas kernels, call(): pl.pallas_call(kernel, out_shape=shapes, in_specs=whole(*ins), out_specs=...  47.4 us
    ppermute x20, starting transfers between devices, swap(): return lax.ppermute(array, axis, [(i, i ^ mask) for i in range(size)])  24.6 us
    unnamed x40, local copies, waits for them, and re-layouts  10.6 us
    ppermute x20, waiting for transfers between devices, swap(): return lax.ppermute(array, axis, [(i, i ^ mask) for i in range(size)])  4.31 us
    another operation x4, local copies, waits for them, and re-layouts, shards(): numbers = jnp.stack([x[area + 1:area + 4, :10] for x in heard]).astype(F32)  2.05 us
  transfers between devices with their start and end apart: 20, of which 3 were waited for; matrix products, arithmetic and copies ran while one was open for 9% of the time, Pallas kernels for 28%

profile of v3, /device:TPU:1, one launch (start us, length us, event | category | flops | bytes accessed | tf_op | source)
XLA Modules:
  0.0 96.0 jit_solution(2676641340632460137)
XLA Ops:
  0.7 1.3 %copy.15.taps_ref = f32[1,3,3]{2,1,0:T(4,128)} copy(f32[1,3,3]{2,0,1:T(1,128)} %param.14) | data formatting | bytes 72 | tf_op args[5]
  1.9 1.3 %copy.14.owner_ref = s32[1,16,1]{2,1,0:T(8,128)} copy(s32[1,16,1]{1,2,0:T(1,128)} %param.10) | data formatting | bytes 128 | tf_op args[1]
  3.2 2.6 %shard_map.91 = (bf16[4,4,8,2048]{3,2,1,0:T(8,128)(2,1)}, bf16[4,4,8,2048]{3,2,1,0:T(8,128)(2,1)}) custom-call(s32[1,16,1]{2,1,0:T(8,128)} %copy.14.owner_ref, s32[1,16]{1,0:T(1,128)} %row_ref.1, bf16[16,8,2048]{2,1,0:T(8,128)(2,1)} %bitcast.19), custom_call_target="tpu_custom_call" | custom-call | tf_op jit(solution)/shard_map/pallas_call | solution.py:512
  5.8 1.6 %shard_map.92.refs_0_ = bf16[40,512]{1,0:T(8,128)(2,1)} custom-call(f32[1]{0:T(128)S(6)} %copy.16.bg_ref, f32[1,3,3]{2,1,0:T(4,128)} %copy.15.taps_ref, f32[4,8,512]{2,1,0:T(8,128)} %est_ref.3, f32[1,257]{1,0:T(1,128)} %psf_ref.1, bf16[4,4,8,2048]{3,2,1,0:T(8,128)(2,1)} %get-tuple-element.15._), custom_call_target="tpu_custom_call" | custom-call | tf_op jit(solution)/shard_map/pallas_call | solution.py:512
  7.3 4.2 %collective-permute-start.2 = (bf16[40,512]{1,0:T(8,128)(2,1)}, bf16[40,512]{1,0:T(8,128)(2,1)S(1)}, u32[]{:S(2)}, u32[]{:S(2)}) collective-permute-start(bf16[40,512]{1,0:T(8,128)(2,1)} %shard_map.92.refs_0_), channel_id=1, source_target_pairs={{0,24},{8,16},{16,8},{24,0},{1,25},{9,17},{17,9},{25,1},{2,26},{10... | collective-permute-start | bytes 122888 | tf_op jit(solution)/shard_map/ppermute | solution.py:21
  11.8 0.8 rev.6
  13.8 1.7 %collective-permute-start.4 = (bf16[4,4,8,2048]{3,2,1,0:T(8,128)(2,1)}, bf16[4,4,8,2048]{3,2,1,0:T(8,128)(2,1)S(1)}, u32[]{:S(2)}, u32[]{:S(2)}) collective-permute-start(bf16[4,4,8,2048]{3,2,1,0:T(8,128)(2,1)} %get-tuple-element.16), channel_id=1, source_target_pairs={{0,1},{1,0},{2,3},{3,2},{4,5},{5,4},{6,7},{7,6},{8,9},{9,8},{10,11... | collective-permute-start | bytes 1572872 | tf_op jit(solution)/shard_map/ppermute | solution.py:21
  16.4 0.9 select_reduce_fusion
  17.5 1.8 %fusion = (bf16[4,8,2048]{2,1,0:T(8,128)(2,1)S(1)}, bf16[4,8,2048]{2,1,0:T(8,128)(2,1)S(1)}, bf16[4,8,2048]{2,1,0:T(8,128)(2,1)S(1)}, bf16[4,8,2048]{2,1,0:T(8,128)(2,1)}) fusion(bf16[4,4,8,2048]{3,2,1,0:T(8,128)(2,1)S(1)} %collective-permute-done.4, bf16[4,4,8,2048]{3,2,1,0:T(8,128)(2,1)} %get-tuple-element.15._), kind=kLoop, calls=%fused_computation.1 | loop fusion | flops 262144 | bytes 1572864 | tf_op jit(solution)/shard_map/add | solution.py:555
  19.3 1.2 %collective-permute-start.5 = (bf16[4,8,2048]{2,1,0:T(8,128)(2,1)S(1)}, bf16[4,8,2048]{2,1,0:T(8,128)(2,1)S(1)}, u32[]{:S(2)}, u32[]{:S(2)}) collective-permute-start(bf16[4,8,2048]{2,1,0:T(8,128)(2,1)S(1)} %get-tuple-element.29.refs_4_), channel_id=1, source_target_pairs={{0,2},{1,3},{2,0},{3,1},{4,6},{5,7},{6,4},{7,5},{8,10},{9,11},{10,... | collective-permute-start | bytes 393224 | tf_op jit(solution)/shard_map/ppermute | solution.py:21
  21.8 1.5 %shard_map.93 = bf16[4,32,512]{2,1,0:T(8,128)(2,1)} custom-call(bf16[40,512]{1,0:T(8,128)(2,1)} %shard_map.92.refs_0_, bf16[40,512]{1,0:T(8,128)(2,1)} %copy-done.8, bf16[40,512]{1,0:T(8,128)(2,1)} %copy-done.7, bf16[40,512]{1,0:T(8,128)(2,1)} %copy-done.6, bf16[4,8,2048]{2,1,0:T(8,128)(2,1)} %copy-done.3), custom_call_target="tpu_custom_call" | custom-call | tf_op jit(solution)/shard_map/pallas_call | solution.py:512
  23.2 0.9 collective-permute-start.8
  24.7 0.7 collective-permute-start.6
  26.1 3.2 %shard_map.94.refs_5_.blocks_ref.refs_12_ = bf16[6,768,256]{2,1,0:T(8,128)(2,1)} custom-call(bf16[40,512]{1,0:T(8,128)(2,1)} %shard_map.92.refs_0_, bf16[40,512]{1,0:T(8,128)(2,1)} %copy-done.8, bf16[40,512]{1,0:T(8,128)(2,1)} %copy-done.7, bf16[40,512]{1,0:T(8,128)(2,1)} %copy-done.6, bf16[4,8,2048]{2,1,0:T(8,128)(2,1)} %copy-done.3), custom_call_target="tpu_custom_call" | custom-call | tf_op jit(solution)/shard_map/pallas_call | solution.py:512
  29.9 1.9 %shard_map.95 = (bf16[4,8,4,512]{3,2,1,0:T(4,128)(2,1)}, bf16[4,8,4,512]{3,2,1,0:T(4,128)(2,1)}) custom-call(bf16[40,512]{1,0:T(8,128)(2,1)} %shard_map.92.refs_0_, bf16[40,512]{1,0:T(8,128)(2,1)} %copy-done.8, bf16[40,512]{1,0:T(8,128)(2,1)} %copy-done.7, bf16[40,512]{1,0:T(8,128)(2,1)} %copy-done.6, bf16[4,32,512]{2,1,0:T(8,128)(2,1)} %copy-done.9, ...), custom_call_target="tpu_custom_call" | custom-call | tf_op jit(solution)/shard_map/pallas_call | solution.py:512
  32.6 2.0 %shard_map.96 = (bf16[8,32,256]{2,1,0:T(8,128)(2,1)}, bf16[8,32,256]{2,1,0:T(8,128)(2,1)}) custom-call(bf16[4,8,2048]{2,1,0:T(8,128)(2,1)} %get-tuple-element.30.refs_0_, bf16[4,8,2048]{2,1,0:T(8,128)(2,1)} %copy-done.14, bf16[4,8,2048]{2,1,0:T(8,128)(2,1)} %copy-done.16, bf16[4,8,2048]{2,1,0:T(8,128)(2,1)} %copy-done.15, ...), custom_call_target="tpu_custom_call" | custom-call | tf_op jit(solution)/shard_map/pallas_call | solution.py:512
  34.5 2.0 %collective-permute-start.10 = (bf16[8,32,256]{2,1,0:T(8,128)(2,1)}, bf16[8,32,256]{2,1,0:T(8,128)(2,1)S(1)}, u32[]{:S(2)}, u32[]{:S(2)}) collective-permute-start(bf16[8,32,256]{2,1,0:T(8,128)(2,1)} %get-tuple-element.19), channel_id=1, source_target_pairs={{0,16},{8,24},{16,0},{24,8},{1,17},{9,25},{17,1},{25,9},{2,18},{10... | collective-permute-start | bytes 393224 | tf_op jit(solution)/shard_map/ppermute | solution.py:21
  37.2 3.3 %collective-permute-start.12 = (bf16[4,8,4,512]{3,2,1,0:T(4,128)(2,1)}, bf16[4,8,4,512]{3,2,1,0:T(4,128)(2,1)S(1)}, u32[]{:S(2)}, u32[]{:S(2)}) collective-permute-start(bf16[4,8,4,512]{3,2,1,0:T(4,128)(2,1)} %get-tuple-element.17.refs_4_), channel_id=1, source_target_pairs={{0,1},{1,0},{2,3},{3,2},{4,5},{5,4},{6,7},{7,6},{8,9},{9,8},{10,11... | collective-permute-start | bytes 393224 | tf_op jit(solution)/shard_map/ppermute | solution.py:21
  40.6 1.8 %collective-permute-start.9 = (bf16[8,32,256]{2,1,0:T(8,128)(2,1)}, bf16[8,32,256]{2,1,0:T(8,128)(2,1)S(1)}, u32[]{:S(2)}, u32[]{:S(2)}) collective-permute-start(bf16[8,32,256]{2,1,0:T(8,128)(2,1)} %get-tuple-element.18.refs_7_.refs_0_), channel_id=1, source_target_pairs={{0,8},{8,0},{16,24},{24,16},{1,9},{9,1},{17,25},{25,17},{2,10},{10... | collective-permute-start | bytes 393224 | tf_op jit(solution)/shard_map/ppermute | solution.py:21
  42.3 1.4 %collective-permute-start.13 = (bf16[4,8,4,512]{3,2,1,0:T(4,128)(2,1)}, bf16[4,8,4,512]{3,2,1,0:T(4,128)(2,1)S(1)}, u32[]{:S(2)}, u32[]{:S(2)}) collective-permute-start(bf16[4,8,4,512]{3,2,1,0:T(4,128)(2,1)} %get-tuple-element.20), channel_id=1, source_target_pairs={{0,3},{1,2},{2,1},{3,0},{4,7},{5,6},{6,5},{7,4},{8,11},{9,10},{10,... | collective-permute-start | bytes 393224 | tf_op jit(solution)/shard_map/ppermute | solution.py:21
  44.6 3.4 %collective-permute-done.13.refs_6_ = bf16[4,8,4,512]{3,2,1,0:T(4,128)(2,1)S(1)} collective-permute-done((bf16[4,8,4,512]{3,2,1,0:T(4,128)(2,1)}, bf16[4,8,4,512]{3,2,1,0:T(4,128)(2,1)S(1)}, u32[]{:S(2)}, u32[]{:S(2)}) %collective-permute-start.13) | collective-permute-done | bytes 131104 | tf_op jit(solution)/shard_map/ppermute | solution.py:21
  49.3 2.1 %shard_map.97.refs_2_.frame_ref.refs_13_ = bf16[10,128,256]{2,1,0:T(8,128)(2,1)} custom-call(bf16[40,512]{1,0:T(8,128)(2,1)} %shard_map.92.refs_0_, bf16[40,512]{1,0:T(8,128)(2,1)} %copy-done.8, bf16[40,512]{1,0:T(8,128)(2,1)} %copy-done.7, bf16[40,512]{1,0:T(8,128)(2,1)} %copy-done.6, bf16[4,32,512]{2,1,0:T(8,128)(2,1)} %copy-done.9, ...), custom_call_target="tpu_custom_call" | custom-call | tf_op jit(solution)/shard_map/pallas_call | solution.py:512
  52.1 1.7 %shard_map.98._ = bf16[2,8,24,256]{3,2,1,0:T(8,128)(2,1)} custom-call(bf16[8,32,256]{2,1,0:T(8,128)(2,1)} %get-tuple-element.18.refs_7_.refs_0_, bf16[8,32,256]{2,1,0:T(8,128)(2,1)} %copy-done, bf16[10,128,256]{2,1,0:T(8,128)(2,1)} %shard_map.97.refs_2_.frame_ref.refs_13_), custom_call_target="tpu_custom_call" | custom-call | tf_op jit(solution)/shard_map/pallas_call | solution.py:512
  53.7 0.9 collective-permute-start.14
  54.6 5.5 %shard_map.99.refs_2_.refs_10_ = bf16[2,8,112,256]{3,2,1,0:T(8,128)(2,1)} custom-call(f32[40]{0:T(128)} %pad_maximum_fusion.3.num_ref, bf16[6,768,256]{2,1,0:T(8,128)(2,1)} %shard_map.94.refs_5_.blocks_ref.refs_12_, bf16[10,128,256]{2,1,0:T(8,128)(2,1)} %shard_map.97.refs_2_.frame_ref.refs_13_, bf16[2,8,24,256]{3,2,1,0:T(8,128)(2,1)} %shard_map.98._), custom_call_target="tpu_custom_call" | custom-call | tf_op jit(solution)/shard_map/pallas_call | solution.py:512
  60.8 1.6 %shard_map.100.refs_3_ = bf16[2,8,24,256]{3,2,1,0:T(8,128)(2,1)} custom-call(bf16[8,32,256]{2,1,0:T(8,128)(2,1)} %copy-done.1, bf16[8,32,256]{2,1,0:T(8,128)(2,1)} %copy-done.2, bf16[2,8,112,256]{3,2,1,0:T(8,128)(2,1)} %shard_map.99.refs_2_.refs_10_), custom_call_target="tpu_custom_call" | custom-call | tf_op jit(solution)/shard_map/pallas_call | solution.py:512
  63.7 2.1 %shard_map.101 = (bf16[2,8,7,4,256]{4,3,2,1,0:T(4,128)(2,1)}, bf16[2,8,7,4,256]{4,3,2,1,0:T(4,128)(2,1)}) custom-call(bf16[8,32,256]{2,1,0:T(8,128)(2,1)} %get-tuple-element.18.refs_7_.refs_0_, bf16[8,32,256]{2,1,0:T(8,128)(2,1)} %copy-done, bf16[2,8,24,256]{3,2,1,0:T(8,128)(2,1)} %copy-done.4, bf16[2,8,24,256]{3,2,1,0:T(8,128)(2,1)} %shard_map.100.refs_3_), custom_call_target="tpu_custom_call" | custom-call | tf_op jit(solution)/shard_map/pallas_call | solution.py:512
  65.8 2.0 %collective-permute-start.18 = (bf16[2,8,7,4,256]{4,3,2,1,0:T(4,128)(2,1)}, bf16[2,8,7,4,256]{4,3,2,1,0:T(4,128)(2,1)S(1)}, u32[]{:S(2)}, u32[]{:S(2)}) collective-permute-start(bf16[2,8,7,4,256]{4,3,2,1,0:T(4,128)(2,1)} %get-tuple-element.23), channel_id=1, source_target_pairs={{0,3},{1,2},{2,1},{3,0},{4,7},{5,6},{6,5},{7,4},{8,11},{9,10},{10,... | collective-permute-start | bytes 688136 | tf_op jit(solution)/shard_map/ppermute | solution.py:21
  69.1 2.0 %shard_map.102 = (bf16[2,8,7,4,256]{4,3,2,1,0:T(4,128)(2,1)}, bf16[2,8,7,4,256]{4,3,2,1,0:T(4,128)(2,1)}) custom-call(bf16[8,32,256]{2,1,0:T(8,128)(2,1)} %copy-done.1, bf16[8,32,256]{2,1,0:T(8,128)(2,1)} %copy-done.2, bf16[2,8,24,256]{3,2,1,0:T(8,128)(2,1)} %copy-done.5, bf16[2,8,7,4,256]{4,3,2,1,0:T(4,128)(2,1)} %get-tuple-element.21.refs_3_), custom_call_target="tpu_custom_call" | custom-call | tf_op jit(solution)/shard_map/pallas_call | solution.py:512
  71.1 2.6 %collective-permute-start.19 = (bf16[2,8,7,4,256]{4,3,2,1,0:T(4,128)(2,1)}, bf16[2,8,7,4,256]{4,3,2,1,0:T(4,128)(2,1)S(1)}, u32[]{:S(2)}, u32[]{:S(2)}) collective-permute-start(bf16[2,8,7,4,256]{4,3,2,1,0:T(4,128)(2,1)} %get-tuple-element.24), channel_id=1, source_target_pairs={{0,3},{1,2},{2,1},{3,0},{4,7},{5,6},{6,5},{7,4},{8,11},{9,10},{10,... | collective-permute-start | bytes 688136 | tf_op jit(solution)/shard_map/ppermute | solution.py:21
  74.6 5.5 %shard_map.103.refs_11_ = bf16[2,8,112,256]{3,2,1,0:T(8,128)(2,1)} custom-call(f32[40]{0:T(128)} %pad_maximum_fusion.3.num_ref, bf16[6,768,256]{2,1,0:T(8,128)(2,1)} %shard_map.94.refs_5_.blocks_ref.refs_12_, bf16[10,128,256]{2,1,0:T(8,128)(2,1)} %shard_map.97.refs_2_.frame_ref.refs_13_, bf16[2,8,7,4,256]{4,3,2,1,0:T(4,128)(2,1)} %get-tuple-element.22._), custom_call_target="tpu_custom_call" | custom-call | tf_op jit(solution)/shard_map/pallas_call | solution.py:512
  81.7 14.3 %shard_map.104 = f32[4,8,512]{2,1,0:T(8,128)} custom-call(f32[40]{0:T(128)} %pad_maximum_fusion.3.num_ref, f32[288]{0:T(512)} %mul.20.wt_ref, f32[4,8,512]{2,1,0:T(8,128)} %est_ref.3, bf16[8,32,256]{2,1,0:T(8,128)(2,1)} %get-tuple-element.18.refs_7_.refs_0_, bf16[8,32,256]{2,1,0:T(8,128)(2,1)} %copy-done, bf16[8,32,256]{2,1,0:T(8,128)(2,1)} %copy-done.1, ...), custom_call_target="tpu_custom_call" | custom-call | tf_op jit(solution)/shard_map/pallas_call | solution.py:512
  (84 shorter events, 15.6 us)
Async XLA Ops:
  7.3 10.1 %collective-permute-start.2 = (bf16[40,512]{1,0:T(8,128)(2,1)}, bf16[40,512]{1,0:T(8,128)(2,1)S(1)}, u32[]{:S(2)}, u32[]{:S(2)}) collective-permute-start(bf16[40,512]{1,0:T(8,128)(2,1)} %shard_map.92.refs_0_), channel_id=1, source_target_pairs={{0,24},{8,16},{16,8},{24,0},{1,25},{9,17},{17,9},{25,1},{2,26},{10... | collective-permute-start | bytes 122888 | tf_op jit(solution)/shard_map/ppermute | solution.py:21
  11.5 9.0 %collective-permute-start.1 = (bf16[40,512]{1,0:T(8,128)(2,1)}, bf16[40,512]{1,0:T(8,128)(2,1)S(1)}, u32[]{:S(2)}, u32[]{:S(2)}) collective-permute-start(bf16[40,512]{1,0:T(8,128)(2,1)} %shard_map.92.refs_0_), channel_id=1, source_target_pairs={{0,16},{8,24},{16,0},{24,8},{1,17},{9,25},{17,1},{25,9},{2,18},{10... | collective-permute-start | bytes 122888 | tf_op jit(solution)/shard_map/ppermute | solution.py:21
  11.5 9.0 %collective-permute-start = (bf16[40,512]{1,0:T(8,128)(2,1)}, bf16[40,512]{1,0:T(8,128)(2,1)S(1)}, u32[]{:S(2)}, u32[]{:S(2)}) collective-permute-start(bf16[40,512]{1,0:T(8,128)(2,1)} %shard_map.92.refs_0_), channel_id=1, source_target_pairs={{0,8},{8,0},{16,24},{24,16},{1,9},{9,1},{17,25},{25,17},{2,10},{10... | collective-permute-start | bytes 122888 | tf_op jit(solution)/shard_map/ppermute | solution.py:21
  13.2 3.0 %collective-permute-start.3 = (s32[4,4]{1,0:T(4,128)S(1)}, s32[4,4]{1,0:T(4,128)S(1)}, u32[]{:S(2)}, u32[]{:S(2)}) collective-permute-start(s32[4,4]{1,0:T(4,128)S(1)} %broadcast_select_fusion), channel_id=1, source_target_pairs={{0,4},{4,0},{1,5},{5,1},{2,6},{6,2},{3,7},{7,3},{8,12},{12,8},{9,1... | collective-permute-start | bytes 200 | tf_op jit(solution)/shard_map/ppermute | solution.py:21
  13.8 3.6 %collective-permute-start.4 = (bf16[4,4,8,2048]{3,2,1,0:T(8,128)(2,1)}, bf16[4,4,8,2048]{3,2,1,0:T(8,128)(2,1)S(1)}, u32[]{:S(2)}, u32[]{:S(2)}) collective-permute-start(bf16[4,4,8,2048]{3,2,1,0:T(8,128)(2,1)} %get-tuple-element.16), channel_id=1, source_target_pairs={{0,1},{1,0},{2,3},{3,2},{4,5},{5,4},{6,7},{7,6},{8,9},{9,8},{10,11... | collective-permute-start | bytes 1572872 | tf_op jit(solution)/shard_map/ppermute | solution.py:21
  17.4 3.1 %copy-start.6 = (bf16[40,512]{1,0:T(8,128)(2,1)}, bf16[40,512]{1,0:T(8,128)(2,1)S(1)}, u32[]{:S(2)}) copy-start(bf16[40,512]{1,0:T(8,128)(2,1)S(1)} %collective-permute-done.2.refs_3_) | copy-start | bytes 122884
  19.3 1.3 %copy-start.3 = (bf16[4,8,2048]{2,1,0:T(8,128)(2,1)}, bf16[4,8,2048]{2,1,0:T(8,128)(2,1)S(1)}, u32[]{:S(2)}) copy-start(bf16[4,8,2048]{2,1,0:T(8,128)(2,1)S(1)} %get-tuple-element.29.refs_4_) | copy-start | bytes 393220
  19.3 12.5 %collective-permute-start.5 = (bf16[4,8,2048]{2,1,0:T(8,128)(2,1)S(1)}, bf16[4,8,2048]{2,1,0:T(8,128)(2,1)S(1)}, u32[]{:S(2)}, u32[]{:S(2)}) collective-permute-start(bf16[4,8,2048]{2,1,0:T(8,128)(2,1)S(1)} %get-tuple-element.29.refs_4_), channel_id=1, source_target_pairs={{0,2},{1,3},{2,0},{3,1},{4,6},{5,7},{6,4},{7,5},{8,10},{9,11},{10,... | collective-permute-start | bytes 393224 | tf_op jit(solution)/shard_map/ppermute | solution.py:21
  23.2 6.0 %collective-permute-start.8 = (bf16[4,32,512]{2,1,0:T(8,128)(2,1)}, bf16[4,32,512]{2,1,0:T(8,128)(2,1)S(1)}, u32[]{:S(2)}, u32[]{:S(2)}) collective-permute-start(bf16[4,32,512]{2,1,0:T(8,128)(2,1)} %shard_map.93), channel_id=1, source_target_pairs={{0,4},{4,0},{1,5},{5,1},{2,6},{6,2},{3,7},{7,3},{8,12},{12,8},{9,1... | collective-permute-start | bytes 393224 | tf_op jit(solution)/shard_map/ppermute | solution.py:21
  24.1 7.7 %collective-permute-start.7 = (bf16[4,8,2048]{2,1,0:T(8,128)(2,1)S(1)}, bf16[4,8,2048]{2,1,0:T(8,128)(2,1)S(1)}, u32[]{:S(2)}, u32[]{:S(2)}) collective-permute-start(bf16[4,8,2048]{2,1,0:T(8,128)(2,1)S(1)} %get-tuple-element.27), channel_id=1, source_target_pairs={{0,6},{1,7},{2,4},{3,5},{4,2},{5,3},{6,0},{7,1},{8,14},{9,15},{10,... | collective-permute-start | bytes 393224 | tf_op jit(solution)/shard_map/ppermute | solution.py:21
  24.7 7.1 %collective-permute-start.6 = (bf16[4,8,2048]{2,1,0:T(8,128)(2,1)S(1)}, bf16[4,8,2048]{2,1,0:T(8,128)(2,1)S(1)}, u32[]{:S(2)}, u32[]{:S(2)}) collective-permute-start(bf16[4,8,2048]{2,1,0:T(8,128)(2,1)S(1)} %get-tuple-element.28), channel_id=1, source_target_pairs={{0,4},{1,5},{2,6},{3,7},{4,0},{5,1},{6,2},{7,3},{8,12},{9,13},{10,... | collective-permute-start | bytes 393224 | tf_op jit(solution)/shard_map/ppermute | solution.py:21
  29.2 0.7 copy-start.9
  31.8 0.7 copy-start.16
  31.8 0.7 copy-start.14
  34.5 9.1 %collective-permute-start.10 = (bf16[8,32,256]{2,1,0:T(8,128)(2,1)}, bf16[8,32,256]{2,1,0:T(8,128)(2,1)S(1)}, u32[]{:S(2)}, u32[]{:S(2)}) collective-permute-start(bf16[8,32,256]{2,1,0:T(8,128)(2,1)} %get-tuple-element.19), channel_id=1, source_target_pairs={{0,16},{8,24},{16,0},{24,8},{1,17},{9,25},{17,1},{25,9},{2,18},{10... | collective-permute-start | bytes 393224 | tf_op jit(solution)/shard_map/ppermute | solution.py:21
  37.2 10.8 %collective-permute-start.12 = (bf16[4,8,4,512]{3,2,1,0:T(4,128)(2,1)}, bf16[4,8,4,512]{3,2,1,0:T(4,128)(2,1)S(1)}, u32[]{:S(2)}, u32[]{:S(2)}) collective-permute-start(bf16[4,8,4,512]{3,2,1,0:T(4,128)(2,1)} %get-tuple-element.17.refs_4_), channel_id=1, source_target_pairs={{0,1},{1,0},{2,3},{3,2},{4,5},{5,4},{6,7},{7,6},{8,9},{9,8},{10,11... | collective-permute-start | bytes 393224 | tf_op jit(solution)/shard_map/ppermute | solution.py:21
  40.6 10.9 %collective-permute-start.9 = (bf16[8,32,256]{2,1,0:T(8,128)(2,1)}, bf16[8,32,256]{2,1,0:T(8,128)(2,1)S(1)}, u32[]{:S(2)}, u32[]{:S(2)}) collective-permute-start(bf16[8,32,256]{2,1,0:T(8,128)(2,1)} %get-tuple-element.18.refs_7_.refs_0_), channel_id=1, source_target_pairs={{0,8},{8,0},{16,24},{24,16},{1,9},{9,1},{17,25},{25,17},{2,10},{10... | collective-permute-start | bytes 393224 | tf_op jit(solution)/shard_map/ppermute | solution.py:21
  42.3 5.7 %collective-permute-start.13 = (bf16[4,8,4,512]{3,2,1,0:T(4,128)(2,1)}, bf16[4,8,4,512]{3,2,1,0:T(4,128)(2,1)S(1)}, u32[]{:S(2)}, u32[]{:S(2)}) collective-permute-start(bf16[4,8,4,512]{3,2,1,0:T(4,128)(2,1)} %get-tuple-element.20), channel_id=1, source_target_pairs={{0,3},{1,2},{2,1},{3,0},{4,7},{5,6},{6,5},{7,4},{8,11},{9,10},{10,... | collective-permute-start | bytes 393224 | tf_op jit(solution)/shard_map/ppermute | solution.py:21
  43.7 16.5 %copy-start.1 = (bf16[8,32,256]{2,1,0:T(8,128)(2,1)}, bf16[8,32,256]{2,1,0:T(8,128)(2,1)S(1)}, u32[]{:S(2)}) copy-start(bf16[8,32,256]{2,1,0:T(8,128)(2,1)S(1)} %collective-permute-done.10.refs_0_.refs_2_) | copy-start | bytes 393220
  43.7 16.5 %collective-permute-start.11 = (bf16[8,32,256]{2,1,0:T(8,128)(2,1)S(1)}, bf16[8,32,256]{2,1,0:T(8,128)(2,1)S(1)}, u32[]{:S(2)}, u32[]{:S(2)}) collective-permute-start(bf16[8,32,256]{2,1,0:T(8,128)(2,1)S(1)} %collective-permute-done.10.refs_0_.refs_2_), channel_id=1, source_target_pairs={{0,8},{8,0},{16,24},{24,16},{1,9},{9,1},{17,25},{25,17},{2,10},{10... | collective-permute-start | bytes 393224 | tf_op jit(solution)/shard_map/ppermute | solution.py:21
  53.7 9.3 %collective-permute-start.14 = (bf16[2,8,24,256]{3,2,1,0:T(8,128)(2,1)}, bf16[2,8,24,256]{3,2,1,0:T(8,128)(2,1)S(1)}, u32[]{:S(2)}, u32[]{:S(2)}) collective-permute-start(bf16[2,8,24,256]{3,2,1,0:T(8,128)(2,1)} %shard_map.98._), channel_id=1, source_target_pairs={{0,4},{4,0},{1,5},{5,1},{2,6},{6,2},{3,7},{7,3},{8,12},{12,8},{9,1... | collective-permute-start | bytes 589832 | tf_op jit(solution)/shard_map/ppermute | solution.py:21
  62.5 6.0 %collective-permute-start.15 = (bf16[2,8,24,256]{3,2,1,0:T(8,128)(2,1)}, bf16[2,8,24,256]{3,2,1,0:T(8,128)(2,1)S(1)}, u32[]{:S(2)}, u32[]{:S(2)}) collective-permute-start(bf16[2,8,24,256]{3,2,1,0:T(8,128)(2,1)} %shard_map.100.refs_3_), channel_id=1, source_target_pairs={{0,4},{4,0},{1,5},{5,1},{2,6},{6,2},{3,7},{7,3},{8,12},{12,8},{9,1... | collective-permute-start | bytes 589832 | tf_op jit(solution)/shard_map/ppermute | solution.py:21
  63.1 0.7 copy-start.4
  65.8 14.3 %collective-permute-start.18 = (bf16[2,8,7,4,256]{4,3,2,1,0:T(4,128)(2,1)}, bf16[2,8,7,4,256]{4,3,2,1,0:T(4,128)(2,1)S(1)}, u32[]{:S(2)}, u32[]{:S(2)}) collective-permute-start(bf16[2,8,7,4,256]{4,3,2,1,0:T(4,128)(2,1)} %get-tuple-element.23), channel_id=1, source_target_pairs={{0,3},{1,2},{2,1},{3,0},{4,7},{5,6},{6,5},{7,4},{8,11},{9,10},{10,... | collective-permute-start | bytes 688136 | tf_op jit(solution)/shard_map/ppermute | solution.py:21
  67.8 12.4 %collective-permute-start.16 = (bf16[2,8,7,4,256]{4,3,2,1,0:T(4,128)(2,1)}, bf16[2,8,7,4,256]{4,3,2,1,0:T(4,128)(2,1)S(1)}, u32[]{:S(2)}, u32[]{:S(2)}) collective-permute-start(bf16[2,8,7,4,256]{4,3,2,1,0:T(4,128)(2,1)} %get-tuple-element.21.refs_3_), channel_id=1, source_target_pairs={{0,1},{1,0},{2,3},{3,2},{4,5},{5,4},{6,7},{7,6},{8,9},{9,8},{10,11... | collective-permute-start | bytes 688136 | tf_op jit(solution)/shard_map/ppermute | solution.py:21
  68.4 0.7 copy-start.5
  71.1 9.2 %collective-permute-start.19 = (bf16[2,8,7,4,256]{4,3,2,1,0:T(4,128)(2,1)}, bf16[2,8,7,4,256]{4,3,2,1,0:T(4,128)(2,1)S(1)}, u32[]{:S(2)}, u32[]{:S(2)}) collective-permute-start(bf16[2,8,7,4,256]{4,3,2,1,0:T(4,128)(2,1)} %get-tuple-element.24), channel_id=1, source_target_pairs={{0,3},{1,2},{2,1},{3,0},{4,7},{5,6},{6,5},{7,4},{8,11},{9,10},{10,... | collective-permute-start | bytes 688136 | tf_op jit(solution)/shard_map/ppermute | solution.py:21
  73.7 6.6 %collective-permute-start.17 = (bf16[2,8,7,4,256]{4,3,2,1,0:T(4,128)(2,1)}, bf16[2,8,7,4,256]{4,3,2,1,0:T(4,128)(2,1)S(1)}, u32[]{:S(2)}, u32[]{:S(2)}) collective-permute-start(bf16[2,8,7,4,256]{4,3,2,1,0:T(4,128)(2,1)} %get-tuple-element.22._), channel_id=1, source_target_pairs={{0,1},{1,0},{2,3},{3,2},{4,5},{5,4},{6,7},{7,6},{8,9},{9,8},{10,11... | collective-permute-start | bytes 688136 | tf_op jit(solution)/shard_map/ppermute | solution.py:21
  80.1 0.7 copy-start.10
  80.1 0.8 copy-start.11
  80.3 0.7 copy-start.12
  81.0 0.7 copy-start.13
  (7 other events, 4.5 us)

commit v4 on v3

--- a/solution.py
+++ b/solution.py
@@ -21,9 +21,11 @@
     return lax.ppermute(array, axis, [(i, i ^ mask) for i in range(size)])
 
 
-def core_side(own, bands):
+def core_side(own, bands, all_take_part):
     first = swap(own[0], "gy", bands, 1)
-    return first, swap(own[1], "gy", bands, 3)
+    if all_take_part:
+        return first, swap(own[1], "gy", bands, 3)
+    return first, lax.ppermute(own[1], "gy", [(1, 2), (2, 1)])
 
 
 def upward(array, axis, size):
@@ -139,15 +141,27 @@
     out_ref[depth * height :, :] = tail[...].astype(BF)
 
 
+def numbers_of(heard, at):
+    rows = heard[at : at + 8, :128].astype(F32)
+    exact = rows[1:2] + rows[2:3] + rows[3:4]
+    wide = jnp.broadcast_to(exact, (16, 128))
+    spot = lax.broadcasted_iota(jnp.int32, (16, 128), 0) == lax.broadcasted_iota(
+        jnp.int32, (16, 128), 1
+    )
+    column = jnp.sum(jnp.where(spot, wide, 0.0), axis=1, keepdims=True)
+    return jnp.broadcast_to(column, (16, 128))
+
+
 def stack_kernel(rows, *refs):
     ins, out_ref = refs[:-2], refs[-1]
     for v, ref in enumerate(ins):
         out_ref[v] = ref[..., rows, :]
 
 
-def edges_kernel(height, depth, groups, *refs):
+def edges_kernel(height, depth, sides, *refs):
     out1, out2 = refs[-2:]
-    views, fars = refs[: groups[0]], refs[groups[0] : groups[0] + groups[1]]
+    count = out1.shape[0]
+    views, fars = refs[:count], refs[count:-3]
     half = height // 2
     gy = lax.axis_index("gy")
     even = gy % 2 == 0
@@ -161,16 +175,26 @@
         out1[at] = one[..., :half, :].astype(BF)
         out2[at] = two[..., :half, :].astype(BF)
 
+    def far_of(v, side):
+        for ref in fars[side::sides]:
+            if v < ref.shape[0]:
+                return ref.at[v]
+            v -= ref.shape[0]
+
     for v, own in enumerate(views):
         n = 0
         for number, source in [(depth, own)] + [
-            (far.shape[-2] // height, far.at[v]) for far in fars
+            (fars[side].shape[-2] // height, far_of(v, side)) for side in range(sides)
         ]:
             for k in range(number):
                 rows = slice(k * height, (k + 1) * height)
                 if lead:
-                    for t in range(lead[0]):
+
+                    def one_tile(t, carry, v=v, n=n, source=source, rows=rows):
                         put((v, t, n), source[t, rows, :].astype(F32))
+                        return carry
+
+                    lax.fori_loop(0, lead[0], one_tile, 0, unroll=True)
                 else:
                     put((v, n), source[rows, :].astype(F32))
                 n += 1
@@ -189,15 +213,18 @@
     return jnp.where(rows + cols == TILE - 1, F32(1.0), F32(0.0)).astype(BF)
 
 
-def total_kernel(parts, *refs):
-    ins, (out_ref, rev_ref) = refs[:parts], refs[parts + 1 :]
+def total_kernel(parts, far_rows, *refs):
+    ins, (out_ref, rev_ref, *far_refs) = refs[:parts], refs[parts + 1 :]
     tiles, rows, _ = out_ref.shape
     for t in range(tiles):
         cut = slice(t * TILE, (t + 1) * TILE)
         acc = ins[0][:, :, cut].astype(F32)
         for ref in ins[1:]:
             acc = acc + ref[:, :, cut].astype(F32)
-        out_ref[t] = acc.reshape(rows, TILE).astype(BF)
+        block = acc.reshape(rows, TILE).astype(BF)
+        out_ref[t] = block
+        for ref, part in zip(far_refs, far_rows):
+            ref[0, t] = block[part]
     back = jnp.dot(
         out_ref[...].reshape(tiles * rows, TILE), reversal(), preferred_element_type=F32
     ).astype(BF)
@@ -206,7 +233,9 @@
 
 
 def band_kernel(at, *refs):
-    heard, out_ref = refs[:4], refs[5]
+    heard, (out_ref, num_ref) = refs[:4], refs[5:]
+    for v in range(4):
+        num_ref[v * 16 : (v + 1) * 16, :] = numbers_of(heard[v], at)
     flip = reversal()
     for v in range(4):
         row = heard[v][at : at + 8, : 3 * 128].astype(F32)[0:1]
@@ -316,25 +345,27 @@
                     f: c[from_t, f * 16 : (f + 1) * 16, cut].astype(F32)
                     for f in range(size)
                 }
-                sums = taps_sum(slices, zs, lambda z, i, j: num_ref[v * 9 + i * 3 + j])
+                sums = taps_sum(slices, zs, lambda z, i, j: num_ref[v * 16 + i * 3 + j : v * 16 + i * 3 + j + 1, :])
                 for n, z in enumerate(zs):
                     recip_ref[at, t, n * 16 : (n + 1) * 16, cut] = (
-                        1.0 / (along_y(sums[z]) + num_ref[36 + v])
+                        1.0 / (along_y(sums[z]) + num_ref[v * 16 + 9 : v * 16 + 10, :])
                     ).astype(BF)
             return carry
 
         lax.fori_loop(0, tiles, divide, 0)
 
 
-def main_kernel(frame, tiles, sides, num_ref, wt_ref, est_ref, *refs):
+def main_kernel(frame, tiles, sides, table_ref, *refs):
+    count = len(sides)
+    index_refs, refs = refs[: count + 1], refs[count + 1 :]
+    num_ref, est_ref, refs = refs[0], refs[1], refs[2:]
     own_refs, refs = refs[:4], refs[4:]
-    count = len(sides)
     far_refs, refs = refs[: 2 * count], refs[2 * count :]
-    one_refs, two_refs = refs[0:2], refs[2:4]
+    one_ref, two_ref = refs[:2]
+    recip_refs = refs[2:4]
+    blocks_ref, frame_ref, out_ref = refs[4:7]
+    m1, u2, m2, c0, c1, c2, c3, kept, wt = refs[7:]
     even = lax.axis_index("gy") % 2 == 0
-    recip_refs = refs[4:6]
-    blocks_ref, frame_ref, out_ref = refs[6:9]
-    m1, u2, m2, c0, c1, c2, c3, kept = refs[9:]
     c = [c0, c1, c2, c3]
     view = lax.axis_index("view")
     upside = lax.axis_index("gz") if frame.mirrored else 0
@@ -342,23 +373,42 @@
     z3, z2, z1, z0 = (frame.need(r) for r in (3, 2, 1, 0))
     sent = frame.sent(3)
 
+    for f in z2:
+        where, k = frame.source(f)
+        index_ref = index_refs[0 if where == "own" else 1 + sides.index(where)]
+        over = upside if where == "own" else 1 - upside
+        raw = k + over * (depth - 1 - 2 * k) if frame.mirrored else k
+        weights = [
+            jnp.full((16, 128), table_ref[v, index_ref[v, raw]], F32) for v in range(4)
+        ]
+        total = (weights[0] + weights[1]) + (weights[2] + weights[3])
+        for v in range(4):
+            mine = jnp.full(
+                (16, 128), table_ref[view ^ v, index_ref[view ^ v, raw]], F32
+            )
+            at = (v * frame.size + f) * 16
+            wt[at : at + 16, :] = num_ref[v * 16 : (v + 1) * 16, :] * (mine / total)
+
+    def weighted(v, z, n):
+        at = (v * frame.size + z) * 16 + 8 - n
+        return wt[at : at + 1, :]
+
     def measured(v, t, z, cut):
         where, k = frame.source(z)
-        pair, w = v // 2, v % 2
         if where == "own":
             own = own_refs[v][t, k * 8 : (k + 1) * 8, cut]
         else:
             k = k - sent[where].start
-            far = far_refs[pair * count + sides.index(where)]
-            own = far[w, t, k * 8 : (k + 1) * 8, cut]
+            far = far_refs[(count if v else 0) + sides.index(where)]
+            own = far[v - 1 if v else 0, t, k * 8 : (k + 1) * 8, cut]
         n = frame.place(z, 3)
         return jnp.concatenate(
             [
                 own.astype(F32),
                 beside(
                     even,
-                    one_refs[pair][w, t, n, :, cut],
-                    two_refs[pair][w, t, n, :, cut],
+                    one_ref[v, t, n, :, cut],
+                    two_ref[v, t, n, :, cut],
                 ),
             ],
             axis=0,
@@ -404,7 +454,7 @@
             sums = taps_sum(
                 slices,
                 zs,
-                lambda z, i, j, v=v: wt_ref[(v * frame.size + z) * 9 + i * 3 + j],
+                lambda z, i, j, v=v: weighted(v, z, i * 3 + j),
             )
             for z in zs:
                 for j in range(3):
@@ -452,10 +502,10 @@
                         for n, z in enumerate(z2)
                     }
                     sums = taps_sum(
-                        slices, z1, lambda z, i, j, w=w: num_ref[w * 9 + i * 3 + j]
+                        slices, z1, lambda z, i, j, w=w: num_ref[w * 16 + i * 3 + j : w * 16 + i * 3 + j + 1, :]
                     )
                     recips.append(
-                        {z: 1.0 / (along_y(sums[z]) + num_ref[36 + w]) for z in z1}
+                        {z: 1.0 / (along_y(sums[z]) + num_ref[w * 16 + 9 : w * 16 + 10, :]) for z in z1}
                     )
                 for n, z in enumerate(z1):
                     m2[t + 1, n * 16 : (n + 1) * 16, cut] = mix(
@@ -504,7 +554,6 @@
     frame = Frame(slabs, depth)
     size = frame.size
     sides = tuple(frame.sent(1))
-    view = lax.axis_index("view")
     vmem, smem = pltpu.VMEM, pltpu.SMEM
     params = pltpu.CompilerParams(vmem_limit_bytes=LIMIT)
 
@@ -536,6 +585,8 @@
     other = swap(odd, "gy", bands, 1)
 
     free = pl.ANY
+    kept = [even[k] + other[k] for k in range(pairs)]
+    moved = [swap(kept[k], ("gz", "gy"), blocks, 2 * k) for k in range(1, pairs)]
 
     area = depth * height
     payload = call(
@@ -547,13 +598,10 @@
         stencil,
         estimate,
         psf_x,
-        even,
+        kept[pairs - 1],
         scratch=[vmem((8, chunk), F32)],
     )
     heard = [payload] + [swap(payload, "view", 4, mask) for mask in (1, 2, 3)]
-
-    kept = [even[k] + other[k] for k in range(pairs)]
-    moved = [swap(kept[k], ("gz", "gy"), blocks, 2 * k) for k in range(1, pairs)]
 
     def stack(arrays, slices, token):
         rows = slice(slices.start * height, slices.stop * height)
@@ -567,11 +615,10 @@
             token,
         )
 
-    def edges(arrays, far, token, count):
+    def edges(arrays, fars, token, count):
         dims = (len(arrays),) + arrays[0].shape[:-2] + (count, height // 2, arrays[0].shape[-1])
-        fars = [far[s] for s in sides]
         return call(
-            functools.partial(edges_kernel, height, depth, (len(arrays), len(fars))),
+            functools.partial(edges_kernel, height, depth, len(sides)),
             (shape(*dims), shape(*dims)),
             [vmem] * (len(arrays) + len(fars)) + [free],
             (vmem, vmem),
@@ -580,57 +627,41 @@
             token,
         )
 
-    far_est = exchange_z(frame, lambda s: stack(heard, s, kept[1]), slabs, depth)
-    table = call(
+    far_est = exchange_z(frame, lambda s: stack(heard, s, payload), slabs, depth)
+    far_est = [far_est[s] for s in sides]
+    table, nums = call(
         functools.partial(band_kernel, area),
-        shape(6, 3 * TILE, TILE),
+        (shape(6, 3 * TILE, TILE), shape(64, 128, dtype=F32)),
         [vmem] * 4 + [free],
-        (vmem,),
+        (vmem, vmem),
         *heard,
-        kept[1],
+        payload,
     )
     est_edges = edges(heard, far_est, table, size)
-    one_est, two_est = core_side(est_edges, bands)
-
-    plain, turned = call(
-        functools.partial(total_kernel, pairs),
-        (shape(tiles, area, TILE), shape(tiles, area, TILE)),
+    one_est, two_est = core_side(est_edges, bands, True)
+    index_far = exchange_z(frame, lambda s: bleach_index[:, s.start : s.stop], slabs, depth)
+
+    far_slices = frame.sent(3)
+    plain, turned, *own_far = call(
+        functools.partial(
+            total_kernel,
+            pairs,
+            [slice(s.start * height, s.stop * height) for s in far_slices.values()],
+        ),
+        (shape(tiles, area, TILE), shape(tiles, area, TILE))
+        + tuple(shape(1, tiles, len(s) * height, TILE) for s in far_slices.values()),
         [vmem] * pairs + [free],
-        (vmem, vmem),
+        [vmem] * (2 + len(sides)),
         kept[0],
         *moved,
         est_edges[0],
     )
-
-    numbers = jnp.stack([x[area + 1 : area + 4, :10] for x in heard]).astype(F32)
-    exacts = numbers[:, 0] + numbers[:, 1] + numbers[:, 2]
-    taps_all = exacts[:, :9]
-    nums = jnp.concatenate([taps_all.reshape(-1), exacts[:, 9]])
-
-    def relative(x):
-        a = jnp.where(view % 2 == 1, jnp.stack([x[1], x[0], x[3], x[2]]), x)
-        return jnp.where(view // 2 == 1, jnp.concatenate([a[2:], a[:2]]), a)
-
-    index_own = bleach_index
-    if frame.mirrored:
-        index_own = jnp.where(lax.axis_index("gz") == 1, index_own[:, ::-1], index_own)
-    index_far = exchange_z(frame, lambda s: index_own[:, s.start : s.stop], slabs, depth)
-
-    def frame_index(f):
-        where, k = frame.source(f)
-        return (index_own if where == "own" else index_far[where])[:, k]
-
-    indices = jnp.stack([frame_index(f) for f in range(size)], axis=1)
-    levels = jnp.arange(bleach_table.shape[1])
-    matches = indices[:, :, None] == levels[None, None, :]
-    weight = jnp.sum(jnp.where(matches, bleach_table[:, None, :], F32(0.0)), axis=-1)
-    share = relative(weight / jnp.sum(weight, axis=0))
-    weighted = (share[:, :, None] * taps_all[:, ::-1][:, None, :]).reshape(-1)
-
     near = swap(plain, "view", 4, 1)
     opposite = swap(turned, "view", 4, 2)
     last = swap(opposite, "view", 4, 1)
-
+    ready = dict(zip([(s.start, s.stop) for s in far_slices.values()], own_far))
+    far_own = exchange_z(frame, lambda s: ready[s.start, s.stop], slabs, 3)
+    far_own = [far_own[s] for s in sides]
     n3, n2, n1 = (len(frame.need(r)) * 16 for r in (3, 2, 1))
 
     est_frame = call(
@@ -639,26 +670,17 @@
         [vmem] * (6 + len(sides)) + [free],
         (vmem,),
         *heard,
-        *[far_est[s] for s in sides],
+        *far_est,
         one_est,
         two_est,
         plain,
     )
-
-    def far_rows(pair, token):
-        tokens = []
-
-        def make(slices):
-            tokens.append(stack(pair, slices, token))
-            return tokens[-1]
-
-        return exchange_z(frame, make, slabs, 3), tokens[-1]
 
     def forward(views, token):
         return call(
             functools.partial(forward_kernel, frame, tiles, views),
             shape(2, tiles, n3, TILE),
-            (smem, vmem, vmem, free),
+            (vmem, vmem, vmem, free),
             (vmem,),
             nums,
             table,
@@ -667,33 +689,38 @@
             scratch=[vmem((tiles, size * 16, TILE), BF)],
         )
 
-    count3 = len(frame.need(3))
-    far_a, token = far_rows((plain, near), est_frame)
-    recip_a = forward((0, 1), token)
-    far_b, token = far_rows((opposite, last), recip_a)
-    edges_a = edges((plain, near), far_a, token, count3)
-    one_a, two_a = core_side(edges_a, bands)
-    edges_b = edges((opposite, last), far_b, edges_a[0], count3)
-    one_b, two_b = core_side(edges_b, bands)
-    recip_b = forward((2, 3), edges_b[0])
+    recip_a = forward((0, 1), plain)
+    tokens = []
+
+    def others(slices):
+        tokens.append(stack((near, opposite, last), slices, recip_a))
+        return tokens[-1]
+
+    far_others = exchange_z(frame, others, slabs, 3)
+    far_others = [far_others[s] for s in sides]
+    recip_b = forward((2, 3), tokens[-1])
+    all_edges = edges(
+        (plain, near, opposite, last), far_own + far_others, recip_b, len(frame.need(3))
+    )
+    one, two = core_side(all_edges, bands, False)
     return call(
         functools.partial(main_kernel, frame, tiles, sides),
         shape(*estimate.shape, dtype=F32),
-        [smem, smem] + [vmem] * (13 + 2 * len(sides)),
+        [smem] * (2 + len(sides)) + [vmem] * (12 + 2 * len(sides)),
         (vmem,),
+        bleach_table,
+        bleach_index,
+        *[index_far[s] for s in sides],
         nums,
-        weighted,
         estimate,
         plain,
         near,
         opposite,
         last,
-        *[far_a[s] for s in sides],
-        *[far_b[s] for s in sides],
-        one_a,
-        one_b,
-        two_a,
-        two_b,
+        *far_own,
+        *far_others,
+        one,
+        two,
         recip_a,
         recip_b,
         table,
@@ -704,7 +731,7 @@
             vmem((tiles + 2, n1, TILE), BF),
         ]
         + [vmem((tiles, n3, TILE), BF)] * 4
-        + [vmem((tiles, area, TILE), F32)],
+        + [vmem((tiles, area, TILE), F32), vmem((4 * size * 16, 128), F32)],
     )
 
 

time: 97.1 us -> 94.8 us (0.976)
  waiting for transfers between devices: 4.31 us -> 18.1 us
  local copies, waits for them, and re-layouts: 14.6 us -> 8.63 us
  starting transfers between devices: 24.6 us -> 20.9 us
  Pallas kernels: 47.4 us -> 44 us
  other arithmetic: 4.2 us -> 1.89 us
    ppermute x20 -> x17, waiting for transfers between devices: 4.31 us -> 13.7 us  [swap(): return lax.ppermute(array, axis, [(i, i ^ mask) for i in range(size)])]
    ppermute x20 -> x17, starting transfers between devices: 24.6 us -> 17.9 us  [swap(): return lax.ppermute(array, axis, [(i, i ^ mask) for i in range(size)])]
    ppermute x0 -> x1, waiting for transfers between devices: none -> 4.44 us  [core_side(): return (first, lax.ppermute(own[1], 'gy', [(1, 2), (2, 1)]))]
    pallas_call x14 -> x12, Pallas kernels: 47.4 us -> 44 us  [call(): pl.pallas_call(kernel, out_shape=shapes, in_specs=whole(*ins), out_specs=...]
    ppermute x0 -> x1, starting transfers between devices: none -> 3.02 us  [core_side(): return (first, lax.ppermute(own[1], 'gy', [(1, 2), (2, 1)]))]
    another operation x5 -> x0, local copies, waits for them, and re-layouts: 2.14 us -> none  [the longest x4 2.05 us: shards(): numbers = jnp.stack([x[area + 1:area + 4, :10] for x in heard]).astype(F32)]
    unnamed x40, local copies, waits for them, and re-layouts: 10.6 us -> 8.63 us
  transfers between devices with their start and end apart: 20 -> 18, of which waited for: 3 -> 9; matrix products, arithmetic and copies ran while one was open for 9% -> 1% of each run, Pallas kernels for 28% -> 19%
where the time goes in v4:
time: 94.8 us; the launch traced here: 94.3 us
  Pallas kernels  44 us (46%)
  starting transfers between devices  20.9 us (22%)
  waiting for transfers between devices  18.1 us (19%)
  local copies, waits for them, and re-layouts  8.63 us (9%)
  other arithmetic  1.89 us (2%)
    pallas_call x12, Pallas kernels, call(): pl.pallas_call(kernel, out_shape=shapes, in_specs=whole(*ins), out_specs=...  44 us
    ppermute x17, starting transfers between devices, swap(): return lax.ppermute(array, axis, [(i, i ^ mask) for i in range(size)])  17.9 us
    ppermute x17, waiting for transfers between devices, swap(): return lax.ppermute(array, axis, [(i, i ^ mask) for i in range(size)])  13.7 us
    unnamed x40, local copies, waits for them, and re-layouts  8.63 us
    ppermute x1, waiting for transfers between devices, core_side(): return (first, lax.ppermute(own[1], 'gy', [(1, 2), (2, 1)]))  4.44 us
    ppermute x1, starting transfers between devices, core_side(): return (first, lax.ppermute(own[1], 'gy', [(1, 2), (2, 1)]))  3.02 us
  transfers between devices with their start and end apart: 18, of which 9 were waited for; matrix products, arithmetic and copies ran while one was open for 1% of the time, Pallas kernels for 19%

profile of v4, /device:TPU:1, one launch (start us, length us, event | category | flops | bytes accessed | tf_op | source)
XLA Modules:
  0.0 94.3 jit_solution(9461380553135588438)
XLA Ops:
  0.0 1.3 %copy.10.owner_ref = s32[1,16,1]{2,1,0:T(8,128)} copy(s32[1,16,1]{1,2,0:T(1,128)} %param.10) | data formatting | bytes 128 | tf_op args[1]
  1.3 2.6 %shard_map.91 = (bf16[4,4,8,2048]{3,2,1,0:T(8,128)(2,1)}, bf16[4,4,8,2048]{3,2,1,0:T(8,128)(2,1)}) custom-call(s32[1,16,1]{2,1,0:T(8,128)} %copy.10.owner_ref, s32[1,16]{1,0:T(1,128)} %row_ref.1, bf16[16,8,2048]{2,1,0:T(8,128)(2,1)} %bitcast.9), custom_call_target="tpu_custom_call" | custom-call | tf_op jit(solution)/shard_map/pallas_call | solution.py:561
  4.0 1.3 %copy.11.taps_ref = f32[1,3,3]{2,1,0:T(4,128)} copy(f32[1,3,3]{2,0,1:T(1,128)} %param.14) | data formatting | bytes 72 | tf_op args[5]
  6.0 1.9 %fusion = (bf16[4,8,2048]{2,1,0:T(8,128)(2,1)S(1)}, bf16[4,8,2048]{2,1,0:T(8,128)(2,1)S(1)}, bf16[4,8,2048]{2,1,0:T(8,128)(2,1)}, bf16[4,8,2048]{2,1,0:T(8,128)(2,1)}) fusion(bf16[4,4,8,2048]{3,2,1,0:T(8,128)(2,1)S(1)} %collective-permute-done.1, bf16[4,4,8,2048]{3,2,1,0:T(8,128)(2,1)} %get-tuple-element.16), kind=kLoop, calls=%fused_computation.1 | loop fusion | flops 262144 | bytes 1572864 | tf_op jit(solution)/shard_map/add | solution.py:588
  7.9 1.6 %shard_map.92.refs_0_.refs_4_ = bf16[40,512]{1,0:T(8,128)(2,1)} custom-call(f32[1]{0:T(128)S(6)} %copy.12.bg_ref, f32[1,3,3]{2,1,0:T(4,128)} %copy.11.taps_ref, f32[4,8,512]{2,1,0:T(8,128)} %refs_3_.1, f32[1,257]{1,0:T(1,128)} %psf_ref.1, bf16[4,8,2048]{2,1,0:T(8,128)(2,1)} %get-tuple-element.30._), custom_call_target="tpu_custom_call" | custom-call | tf_op jit(solution)/shard_map/pallas_call | solution.py:561
  9.5 2.6 %collective-permute-start.2 = (bf16[40,512]{1,0:T(8,128)(2,1)}, bf16[40,512]{1,0:T(8,128)(2,1)S(1)}, u32[]{:S(2)}, u32[]{:S(2)}) collective-permute-start(bf16[40,512]{1,0:T(8,128)(2,1)} %shard_map.92.refs_0_.refs_4_), channel_id=1, source_target_pairs={{0,8},{8,0},{16,24},{24,16},{1,9},{9,1},{17,25},{25,17},{2,10},{10... | collective-permute-start | bytes 122888 | tf_op jit(solution)/shard_map/ppermute | solution.py:21
  12.1 2.3 %collective-permute-start.3 = (bf16[40,512]{1,0:T(8,128)(2,1)}, bf16[40,512]{1,0:T(8,128)(2,1)S(1)}, u32[]{:S(2)}, u32[]{:S(2)}) collective-permute-start(bf16[40,512]{1,0:T(8,128)(2,1)} %shard_map.92.refs_0_.refs_4_), channel_id=1, source_target_pairs={{0,16},{8,24},{16,0},{24,8},{1,17},{9,25},{17,1},{25,9},{2,18},{10... | collective-permute-start | bytes 122888 | tf_op jit(solution)/shard_map/ppermute | solution.py:21
  14.4 2.0 %collective-permute-done.3.refs_2_ = bf16[40,512]{1,0:T(8,128)(2,1)S(1)} collective-permute-done((bf16[40,512]{1,0:T(8,128)(2,1)}, bf16[40,512]{1,0:T(8,128)(2,1)S(1)}, u32[]{:S(2)}, u32[]{:S(2)}) %collective-permute-start.3) | collective-permute-done | bytes 40992 | tf_op jit(solution)/shard_map/ppermute | solution.py:21
  16.4 2.8 %collective-permute-done.4.refs_3_ = bf16[40,512]{1,0:T(8,128)(2,1)S(1)} collective-permute-done((bf16[40,512]{1,0:T(8,128)(2,1)}, bf16[40,512]{1,0:T(8,128)(2,1)S(1)}, u32[]{:S(2)}, u32[]{:S(2)}) %collective-permute-start.4) | collective-permute-done | bytes 40992 | tf_op jit(solution)/shard_map/ppermute | solution.py:21
  19.9 1.5 %shard_map.94 = bf16[4,32,512]{2,1,0:T(8,128)(2,1)} custom-call(bf16[40,512]{1,0:T(8,128)(2,1)} %shard_map.92.refs_0_.refs_4_, bf16[40,512]{1,0:T(8,128)(2,1)} %copy-done.4, bf16[40,512]{1,0:T(8,128)(2,1)} %copy-done.5, bf16[40,512]{1,0:T(8,128)(2,1)} %copy-done.6, bf16[40,512]{1,0:T(8,128)(2,1)} %shard_map.92.refs_0_.refs_4_), custom_call_target="tpu_custom_call" | custom-call | tf_op jit(solution)/shard_map/pallas_call | solution.py:561
  21.4 1.2 %collective-permute-start.8 = (bf16[4,32,512]{2,1,0:T(8,128)(2,1)}, bf16[4,32,512]{2,1,0:T(8,128)(2,1)S(1)}, u32[]{:S(2)}, u32[]{:S(2)}) collective-permute-start(bf16[4,32,512]{2,1,0:T(8,128)(2,1)} %shard_map.94), channel_id=1, source_target_pairs={{0,4},{4,0},{1,5},{5,1},{2,6},{6,2},{3,7},{7,3},{8,12},{12,8},{9,1... | collective-permute-start | bytes 393224 | tf_op jit(solution)/shard_map/ppermute | solution.py:21
  22.6 1.2 %collective-permute-start.7 = (bf16[4,8,2048]{2,1,0:T(8,128)(2,1)}, bf16[4,8,2048]{2,1,0:T(8,128)(2,1)S(1)}, u32[]{:S(2)}, u32[]{:S(2)}) collective-permute-start(bf16[4,8,2048]{2,1,0:T(8,128)(2,1)} %get-tuple-element.30._), channel_id=1, source_target_pairs={{0,6},{1,7},{2,4},{3,5},{4,2},{5,3},{6,0},{7,1},{8,14},{9,15},{10,... | collective-permute-start | bytes 393224 | tf_op jit(solution)/shard_map/ppermute | solution.py:21
  24.0 1.2 %collective-permute-start.6 = (bf16[4,8,2048]{2,1,0:T(8,128)(2,1)S(1)}, bf16[4,8,2048]{2,1,0:T(8,128)(2,1)S(1)}, u32[]{:S(2)}, u32[]{:S(2)}) collective-permute-start(bf16[4,8,2048]{2,1,0:T(8,128)(2,1)S(1)} %get-tuple-element.27), channel_id=1, source_target_pairs={{0,4},{1,5},{2,6},{3,7},{4,0},{5,1},{6,2},{7,3},{8,12},{9,13},{10,... | collective-permute-start | bytes 393224 | tf_op jit(solution)/shard_map/ppermute | solution.py:21
  25.2 3.2 %shard_map.93 = (bf16[6,768,256]{2,1,0:T(8,128)(2,1)}, f32[64,128]{1,0:T(8,128)}) custom-call(bf16[40,512]{1,0:T(8,128)(2,1)} %shard_map.92.refs_0_.refs_4_, bf16[40,512]{1,0:T(8,128)(2,1)} %copy-done.4, bf16[40,512]{1,0:T(8,128)(2,1)} %copy-done.5, bf16[40,512]{1,0:T(8,128)(2,1)} %copy-done.6, bf16[40,512]{1,0:T(8,128)(2,1)} %shard_map.92.refs_0_.refs_4_), custom_call_target="tpu_custom_call" | custom-call | tf_op jit(solution)/shard_map/pallas_call | solution.py:561
  29.1 1.9 %shard_map.95 = (bf16[4,8,4,512]{3,2,1,0:T(4,128)(2,1)}, bf16[4,8,4,512]{3,2,1,0:T(4,128)(2,1)}) custom-call(bf16[40,512]{1,0:T(8,128)(2,1)} %shard_map.92.refs_0_.refs_4_, bf16[40,512]{1,0:T(8,128)(2,1)} %copy-done.4, bf16[40,512]{1,0:T(8,128)(2,1)} %copy-done.5, bf16[40,512]{1,0:T(8,128)(2,1)} %copy-done.6, bf16[4,32,512]{2,1,0:T(8,128)(2,1)} %copy-done.7, ...), custom_call_target="tpu_custom_call" | custom-call | tf_op jit(solution)/shard_map/pallas_call | solution.py:561
  32.5 2.0 %shard_map.96 = (bf16[8,32,256]{2,1,0:T(8,128)(2,1)}, bf16[8,32,256]{2,1,0:T(8,128)(2,1)}, bf16[1,8,24,256]{3,2,1,0:T(8,128)(2,1)}) custom-call(bf16[4,8,2048]{2,1,0:T(8,128)(2,1)} %get-tuple-element.29.refs_0_, bf16[4,8,2048]{2,1,0:T(8,128)(2,1)} %copy-done.12, bf16[4,8,2048]{2,1,0:T(8,128)(2,1)} %copy-done.13, bf16[4,8,2048]{2,1,0:T(8,128)(2,1)} %copy-done.11, ...), custom_call_target="tpu_custom_call" | custom-call | tf_op jit(solution)/shard_map/pallas_call | solution.py:561
  34.5 2.5 %collective-permute-start.13 = (bf16[4,8,4,512]{3,2,1,0:T(4,128)(2,1)}, bf16[4,8,4,512]{3,2,1,0:T(4,128)(2,1)S(1)}, u32[]{:S(2)}, u32[]{:S(2)}) collective-permute-start(bf16[4,8,4,512]{3,2,1,0:T(4,128)(2,1)} %get-tuple-element.20.refs_4_), channel_id=1, source_target_pairs={{0,1},{1,0},{2,3},{3,2},{4,5},{5,4},{6,7},{7,6},{8,9},{9,8},{10,11... | collective-permute-start | bytes 393224 | tf_op jit(solution)/shard_map/ppermute | solution.py:21
  37.0 1.1 %collective-permute-start.14 = (bf16[4,8,4,512]{3,2,1,0:T(4,128)(2,1)}, bf16[4,8,4,512]{3,2,1,0:T(4,128)(2,1)S(1)}, u32[]{:S(2)}, u32[]{:S(2)}) collective-permute-start(bf16[4,8,4,512]{3,2,1,0:T(4,128)(2,1)} %get-tuple-element.24), channel_id=1, source_target_pairs={{0,3},{1,2},{2,1},{3,0},{4,7},{5,6},{6,5},{7,4},{8,11},{9,10},{10,... | collective-permute-start | bytes 393224 | tf_op jit(solution)/shard_map/ppermute | solution.py:21
  38.1 1.4 %collective-permute-start.9 = (bf16[8,32,256]{2,1,0:T(8,128)(2,1)}, bf16[8,32,256]{2,1,0:T(8,128)(2,1)S(1)}, u32[]{:S(2)}, u32[]{:S(2)}) collective-permute-start(bf16[8,32,256]{2,1,0:T(8,128)(2,1)} %get-tuple-element.21.refs_7_._.refs_0_.refs_4_), channel_id=1, source_target_pairs={{0,8},{8,0},{16,24},{24,16},{1,9},{9,1},{17,25},{25,17},{2,10},{10... | collective-permute-start | bytes 393224 | tf_op jit(solution)/shard_map/ppermute | solution.py:21
  39.5 2.2 %collective-permute-done.10.refs_1_.refs_2_.refs_6_ = bf16[8,32,256]{2,1,0:T(8,128)(2,1)S(1)} collective-permute-done((bf16[8,32,256]{2,1,0:T(8,128)(2,1)}, bf16[8,32,256]{2,1,0:T(8,128)(2,1)S(1)}, u32[]{:S(2)}, u32[]{:S(2)}) %collective-permute-start.10) | collective-permute-done | bytes 131104 | tf_op jit(solution)/shard_map/ppermute | solution.py:21
  43.3 2.1 %shard_map.97.frame_ref.refs_15_ = bf16[10,128,256]{2,1,0:T(8,128)(2,1)} custom-call(bf16[40,512]{1,0:T(8,128)(2,1)} %shard_map.92.refs_0_.refs_4_, bf16[40,512]{1,0:T(8,128)(2,1)} %copy-done.4, bf16[40,512]{1,0:T(8,128)(2,1)} %copy-done.5, bf16[40,512]{1,0:T(8,128)(2,1)} %copy-done.6, bf16[4,32,512]{2,1,0:T(8,128)(2,1)} %copy-done.7, ...), custom_call_target="tpu_custom_call" | custom-call | tf_op jit(solution)/shard_map/pallas_call | solution.py:561
  45.4 5.6 %shard_map.98.refs_3_.refs_12_ = bf16[2,8,112,256]{3,2,1,0:T(8,128)(2,1)} custom-call(f32[64,128]{1,0:T(8,128)} %get-tuple-element.18.num_ref.refs_2_, bf16[6,768,256]{2,1,0:T(8,128)(2,1)} %get-tuple-element.19.refs_5_.blocks_ref.refs_14_, bf16[10,128,256]{2,1,0:T(8,128)(2,1)} %shard_map.97.frame_ref.refs_15_, ...), custom_call_target="tpu_custom_call" | custom-call | tf_op jit(solution)/shard_map/pallas_call | solution.py:561
  52.2 1.8 %shard_map.99._ = bf16[3,8,24,256]{3,2,1,0:T(8,128)(2,1)} custom-call(bf16[8,32,256]{2,1,0:T(8,128)(2,1)} %copy-done.1, bf16[8,32,256]{2,1,0:T(8,128)(2,1)} %copy-done, bf16[8,32,256]{2,1,0:T(8,128)(2,1)} %copy-done.2, bf16[2,8,112,256]{3,2,1,0:T(8,128)(2,1)} %shard_map.98.refs_3_.refs_12_), custom_call_target="tpu_custom_call" | custom-call | tf_op jit(solution)/shard_map/pallas_call | solution.py:561
  54.3 1.2 %collective-permute-start.12 = (bf16[1,8,24,256]{3,2,1,0:T(8,128)(2,1)S(1)}, bf16[1,8,24,256]{3,2,1,0:T(8,128)(2,1)S(1)}, u32[]{:S(2)}, u32[]{:S(2)}) collective-permute-start(bf16[1,8,24,256]{3,2,1,0:T(8,128)(2,1)S(1)} %copy-done.18), channel_id=1, source_target_pairs={{0,4},{4,0},{1,5},{5,1},{2,6},{6,2},{3,7},{7,3},{8,12},{12,8},{9,1... | collective-permute-start | bytes 294920 | tf_op jit(solution)/shard_map/ppermute | solution.py:21
  55.5 5.5 %shard_map.100.refs_6_.refs_13_ = bf16[2,8,112,256]{3,2,1,0:T(8,128)(2,1)} custom-call(f32[64,128]{1,0:T(8,128)} %get-tuple-element.18.num_ref.refs_2_, bf16[6,768,256]{2,1,0:T(8,128)(2,1)} %get-tuple-element.19.refs_5_.blocks_ref.refs_14_, bf16[10,128,256]{2,1,0:T(8,128)(2,1)} %shard_map.97.frame_ref.refs_15_, bf16[3,8,24,256]{3,2,1,0:T(8,128)(2,1)} %shard_map.99._), custom_call_target="tpu_custom_call" | custom-call | tf_op jit(solution)/shard_map/pallas_call | solution.py:561
  61.0 2.4 %collective-permute-done.12.refs_4_.refs_8_ = bf16[1,8,24,256]{3,2,1,0:T(8,128)(2,1)S(1)} collective-permute-done((bf16[1,8,24,256]{3,2,1,0:T(8,128)(2,1)S(1)}, bf16[1,8,24,256]{3,2,1,0:T(8,128)(2,1)S(1)}, u32[]{:S(2)}, u32[]{:S(2)}) %collective-permute-start.12) | collective-permute-done | bytes 98336 | tf_op jit(solution)/shard_map/ppermute | solution.py:21
  64.8 2.6 %shard_map.101 = (bf16[4,8,7,4,256]{4,3,2,1,0:T(4,128)(2,1)}, bf16[4,8,7,4,256]{4,3,2,1,0:T(4,128)(2,1)}) custom-call(bf16[8,32,256]{2,1,0:T(8,128)(2,1)} %get-tuple-element.21.refs_7_._.refs_0_.refs_4_, bf16[8,32,256]{2,1,0:T(8,128)(2,1)} %copy-done.1, bf16[8,32,256]{2,1,0:T(8,128)(2,1)} %copy-done, bf16[8,32,256]{2,1,0:T(8,128)(2,1)} %copy-done.2, ...), custom_call_target="tpu_custom_call" | custom-call | tf_op jit(solution)/shard_map/pallas_call | solution.py:561
  67.4 2.3 %collective-permute-start.16 = (bf16[4,8,7,4,256]{4,3,2,1,0:T(4,128)(2,1)}, bf16[4,8,7,4,256]{4,3,2,1,0:T(4,128)(2,1)S(1)}, u32[]{:S(2)}, u32[]{:S(2)}) collective-permute-start(bf16[4,8,7,4,256]{4,3,2,1,0:T(4,128)(2,1)} %get-tuple-element.25), channel_id=1, source_target_pairs={{0,1},{1,0},{2,3},{3,2},{4,5},{5,4},{6,7},{7,6},{8,9},{9,8},{10,11... | collective-permute-start | bytes 1376264 | tf_op jit(solution)/shard_map/ppermute | solution.py:21
  69.7 3.0 %collective-permute-start.17 = (bf16[4,8,7,4,256]{4,3,2,1,0:T(4,128)(2,1)}, bf16[4,8,7,4,256]{4,3,2,1,0:T(4,128)(2,1)S(1)}, u32[]{:S(2)}, u32[]{:S(2)}) collective-permute-start(bf16[4,8,7,4,256]{4,3,2,1,0:T(4,128)(2,1)} %get-tuple-element.26), channel_id=1, source_target_pairs={{1,2},{2,1},{5,6},{6,5},{9,10},{10,9},{13,14},{14,13},{17,18},{18,... | collective-permute-start | bytes 1376264 | tf_op jit(solution)/shard_map/ppermute | solution.py:28
  73.1 2.2 %collective-permute-done.refs_1_ = s32[4,4]{1,0:T(4,128)S(1)} collective-permute-done((s32[4,4]{1,0:T(4,128)S(1)}, s32[4,4]{1,0:T(4,128)S(1)}, u32[]{:S(2)}, u32[]{:S(2)}) %collective-permute-start) | collective-permute-done | bytes 96 | tf_op jit(solution)/shard_map/ppermute | solution.py:21
  75.2 4.4 %collective-permute-done.17.refs_11_ = bf16[4,8,7,4,256]{4,3,2,1,0:T(4,128)(2,1)S(1)} collective-permute-done((bf16[4,8,7,4,256]{4,3,2,1,0:T(4,128)(2,1)}, bf16[4,8,7,4,256]{4,3,2,1,0:T(4,128)(2,1)S(1)}, u32[]{:S(2)}, u32[]{:S(2)}) %collective-permute-start.17) | collective-permute-done | bytes 458784 | tf_op jit(solution)/shard_map/ppermute | solution.py:28
  80.5 13.8 %shard_map.102 = f32[4,8,512]{2,1,0:T(8,128)} custom-call(f32[4,16]{1,0:T(4,128)} %table_ref.1, s32[4,4]{1,0:T(4,128)} %refs_0_.1, s32[4,4]{1,0:T(4,128)} %copy-done.17, f32[64,128]{1,0:T(8,128)} %get-tuple-element.18.num_ref.refs_2_, f32[4,8,512]{2,1,0:T(8,128)} %refs_3_.1, bf16[8,32,256]{2,1,0:T(8,128)(2,1)} %get-tuple-element.21.refs_7_._.refs_0_.refs_4_, ...), custom_call_target="tpu_custom_call" | custom-call | tf_op jit(solution)/shard_map/pallas_call | solution.py:561
  (57 shorter events, 8.9 us)
Async XLA Ops:
  3.9 2.1 %collective-permute-start.1 = (bf16[4,4,8,2048]{3,2,1,0:T(8,128)(2,1)}, bf16[4,4,8,2048]{3,2,1,0:T(8,128)(2,1)S(1)}, u32[]{:S(2)}, u32[]{:S(2)}) collective-permute-start(bf16[4,4,8,2048]{3,2,1,0:T(8,128)(2,1)} %get-tuple-element.17), channel_id=1, source_target_pairs={{0,1},{1,0},{2,3},{3,2},{4,5},{5,4},{6,7},{7,6},{8,9},{9,8},{10,11... | collective-permute-start | bytes 1572872 | tf_op jit(solution)/shard_map/ppermute | solution.py:21
  9.5 4.9 %collective-permute-start.2 = (bf16[40,512]{1,0:T(8,128)(2,1)}, bf16[40,512]{1,0:T(8,128)(2,1)S(1)}, u32[]{:S(2)}, u32[]{:S(2)}) collective-permute-start(bf16[40,512]{1,0:T(8,128)(2,1)} %shard_map.92.refs_0_.refs_4_), channel_id=1, source_target_pairs={{0,8},{8,0},{16,24},{24,16},{1,9},{9,1},{17,25},{25,17},{2,10},{10... | collective-permute-start | bytes 122888 | tf_op jit(solution)/shard_map/ppermute | solution.py:21
  12.1 4.3 %collective-permute-start.3 = (bf16[40,512]{1,0:T(8,128)(2,1)}, bf16[40,512]{1,0:T(8,128)(2,1)S(1)}, u32[]{:S(2)}, u32[]{:S(2)}) collective-permute-start(bf16[40,512]{1,0:T(8,128)(2,1)} %shard_map.92.refs_0_.refs_4_), channel_id=1, source_target_pairs={{0,16},{8,24},{16,0},{24,8},{1,17},{9,25},{17,1},{25,9},{2,18},{10... | collective-permute-start | bytes 122888 | tf_op jit(solution)/shard_map/ppermute | solution.py:21
  14.4 4.9 %collective-permute-start.4 = (bf16[40,512]{1,0:T(8,128)(2,1)}, bf16[40,512]{1,0:T(8,128)(2,1)S(1)}, u32[]{:S(2)}, u32[]{:S(2)}) collective-permute-start(bf16[40,512]{1,0:T(8,128)(2,1)} %shard_map.92.refs_0_.refs_4_), channel_id=1, source_target_pairs={{0,24},{8,16},{16,8},{24,0},{1,25},{9,17},{17,9},{25,1},{2,26},{10... | collective-permute-start | bytes 122888 | tf_op jit(solution)/shard_map/ppermute | solution.py:21
  14.4 4.9 %copy-start.4 = (bf16[40,512]{1,0:T(8,128)(2,1)}, bf16[40,512]{1,0:T(8,128)(2,1)S(1)}, u32[]{:S(2)}) copy-start(bf16[40,512]{1,0:T(8,128)(2,1)S(1)} %collective-permute-done.2.refs_1_) | copy-start | bytes 122884
  16.4 2.8 %copy-start.5 = (bf16[40,512]{1,0:T(8,128)(2,1)}, bf16[40,512]{1,0:T(8,128)(2,1)S(1)}, u32[]{:S(2)}) copy-start(bf16[40,512]{1,0:T(8,128)(2,1)S(1)} %collective-permute-done.3.refs_2_) | copy-start | bytes 122884
  21.4 7.0 %collective-permute-start.8 = (bf16[4,32,512]{2,1,0:T(8,128)(2,1)}, bf16[4,32,512]{2,1,0:T(8,128)(2,1)S(1)}, u32[]{:S(2)}, u32[]{:S(2)}) collective-permute-start(bf16[4,32,512]{2,1,0:T(8,128)(2,1)} %shard_map.94), channel_id=1, source_target_pairs={{0,4},{4,0},{1,5},{5,1},{2,6},{6,2},{3,7},{7,3},{8,12},{12,8},{9,1... | collective-permute-start | bytes 393224 | tf_op jit(solution)/shard_map/ppermute | solution.py:21
  22.6 8.4 %collective-permute-start.7 = (bf16[4,8,2048]{2,1,0:T(8,128)(2,1)}, bf16[4,8,2048]{2,1,0:T(8,128)(2,1)S(1)}, u32[]{:S(2)}, u32[]{:S(2)}) collective-permute-start(bf16[4,8,2048]{2,1,0:T(8,128)(2,1)} %get-tuple-element.30._), channel_id=1, source_target_pairs={{0,6},{1,7},{2,4},{3,5},{4,2},{5,3},{6,0},{7,1},{8,14},{9,15},{10,... | collective-permute-start | bytes 393224 | tf_op jit(solution)/shard_map/ppermute | solution.py:21
  23.8 7.2 %collective-permute-start.5 = (bf16[4,8,2048]{2,1,0:T(8,128)(2,1)S(1)}, bf16[4,8,2048]{2,1,0:T(8,128)(2,1)S(1)}, u32[]{:S(2)}, u32[]{:S(2)}) collective-permute-start(bf16[4,8,2048]{2,1,0:T(8,128)(2,1)S(1)} %get-tuple-element.28), channel_id=1, source_target_pairs={{0,2},{1,3},{2,0},{3,1},{4,6},{5,7},{6,4},{7,5},{8,10},{9,11},{10,... | collective-permute-start | bytes 393224 | tf_op jit(solution)/shard_map/ppermute | solution.py:21
  24.0 7.9 %collective-permute-start.6 = (bf16[4,8,2048]{2,1,0:T(8,128)(2,1)S(1)}, bf16[4,8,2048]{2,1,0:T(8,128)(2,1)S(1)}, u32[]{:S(2)}, u32[]{:S(2)}) collective-permute-start(bf16[4,8,2048]{2,1,0:T(8,128)(2,1)S(1)} %get-tuple-element.27), channel_id=1, source_target_pairs={{0,4},{1,5},{2,6},{3,7},{4,0},{5,1},{6,2},{7,3},{8,12},{9,13},{10,... | collective-permute-start | bytes 393224 | tf_op jit(solution)/shard_map/ppermute | solution.py:21
  28.4 0.7 copy-start.7
  30.9 0.9 copy-start.11
  30.9 0.9 copy-start.12
  34.5 7.2 %collective-permute-start.10 = (bf16[8,32,256]{2,1,0:T(8,128)(2,1)}, bf16[8,32,256]{2,1,0:T(8,128)(2,1)S(1)}, u32[]{:S(2)}, u32[]{:S(2)}) collective-permute-start(bf16[8,32,256]{2,1,0:T(8,128)(2,1)} %get-tuple-element.22), channel_id=1, source_target_pairs={{0,16},{8,24},{16,0},{24,8},{1,17},{9,25},{17,1},{25,9},{2,18},{10... | collective-permute-start | bytes 393224 | tf_op jit(solution)/shard_map/ppermute | solution.py:21
  34.5 7.2 %collective-permute-start.13 = (bf16[4,8,4,512]{3,2,1,0:T(4,128)(2,1)}, bf16[4,8,4,512]{3,2,1,0:T(4,128)(2,1)S(1)}, u32[]{:S(2)}, u32[]{:S(2)}) collective-permute-start(bf16[4,8,4,512]{3,2,1,0:T(4,128)(2,1)} %get-tuple-element.20.refs_4_), channel_id=1, source_target_pairs={{0,1},{1,0},{2,3},{3,2},{4,5},{5,4},{6,7},{7,6},{8,9},{9,8},{10,11... | collective-permute-start | bytes 393224 | tf_op jit(solution)/shard_map/ppermute | solution.py:21
  37.0 5.6 %collective-permute-start.14 = (bf16[4,8,4,512]{3,2,1,0:T(4,128)(2,1)}, bf16[4,8,4,512]{3,2,1,0:T(4,128)(2,1)S(1)}, u32[]{:S(2)}, u32[]{:S(2)}) collective-permute-start(bf16[4,8,4,512]{3,2,1,0:T(4,128)(2,1)} %get-tuple-element.24), channel_id=1, source_target_pairs={{0,3},{1,2},{2,1},{3,0},{4,7},{5,6},{6,5},{7,4},{8,11},{9,10},{10,... | collective-permute-start | bytes 393224 | tf_op jit(solution)/shard_map/ppermute | solution.py:21
  38.1 12.8 %collective-permute-start.9 = (bf16[8,32,256]{2,1,0:T(8,128)(2,1)}, bf16[8,32,256]{2,1,0:T(8,128)(2,1)S(1)}, u32[]{:S(2)}, u32[]{:S(2)}) collective-permute-start(bf16[8,32,256]{2,1,0:T(8,128)(2,1)} %get-tuple-element.21.refs_7_._.refs_0_.refs_4_), channel_id=1, source_target_pairs={{0,8},{8,0},{16,24},{24,16},{1,9},{9,1},{17,25},{25,17},{2,10},{10... | collective-permute-start | bytes 393224 | tf_op jit(solution)/shard_map/ppermute | solution.py:21
  41.7 9.2 %copy-start = (bf16[8,32,256]{2,1,0:T(8,128)(2,1)}, bf16[8,32,256]{2,1,0:T(8,128)(2,1)S(1)}, u32[]{:S(2)}) copy-start(bf16[8,32,256]{2,1,0:T(8,128)(2,1)S(1)} %collective-permute-done.10.refs_1_.refs_2_.refs_6_) | copy-start | bytes 393220
  41.7 9.2 %collective-permute-start.11 = (bf16[8,32,256]{2,1,0:T(8,128)(2,1)S(1)}, bf16[8,32,256]{2,1,0:T(8,128)(2,1)S(1)}, u32[]{:S(2)}, u32[]{:S(2)}) collective-permute-start(bf16[8,32,256]{2,1,0:T(8,128)(2,1)S(1)} %collective-permute-done.10.refs_1_.refs_2_.refs_6_), channel_id=1, source_target_pairs={{0,8},{8,0},{16,24},{24,16},{1,9},{9,1},{17,25},{25,17},{2,10},{10... | collective-permute-start | bytes 393224 | tf_op jit(solution)/shard_map/ppermute | solution.py:21
  41.7 0.9 copy-start.14
  42.6 0.7 copy-start.15
  45.4 8.9 %copy-start.18 = (bf16[1,8,24,256]{3,2,1,0:T(8,128)(2,1)S(1)}, bf16[1,8,24,256]{3,2,1,0:T(8,128)(2,1)}, u32[]{:S(2)}) copy-start(bf16[1,8,24,256]{3,2,1,0:T(8,128)(2,1)} %get-tuple-element.23) | copy-start | bytes 294916
  54.0 9.4 %collective-permute-start.15 = (bf16[3,8,24,256]{3,2,1,0:T(8,128)(2,1)}, bf16[3,8,24,256]{3,2,1,0:T(8,128)(2,1)S(1)}, u32[]{:S(2)}, u32[]{:S(2)}) collective-permute-start(bf16[3,8,24,256]{3,2,1,0:T(8,128)(2,1)} %shard_map.99._), channel_id=1, source_target_pairs={{0,4},{4,0},{1,5},{5,1},{2,6},{6,2},{3,7},{7,3},{8,12},{12,8},{9,1... | collective-permute-start | bytes 884744 | tf_op jit(solution)/shard_map/ppermute | solution.py:21
  54.3 18.4 %copy-start.16 = (s32[4,4]{1,0:T(4,128)S(1)}, s32[4,4]{1,0:T(4,128)}, u32[]{:S(2)}) copy-start(s32[4,4]{1,0:T(4,128)} %refs_0_.1) | copy-start | bytes 196
  54.3 9.2 %collective-permute-start.12 = (bf16[1,8,24,256]{3,2,1,0:T(8,128)(2,1)S(1)}, bf16[1,8,24,256]{3,2,1,0:T(8,128)(2,1)S(1)}, u32[]{:S(2)}, u32[]{:S(2)}) collective-permute-start(bf16[1,8,24,256]{3,2,1,0:T(8,128)(2,1)S(1)} %copy-done.18), channel_id=1, source_target_pairs={{0,4},{4,0},{1,5},{5,1},{2,6},{6,2},{3,7},{7,3},{8,12},{12,8},{9,1... | collective-permute-start | bytes 294920 | tf_op jit(solution)/shard_map/ppermute | solution.py:21
  64.1 0.7 copy-start.3
  67.4 7.9 %collective-permute-start.16 = (bf16[4,8,7,4,256]{4,3,2,1,0:T(4,128)(2,1)}, bf16[4,8,7,4,256]{4,3,2,1,0:T(4,128)(2,1)S(1)}, u32[]{:S(2)}, u32[]{:S(2)}) collective-permute-start(bf16[4,8,7,4,256]{4,3,2,1,0:T(4,128)(2,1)} %get-tuple-element.25), channel_id=1, source_target_pairs={{0,1},{1,0},{2,3},{3,2},{4,5},{5,4},{6,7},{7,6},{8,9},{9,8},{10,11... | collective-permute-start | bytes 1376264 | tf_op jit(solution)/shard_map/ppermute | solution.py:21
  69.7 10.0 %collective-permute-start.17 = (bf16[4,8,7,4,256]{4,3,2,1,0:T(4,128)(2,1)}, bf16[4,8,7,4,256]{4,3,2,1,0:T(4,128)(2,1)S(1)}, u32[]{:S(2)}, u32[]{:S(2)}) collective-permute-start(bf16[4,8,7,4,256]{4,3,2,1,0:T(4,128)(2,1)} %get-tuple-element.26), channel_id=1, source_target_pairs={{1,2},{2,1},{5,6},{6,5},{9,10},{10,9},{13,14},{14,13},{17,18},{18,... | collective-permute-start | bytes 1376264 | tf_op jit(solution)/shard_map/ppermute | solution.py:28
  72.7 2.5 %collective-permute-start = (s32[4,4]{1,0:T(4,128)S(1)}, s32[4,4]{1,0:T(4,128)S(1)}, u32[]{:S(2)}, u32[]{:S(2)}) collective-permute-start(s32[4,4]{1,0:T(4,128)S(1)} %copy-done.16), channel_id=1, source_target_pairs={{0,4},{4,0},{1,5},{5,1},{2,6},{6,2},{3,7},{7,3},{8,12},{12,8},{9,1... | collective-permute-start | bytes 200 | tf_op jit(solution)/shard_map/ppermute | solution.py:21
  75.2 4.5 %copy-start.17 = (s32[4,4]{1,0:T(4,128)}, s32[4,4]{1,0:T(4,128)S(1)}, u32[]{:S(2)}) copy-start(s32[4,4]{1,0:T(4,128)S(1)} %collective-permute-done.refs_1_) | copy-start | bytes 196
  75.2 4.5 %copy-start.8 = (bf16[4,8,7,4,256]{4,3,2,1,0:T(4,128)(2,1)}, bf16[4,8,7,4,256]{4,3,2,1,0:T(4,128)(2,1)S(1)}, u32[]{:S(2)}) copy-start(bf16[4,8,7,4,256]{4,3,2,1,0:T(4,128)(2,1)S(1)} %collective-permute-done.16.refs_10_) | copy-start | bytes 1376260
  79.7 0.8 copy-start.9
  (5 other events, 3.2 us)

commit v5 on v4

--- a/solution.py
+++ b/solution.py
@@ -90,7 +90,24 @@
     return lax.axis_index("view"), lax.axis_index("gz")
 
 
-def cells_kernel(pairs, bands, mirrored, owner_ref, row_ref, pieces_ref, even_ref, odd_ref, acc):
+def first_kernel(
+    pairs,
+    bands,
+    mirrored,
+    owner_ref,
+    row_ref,
+    bg_ref,
+    pieces_ref,
+    taps_ref,
+    est_ref,
+    psf_ref,
+    even_ref,
+    odd_ref,
+    payload_ref,
+    acc,
+    tail,
+):
+    write_payload(mirrored, bg_ref, taps_ref, est_ref, psf_ref, payload_ref, tail)
     count = pieces_ref.shape[0]
     depth = even_ref.shape[1]
     me = lax.axis_index("gz") * bands + lax.axis_index("gy")
@@ -102,7 +119,7 @@
     lax.fori_loop(0, acc.shape[0], clear, 0)
 
     def add(i, carry):
-        owner = owner_ref[0, i, 0]
+        owner = owner_ref[0, 0, i]
         row = row_ref[0, i]
         if mirrored:
             row = jnp.where(owner >= bands, depth - 1 - row, row)
@@ -121,7 +138,7 @@
     lax.fori_loop(0, pairs, put, 0)
 
 
-def payload_kernel(mirrored, bg_ref, taps_ref, est_ref, psf_ref, _, out_ref, tail):
+def write_payload(mirrored, bg_ref, taps_ref, est_ref, psf_ref, out_ref, tail):
     depth, height = est_ref.shape[:2]
     upside = lax.axis_index("gz") if mirrored else 0
     for k in range(depth):
@@ -130,7 +147,7 @@
         ].astype(BF)
     tail[...] = jnp.zeros(tail.shape, F32)
     for i in range(3):
-        tail[0:1, 3 * i : 3 * i + 3] = taps_ref[0, pl.ds(i + upside * (2 - 2 * i), 1), :]
+        tail[0:1, 3 * i : 3 * i + 3] = taps_ref[i + upside * (2 - 2 * i)]
     lanes = lax.broadcasted_iota(jnp.int32, (1, 128), 1)
     exact = jnp.where(lanes == 9, bg_ref[0], tail[0:1, :128])
     for n in range(3):
@@ -150,6 +167,17 @@
     )
     column = jnp.sum(jnp.where(spot, wide, 0.0), axis=1, keepdims=True)
     return jnp.broadcast_to(column, (16, 128))
+
+
+def sum_kernel(pairs, parts, *refs):
+    even_ref, other_ref = refs[:2]
+    heard = refs[2:6]
+    sums, stacks = refs[7 : 7 + pairs], refs[7 + pairs :]
+    for k in range(pairs):
+        sums[k][...] = (even_ref[k].astype(F32) + other_ref[k].astype(F32)).astype(BF)
+    for rows, ref in zip(parts, stacks):
+        for v in range(4):
+            ref[v] = heard[v][rows, :]
 
 
 def stack_kernel(rows, *refs):
@@ -233,7 +261,8 @@
 
 
 def band_kernel(at, *refs):
-    heard, (out_ref, num_ref) = refs[:4], refs[5:]
+    heard, (out_ref, num_ref, done_ref) = refs[:4], refs[5:]
+    done_ref[...] = jnp.zeros(done_ref.shape, F32)
     for v in range(4):
         num_ref[v * 16 : (v + 1) * 16, :] = numbers_of(heard[v], at)
     flip = reversal()
@@ -302,10 +331,10 @@
     return pltpu.roll(sums[0], 1, 0) + sums[1] + pltpu.roll(sums[2], n - 1, 0)
 
 
-def frame_kernel(frame, tiles, sides, *refs):
+def write_frame(frame, tiles, sides, *refs):
     own_refs, refs = refs[:4], refs[4:]
     side_refs = dict(zip(sides, refs[: len(sides)]))
-    one_ref, two_ref, _, out_ref = refs[len(sides) :]
+    one_ref, two_ref, out_ref = refs[len(sides) :]
     view = lax.axis_index("view")
     even = lax.axis_index("gy") % 2 == 0
     for e in (0, tiles + 1):
@@ -331,7 +360,20 @@
                 ).astype(BF)
 
 
-def forward_kernel(frame, tiles, views, num_ref, blocks_ref, frame_ref, _, recip_ref, c):
+def start_kernel(frame, tiles, sides, views, num_ref, blocks_ref, *refs):
+    count = len(sides)
+    out_ref, recip_ref, done_ref, c = refs[7 + count :]
+    write_frame(frame, tiles, sides, *refs[: 6 + count], out_ref)
+    forward_views(frame, tiles, views, num_ref, blocks_ref, out_ref, recip_ref, c)
+    done_ref[...] = jnp.zeros(done_ref.shape, F32)
+
+
+def forward_kernel(frame, tiles, views, num_ref, blocks_ref, frame_ref, _, recip_ref, done_ref, c):
+    forward_views(frame, tiles, views, num_ref, blocks_ref, frame_ref, recip_ref, c)
+    done_ref[...] = jnp.zeros(done_ref.shape, F32)
+
+
+def forward_views(frame, tiles, views, num_ref, blocks_ref, frame_ref, recip_ref, c):
     size = frame.size
     zs = frame.need(3)
     for at, v in enumerate(views):
@@ -567,41 +609,55 @@
             compiler_params=params,
         )(*args)
 
+    def resident(*dims, dtype=BF):
+        return pltpu.VMEM(dims, dtype)
+
+    def stay(array):
+        return pltpu.with_memory_space_constraint(array, pltpu.VMEM)
+
     def shape(*dims, dtype=BF):
         return jax.ShapeDtypeStruct(dims, dtype)
 
+    free = pl.ANY
+    area = depth * height
+
     pairs = blocks // 2
     half_cells = shape(pairs, depth, height, width)
-    even, odd = call(
-        functools.partial(cells_kernel, pairs, bands, frame.mirrored),
-        (half_cells, half_cells),
-        (smem, smem, vmem),
-        (vmem, vmem),
-        piece_owner,
+    even, odd, payload = call(
+        functools.partial(first_kernel, pairs, bands, frame.mirrored),
+        (half_cells, half_cells, shape(area + 8, chunk)),
+        (smem, smem, smem, vmem, vmem, vmem, vmem),
+        (vmem, vmem, vmem),
+        piece_owner.transpose(0, 2, 1),
         piece_row,
+        background,
         pieces[0],
-        scratch=[vmem((blocks * depth, height, width), F32)],
-    )
-    other = swap(odd, "gy", bands, 1)
-
-    free = pl.ANY
-    kept = [even[k] + other[k] for k in range(pairs)]
-    moved = [swap(kept[k], ("gz", "gy"), blocks, 2 * k) for k in range(1, pairs)]
-
-    area = depth * height
-    payload = call(
-        functools.partial(payload_kernel, frame.mirrored),
-        shape(area + 8, chunk),
-        (smem, vmem, vmem, vmem, free),
-        (vmem,),
-        background,
-        stencil,
+        stencil.transpose(1, 0, 2),
         estimate,
         psf_x,
-        kept[pairs - 1],
-        scratch=[vmem((8, chunk), F32)],
-    )
+        scratch=[vmem((blocks * depth, height, width), F32), vmem((8, chunk), F32)],
+    )
+    other = swap(odd, "gy", bands, 1)
     heard = [payload] + [swap(payload, "view", 4, mask) for mask in (1, 2, 3)]
+    index_far = exchange_z(frame, lambda s: bleach_index[:, s.start : s.stop], slabs, depth)
+    est_slices = frame.sent(depth)
+    out = call(
+        functools.partial(
+            sum_kernel,
+            pairs,
+            [slice(s.start * height, s.stop * height) for s in est_slices.values()],
+        ),
+        (shape(depth, height, width),) * pairs
+        + tuple(shape(4, len(s) * height, chunk) for s in est_slices.values()),
+        [vmem] * 6 + [free],
+        [vmem] * (pairs + len(sides)),
+        even,
+        other,
+        *heard,
+        index_far[sides[0]],
+    )
+    kept, est_stacks = out[:pairs], out[pairs:]
+    moved = [swap(kept[k], ("gz", "gy"), blocks, 2 * k) for k in range(1, pairs)]
 
     def stack(arrays, slices, token):
         rows = slice(slices.start * height, slices.stop * height)
@@ -627,19 +683,20 @@
             token,
         )
 
-    far_est = exchange_z(frame, lambda s: stack(heard, s, payload), slabs, depth)
+    stacks = dict(zip([(s.start, s.stop) for s in est_slices.values()], est_stacks))
+    far_est = exchange_z(frame, lambda s: stacks[s.start, s.stop], slabs, depth)
     far_est = [far_est[s] for s in sides]
-    table, nums = call(
+    table, nums, token = call(
         functools.partial(band_kernel, area),
-        (shape(6, 3 * TILE, TILE), shape(64, 128, dtype=F32)),
+        (resident(6, 3 * TILE, TILE), resident(64, 128, dtype=F32), shape(8, 128, dtype=F32)),
         [vmem] * 4 + [free],
-        (vmem, vmem),
+        (vmem, vmem, vmem),
         *heard,
-        payload,
-    )
-    est_edges = edges(heard, far_est, table, size)
+        kept[0],
+    )
+    kept_table, kept_nums = stay(table), stay(nums)
+    est_edges = edges(heard, far_est, token, size)
     one_est, two_est = core_side(est_edges, bands, True)
-    index_far = exchange_z(frame, lambda s: bleach_index[:, s.start : s.stop], slabs, depth)
 
     far_slices = frame.sent(3)
     plain, turned, *own_far = call(
@@ -664,43 +721,46 @@
     far_own = [far_own[s] for s in sides]
     n3, n2, n1 = (len(frame.need(r)) * 16 for r in (3, 2, 1))
 
-    est_frame = call(
-        functools.partial(frame_kernel, frame, tiles, sides),
-        shape(tiles + 2, size * 16, TILE),
-        [vmem] * (6 + len(sides)) + [free],
-        (vmem,),
+    scratch = [vmem((tiles, size * 16, TILE), BF)]
+    est_frame, recip_a, token = call(
+        functools.partial(start_kernel, frame, tiles, sides, (0, 1)),
+        (
+            resident(tiles + 2, size * 16, TILE),
+            resident(2, tiles, n3, TILE),
+            shape(8, 128, dtype=F32),
+        ),
+        [vmem] * (8 + len(sides)) + [free],
+        (vmem, vmem, vmem),
+        kept_nums,
+        kept_table,
         *heard,
         *far_est,
         one_est,
         two_est,
         plain,
-    )
-
-    def forward(views, token):
-        return call(
-            functools.partial(forward_kernel, frame, tiles, views),
-            shape(2, tiles, n3, TILE),
-            (vmem, vmem, vmem, free),
-            (vmem,),
-            nums,
-            table,
-            est_frame,
-            token,
-            scratch=[vmem((tiles, size * 16, TILE), BF)],
-        )
-
-    recip_a = forward((0, 1), plain)
+        scratch=scratch,
+    )
     tokens = []
 
     def others(slices):
-        tokens.append(stack((near, opposite, last), slices, recip_a))
+        tokens.append(stack((near, opposite, last), slices, token))
         return tokens[-1]
 
     far_others = exchange_z(frame, others, slabs, 3)
     far_others = [far_others[s] for s in sides]
-    recip_b = forward((2, 3), tokens[-1])
+    recip_b, token_b = call(
+        functools.partial(forward_kernel, frame, tiles, (2, 3)),
+        (resident(2, tiles, n3, TILE), shape(8, 128, dtype=F32)),
+        (vmem, vmem, vmem, free),
+        (vmem, vmem),
+        kept_nums,
+        kept_table,
+        stay(est_frame),
+        tokens[-1],
+        scratch=scratch,
+    )
     all_edges = edges(
-        (plain, near, opposite, last), far_own + far_others, recip_b, len(frame.need(3))
+        (plain, near, opposite, last), far_own + far_others, token_b, len(frame.need(3))
     )
     one, two = core_side(all_edges, bands, False)
     return call(
@@ -711,7 +771,7 @@
         bleach_table,
         bleach_index,
         *[index_far[s] for s in sides],
-        nums,
+        kept_nums,
         estimate,
         plain,
         near,
@@ -721,10 +781,10 @@
         *far_others,
         one,
         two,
-        recip_a,
-        recip_b,
-        table,
-        est_frame,
+        stay(recip_a),
+        stay(recip_b),
+        kept_table,
+        stay(est_frame),
         scratch=[
             vmem((tiles + 2, n3, TILE), BF),
             vmem((tiles + 2, n2, TILE), BF),

time: 94.8 us -> 83.5 us (0.88)
  Pallas kernels: 44 us -> 35 us
  local copies, waits for them, and re-layouts: 8.63 us -> 5.04 us
  starting transfers between devices: 20.9 us -> 23.1 us
  other arithmetic: 1.89 us -> 0 us
  waiting for transfers between devices: 18.1 us -> 19.1 us
    pallas_call x12 -> x10, Pallas kernels: 44 us -> 35 us  [call(): pl.pallas_call(kernel, out_shape=shapes, in_specs=whole(*ins), out_specs=...]
    unnamed x40 -> x38, local copies, waits for them, and re-layouts: 8.63 us -> 5.04 us
    ppermute x1, waiting for transfers between devices: 4.44 us -> 7.23 us  [core_side(): return (first, lax.ppermute(own[1], 'gy', [(1, 2), (2, 1)]))]
    ppermute x17, starting transfers between devices: 17.9 us -> 20.4 us  [swap(): return lax.ppermute(array, axis, [(i, i ^ mask) for i in range(size)])]
    add x1 -> x0, other arithmetic: 1.89 us -> none  [shards(): kept = [even[k] + other[k] for k in range(pairs)]]
    ppermute x17, waiting for transfers between devices: 13.7 us -> 11.9 us  [swap(): return lax.ppermute(array, axis, [(i, i ^ mask) for i in range(size)])]
  transfers between devices with their start and end apart: 18 -> 18, of which waited for: 9 -> 7; matrix products, arithmetic and copies ran while one was open for 1% -> 0% of each run, Pallas kernels for 19% -> 14%
where the time goes in v5:
time: 83.5 us; the launch traced here: 83.1 us
  Pallas kernels  35 us (42%)
  starting transfers between devices  23.1 us (28%)
  waiting for transfers between devices  19.1 us (23%)
  local copies, waits for them, and re-layouts  5.04 us (6%)
    pallas_call x10, Pallas kernels, call(): pl.pallas_call(kernel, out_shape=shapes, in_specs=whole(*ins), out_specs=...  35 us
    ppermute x17, starting transfers between devices, swap(): return lax.ppermute(array, axis, [(i, i ^ mask) for i in range(size)])  20.4 us
    ppermute x17, waiting for transfers between devices, swap(): return lax.ppermute(array, axis, [(i, i ^ mask) for i in range(size)])  11.9 us
    ppermute x1, waiting for transfers between devices, core_side(): return (first, lax.ppermute(own[1], 'gy', [(1, 2), (2, 1)]))  7.23 us
    unnamed x38, local copies, waits for them, and re-layouts  5.04 us
    ppermute x1, starting transfers between devices, core_side(): return (first, lax.ppermute(own[1], 'gy', [(1, 2), (2, 1)]))  2.74 us
  transfers between devices with their start and end apart: 18, of which 7 were waited for; matrix products, arithmetic and copies ran while one was open for 0% of the time, Pallas kernels for 14%

profile of v5, /device:TPU:1, one launch (start us, length us, event | category | flops | bytes accessed | tf_op | source)
XLA Modules:
  0.0 83.1 jit_solution(8091416992939891119)
XLA Ops:
  0.7 2.7 %shard_map.91 = (bf16[4,4,8,2048]{3,2,1,0:T(8,128)(2,1)}, bf16[4,4,8,2048]{3,2,1,0:T(8,128)(2,1)}, bf16[40,512]{1,0:T(8,128)(2,1)}) custom-call(s32[1,1,16]{2,1,0:T(1,128)} %bitcast.5, s32[1,16]{1,0:T(1,128)} %row_ref.1, f32[1]{0:T(128)S(6)} %copy.10.bg_ref, bf16[16,8,2048]{2,1,0:T(8,128)(2,1)} %bitcast.3, f32[3,1,3]{2,1,0:T(1,128)} %bitcast.4, ...), custom_call_target="tpu_custom_call" | custom-call | tf_op jit(solution)/shard_map/pallas_call | solution.py:603
  3.4 4.8 %collective-permute-start.3 = (bf16[40,512]{1,0:T(8,128)(2,1)}, bf16[40,512]{1,0:T(8,128)(2,1)S(1)}, u32[]{:S(2)}, u32[]{:S(2)}) collective-permute-start(bf16[40,512]{1,0:T(8,128)(2,1)} %get-tuple-element.28.refs_2_.refs_0_), channel_id=1, source_target_pairs={{0,24},{8,16},{16,8},{24,0},{1,25},{9,17},{17,9},{25,1},{2,26},{10... | collective-permute-start | bytes 122888 | tf_op jit(solution)/shard_map/ppermute | solution.py:21
  8.4 1.2 %collective-permute-start = (s32[4,4]{1,0:T(4,128)}, s32[4,4]{1,0:T(4,128)S(1)}, u32[]{:S(2)}, u32[]{:S(2)}) collective-permute-start(s32[4,4]{1,0:T(4,128)} %refs_0_.1), channel_id=1, source_target_pairs={{0,4},{4,0},{1,5},{5,1},{2,6},{6,2},{3,7},{7,3},{8,12},{12,8},{9,1... | collective-permute-start | bytes 200 | tf_op jit(solution)/shard_map/ppermute | solution.py:21
  9.6 1.4 %collective-permute-done.refs_6_.refs_1_ = s32[4,4]{1,0:T(4,128)S(1)} collective-permute-done((s32[4,4]{1,0:T(4,128)}, s32[4,4]{1,0:T(4,128)S(1)}, u32[]{:S(2)}, u32[]{:S(2)}) %collective-permute-start) | collective-permute-done | bytes 96 | tf_op jit(solution)/shard_map/ppermute | solution.py:21
  11.1 1.3 %collective-permute-done.2.refs_4_.refs_2_ = bf16[40,512]{1,0:T(8,128)(2,1)S(1)} collective-permute-done((bf16[40,512]{1,0:T(8,128)(2,1)}, bf16[40,512]{1,0:T(8,128)(2,1)S(1)}, u32[]{:S(2)}, u32[]{:S(2)}) %collective-permute-start.2) | collective-permute-done | bytes 40992 | tf_op jit(solution)/shard_map/ppermute | solution.py:21
  13.2 2.1 %shard_map.92 = (bf16[4,8,2048]{2,1,0:T(8,128)(2,1)}, bf16[4,8,2048]{2,1,0:T(8,128)(2,1)}, bf16[4,8,2048]{2,1,0:T(8,128)(2,1)}, bf16[4,8,2048]{2,1,0:T(8,128)(2,1)}, bf16[4,32,512]{2,1,0:T(8,128)(2,1)}) custom-call(bf16[4,4,8,2048]{3,2,1,0:T(8,128)(2,1)} %get-tuple-element.29.refs_0_, bf16[4,4,8,2048]{3,2,1,0:T(8,128)(2,1)} %copy-done.8, ...), custom_call_target="tpu_custom_call" | custom-call | tf_op jit(solution)/shard_map/pallas_call | solution.py:603
  15.3 1.2 %collective-permute-start.8 = (bf16[4,32,512]{2,1,0:T(8,128)(2,1)}, bf16[4,32,512]{2,1,0:T(8,128)(2,1)S(1)}, u32[]{:S(2)}, u32[]{:S(2)}) collective-permute-start(bf16[4,32,512]{2,1,0:T(8,128)(2,1)} %get-tuple-element.36), channel_id=1, source_target_pairs={{0,4},{4,0},{1,5},{5,1},{2,6},{6,2},{3,7},{7,3},{8,12},{12,8},{9,1... | collective-permute-start | bytes 393224 | tf_op jit(solution)/shard_map/ppermute | solution.py:21
  16.5 1.2 %collective-permute-start.5 = (bf16[4,8,2048]{2,1,0:T(8,128)(2,1)}, bf16[4,8,2048]{2,1,0:T(8,128)(2,1)S(1)}, u32[]{:S(2)}, u32[]{:S(2)}) collective-permute-start(bf16[4,8,2048]{2,1,0:T(8,128)(2,1)} %get-tuple-element.33), channel_id=1, source_target_pairs={{0,2},{1,3},{2,0},{3,1},{4,6},{5,7},{6,4},{7,5},{8,10},{9,11},{10,... | collective-permute-start | bytes 393224 | tf_op jit(solution)/shard_map/ppermute | solution.py:21
  18.0 1.2 %collective-permute-start.7 = (bf16[4,8,2048]{2,1,0:T(8,128)(2,1)}, bf16[4,8,2048]{2,1,0:T(8,128)(2,1)S(1)}, u32[]{:S(2)}, u32[]{:S(2)}) collective-permute-start(bf16[4,8,2048]{2,1,0:T(8,128)(2,1)} %get-tuple-element.35), channel_id=1, source_target_pairs={{0,6},{1,7},{2,4},{3,5},{4,2},{5,3},{6,0},{7,1},{8,14},{9,15},{10,... | collective-permute-start | bytes 393224 | tf_op jit(solution)/shard_map/ppermute | solution.py:21
  19.2 1.8 %shard_map.93 = (bf16[6,768,256]{2,1,0:T(8,128)(2,1)S(1)}, f32[64,128]{1,0:T(8,128)S(1)}, f32[8,128]{1,0:T(8,128)}) custom-call(bf16[40,512]{1,0:T(8,128)(2,1)} %get-tuple-element.28.refs_2_.refs_0_, bf16[40,512]{1,0:T(8,128)(2,1)} %copy-done.6, bf16[40,512]{1,0:T(8,128)(2,1)} %copy-done.5, bf16[40,512]{1,0:T(8,128)(2,1)} %copy-done.4, ...), custom_call_target="tpu_custom_call" | custom-call | tf_op jit(solution)/shard_map/pallas_call | solution.py:603
  21.0 0.6 copy-done.7
  21.6 1.8 %shard_map.94 = (bf16[4,8,4,512]{3,2,1,0:T(4,128)(2,1)}, bf16[4,8,4,512]{3,2,1,0:T(4,128)(2,1)}) custom-call(bf16[40,512]{1,0:T(8,128)(2,1)} %get-tuple-element.28.refs_2_.refs_0_, bf16[40,512]{1,0:T(8,128)(2,1)} %copy-done.6, bf16[40,512]{1,0:T(8,128)(2,1)} %copy-done.5, bf16[40,512]{1,0:T(8,128)(2,1)} %copy-done.4, bf16[4,32,512]{2,1,0:T(8,128)(2,1)} %copy-done.7, ...), custom_call_target="tpu_custom_call" | custom-call | tf_op jit(solution)/shard_map/pallas_call | solution.py:603
  23.5 2.3 %collective-permute-done.7.refs_3_ = bf16[4,8,2048]{2,1,0:T(8,128)(2,1)S(1)} collective-permute-done((bf16[4,8,2048]{2,1,0:T(8,128)(2,1)}, bf16[4,8,2048]{2,1,0:T(8,128)(2,1)S(1)}, u32[]{:S(2)}, u32[]{:S(2)}) %collective-permute-start.7) | collective-permute-done | bytes 131104 | tf_op jit(solution)/shard_map/ppermute | solution.py:21
  25.8 0.6 copy-done.15
  26.4 2.0 %shard_map.95 = (bf16[8,32,256]{2,1,0:T(8,128)(2,1)}, bf16[8,32,256]{2,1,0:T(8,128)(2,1)}, bf16[1,8,24,256]{3,2,1,0:T(8,128)(2,1)}) custom-call(bf16[4,8,2048]{2,1,0:T(8,128)(2,1)} %get-tuple-element.31.refs_4_.refs_0_, bf16[4,8,2048]{2,1,0:T(8,128)(2,1)} %copy-done.12, bf16[4,8,2048]{2,1,0:T(8,128)(2,1)} %copy-done.13, bf16[4,8,2048]{2,1,0:T(8,128)(2,1)} %copy-done.15, ...), custom_call_target="tpu_custom_call" | custom-call | tf_op jit(solution)/shard_map/pallas_call | solution.py:603
  28.4 1.3 %collective-permute-start.10 = (bf16[8,32,256]{2,1,0:T(8,128)(2,1)}, bf16[8,32,256]{2,1,0:T(8,128)(2,1)S(1)}, u32[]{:S(2)}, u32[]{:S(2)}) collective-permute-start(bf16[8,32,256]{2,1,0:T(8,128)(2,1)} %get-tuple-element.40), channel_id=1, source_target_pairs={{0,16},{8,24},{16,0},{24,8},{1,17},{9,25},{17,1},{25,9},{2,18},{10... | collective-permute-start | bytes 393224 | tf_op jit(solution)/shard_map/ppermute | solution.py:21
  29.7 3.3 %collective-permute-start.14 = (bf16[4,8,4,512]{3,2,1,0:T(4,128)(2,1)}, bf16[4,8,4,512]{3,2,1,0:T(4,128)(2,1)S(1)}, u32[]{:S(2)}, u32[]{:S(2)}) collective-permute-start(bf16[4,8,4,512]{3,2,1,0:T(4,128)(2,1)} %get-tuple-element.43), channel_id=1, source_target_pairs={{0,3},{1,2},{2,1},{3,0},{4,7},{5,6},{6,5},{7,4},{8,11},{9,10},{10,... | collective-permute-start | bytes 393224 | tf_op jit(solution)/shard_map/ppermute | solution.py:21
  33.0 1.4 %collective-permute-start.9 = (bf16[8,32,256]{2,1,0:T(8,128)(2,1)}, bf16[8,32,256]{2,1,0:T(8,128)(2,1)S(1)}, u32[]{:S(2)}, u32[]{:S(2)}) collective-permute-start(bf16[8,32,256]{2,1,0:T(8,128)(2,1)} %get-tuple-element.39.refs_7_.refs_0_.refs_4_), channel_id=1, source_target_pairs={{0,8},{8,0},{16,24},{24,16},{1,9},{9,1},{17,25},{25,17},{2,10},{10... | collective-permute-start | bytes 393224 | tf_op jit(solution)/shard_map/ppermute | solution.py:21
  35.0 2.2 %collective-permute-done.14.refs_6_ = bf16[4,8,4,512]{3,2,1,0:T(4,128)(2,1)S(1)} collective-permute-done((bf16[4,8,4,512]{3,2,1,0:T(4,128)(2,1)}, bf16[4,8,4,512]{3,2,1,0:T(4,128)(2,1)S(1)}, u32[]{:S(2)}, u32[]{:S(2)}) %collective-permute-start.14) | collective-permute-done | bytes 131104 | tf_op jit(solution)/shard_map/ppermute | solution.py:21
  37.1 0.7 copy-done.14
  37.8 4.6 %shard_map.96 = (bf16[10,128,256]{2,1,0:T(8,128)(2,1)S(1)}, bf16[2,8,112,256]{3,2,1,0:T(8,128)(2,1)S(1)}, f32[8,128]{1,0:T(8,128)}) custom-call(f32[64,128]{1,0:T(8,128)S(1)} %get-tuple-element.32.num_ref.refs_2_, bf16[6,768,256]{2,1,0:T(8,128)(2,1)S(1)} %get-tuple-element.42.blocks_ref.refs_14_, bf16[40,512]{1,0:T(8,128)(2,1)} %get-tuple-element.28.refs_2_.refs_0_, ...), custom_call_target="tpu_custom_call" | custom-call | tf_op jit(solution)/shard_map/pallas_call | solution.py:603
  43.1 1.8 %shard_map.97._ = bf16[3,8,24,256]{3,2,1,0:T(8,128)(2,1)} custom-call(bf16[8,32,256]{2,1,0:T(8,128)(2,1)} %copy-done.2, bf16[8,32,256]{2,1,0:T(8,128)(2,1)} %copy-done.1, bf16[8,32,256]{2,1,0:T(8,128)(2,1)} %copy-done.3, f32[8,128]{1,0:T(8,128)} %get-tuple-element.44.refs_3_), custom_call_target="tpu_custom_call" | custom-call | tf_op jit(solution)/shard_map/pallas_call | solution.py:603
  45.3 1.0 %collective-permute-start.12 = (bf16[1,8,24,256]{3,2,1,0:T(8,128)(2,1)S(1)}, bf16[1,8,24,256]{3,2,1,0:T(8,128)(2,1)S(1)}, u32[]{:S(2)}, u32[]{:S(2)}) collective-permute-start(bf16[1,8,24,256]{3,2,1,0:T(8,128)(2,1)S(1)} %copy-done.18), channel_id=1, source_target_pairs={{0,4},{4,0},{1,5},{5,1},{2,6},{6,2},{3,7},{7,3},{8,12},{12,8},{9,1... | collective-permute-start | bytes 294920 | tf_op jit(solution)/shard_map/ppermute | solution.py:21
  46.3 3.4 %shard_map.98 = (bf16[2,8,112,256]{3,2,1,0:T(8,128)(2,1)S(1)}, f32[8,128]{1,0:T(8,128)}) custom-call(f32[64,128]{1,0:T(8,128)S(1)} %get-tuple-element.32.num_ref.refs_2_, bf16[6,768,256]{2,1,0:T(8,128)(2,1)S(1)} %get-tuple-element.42.blocks_ref.refs_14_, bf16[10,128,256]{2,1,0:T(8,128)(2,1)S(1)} %get-tuple-element.45.frame_ref.refs_15_, ...), custom_call_target="tpu_custom_call" | custom-call | tf_op jit(solution)/shard_map/pallas_call | solution.py:603
  49.7 4.3 %collective-permute-done.12.refs_4_.refs_8_ = bf16[1,8,24,256]{3,2,1,0:T(8,128)(2,1)S(1)} collective-permute-done((bf16[1,8,24,256]{3,2,1,0:T(8,128)(2,1)S(1)}, bf16[1,8,24,256]{3,2,1,0:T(8,128)(2,1)S(1)}, u32[]{:S(2)}, u32[]{:S(2)}) %collective-permute-start.12) | collective-permute-done | bytes 98336 | tf_op jit(solution)/shard_map/ppermute | solution.py:21
  54.0 0.6 copy-done.11
  54.8 2.6 %shard_map.99 = (bf16[4,8,7,4,256]{4,3,2,1,0:T(4,128)(2,1)}, bf16[4,8,7,4,256]{4,3,2,1,0:T(4,128)(2,1)}) custom-call(bf16[8,32,256]{2,1,0:T(8,128)(2,1)} %get-tuple-element.39.refs_7_.refs_0_.refs_4_, bf16[8,32,256]{2,1,0:T(8,128)(2,1)} %copy-done.2, bf16[8,32,256]{2,1,0:T(8,128)(2,1)} %copy-done.1, bf16[8,32,256]{2,1,0:T(8,128)(2,1)} %copy-done.3, ...), custom_call_target="tpu_custom_call" | custom-call | tf_op jit(solution)/shard_map/pallas_call | solution.py:603
  57.3 2.6 %collective-permute-start.16 = (bf16[4,8,7,4,256]{4,3,2,1,0:T(4,128)(2,1)}, bf16[4,8,7,4,256]{4,3,2,1,0:T(4,128)(2,1)S(1)}, u32[]{:S(2)}, u32[]{:S(2)}) collective-permute-start(bf16[4,8,7,4,256]{4,3,2,1,0:T(4,128)(2,1)} %get-tuple-element.47), channel_id=1, source_target_pairs={{0,1},{1,0},{2,3},{3,2},{4,5},{5,4},{6,7},{7,6},{8,9},{9,8},{10,11... | collective-permute-start | bytes 1376264 | tf_op jit(solution)/shard_map/ppermute | solution.py:21
  59.9 2.7 %collective-permute-start.17 = (bf16[4,8,7,4,256]{4,3,2,1,0:T(4,128)(2,1)}, bf16[4,8,7,4,256]{4,3,2,1,0:T(4,128)(2,1)S(1)}, u32[]{:S(2)}, u32[]{:S(2)}) collective-permute-start(bf16[4,8,7,4,256]{4,3,2,1,0:T(4,128)(2,1)} %get-tuple-element.48), channel_id=1, source_target_pairs={{1,2},{2,1},{5,6},{6,5},{9,10},{10,9},{13,14},{14,13},{17,18},{18,... | collective-permute-start | bytes 1376264 | tf_op jit(solution)/shard_map/ppermute | solution.py:28
  62.7 7.2 %collective-permute-done.17.refs_11_ = bf16[4,8,7,4,256]{4,3,2,1,0:T(4,128)(2,1)S(1)} collective-permute-done((bf16[4,8,7,4,256]{4,3,2,1,0:T(4,128)(2,1)}, bf16[4,8,7,4,256]{4,3,2,1,0:T(4,128)(2,1)S(1)}, u32[]{:S(2)}, u32[]{:S(2)}) %collective-permute-start.17) | collective-permute-done | bytes 458784 | tf_op jit(solution)/shard_map/ppermute | solution.py:28
  69.9 0.8 copy-done.10
  70.7 12.4 %shard_map.100 = f32[4,8,512]{2,1,0:T(8,128)} custom-call(f32[4,16]{1,0:T(4,128)} %table_ref.1, s32[4,4]{1,0:T(4,128)} %refs_0_.1, s32[4,4]{1,0:T(4,128)} %copy-done.17, f32[64,128]{1,0:T(8,128)S(1)} %get-tuple-element.32.num_ref.refs_2_, f32[4,8,512]{2,1,0:T(8,128)} %refs_3_.1, bf16[8,32,256]{2,1,0:T(8,128)(2,1)} %get-tuple-element.39.refs_7_.refs_0_.refs_4_, ...), custom_call_target="tpu_custom_call" | custom-call | tf_op jit(solution)/shard_map/pallas_call | solution.py:603
  (52 shorter events, 3.3 us)
Async XLA Ops:
  3.3 9.1 %collective-permute-start.4 = (bf16[4,4,8,2048]{3,2,1,0:T(8,128)(2,1)}, bf16[4,4,8,2048]{3,2,1,0:T(8,128)(2,1)S(1)}, u32[]{:S(2)}, u32[]{:S(2)}) collective-permute-start(bf16[4,4,8,2048]{3,2,1,0:T(8,128)(2,1)} %get-tuple-element.30), channel_id=1, source_target_pairs={{0,1},{1,0},{2,3},{3,2},{4,5},{5,4},{6,7},{7,6},{8,9},{9,8},{10,11... | collective-permute-start | bytes 1572872 | tf_op jit(solution)/shard_map/ppermute | solution.py:21
  3.4 7.7 %collective-permute-start.3 = (bf16[40,512]{1,0:T(8,128)(2,1)}, bf16[40,512]{1,0:T(8,128)(2,1)S(1)}, u32[]{:S(2)}, u32[]{:S(2)}) collective-permute-start(bf16[40,512]{1,0:T(8,128)(2,1)} %get-tuple-element.28.refs_2_.refs_0_), channel_id=1, source_target_pairs={{0,24},{8,16},{16,8},{24,0},{1,25},{9,17},{17,9},{25,1},{2,26},{10... | collective-permute-start | bytes 122888 | tf_op jit(solution)/shard_map/ppermute | solution.py:21
  8.1 4.2 %collective-permute-start.2 = (bf16[40,512]{1,0:T(8,128)(2,1)}, bf16[40,512]{1,0:T(8,128)(2,1)S(1)}, u32[]{:S(2)}, u32[]{:S(2)}) collective-permute-start(bf16[40,512]{1,0:T(8,128)(2,1)} %get-tuple-element.28.refs_2_.refs_0_), channel_id=1, source_target_pairs={{0,16},{8,24},{16,0},{24,8},{1,17},{9,25},{17,1},{25,9},{2,18},{10... | collective-permute-start | bytes 122888 | tf_op jit(solution)/shard_map/ppermute | solution.py:21
  8.1 4.2 %collective-permute-start.1 = (bf16[40,512]{1,0:T(8,128)(2,1)}, bf16[40,512]{1,0:T(8,128)(2,1)S(1)}, u32[]{:S(2)}, u32[]{:S(2)}) collective-permute-start(bf16[40,512]{1,0:T(8,128)(2,1)} %get-tuple-element.28.refs_2_.refs_0_), channel_id=1, source_target_pairs={{0,8},{8,0},{16,24},{24,16},{1,9},{9,1},{17,25},{25,17},{2,10},{10... | collective-permute-start | bytes 122888 | tf_op jit(solution)/shard_map/ppermute | solution.py:21
  8.4 2.6 %collective-permute-start = (s32[4,4]{1,0:T(4,128)}, s32[4,4]{1,0:T(4,128)S(1)}, u32[]{:S(2)}, u32[]{:S(2)}) collective-permute-start(s32[4,4]{1,0:T(4,128)} %refs_0_.1), channel_id=1, source_target_pairs={{0,4},{4,0},{1,5},{5,1},{2,6},{6,2},{3,7},{7,3},{8,12},{12,8},{9,1... | collective-permute-start | bytes 200 | tf_op jit(solution)/shard_map/ppermute | solution.py:21
  11.1 1.3 %copy-start.17 = (s32[4,4]{1,0:T(4,128)}, s32[4,4]{1,0:T(4,128)S(1)}, u32[]{:S(2)}) copy-start(s32[4,4]{1,0:T(4,128)S(1)} %collective-permute-done.refs_6_.refs_1_) | copy-start | bytes 196
  11.1 1.3 %copy-start.4 = (bf16[40,512]{1,0:T(8,128)(2,1)}, bf16[40,512]{1,0:T(8,128)(2,1)S(1)}, u32[]{:S(2)}) copy-start(bf16[40,512]{1,0:T(8,128)(2,1)S(1)} %collective-permute-done.3.refs_5_.refs_3_) | copy-start | bytes 122884
  12.4 0.8 %copy-start.8 = (bf16[4,4,8,2048]{3,2,1,0:T(8,128)(2,1)}, bf16[4,4,8,2048]{3,2,1,0:T(8,128)(2,1)S(1)}, u32[]{:S(2)}) copy-start(bf16[4,4,8,2048]{3,2,1,0:T(8,128)(2,1)S(1)} %collective-permute-done.4.refs_1_) | copy-start | bytes 1572868
  15.3 5.6 %collective-permute-start.8 = (bf16[4,32,512]{2,1,0:T(8,128)(2,1)}, bf16[4,32,512]{2,1,0:T(8,128)(2,1)S(1)}, u32[]{:S(2)}, u32[]{:S(2)}) collective-permute-start(bf16[4,32,512]{2,1,0:T(8,128)(2,1)} %get-tuple-element.36), channel_id=1, source_target_pairs={{0,4},{4,0},{1,5},{5,1},{2,6},{6,2},{3,7},{7,3},{8,12},{12,8},{9,1... | collective-permute-start | bytes 393224 | tf_op jit(solution)/shard_map/ppermute | solution.py:21
  16.5 6.9 %collective-permute-start.5 = (bf16[4,8,2048]{2,1,0:T(8,128)(2,1)}, bf16[4,8,2048]{2,1,0:T(8,128)(2,1)S(1)}, u32[]{:S(2)}, u32[]{:S(2)}) collective-permute-start(bf16[4,8,2048]{2,1,0:T(8,128)(2,1)} %get-tuple-element.33), channel_id=1, source_target_pairs={{0,2},{1,3},{2,0},{3,1},{4,6},{5,7},{6,4},{7,5},{8,10},{9,11},{10,... | collective-permute-start | bytes 393224 | tf_op jit(solution)/shard_map/ppermute | solution.py:21
  17.8 5.7 %collective-permute-start.6 = (bf16[4,8,2048]{2,1,0:T(8,128)(2,1)}, bf16[4,8,2048]{2,1,0:T(8,128)(2,1)S(1)}, u32[]{:S(2)}, u32[]{:S(2)}) collective-permute-start(bf16[4,8,2048]{2,1,0:T(8,128)(2,1)} %get-tuple-element.34), channel_id=1, source_target_pairs={{0,4},{1,5},{2,6},{3,7},{4,0},{5,1},{6,2},{7,3},{8,12},{9,13},{10,... | collective-permute-start | bytes 393224 | tf_op jit(solution)/shard_map/ppermute | solution.py:21
  18.0 7.7 %collective-permute-start.7 = (bf16[4,8,2048]{2,1,0:T(8,128)(2,1)}, bf16[4,8,2048]{2,1,0:T(8,128)(2,1)S(1)}, u32[]{:S(2)}, u32[]{:S(2)}) collective-permute-start(bf16[4,8,2048]{2,1,0:T(8,128)(2,1)} %get-tuple-element.35), channel_id=1, source_target_pairs={{0,6},{1,7},{2,4},{3,5},{4,2},{5,3},{6,0},{7,1},{8,14},{9,15},{10,... | collective-permute-start | bytes 393224 | tf_op jit(solution)/shard_map/ppermute | solution.py:21
  23.5 2.3 %copy-start.12 = (bf16[4,8,2048]{2,1,0:T(8,128)(2,1)}, bf16[4,8,2048]{2,1,0:T(8,128)(2,1)S(1)}, u32[]{:S(2)}) copy-start(bf16[4,8,2048]{2,1,0:T(8,128)(2,1)S(1)} %collective-permute-done.5.refs_1_) | copy-start | bytes 393220
  23.5 2.3 %copy-start.13 = (bf16[4,8,2048]{2,1,0:T(8,128)(2,1)}, bf16[4,8,2048]{2,1,0:T(8,128)(2,1)S(1)}, u32[]{:S(2)}) copy-start(bf16[4,8,2048]{2,1,0:T(8,128)(2,1)S(1)} %collective-permute-done.6.refs_2_) | copy-start | bytes 393220
  25.8 0.7 copy-start.15
  28.4 16.9 %copy-start.18 = (bf16[1,8,24,256]{3,2,1,0:T(8,128)(2,1)S(1)}, bf16[1,8,24,256]{3,2,1,0:T(8,128)(2,1)}, u32[]{:S(2)}) copy-start(bf16[1,8,24,256]{3,2,1,0:T(8,128)(2,1)} %get-tuple-element.41) | copy-start | bytes 294916
  28.4 6.3 %collective-permute-start.10 = (bf16[8,32,256]{2,1,0:T(8,128)(2,1)}, bf16[8,32,256]{2,1,0:T(8,128)(2,1)S(1)}, u32[]{:S(2)}, u32[]{:S(2)}) collective-permute-start(bf16[8,32,256]{2,1,0:T(8,128)(2,1)} %get-tuple-element.40), channel_id=1, source_target_pairs={{0,16},{8,24},{16,0},{24,8},{1,17},{9,25},{17,1},{25,9},{2,18},{10... | collective-permute-start | bytes 393224 | tf_op jit(solution)/shard_map/ppermute | solution.py:21
  29.7 7.4 %collective-permute-start.14 = (bf16[4,8,4,512]{3,2,1,0:T(4,128)(2,1)}, bf16[4,8,4,512]{3,2,1,0:T(4,128)(2,1)S(1)}, u32[]{:S(2)}, u32[]{:S(2)}) collective-permute-start(bf16[4,8,4,512]{3,2,1,0:T(4,128)(2,1)} %get-tuple-element.43), channel_id=1, source_target_pairs={{0,3},{1,2},{2,1},{3,0},{4,7},{5,6},{6,5},{7,4},{8,11},{9,10},{10,... | collective-permute-start | bytes 393224 | tf_op jit(solution)/shard_map/ppermute | solution.py:21
  33.0 4.1 %collective-permute-start.13 = (bf16[4,8,4,512]{3,2,1,0:T(4,128)(2,1)}, bf16[4,8,4,512]{3,2,1,0:T(4,128)(2,1)S(1)}, u32[]{:S(2)}, u32[]{:S(2)}) collective-permute-start(bf16[4,8,4,512]{3,2,1,0:T(4,128)(2,1)} %get-tuple-element.38.refs_4_), channel_id=1, source_target_pairs={{0,1},{1,0},{2,3},{3,2},{4,5},{5,4},{6,7},{7,6},{8,9},{9,8},{10,11... | collective-permute-start | bytes 393224 | tf_op jit(solution)/shard_map/ppermute | solution.py:21
  33.0 9.4 %collective-permute-start.9 = (bf16[8,32,256]{2,1,0:T(8,128)(2,1)}, bf16[8,32,256]{2,1,0:T(8,128)(2,1)S(1)}, u32[]{:S(2)}, u32[]{:S(2)}) collective-permute-start(bf16[8,32,256]{2,1,0:T(8,128)(2,1)} %get-tuple-element.39.refs_7_.refs_0_.refs_4_), channel_id=1, source_target_pairs={{0,8},{8,0},{16,24},{24,16},{1,9},{9,1},{17,25},{25,17},{2,10},{10... | collective-permute-start | bytes 393224 | tf_op jit(solution)/shard_map/ppermute | solution.py:21
  34.7 7.7 %copy-start.1 = (bf16[8,32,256]{2,1,0:T(8,128)(2,1)}, bf16[8,32,256]{2,1,0:T(8,128)(2,1)S(1)}, u32[]{:S(2)}) copy-start(bf16[8,32,256]{2,1,0:T(8,128)(2,1)S(1)} %collective-permute-done.10.refs_1_.refs_2_.refs_6_) | copy-start | bytes 393220
  34.7 7.6 %collective-permute-start.11 = (bf16[8,32,256]{2,1,0:T(8,128)(2,1)S(1)}, bf16[8,32,256]{2,1,0:T(8,128)(2,1)S(1)}, u32[]{:S(2)}, u32[]{:S(2)}) collective-permute-start(bf16[8,32,256]{2,1,0:T(8,128)(2,1)S(1)} %collective-permute-done.10.refs_1_.refs_2_.refs_6_), channel_id=1, source_target_pairs={{0,8},{8,0},{16,24},{24,16},{1,9},{9,1},{17,25},{25,17},{2,10},{10... | collective-permute-start | bytes 393224 | tf_op jit(solution)/shard_map/ppermute | solution.py:21
  37.1 0.7 copy-start.14
  37.1 0.7 copy-start.16
  42.4 0.7 copy-start.3
  44.9 9.2 %collective-permute-start.15 = (bf16[3,8,24,256]{3,2,1,0:T(8,128)(2,1)}, bf16[3,8,24,256]{3,2,1,0:T(8,128)(2,1)S(1)}, u32[]{:S(2)}, u32[]{:S(2)}) collective-permute-start(bf16[3,8,24,256]{3,2,1,0:T(8,128)(2,1)} %shard_map.97._), channel_id=1, source_target_pairs={{0,4},{4,0},{1,5},{5,1},{2,6},{6,2},{3,7},{7,3},{8,12},{12,8},{9,1... | collective-permute-start | bytes 884744 | tf_op jit(solution)/shard_map/ppermute | solution.py:21
  45.3 8.7 %collective-permute-start.12 = (bf16[1,8,24,256]{3,2,1,0:T(8,128)(2,1)S(1)}, bf16[1,8,24,256]{3,2,1,0:T(8,128)(2,1)S(1)}, u32[]{:S(2)}, u32[]{:S(2)}) collective-permute-start(bf16[1,8,24,256]{3,2,1,0:T(8,128)(2,1)S(1)} %copy-done.18), channel_id=1, source_target_pairs={{0,4},{4,0},{1,5},{5,1},{2,6},{6,2},{3,7},{7,3},{8,12},{12,8},{9,1... | collective-permute-start | bytes 294920 | tf_op jit(solution)/shard_map/ppermute | solution.py:21
  54.0 0.8 copy-start
  57.3 5.3 %collective-permute-start.16 = (bf16[4,8,7,4,256]{4,3,2,1,0:T(4,128)(2,1)}, bf16[4,8,7,4,256]{4,3,2,1,0:T(4,128)(2,1)S(1)}, u32[]{:S(2)}, u32[]{:S(2)}) collective-permute-start(bf16[4,8,7,4,256]{4,3,2,1,0:T(4,128)(2,1)} %get-tuple-element.47), channel_id=1, source_target_pairs={{0,1},{1,0},{2,3},{3,2},{4,5},{5,4},{6,7},{7,6},{8,9},{9,8},{10,11... | collective-permute-start | bytes 1376264 | tf_op jit(solution)/shard_map/ppermute | solution.py:21
  59.9 10.0 %collective-permute-start.17 = (bf16[4,8,7,4,256]{4,3,2,1,0:T(4,128)(2,1)}, bf16[4,8,7,4,256]{4,3,2,1,0:T(4,128)(2,1)S(1)}, u32[]{:S(2)}, u32[]{:S(2)}) collective-permute-start(bf16[4,8,7,4,256]{4,3,2,1,0:T(4,128)(2,1)} %get-tuple-element.48), channel_id=1, source_target_pairs={{1,2},{2,1},{5,6},{6,5},{9,10},{10,9},{13,14},{14,13},{17,18},{18,... | collective-permute-start | bytes 1376264 | tf_op jit(solution)/shard_map/ppermute | solution.py:28
  62.7 7.2 %copy-start.9 = (bf16[4,8,7,4,256]{4,3,2,1,0:T(4,128)(2,1)}, bf16[4,8,7,4,256]{4,3,2,1,0:T(4,128)(2,1)S(1)}, u32[]{:S(2)}) copy-start(bf16[4,8,7,4,256]{4,3,2,1,0:T(4,128)(2,1)S(1)} %collective-permute-done.16.refs_10_) | copy-start | bytes 1376260
  69.9 0.8 copy-start.10
  (5 other events, 3.2 us)

commit v6 on v5

--- a/solution.py
+++ b/solution.py
@@ -10,7 +10,7 @@
 BF = jnp.bfloat16
 F32 = jnp.float32
 TILE = 256
-LIMIT = 56 << 20
+LIMIT = 24 << 20
 
 
 def whole(*spaces):
@@ -172,7 +172,8 @@
 def sum_kernel(pairs, parts, *refs):
     even_ref, other_ref = refs[:2]
     heard = refs[2:6]
-    sums, stacks = refs[7 : 7 + pairs], refs[7 + pairs :]
+    sums, stacks, done_ref = refs[7 : 7 + pairs], refs[7 + pairs : -1], refs[-1]
+    done_ref[...] = jnp.zeros(done_ref.shape, F32)
     for k in range(pairs):
         sums[k][...] = (even_ref[k].astype(F32) + other_ref[k].astype(F32)).astype(BF)
     for rows, ref in zip(parts, stacks):
@@ -181,15 +182,18 @@
 
 
 def stack_kernel(rows, *refs):
-    ins, out_ref = refs[:-2], refs[-1]
+    ins, (out_ref, done_ref) = refs[:-3], refs[-2:]
+    done_ref[...] = jnp.zeros(done_ref.shape, F32)
     for v, ref in enumerate(ins):
         out_ref[v] = ref[..., rows, :]
 
 
 def edges_kernel(height, depth, sides, *refs):
-    out1, out2 = refs[-2:]
+    out1, out2, done_ref = refs[-3:]
+    done_ref[...] = jnp.zeros(done_ref.shape, F32)
     count = out1.shape[0]
-    views, fars = refs[:count], refs[count:-3]
+    views = refs[:count] if depth else [None] * count
+    fars = refs[count if depth else 0 : -4]
     half = height // 2
     gy = lax.axis_index("gy")
     even = gy % 2 == 0
@@ -211,9 +215,12 @@
 
     for v, own in enumerate(views):
         n = 0
-        for number, source in [(depth, own)] + [
-            (fars[side].shape[-2] // height, far_of(v, side)) for side in range(sides)
-        ]:
+        sources = [(depth, own)] if depth else []
+        if fars:
+            sources += [
+                (fars[side].shape[-2] // height, far_of(v, side)) for side in range(sides)
+            ]
+        for number, source in sources:
             for k in range(number):
                 rows = slice(k * height, (k + 1) * height)
                 if lead:
@@ -242,7 +249,8 @@
 
 
 def total_kernel(parts, far_rows, *refs):
-    ins, (out_ref, rev_ref, *far_refs) = refs[:parts], refs[parts + 1 :]
+    ins, (out_ref, rev_ref, *far_refs, done_ref) = refs[:parts], refs[parts + 1 :]
+    done_ref[...] = jnp.zeros(done_ref.shape, F32)
     tiles, rows, _ = out_ref.shape
     for t in range(tiles):
         cut = slice(t * TILE, (t + 1) * TILE)
@@ -403,10 +411,10 @@
     num_ref, est_ref, refs = refs[0], refs[1], refs[2:]
     own_refs, refs = refs[:4], refs[4:]
     far_refs, refs = refs[: 2 * count], refs[2 * count :]
-    one_ref, two_ref = refs[:2]
-    recip_refs = refs[2:4]
-    blocks_ref, frame_ref, out_ref = refs[4:7]
-    m1, u2, m2, c0, c1, c2, c3, kept, wt = refs[7:]
+    near_refs, beyond_refs = refs[:2], refs[2:4]
+    recip_refs = refs[4:6]
+    blocks_ref, frame_ref, out_ref = refs[6:9]
+    m1, u2, m2, c0, c1, c2, c3, kept, wt = refs[9:]
     even = lax.axis_index("gy") % 2 == 0
     c = [c0, c1, c2, c3]
     view = lax.axis_index("view")
@@ -444,6 +452,8 @@
             far = far_refs[(count if v else 0) + sides.index(where)]
             own = far[v - 1 if v else 0, t, k * 8 : (k + 1) * 8, cut]
         n = frame.place(z, 3)
+        one_ref, two_ref = near_refs if n < depth else beyond_refs
+        n = n if n < depth else n - depth
         return jnp.concatenate(
             [
                 own.astype(F32),
@@ -599,8 +609,15 @@
     vmem, smem = pltpu.VMEM, pltpu.SMEM
     params = pltpu.CompilerParams(vmem_limit_bytes=LIMIT)
 
+    def stay(array):
+        return pltpu.with_memory_space_constraint(array, pltpu.VMEM)
+
     def call(kernel, shapes, ins, outs, *args, scratch=()):
-        return pl.pallas_call(
+        args = [
+            stay(x) if space is vmem else x
+            for space, x in zip(ins, args)
+        ]
+        out = pl.pallas_call(
             kernel,
             out_shape=shapes,
             in_specs=whole(*ins),
@@ -608,24 +625,21 @@
             scratch_shapes=list(scratch),
             compiler_params=params,
         )(*args)
+        return out
 
     def resident(*dims, dtype=BF):
         return pltpu.VMEM(dims, dtype)
 
-    def stay(array):
-        return pltpu.with_memory_space_constraint(array, pltpu.VMEM)
-
-    def shape(*dims, dtype=BF):
-        return jax.ShapeDtypeStruct(dims, dtype)
+    mark = jax.ShapeDtypeStruct((8, 128), F32)
 
     free = pl.ANY
     area = depth * height
 
     pairs = blocks // 2
-    half_cells = shape(pairs, depth, height, width)
+    half_cells = resident(pairs, depth, height, width)
     even, odd, payload = call(
         functools.partial(first_kernel, pairs, bands, frame.mirrored),
-        (half_cells, half_cells, shape(area + 8, chunk)),
+        (half_cells, half_cells, resident(area + 8, chunk)),
         (smem, smem, smem, vmem, vmem, vmem, vmem),
         (vmem, vmem, vmem),
         piece_owner.transpose(0, 2, 1),
@@ -647,16 +661,17 @@
             pairs,
             [slice(s.start * height, s.stop * height) for s in est_slices.values()],
         ),
-        (shape(depth, height, width),) * pairs
-        + tuple(shape(4, len(s) * height, chunk) for s in est_slices.values()),
+        (resident(depth, height, width),) * pairs
+        + tuple(resident(4, len(s) * height, chunk) for s in est_slices.values())
+        + (mark,),
         [vmem] * 6 + [free],
-        [vmem] * (pairs + len(sides)),
+        [vmem] * (pairs + len(sides) + 1),
         even,
         other,
         *heard,
         index_far[sides[0]],
     )
-    kept, est_stacks = out[:pairs], out[pairs:]
+    kept, est_stacks, sums_done = out[:pairs], out[pairs:-1], out[-1]
     moved = [swap(kept[k], ("gz", "gy"), blocks, 2 * k) for k in range(1, pairs)]
 
     def stack(arrays, slices, token):
@@ -664,20 +679,22 @@
         dims = (len(arrays),) + arrays[0].shape[:-2] + (len(slices) * height, arrays[0].shape[-1])
         return call(
             functools.partial(stack_kernel, rows),
-            shape(*dims),
+            (resident(*dims), mark),
             [vmem] * len(arrays) + [free],
-            (vmem,),
+            (vmem, vmem),
             *arrays,
             token,
         )
 
-    def edges(arrays, fars, token, count):
-        dims = (len(arrays),) + arrays[0].shape[:-2] + (count, height // 2, arrays[0].shape[-1])
+    def edges(arrays, fars, token, slices, dims):
+        out = resident(4, *dims[:-2], slices, height // 2, dims[-1])
         return call(
-            functools.partial(edges_kernel, height, depth, len(sides)),
-            (shape(*dims), shape(*dims)),
+            functools.partial(
+                edges_kernel, height, depth if arrays else 0, len(sides)
+            ),
+            (out, out, mark),
             [vmem] * (len(arrays) + len(fars)) + [free],
-            (vmem, vmem),
+            (vmem, vmem, vmem),
             *arrays,
             *fars,
             token,
@@ -688,30 +705,31 @@
     far_est = [far_est[s] for s in sides]
     table, nums, token = call(
         functools.partial(band_kernel, area),
-        (resident(6, 3 * TILE, TILE), resident(64, 128, dtype=F32), shape(8, 128, dtype=F32)),
+        (resident(6, 3 * TILE, TILE), resident(64, 128, dtype=F32), mark),
         [vmem] * 4 + [free],
         (vmem, vmem, vmem),
         *heard,
-        kept[0],
-    )
-    kept_table, kept_nums = stay(table), stay(nums)
-    est_edges = edges(heard, far_est, token, size)
+        sums_done,
+    )
+    kept_table, kept_nums = table, nums
+    est_edges = edges(heard, far_est, token, size, payload.shape)
     one_est, two_est = core_side(est_edges, bands, True)
 
     far_slices = frame.sent(3)
-    plain, turned, *own_far = call(
+    plain, turned, *own_far, total_done = call(
         functools.partial(
             total_kernel,
             pairs,
             [slice(s.start * height, s.stop * height) for s in far_slices.values()],
         ),
-        (shape(tiles, area, TILE), shape(tiles, area, TILE))
-        + tuple(shape(1, tiles, len(s) * height, TILE) for s in far_slices.values()),
+        (resident(tiles, area, TILE), resident(tiles, area, TILE))
+        + tuple(resident(1, tiles, len(s) * height, TILE) for s in far_slices.values())
+        + (mark,),
         [vmem] * pairs + [free],
-        [vmem] * (2 + len(sides)),
+        [vmem] * (3 + len(sides)),
         kept[0],
         *moved,
-        est_edges[0],
+        est_edges[2],
     )
     near = swap(plain, "view", 4, 1)
     opposite = swap(turned, "view", 4, 2)
@@ -727,7 +745,7 @@
         (
             resident(tiles + 2, size * 16, TILE),
             resident(2, tiles, n3, TILE),
-            shape(8, 128, dtype=F32),
+            mark,
         ),
         [vmem] * (8 + len(sides)) + [free],
         (vmem, vmem, vmem),
@@ -737,36 +755,39 @@
         *far_est,
         one_est,
         two_est,
-        plain,
+        total_done,
         scratch=scratch,
     )
     tokens = []
 
     def others(slices):
-        tokens.append(stack((near, opposite, last), slices, token))
-        return tokens[-1]
+        rows, done = stack((near, opposite, last), slices, token)
+        tokens.append(done)
+        return rows
 
     far_others = exchange_z(frame, others, slabs, 3)
     far_others = [far_others[s] for s in sides]
+    own_edges = edges((plain, near, opposite, last), (), tokens[-1], depth, plain.shape)
+    near_halo = core_side(own_edges, bands, False)
     recip_b, token_b = call(
         functools.partial(forward_kernel, frame, tiles, (2, 3)),
-        (resident(2, tiles, n3, TILE), shape(8, 128, dtype=F32)),
+        (resident(2, tiles, n3, TILE), mark),
         (vmem, vmem, vmem, free),
         (vmem, vmem),
         kept_nums,
         kept_table,
-        stay(est_frame),
-        tokens[-1],
+        est_frame,
+        own_edges[2],
         scratch=scratch,
     )
-    all_edges = edges(
-        (plain, near, opposite, last), far_own + far_others, token_b, len(frame.need(3))
-    )
-    one, two = core_side(all_edges, bands, False)
+    far_edges = edges(
+        (), far_own + far_others, token_b, len(frame.need(3)) - depth, plain.shape
+    )
+    far_halo = core_side(far_edges, bands, False)
     return call(
         functools.partial(main_kernel, frame, tiles, sides),
-        shape(*estimate.shape, dtype=F32),
-        [smem] * (2 + len(sides)) + [vmem] * (12 + 2 * len(sides)),
+        jax.ShapeDtypeStruct(estimate.shape, F32),
+        [smem] * (2 + len(sides)) + [vmem] * (14 + 2 * len(sides)),
         (vmem,),
         bleach_table,
         bleach_index,
@@ -779,12 +800,12 @@
         last,
         *far_own,
         *far_others,
-        one,
-        two,
-        stay(recip_a),
-        stay(recip_b),
+        *near_halo,
+        *far_halo,
+        recip_a,
+        recip_b,
         kept_table,
-        stay(est_frame),
+        est_frame,
         scratch=[
             vmem((tiles + 2, n3, TILE), BF),
             vmem((tiles + 2, n2, TILE), BF),

time: 83.5 us -> 69.6 us (0.83)
  Pallas kernels: 35 us -> 20.6 us
  starting transfers between devices: 23.1 us -> 27.7 us
  waiting for transfers between devices: 19.1 us -> 15.6 us
    pallas_call x10 -> x11, Pallas kernels: 35 us -> 20.6 us  [call(): pl.pallas_call(kernel, out_shape=shapes, in_specs=whole(*ins), out_specs=...]
    ppermute x1 -> x2, waiting for transfers between devices: 7.23 us -> 4.36 us  [core_side(): return (first, lax.ppermute(own[1], 'gy', [(1, 2), (2, 1)]))]
    ppermute x17 -> x18, starting transfers between devices: 20.4 us -> 22.9 us  [swap(): return lax.ppermute(array, axis, [(i, i ^ mask) for i in range(size)])]
    ppermute x1 -> x2, starting transfers between devices: 2.74 us -> 4.72 us  [core_side(): return (first, lax.ppermute(own[1], 'gy', [(1, 2), (2, 1)]))]
    ppermute x17 -> x18, waiting for transfers between devices: 11.9 us -> 11.2 us  [swap(): return lax.ppermute(array, axis, [(i, i ^ mask) for i in range(size)])]
    unnamed x38 -> x18, local copies, waits for them, and re-layouts: 5.04 us -> 4.56 us
  transfers between devices with their start and end apart: 18 -> 20, of which waited for: 7 -> 9; matrix products, arithmetic and copies ran while one was open for 0% -> 0% of each run, Pallas kernels for 14% -> 11%
where the time goes in v6:
time: 69.6 us; the launch traced here: 69.3 us
  starting transfers between devices  27.7 us (40%)
  Pallas kernels  20.6 us (30%)
  waiting for transfers between devices  15.6 us (22%)
  local copies, waits for them, and re-layouts  4.56 us (7%)
  between operations  0.84 us (1%)
    ppermute x18, starting transfers between devices, swap(): return lax.ppermute(array, axis, [(i, i ^ mask) for i in range(size)])  22.9 us
    pallas_call x11, Pallas kernels, call(): pl.pallas_call(kernel, out_shape=shapes, in_specs=whole(*ins), out_specs=...  20.6 us
    ppermute x18, waiting for transfers between devices, swap(): return lax.ppermute(array, axis, [(i, i ^ mask) for i in range(size)])  11.2 us
    ppermute x2, starting transfers between devices, core_side(): return (first, lax.ppermute(own[1], 'gy', [(1, 2), (2, 1)]))  4.72 us
    unnamed x18, local copies, waits for them, and re-layouts  4.56 us
    ppermute x2, waiting for transfers between devices, core_side(): return (first, lax.ppermute(own[1], 'gy', [(1, 2), (2, 1)]))  4.36 us
  transfers between devices with their start and end apart: 20, of which 9 were waited for; matrix products, arithmetic and copies ran while one was open for 0% of the time, Pallas kernels for 11%

profile of v6, /device:TPU:1, one launch (start us, length us, event | category | flops | bytes accessed | tf_op | source)
XLA Modules:
  0.0 69.3 jit_solution(10599077737204172195)
XLA Ops:
  0.7 1.0 %copy-done = bf16[1,16,8,2048]{3,2,1,0:T(8,128)(2,1)S(1)} copy-done((bf16[1,16,8,2048]{3,2,1,0:T(8,128)(2,1)S(1)}, bf16[1,16,8,2048]{3,2,1,0:T(8,128)(2,1)}, u32[]{:S(2)}) %copy-start) | copy-done | bytes 524312
  1.7 0.8 %copy-done.1 = f32[4,8,512]{2,1,0:T(8,128)S(1)} copy-done((f32[4,8,512]{2,1,0:T(8,128)S(1)}, f32[4,8,512]{2,1,0:T(8,128)}, u32[]{:S(2)}) %copy-start.1) | copy-done | bytes 65560
  2.5 0.7 copy-done.5
  3.2 0.7 copy-done.6
  3.9 0.7 copy-done.7
  4.6 0.7 copy-done.8
  5.2 1.1 %shard_map.91 = (bf16[4,4,8,2048]{3,2,1,0:T(8,128)(2,1)S(1)}, bf16[4,4,8,2048]{3,2,1,0:T(8,128)(2,1)S(1)}, bf16[40,512]{1,0:T(8,128)(2,1)S(1)}) custom-call(s32[1,1,16]{2,1,0:T(1,128)S(1)} %bitcast.5, s32[1,16]{1,0:T(1,128)S(1)} %copy-done.8, f32[1]{0:T(128)S(6)} %copy.10.bg_ref, bf16[16,8,2048]{2,1,0:T(8,128)(2,1)S(1)} %bitcast.3, f32[3,1,3]{2,1,0:T(1,128)S(1)} %bitcast.4, ...), custom_call_target="tpu_custom_call" | custom-call | tf_op jit(solution)/shard_map/pallas_call | solution.py:620
  6.5 4.8 %collective-permute-start.3 = (bf16[40,512]{1,0:T(8,128)(2,1)S(1)}, bf16[40,512]{1,0:T(8,128)(2,1)S(1)}, u32[]{:S(2)}, u32[]{:S(2)}) collective-permute-start(bf16[40,512]{1,0:T(8,128)(2,1)S(1)} %get-tuple-element.36.refs_2_.refs_0_), channel_id=1, source_target_pairs={{0,24},{8,16},{16,8},{24,0},{1,25},{9,17},{17,9},{25,1},{2,26},{10... | collective-permute-start | bytes 122888 | tf_op jit(solution)/shard_map/ppermute | solution.py:21
  11.5 1.2 %collective-permute-start = (s32[4,4]{1,0:T(4,128)}, s32[4,4]{1,0:T(4,128)S(1)}, u32[]{:S(2)}, u32[]{:S(2)}) collective-permute-start(s32[4,4]{1,0:T(4,128)} %refs_0_.1), channel_id=1, source_target_pairs={{0,4},{4,0},{1,5},{5,1},{2,6},{6,2},{3,7},{7,3},{8,12},{12,8},{9,1... | collective-permute-start | bytes 200 | tf_op jit(solution)/shard_map/ppermute | solution.py:21
  12.8 1.4 %collective-permute-done.refs_6_.refs_1_ = s32[4,4]{1,0:T(4,128)S(1)} collective-permute-done((s32[4,4]{1,0:T(4,128)}, s32[4,4]{1,0:T(4,128)S(1)}, u32[]{:S(2)}, u32[]{:S(2)}) %collective-permute-start) | collective-permute-done | bytes 96 | tf_op jit(solution)/shard_map/ppermute | solution.py:21
  14.2 1.2 %collective-permute-done.2.refs_4_.refs_2_ = bf16[40,512]{1,0:T(8,128)(2,1)S(1)} collective-permute-done((bf16[40,512]{1,0:T(8,128)(2,1)S(1)}, bf16[40,512]{1,0:T(8,128)(2,1)S(1)}, u32[]{:S(2)}, u32[]{:S(2)}) %collective-permute-start.2) | collective-permute-done | bytes 40992 | tf_op jit(solution)/shard_map/ppermute | solution.py:21
  15.5 1.3 %collective-permute-start.8 = (bf16[4,32,512]{2,1,0:T(8,128)(2,1)S(1)}, bf16[4,32,512]{2,1,0:T(8,128)(2,1)S(1)}, u32[]{:S(2)}, u32[]{:S(2)}) collective-permute-start(bf16[4,32,512]{2,1,0:T(8,128)(2,1)S(1)} %get-tuple-element.45), channel_id=1, source_target_pairs={{0,4},{4,0},{1,5},{5,1},{2,6},{6,2},{3,7},{7,3},{8,12},{12,8},{9,1... | collective-permute-start | bytes 393224 | tf_op jit(solution)/shard_map/ppermute | solution.py:21
  16.8 1.2 %collective-permute-start.5 = (bf16[4,8,2048]{2,1,0:T(8,128)(2,1)S(1)}, bf16[4,8,2048]{2,1,0:T(8,128)(2,1)S(1)}, u32[]{:S(2)}, u32[]{:S(2)}) collective-permute-start(bf16[4,8,2048]{2,1,0:T(8,128)(2,1)S(1)} %get-tuple-element.42), channel_id=1, source_target_pairs={{0,2},{1,3},{2,0},{3,1},{4,6},{5,7},{6,4},{7,5},{8,10},{9,11},{10,... | collective-permute-start | bytes 393224 | tf_op jit(solution)/shard_map/ppermute | solution.py:21
  18.3 1.2 %collective-permute-start.7 = (bf16[4,8,2048]{2,1,0:T(8,128)(2,1)S(1)}, bf16[4,8,2048]{2,1,0:T(8,128)(2,1)S(1)}, u32[]{:S(2)}, u32[]{:S(2)}) collective-permute-start(bf16[4,8,2048]{2,1,0:T(8,128)(2,1)S(1)} %get-tuple-element.44), channel_id=1, source_target_pairs={{0,6},{1,7},{2,4},{3,5},{4,2},{5,3},{6,0},{7,1},{8,14},{9,15},{10,... | collective-permute-start | bytes 393224 | tf_op jit(solution)/shard_map/ppermute | solution.py:21
  19.4 0.9 %shard_map.93 = (bf16[6,768,256]{2,1,0:T(8,128)(2,1)S(1)}, f32[64,128]{1,0:T(8,128)S(1)}, f32[8,128]{1,0:T(8,128)S(1)}) custom-call(bf16[40,512]{1,0:T(8,128)(2,1)S(1)} %get-tuple-element.36.refs_2_.refs_0_, bf16[40,512]{1,0:T(8,128)(2,1)S(1)} %collective-permute-done.1.refs_3_.refs_1_, bf16[40,512]{1,0:T(8,128)(2,1)S(1)} %collective-permute-done.2.refs_4_.refs_2_, ...), custom_call_target="tpu_custom_call" | custom-call | tf_op jit(solution)/shard_map/pallas_call | solution.py:620
  20.9 1.8 %collective-permute-done.6.refs_2_ = bf16[4,8,2048]{2,1,0:T(8,128)(2,1)S(1)} collective-permute-done((bf16[4,8,2048]{2,1,0:T(8,128)(2,1)S(1)}, bf16[4,8,2048]{2,1,0:T(8,128)(2,1)S(1)}, u32[]{:S(2)}, u32[]{:S(2)}) %collective-permute-start.6) | collective-permute-done | bytes 131104 | tf_op jit(solution)/shard_map/ppermute | solution.py:21
  22.7 3.1 %collective-permute-done.7.refs_3_ = bf16[4,8,2048]{2,1,0:T(8,128)(2,1)S(1)} collective-permute-done((bf16[4,8,2048]{2,1,0:T(8,128)(2,1)S(1)}, bf16[4,8,2048]{2,1,0:T(8,128)(2,1)S(1)}, u32[]{:S(2)}, u32[]{:S(2)}) %collective-permute-start.7) | collective-permute-done | bytes 131104 | tf_op jit(solution)/shard_map/ppermute | solution.py:21
  26.0 1.2 %collective-permute-start.10 = (bf16[8,32,256]{2,1,0:T(8,128)(2,1)S(1)}, bf16[8,32,256]{2,1,0:T(8,128)(2,1)S(1)}, u32[]{:S(2)}, u32[]{:S(2)}) collective-permute-start(bf16[8,32,256]{2,1,0:T(8,128)(2,1)S(1)} %get-tuple-element.49), channel_id=1, source_target_pairs={{0,16},{8,24},{16,0},{24,8},{1,17},{9,25},{17,1},{25,9},{2,18},{10... | collective-permute-start | bytes 393224 | tf_op jit(solution)/shard_map/ppermute | solution.py:21
  27.3 2.8 %collective-permute-start.13 = (bf16[4,8,4,512]{3,2,1,0:T(4,128)(2,1)S(1)}, bf16[4,8,4,512]{3,2,1,0:T(4,128)(2,1)S(1)}, u32[]{:S(2)}, u32[]{:S(2)}) collective-permute-start(bf16[4,8,4,512]{3,2,1,0:T(4,128)(2,1)S(1)} %get-tuple-element.52), channel_id=1, source_target_pairs={{0,1},{1,0},{2,3},{3,2},{4,5},{5,4},{6,7},{7,6},{8,9},{9,8},{10,11... | collective-permute-start | bytes 393224 | tf_op jit(solution)/shard_map/ppermute | solution.py:21
  30.1 0.6 collective-permute-start.14
  30.7 1.6 %collective-permute-start.9 = (bf16[8,32,256]{2,1,0:T(8,128)(2,1)S(1)}, bf16[8,32,256]{2,1,0:T(8,128)(2,1)S(1)}, u32[]{:S(2)}, u32[]{:S(2)}) collective-permute-start(bf16[8,32,256]{2,1,0:T(8,128)(2,1)S(1)} %get-tuple-element.48.refs_0_.refs_4_), channel_id=1, source_target_pairs={{0,8},{8,0},{16,24},{24,16},{1,9},{9,1},{17,25},{25,17},{2,10},{10... | collective-permute-start | bytes 393224 | tf_op jit(solution)/shard_map/ppermute | solution.py:21
  32.5 3.0 %collective-permute-done.14.refs_6_ = bf16[4,8,4,512]{3,2,1,0:T(4,128)(2,1)S(1)} collective-permute-done((bf16[4,8,4,512]{3,2,1,0:T(4,128)(2,1)S(1)}, bf16[4,8,4,512]{3,2,1,0:T(4,128)(2,1)S(1)}, u32[]{:S(2)}, u32[]{:S(2)}) %collective-permute-start.14) | collective-permute-done | bytes 131104 | tf_op jit(solution)/shard_map/ppermute | solution.py:21
  35.5 2.9 %shard_map.96 = (bf16[10,128,256]{2,1,0:T(8,128)(2,1)S(1)}, bf16[2,8,112,256]{3,2,1,0:T(8,128)(2,1)S(1)}, f32[8,128]{1,0:T(8,128)S(1)}) custom-call(f32[64,128]{1,0:T(8,128)S(1)} %get-tuple-element.40.num_ref.refs_2_, bf16[6,768,256]{2,1,0:T(8,128)(2,1)S(1)} %get-tuple-element.51.blocks_ref.refs_16_, bf16[40,512]{1,0:T(8,128)(2,1)S(1)} %get-tuple-element.36.refs_2_.refs_0_, ...), custom_call_target="tpu_custom_call" | custom-call | tf_op jit(solution)/shard_map/pallas_call | solution.py:620
  38.5 1.1 %collective-permute-start.15 = (bf16[3,8,24,256]{3,2,1,0:T(8,128)(2,1)S(1)}, bf16[3,8,24,256]{3,2,1,0:T(8,128)(2,1)S(1)}, u32[]{:S(2)}, u32[]{:S(2)}) collective-permute-start(bf16[3,8,24,256]{3,2,1,0:T(8,128)(2,1)S(1)} %get-tuple-element.56), channel_id=1, source_target_pairs={{0,4},{4,0},{1,5},{5,1},{2,6},{6,2},{3,7},{7,3},{8,12},{12,8},{9,1... | collective-permute-start | bytes 884744 | tf_op jit(solution)/shard_map/ppermute | solution.py:21
  40.3 2.9 %collective-permute-start.16 = (bf16[4,8,4,4,256]{4,3,2,1,0:T(4,128)(2,1)S(1)}, bf16[4,8,4,4,256]{4,3,2,1,0:T(4,128)(2,1)S(1)}, u32[]{:S(2)}, u32[]{:S(2)}) collective-permute-start(bf16[4,8,4,4,256]{4,3,2,1,0:T(4,128)(2,1)S(1)} %get-tuple-element.58), channel_id=1, source_target_pairs={{0,1},{1,0},{2,3},{3,2},{4,5},{5,4},{6,7},{7,6},{8,9},{9,8},{10,11... | collective-permute-start | bytes 786440 | tf_op jit(solution)/shard_map/ppermute | solution.py:21
  43.2 2.1 %collective-permute-start.17 = (bf16[4,8,4,4,256]{4,3,2,1,0:T(4,128)(2,1)S(1)}, bf16[4,8,4,4,256]{4,3,2,1,0:T(4,128)(2,1)S(1)}, u32[]{:S(2)}, u32[]{:S(2)}) collective-permute-start(bf16[4,8,4,4,256]{4,3,2,1,0:T(4,128)(2,1)S(1)} %get-tuple-element.59), channel_id=1, source_target_pairs={{1,2},{2,1},{5,6},{6,5},{9,10},{10,9},{13,14},{14,13},{17,18},{18,... | collective-permute-start | bytes 786440 | tf_op jit(solution)/shard_map/ppermute | solution.py:28
  45.3 2.8 %shard_map.99 = (bf16[2,8,112,256]{3,2,1,0:T(8,128)(2,1)S(1)}, f32[8,128]{1,0:T(8,128)S(1)}) custom-call(f32[64,128]{1,0:T(8,128)S(1)} %get-tuple-element.40.num_ref.refs_2_, bf16[6,768,256]{2,1,0:T(8,128)(2,1)S(1)} %get-tuple-element.51.blocks_ref.refs_16_, bf16[10,128,256]{2,1,0:T(8,128)(2,1)S(1)} %get-tuple-element.60.frame_ref.refs_17_, ...), custom_call_target="tpu_custom_call" | custom-call | tf_op jit(solution)/shard_map/pallas_call | solution.py:620
  48.2 0.6 shard_map.100
  48.8 2.0 %collective-permute-start.18 = (bf16[4,8,3,4,256]{4,3,2,1,0:T(4,128)(2,1)S(1)}, bf16[4,8,3,4,256]{4,3,2,1,0:T(4,128)(2,1)S(1)}, u32[]{:S(2)}, u32[]{:S(2)}) collective-permute-start(bf16[4,8,3,4,256]{4,3,2,1,0:T(4,128)(2,1)S(1)} %get-tuple-element.63), channel_id=1, source_target_pairs={{0,1},{1,0},{2,3},{3,2},{4,5},{5,4},{6,7},{7,6},{8,9},{9,8},{10,11... | collective-permute-start | bytes 589832 | tf_op jit(solution)/shard_map/ppermute | solution.py:21
  50.7 2.6 %collective-permute-start.19 = (bf16[4,8,3,4,256]{4,3,2,1,0:T(4,128)(2,1)S(1)}, bf16[4,8,3,4,256]{4,3,2,1,0:T(4,128)(2,1)S(1)}, u32[]{:S(2)}, u32[]{:S(2)}) collective-permute-start(bf16[4,8,3,4,256]{4,3,2,1,0:T(4,128)(2,1)S(1)} %get-tuple-element.64), channel_id=1, source_target_pairs={{1,2},{2,1},{5,6},{6,5},{9,10},{10,9},{13,14},{14,13},{17,18},{18,... | collective-permute-start | bytes 589832 | tf_op jit(solution)/shard_map/ppermute | solution.py:28
  53.4 4.4 %collective-permute-done.19.refs_13_ = bf16[4,8,3,4,256]{4,3,2,1,0:T(4,128)(2,1)S(1)} collective-permute-done((bf16[4,8,3,4,256]{4,3,2,1,0:T(4,128)(2,1)S(1)}, bf16[4,8,3,4,256]{4,3,2,1,0:T(4,128)(2,1)S(1)}, u32[]{:S(2)}, u32[]{:S(2)}) %collective-permute-start.19) | collective-permute-done | bytes 196640 | tf_op jit(solution)/shard_map/ppermute | solution.py:28
  57.7 11.6 %shard_map.101 = f32[4,8,512]{2,1,0:T(8,128)} custom-call(f32[4,16]{1,0:T(4,128)S(1)} %copy-done.3, s32[4,4]{1,0:T(4,128)S(1)} %copy-done.4, s32[4,4]{1,0:T(4,128)S(1)} %collective-permute-done.refs_6_.refs_1_, f32[64,128]{1,0:T(8,128)S(1)} %get-tuple-element.40.num_ref.refs_2_, f32[4,8,512]{2,1,0:T(8,128)S(1)} %copy-done.2, ...), custom_call_target="tpu_custom_call" | custom-call | tf_op jit(solution)/shard_map/pallas_call | solution.py:620
  (37 shorter events, 2.6 us)
Async XLA Ops:
  0.7 1.0 %copy-start = (bf16[1,16,8,2048]{3,2,1,0:T(8,128)(2,1)S(1)}, bf16[1,16,8,2048]{3,2,1,0:T(8,128)(2,1)}, u32[]{:S(2)}) copy-start(bf16[1,16,8,2048]{3,2,1,0:T(8,128)(2,1)} %param.9) | copy-start | bytes 1572868
  1.7 0.8 %copy-start.1 = (f32[4,8,512]{2,1,0:T(8,128)S(1)}, f32[4,8,512]{2,1,0:T(8,128)}, u32[]{:S(2)}) copy-start(f32[4,8,512]{2,1,0:T(8,128)} %refs_3_.1) | copy-start | bytes 196612
  2.5 0.7 copy-start.5
  3.2 0.7 copy-start.6
  3.9 0.7 copy-start.7
  4.6 0.7 copy-start.8
  6.4 9.0 %collective-permute-start.4 = (bf16[4,4,8,2048]{3,2,1,0:T(8,128)(2,1)S(1)}, bf16[4,4,8,2048]{3,2,1,0:T(8,128)(2,1)S(1)}, u32[]{:S(2)}, u32[]{:S(2)}) collective-permute-start(bf16[4,4,8,2048]{3,2,1,0:T(8,128)(2,1)S(1)} %get-tuple-element.38), channel_id=1, source_target_pairs={{0,1},{1,0},{2,3},{3,2},{4,5},{5,4},{6,7},{7,6},{8,9},{9,8},{10,11... | collective-permute-start | bytes 1572872 | tf_op jit(solution)/shard_map/ppermute | solution.py:21
  6.5 7.7 %collective-permute-start.3 = (bf16[40,512]{1,0:T(8,128)(2,1)S(1)}, bf16[40,512]{1,0:T(8,128)(2,1)S(1)}, u32[]{:S(2)}, u32[]{:S(2)}) collective-permute-start(bf16[40,512]{1,0:T(8,128)(2,1)S(1)} %get-tuple-element.36.refs_2_.refs_0_), channel_id=1, source_target_pairs={{0,24},{8,16},{16,8},{24,0},{1,25},{9,17},{17,9},{25,1},{2,26},{10... | collective-permute-start | bytes 122888 | tf_op jit(solution)/shard_map/ppermute | solution.py:21
  11.3 4.1 %collective-permute-start.2 = (bf16[40,512]{1,0:T(8,128)(2,1)S(1)}, bf16[40,512]{1,0:T(8,128)(2,1)S(1)}, u32[]{:S(2)}, u32[]{:S(2)}) collective-permute-start(bf16[40,512]{1,0:T(8,128)(2,1)S(1)} %get-tuple-element.36.refs_2_.refs_0_), channel_id=1, source_target_pairs={{0,16},{8,24},{16,0},{24,8},{1,17},{9,25},{17,1},{25,9},{2,18},{10... | collective-permute-start | bytes 122888 | tf_op jit(solution)/shard_map/ppermute | solution.py:21
  11.3 4.1 %collective-permute-start.1 = (bf16[40,512]{1,0:T(8,128)(2,1)S(1)}, bf16[40,512]{1,0:T(8,128)(2,1)S(1)}, u32[]{:S(2)}, u32[]{:S(2)}) collective-permute-start(bf16[40,512]{1,0:T(8,128)(2,1)S(1)} %get-tuple-element.36.refs_2_.refs_0_), channel_id=1, source_target_pairs={{0,8},{8,0},{16,24},{24,16},{1,9},{9,1},{17,25},{25,17},{2,10},{10... | collective-permute-start | bytes 122888 | tf_op jit(solution)/shard_map/ppermute | solution.py:21
  11.5 2.6 %collective-permute-start = (s32[4,4]{1,0:T(4,128)}, s32[4,4]{1,0:T(4,128)S(1)}, u32[]{:S(2)}, u32[]{:S(2)}) collective-permute-start(s32[4,4]{1,0:T(4,128)} %refs_0_.1), channel_id=1, source_target_pairs={{0,4},{4,0},{1,5},{5,1},{2,6},{6,2},{3,7},{7,3},{8,12},{12,8},{9,1... | collective-permute-start | bytes 200 | tf_op jit(solution)/shard_map/ppermute | solution.py:21
  15.5 4.9 %collective-permute-start.8 = (bf16[4,32,512]{2,1,0:T(8,128)(2,1)S(1)}, bf16[4,32,512]{2,1,0:T(8,128)(2,1)S(1)}, u32[]{:S(2)}, u32[]{:S(2)}) collective-permute-start(bf16[4,32,512]{2,1,0:T(8,128)(2,1)S(1)} %get-tuple-element.45), channel_id=1, source_target_pairs={{0,4},{4,0},{1,5},{5,1},{2,6},{6,2},{3,7},{7,3},{8,12},{12,8},{9,1... | collective-permute-start | bytes 393224 | tf_op jit(solution)/shard_map/ppermute | solution.py:21
  16.8 4.1 %collective-permute-start.5 = (bf16[4,8,2048]{2,1,0:T(8,128)(2,1)S(1)}, bf16[4,8,2048]{2,1,0:T(8,128)(2,1)S(1)}, u32[]{:S(2)}, u32[]{:S(2)}) collective-permute-start(bf16[4,8,2048]{2,1,0:T(8,128)(2,1)S(1)} %get-tuple-element.42), channel_id=1, source_target_pairs={{0,2},{1,3},{2,0},{3,1},{4,6},{5,7},{6,4},{7,5},{8,10},{9,11},{10,... | collective-permute-start | bytes 393224 | tf_op jit(solution)/shard_map/ppermute | solution.py:21
  18.0 4.7 %collective-permute-start.6 = (bf16[4,8,2048]{2,1,0:T(8,128)(2,1)S(1)}, bf16[4,8,2048]{2,1,0:T(8,128)(2,1)S(1)}, u32[]{:S(2)}, u32[]{:S(2)}) collective-permute-start(bf16[4,8,2048]{2,1,0:T(8,128)(2,1)S(1)} %get-tuple-element.43), channel_id=1, source_target_pairs={{0,4},{1,5},{2,6},{3,7},{4,0},{5,1},{6,2},{7,3},{8,12},{9,13},{10,... | collective-permute-start | bytes 393224 | tf_op jit(solution)/shard_map/ppermute | solution.py:21
  18.3 7.5 %collective-permute-start.7 = (bf16[4,8,2048]{2,1,0:T(8,128)(2,1)S(1)}, bf16[4,8,2048]{2,1,0:T(8,128)(2,1)S(1)}, u32[]{:S(2)}, u32[]{:S(2)}) collective-permute-start(bf16[4,8,2048]{2,1,0:T(8,128)(2,1)S(1)} %get-tuple-element.44), channel_id=1, source_target_pairs={{0,6},{1,7},{2,4},{3,5},{4,2},{5,3},{6,0},{7,1},{8,14},{9,15},{10,... | collective-permute-start | bytes 393224 | tf_op jit(solution)/shard_map/ppermute | solution.py:21
  26.0 6.5 %collective-permute-start.10 = (bf16[8,32,256]{2,1,0:T(8,128)(2,1)S(1)}, bf16[8,32,256]{2,1,0:T(8,128)(2,1)S(1)}, u32[]{:S(2)}, u32[]{:S(2)}) collective-permute-start(bf16[8,32,256]{2,1,0:T(8,128)(2,1)S(1)} %get-tuple-element.49), channel_id=1, source_target_pairs={{0,16},{8,24},{16,0},{24,8},{1,17},{9,25},{17,1},{25,9},{2,18},{10... | collective-permute-start | bytes 393224 | tf_op jit(solution)/shard_map/ppermute | solution.py:21
  27.3 5.3 %collective-permute-start.13 = (bf16[4,8,4,512]{3,2,1,0:T(4,128)(2,1)S(1)}, bf16[4,8,4,512]{3,2,1,0:T(4,128)(2,1)S(1)}, u32[]{:S(2)}, u32[]{:S(2)}) collective-permute-start(bf16[4,8,4,512]{3,2,1,0:T(4,128)(2,1)S(1)} %get-tuple-element.52), channel_id=1, source_target_pairs={{0,1},{1,0},{2,3},{3,2},{4,5},{5,4},{6,7},{7,6},{8,9},{9,8},{10,11... | collective-permute-start | bytes 393224 | tf_op jit(solution)/shard_map/ppermute | solution.py:21
  30.1 5.4 %collective-permute-start.14 = (bf16[4,8,4,512]{3,2,1,0:T(4,128)(2,1)S(1)}, bf16[4,8,4,512]{3,2,1,0:T(4,128)(2,1)S(1)}, u32[]{:S(2)}, u32[]{:S(2)}) collective-permute-start(bf16[4,8,4,512]{3,2,1,0:T(4,128)(2,1)S(1)} %get-tuple-element.53), channel_id=1, source_target_pairs={{0,3},{1,2},{2,1},{3,0},{4,7},{5,6},{6,5},{7,4},{8,11},{9,10},{10,... | collective-permute-start | bytes 393224 | tf_op jit(solution)/shard_map/ppermute | solution.py:21
  30.7 7.7 %collective-permute-start.9 = (bf16[8,32,256]{2,1,0:T(8,128)(2,1)S(1)}, bf16[8,32,256]{2,1,0:T(8,128)(2,1)S(1)}, u32[]{:S(2)}, u32[]{:S(2)}) collective-permute-start(bf16[8,32,256]{2,1,0:T(8,128)(2,1)S(1)} %get-tuple-element.48.refs_0_.refs_4_), channel_id=1, source_target_pairs={{0,8},{8,0},{16,24},{24,16},{1,9},{9,1},{17,25},{25,17},{2,10},{10... | collective-permute-start | bytes 393224 | tf_op jit(solution)/shard_map/ppermute | solution.py:21
  32.5 6.0 %collective-permute-start.11 = (bf16[8,32,256]{2,1,0:T(8,128)(2,1)S(1)}, bf16[8,32,256]{2,1,0:T(8,128)(2,1)S(1)}, u32[]{:S(2)}, u32[]{:S(2)}) collective-permute-start(bf16[8,32,256]{2,1,0:T(8,128)(2,1)S(1)} %collective-permute-done.10.refs_1_.refs_2_.refs_6_), channel_id=1, source_target_pairs={{0,8},{8,0},{16,24},{24,16},{1,9},{9,1},{17,25},{25,17},{2,10},{10... | collective-permute-start | bytes 393224 | tf_op jit(solution)/shard_map/ppermute | solution.py:21
  38.4 19.4 %copy-start.2 = (f32[4,8,512]{2,1,0:T(8,128)S(1)}, f32[4,8,512]{2,1,0:T(8,128)}, u32[]{:S(2)}) copy-start(f32[4,8,512]{2,1,0:T(8,128)} %refs_3_.1) | copy-start | bytes 196612
  38.4 19.4 %copy-start.3 = (f32[4,16]{1,0:T(4,128)S(1)}, f32[4,16]{1,0:T(4,128)}, u32[]{:S(2)}) copy-start(f32[4,16]{1,0:T(4,128)} %table_ref.1) | copy-start | bytes 772
  38.4 19.4 %copy-start.4 = (s32[4,4]{1,0:T(4,128)S(1)}, s32[4,4]{1,0:T(4,128)}, u32[]{:S(2)}) copy-start(s32[4,4]{1,0:T(4,128)} %refs_0_.1) | copy-start | bytes 196
  38.5 9.6 %collective-permute-start.15 = (bf16[3,8,24,256]{3,2,1,0:T(8,128)(2,1)S(1)}, bf16[3,8,24,256]{3,2,1,0:T(8,128)(2,1)S(1)}, u32[]{:S(2)}, u32[]{:S(2)}) collective-permute-start(bf16[3,8,24,256]{3,2,1,0:T(8,128)(2,1)S(1)} %get-tuple-element.56), channel_id=1, source_target_pairs={{0,4},{4,0},{1,5},{5,1},{2,6},{6,2},{3,7},{7,3},{8,12},{12,8},{9,1... | collective-permute-start | bytes 884744 | tf_op jit(solution)/shard_map/ppermute | solution.py:21
  39.7 8.4 %collective-permute-start.12 = (bf16[1,8,24,256]{3,2,1,0:T(8,128)(2,1)S(1)}, bf16[1,8,24,256]{3,2,1,0:T(8,128)(2,1)S(1)}, u32[]{:S(2)}, u32[]{:S(2)}) collective-permute-start(bf16[1,8,24,256]{3,2,1,0:T(8,128)(2,1)S(1)} %get-tuple-element.50), channel_id=1, source_target_pairs={{0,4},{4,0},{1,5},{5,1},{2,6},{6,2},{3,7},{7,3},{8,12},{12,8},{9,1... | collective-permute-start | bytes 294920 | tf_op jit(solution)/shard_map/ppermute | solution.py:21
  40.3 13.0 %collective-permute-start.16 = (bf16[4,8,4,4,256]{4,3,2,1,0:T(4,128)(2,1)S(1)}, bf16[4,8,4,4,256]{4,3,2,1,0:T(4,128)(2,1)S(1)}, u32[]{:S(2)}, u32[]{:S(2)}) collective-permute-start(bf16[4,8,4,4,256]{4,3,2,1,0:T(4,128)(2,1)S(1)} %get-tuple-element.58), channel_id=1, source_target_pairs={{0,1},{1,0},{2,3},{3,2},{4,5},{5,4},{6,7},{7,6},{8,9},{9,8},{10,11... | collective-permute-start | bytes 786440 | tf_op jit(solution)/shard_map/ppermute | solution.py:21
  43.2 10.2 %collective-permute-start.17 = (bf16[4,8,4,4,256]{4,3,2,1,0:T(4,128)(2,1)S(1)}, bf16[4,8,4,4,256]{4,3,2,1,0:T(4,128)(2,1)S(1)}, u32[]{:S(2)}, u32[]{:S(2)}) collective-permute-start(bf16[4,8,4,4,256]{4,3,2,1,0:T(4,128)(2,1)S(1)} %get-tuple-element.59), channel_id=1, source_target_pairs={{1,2},{2,1},{5,6},{6,5},{9,10},{10,9},{13,14},{14,13},{17,18},{18,... | collective-permute-start | bytes 786440 | tf_op jit(solution)/shard_map/ppermute | solution.py:28
  48.8 4.6 %collective-permute-start.18 = (bf16[4,8,3,4,256]{4,3,2,1,0:T(4,128)(2,1)S(1)}, bf16[4,8,3,4,256]{4,3,2,1,0:T(4,128)(2,1)S(1)}, u32[]{:S(2)}, u32[]{:S(2)}) collective-permute-start(bf16[4,8,3,4,256]{4,3,2,1,0:T(4,128)(2,1)S(1)} %get-tuple-element.63), channel_id=1, source_target_pairs={{0,1},{1,0},{2,3},{3,2},{4,5},{5,4},{6,7},{7,6},{8,9},{9,8},{10,11... | collective-permute-start | bytes 589832 | tf_op jit(solution)/shard_map/ppermute | solution.py:21
  50.7 7.0 %collective-permute-start.19 = (bf16[4,8,3,4,256]{4,3,2,1,0:T(4,128)(2,1)S(1)}, bf16[4,8,3,4,256]{4,3,2,1,0:T(4,128)(2,1)S(1)}, u32[]{:S(2)}, u32[]{:S(2)}) collective-permute-start(bf16[4,8,3,4,256]{4,3,2,1,0:T(4,128)(2,1)S(1)} %get-tuple-element.64), channel_id=1, source_target_pairs={{1,2},{2,1},{5,6},{6,5},{9,10},{10,9},{13,14},{14,13},{17,18},{18,... | collective-permute-start | bytes 589832 | tf_op jit(solution)/shard_map/ppermute | solution.py:28

commit v7 on v6

--- a/solution.py
+++ b/solution.py
@@ -172,7 +172,7 @@
 def sum_kernel(pairs, parts, *refs):
     even_ref, other_ref = refs[:2]
     heard = refs[2:6]
-    sums, stacks, done_ref = refs[7 : 7 + pairs], refs[7 + pairs : -1], refs[-1]
+    sums, stacks, done_ref = refs[6 : 6 + pairs], refs[6 + pairs : -1], refs[-1]
     done_ref[...] = jnp.zeros(done_ref.shape, F32)
     for k in range(pairs):
         sums[k][...] = (even_ref[k].astype(F32) + other_ref[k].astype(F32)).astype(BF)
@@ -181,8 +181,8 @@
             ref[v] = heard[v][rows, :]
 
 
-def stack_kernel(rows, *refs):
-    ins, (out_ref, done_ref) = refs[:-3], refs[-2:]
+def stack_kernel(rows, count, *refs):
+    ins, (out_ref, done_ref) = refs[:count], refs[-2:]
     done_ref[...] = jnp.zeros(done_ref.shape, F32)
     for v, ref in enumerate(ins):
         out_ref[v] = ref[..., rows, :]
@@ -284,15 +284,22 @@
             jnp.broadcast_to(base, (TILE, 3 * TILE)), 0, 1, stride=1, stride_axis=0
         ).astype(BF)
         turned = jnp.dot(flip, wide, preferred_element_type=F32).astype(BF)
-        for k in range(3):
+        half = TILE // 2
+        for k, (rows, to) in enumerate(
+            (
+                (slice(half, TILE), slice(0, half)),
+                (slice(0, TILE), slice(half, half + TILE)),
+                (slice(0, half), slice(half + TILE, 2 * TILE)),
+            )
+        ):
             cut = slice(k * TILE, (k + 1) * TILE)
-            to = slice((2 - k) * TILE, (3 - k) * TILE)
+            across = slice((2 - k) * TILE, (3 - k) * TILE)
             if v >= 2:
-                out_ref[2 + v, cut, :] = turned[:, cut]
+                out_ref[2 + v, to, :] = turned[rows, cut]
             else:
-                out_ref[2 + v, to, :] = wide[:, cut]
-                out_ref[v, cut, :] = jnp.dot(
-                    turned[:, cut], flip, preferred_element_type=F32
+                out_ref[2 + v, to, :] = wide[rows, across]
+                out_ref[v, to, :] = jnp.dot(
+                    turned[rows, cut], flip, preferred_element_type=F32
                 ).astype(BF)
 
 
@@ -305,13 +312,16 @@
 
 
 def conv(src, first, tiles, rows, blocks, dst, step):
+    half = TILE // 2
     s = 0
     while s < tiles:
         n = min(step, tiles - s)
         lhs = jnp.concatenate(
             [
-                src[pl.ds(first + s + k, n)].reshape(n * rows, TILE)
-                for k in range(3)
+                src[pl.ds(first + s + k, n), :, cut].reshape(n * rows, cut.stop - cut.start)
+                for k, cut in enumerate(
+                    (slice(half, TILE), slice(0, TILE), slice(0, half))
+                )
             ],
             axis=1,
         )
@@ -612,9 +622,22 @@
     def stay(array):
         return pltpu.with_memory_space_constraint(array, pltpu.VMEM)
 
+    given = [piece_row, estimate, psf_x, bleach_table]
+    given += [pieces[0], stencil.transpose(1, 0, 2), piece_owner.transpose(0, 2, 1)]
+    first_pieces, first_taps, first_owner = given[-3:]
+
+    def is_given(x):
+        return any(x is y for y in given)
+
     def call(kernel, shapes, ins, outs, *args, scratch=()):
         args = [
-            stay(x) if space is vmem else x
+            (
+                pltpu.with_memory_space_constraint(x, pltpu.HBM)
+                if is_given(x)
+                else stay(x)
+                if space is vmem
+                else x
+            )
             for space, x in zip(ins, args)
         ]
         out = pl.pallas_call(
@@ -642,11 +665,11 @@
         (half_cells, half_cells, resident(area + 8, chunk)),
         (smem, smem, smem, vmem, vmem, vmem, vmem),
         (vmem, vmem, vmem),
-        piece_owner.transpose(0, 2, 1),
+        first_owner,
         piece_row,
         background,
-        pieces[0],
-        stencil.transpose(1, 0, 2),
+        first_pieces,
+        first_taps,
         estimate,
         psf_x,
         scratch=[vmem((blocks * depth, height, width), F32), vmem((8, chunk), F32)],
@@ -664,26 +687,25 @@
         (resident(depth, height, width),) * pairs
         + tuple(resident(4, len(s) * height, chunk) for s in est_slices.values())
         + (mark,),
-        [vmem] * 6 + [free],
+        [vmem] * 6,
         [vmem] * (pairs + len(sides) + 1),
         even,
         other,
         *heard,
-        index_far[sides[0]],
     )
     kept, est_stacks, sums_done = out[:pairs], out[pairs:-1], out[-1]
     moved = [swap(kept[k], ("gz", "gy"), blocks, 2 * k) for k in range(1, pairs)]
 
-    def stack(arrays, slices, token):
+    def stack(arrays, slices, *tokens):
         rows = slice(slices.start * height, slices.stop * height)
         dims = (len(arrays),) + arrays[0].shape[:-2] + (len(slices) * height, arrays[0].shape[-1])
         return call(
-            functools.partial(stack_kernel, rows),
+            functools.partial(stack_kernel, rows, len(arrays)),
             (resident(*dims), mark),
-            [vmem] * len(arrays) + [free],
+            [vmem] * len(arrays) + [free] + [vmem] * (len(tokens) - 1),
             (vmem, vmem),
             *arrays,
-            token,
+            *tokens,
         )
 
     def edges(arrays, fars, token, slices, dims):
@@ -705,7 +727,7 @@
     far_est = [far_est[s] for s in sides]
     table, nums, token = call(
         functools.partial(band_kernel, area),
-        (resident(6, 3 * TILE, TILE), resident(64, 128, dtype=F32), mark),
+        (resident(6, 2 * TILE, TILE), resident(64, 128, dtype=F32), mark),
         [vmem] * 4 + [free],
         (vmem, vmem, vmem),
         *heard,
@@ -740,6 +762,19 @@
     n3, n2, n1 = (len(frame.need(r)) * 16 for r in (3, 2, 1))
 
     scratch = [vmem((tiles, size * 16, TILE), BF)]
+    tokens = []
+
+    def others(slices):
+        rows, done = stack(
+            (near, opposite, last), slices, index_far[sides[0]], one_est, two_est
+        )
+        tokens.append(done)
+        return rows
+
+    far_others = exchange_z(frame, others, slabs, 3)
+    far_others = [far_others[s] for s in sides]
+    own_edges = edges((plain, near, opposite, last), (), tokens[-1], depth, plain.shape)
+    near_halo = core_side(own_edges, bands, False)
     est_frame, recip_a, token = call(
         functools.partial(start_kernel, frame, tiles, sides, (0, 1)),
         (
@@ -755,20 +790,13 @@
         *far_est,
         one_est,
         two_est,
-        total_done,
+        own_edges[2],
         scratch=scratch,
     )
-    tokens = []
-
-    def others(slices):
-        rows, done = stack((near, opposite, last), slices, token)
-        tokens.append(done)
-        return rows
-
-    far_others = exchange_z(frame, others, slabs, 3)
-    far_others = [far_others[s] for s in sides]
-    own_edges = edges((plain, near, opposite, last), (), tokens[-1], depth, plain.shape)
-    near_halo = core_side(own_edges, bands, False)
+    far_edges = edges(
+        (), far_own + far_others, token, len(frame.need(3)) - depth, plain.shape
+    )
+    far_halo = core_side(far_edges, bands, False)
     recip_b, token_b = call(
         functools.partial(forward_kernel, frame, tiles, (2, 3)),
         (resident(2, tiles, n3, TILE), mark),
@@ -777,13 +805,9 @@
         kept_nums,
         kept_table,
         est_frame,
-        own_edges[2],
+        far_edges[2],
         scratch=scratch,
     )
-    far_edges = edges(
-        (), far_own + far_others, token_b, len(frame.need(3)) - depth, plain.shape
-    )
-    far_halo = core_side(far_edges, bands, False)
     return call(
         functools.partial(main_kernel, frame, tiles, sides),
         jax.ShapeDtypeStruct(estimate.shape, F32),

time: 69.6 us -> 63.3 us (0.909)
  local copies, waits for them, and re-layouts: 4.56 us -> 0.01 us
  waiting for transfers between devices: 15.6 us -> 14.8 us
    unnamed x18 -> x2, local copies, waits for them, and re-layouts: 4.56 us -> 0.01 us
    ppermute x2, waiting for transfers between devices: 4.36 us -> 1.11 us  [core_side(): return (first, lax.ppermute(own[1], 'gy', [(1, 2), (2, 1)]))]
    ppermute x18, waiting for transfers between devices: 11.2 us -> 13.7 us  [swap(): return lax.ppermute(array, axis, [(i, i ^ mask) for i in range(size)])]
    ppermute x18, starting transfers between devices: 22.9 us -> 22.2 us  [swap(): return lax.ppermute(array, axis, [(i, i ^ mask) for i in range(size)])]
  transfers between devices with their start and end apart: 20 -> 20, of which waited for: 9 -> 10; matrix products, arithmetic and copies ran while one was open for 0% -> 0% of each run, Pallas kernels for 11% -> 11%
where the time goes in v7:
time: 63.3 us; the launch traced here: 63.1 us
  starting transfers between devices  27.1 us (43%)
  Pallas kernels  20.4 us (32%)
  waiting for transfers between devices  14.8 us (23%)
  between operations  0.78 us (1%)
    ppermute x18, starting transfers between devices, swap(): return lax.ppermute(array, axis, [(i, i ^ mask) for i in range(size)])  22.2 us
    pallas_call x11, Pallas kernels, call(): pl.pallas_call(kernel, out_shape=shapes, in_specs=whole(*ins), out_specs=...  20.4 us
    ppermute x18, waiting for transfers between devices, swap(): return lax.ppermute(array, axis, [(i, i ^ mask) for i in range(size)])  13.7 us
    ppermute x2, starting transfers between devices, core_side(): return (first, lax.ppermute(own[1], 'gy', [(1, 2), (2, 1)]))  4.87 us
  transfers between devices with their start and end apart: 20, of which 10 were waited for; matrix products, arithmetic and copies ran while one was open for 0% of the time, Pallas kernels for 11%

profile of v7, /device:TPU:1, one launch (start us, length us, event | category | flops | bytes accessed | tf_op | source)
XLA Modules:
  0.0 63.1 jit_solution(2013177884843506413)
XLA Ops:
  0.7 1.7 %shard_map.91 = (bf16[4,4,8,2048]{3,2,1,0:T(8,128)(2,1)S(1)}, bf16[4,4,8,2048]{3,2,1,0:T(8,128)(2,1)S(1)}, bf16[40,512]{1,0:T(8,128)(2,1)S(1)}) custom-call(s32[1,1,16]{2,1,0:T(1,128)} %bitcast.5, s32[1,16]{1,0:T(1,128)} %row_ref.1, f32[1]{0:T(128)S(6)} %copy.10.bg_ref, bf16[16,8,2048]{2,1,0:T(8,128)(2,1)} %bitcast.3, f32[3,1,3]{2,1,0:T(1,128)} %bitcast.4, ...), custom_call_target="tpu_custom_call" | custom-call | tf_op jit(solution)/shard_map/pallas_call | solution.py:643
  2.5 4.8 %collective-permute-start.3 = (bf16[40,512]{1,0:T(8,128)(2,1)S(1)}, bf16[40,512]{1,0:T(8,128)(2,1)S(1)}, u32[]{:S(2)}, u32[]{:S(2)}) collective-permute-start(bf16[40,512]{1,0:T(8,128)(2,1)S(1)} %get-tuple-element.35.refs_2_.refs_0_), channel_id=1, source_target_pairs={{0,24},{8,16},{16,8},{24,0},{1,25},{9,17},{17,9},{25,1},{2,26},{10... | collective-permute-start | bytes 122888 | tf_op jit(solution)/shard_map/ppermute | solution.py:21
  7.3 0.3 collective-permute-start.1
  7.5 1.6 %collective-permute-done.3.refs_5_.refs_3_ = bf16[40,512]{1,0:T(8,128)(2,1)S(1)} collective-permute-done((bf16[40,512]{1,0:T(8,128)(2,1)S(1)}, bf16[40,512]{1,0:T(8,128)(2,1)S(1)}, u32[]{:S(2)}, u32[]{:S(2)}) %collective-permute-start.3) | collective-permute-done | bytes 40992 | tf_op jit(solution)/shard_map/ppermute | solution.py:21
  9.1 2.2 %collective-permute-done.2.refs_4_.refs_2_ = bf16[40,512]{1,0:T(8,128)(2,1)S(1)} collective-permute-done((bf16[40,512]{1,0:T(8,128)(2,1)S(1)}, bf16[40,512]{1,0:T(8,128)(2,1)S(1)}, u32[]{:S(2)}, u32[]{:S(2)}) %collective-permute-start.2) | collective-permute-done | bytes 40992 | tf_op jit(solution)/shard_map/ppermute | solution.py:21
  11.5 1.3 %collective-permute-start.8 = (bf16[4,32,512]{2,1,0:T(8,128)(2,1)S(1)}, bf16[4,32,512]{2,1,0:T(8,128)(2,1)S(1)}, u32[]{:S(2)}, u32[]{:S(2)}) collective-permute-start(bf16[4,32,512]{2,1,0:T(8,128)(2,1)S(1)} %get-tuple-element.44), channel_id=1, source_target_pairs={{0,4},{4,0},{1,5},{5,1},{2,6},{6,2},{3,7},{7,3},{8,12},{12,8},{9,1... | collective-permute-start | bytes 393224 | tf_op jit(solution)/shard_map/ppermute | solution.py:21
  12.8 1.2 %collective-permute-start.5 = (bf16[4,8,2048]{2,1,0:T(8,128)(2,1)S(1)}, bf16[4,8,2048]{2,1,0:T(8,128)(2,1)S(1)}, u32[]{:S(2)}, u32[]{:S(2)}) collective-permute-start(bf16[4,8,2048]{2,1,0:T(8,128)(2,1)S(1)} %get-tuple-element.41), channel_id=1, source_target_pairs={{0,2},{1,3},{2,0},{3,1},{4,6},{5,7},{6,4},{7,5},{8,10},{9,11},{10,... | collective-permute-start | bytes 393224 | tf_op jit(solution)/shard_map/ppermute | solution.py:21
  14.0 0.3 collective-permute-start.6
  14.3 1.2 %collective-permute-start.7 = (bf16[4,8,2048]{2,1,0:T(8,128)(2,1)S(1)}, bf16[4,8,2048]{2,1,0:T(8,128)(2,1)S(1)}, u32[]{:S(2)}, u32[]{:S(2)}) collective-permute-start(bf16[4,8,2048]{2,1,0:T(8,128)(2,1)S(1)} %get-tuple-element.43), channel_id=1, source_target_pairs={{0,6},{1,7},{2,4},{3,5},{4,2},{5,3},{6,0},{7,1},{8,14},{9,15},{10,... | collective-permute-start | bytes 393224 | tf_op jit(solution)/shard_map/ppermute | solution.py:21
  15.4 0.9 %shard_map.93 = (bf16[6,512,256]{2,1,0:T(8,128)(2,1)S(1)}, f32[64,128]{1,0:T(8,128)S(1)}, f32[8,128]{1,0:T(8,128)S(1)}) custom-call(bf16[40,512]{1,0:T(8,128)(2,1)S(1)} %get-tuple-element.35.refs_2_.refs_0_, bf16[40,512]{1,0:T(8,128)(2,1)S(1)} %collective-permute-done.1.refs_3_.refs_1_, bf16[40,512]{1,0:T(8,128)(2,1)S(1)} %collective-permute-done.2.refs_4_.refs_2_, ...), custom_call_target="tpu_custom_call" | custom-call | tf_op jit(solution)/shard_map/pallas_call | solution.py:643
  16.5 0.4 collective-permute-done.5.refs_1_
  16.9 1.8 %collective-permute-done.6.refs_2_ = bf16[4,8,2048]{2,1,0:T(8,128)(2,1)S(1)} collective-permute-done((bf16[4,8,2048]{2,1,0:T(8,128)(2,1)S(1)}, bf16[4,8,2048]{2,1,0:T(8,128)(2,1)S(1)}, u32[]{:S(2)}, u32[]{:S(2)}) %collective-permute-start.6) | collective-permute-done | bytes 131104 | tf_op jit(solution)/shard_map/ppermute | solution.py:21
  18.7 3.1 %collective-permute-done.7.refs_3_ = bf16[4,8,2048]{2,1,0:T(8,128)(2,1)S(1)} collective-permute-done((bf16[4,8,2048]{2,1,0:T(8,128)(2,1)S(1)}, bf16[4,8,2048]{2,1,0:T(8,128)(2,1)S(1)}, u32[]{:S(2)}, u32[]{:S(2)}) %collective-permute-start.7) | collective-permute-done | bytes 131104 | tf_op jit(solution)/shard_map/ppermute | solution.py:21
  21.8 0.7 %shard_map.95 = (bf16[8,32,256]{2,1,0:T(8,128)(2,1)S(1)}, bf16[8,32,256]{2,1,0:T(8,128)(2,1)S(1)}, bf16[1,8,24,256]{3,2,1,0:T(8,128)(2,1)S(1)}, f32[8,128]{1,0:T(8,128)}) custom-call(bf16[4,8,2048]{2,1,0:T(8,128)(2,1)S(1)} %get-tuple-element.40.refs_0_, bf16[4,8,2048]{2,1,0:T(8,128)(2,1)S(1)} %collective-permute-done.5.refs_1_, ...), custom_call_target="tpu_custom_call" | custom-call | tf_op jit(solution)/shard_map/pallas_call | solution.py:643
  22.5 1.2 %collective-permute-start.10 = (bf16[8,32,256]{2,1,0:T(8,128)(2,1)S(1)}, bf16[8,32,256]{2,1,0:T(8,128)(2,1)S(1)}, u32[]{:S(2)}, u32[]{:S(2)}) collective-permute-start(bf16[8,32,256]{2,1,0:T(8,128)(2,1)S(1)} %get-tuple-element.48), channel_id=1, source_target_pairs={{0,16},{8,24},{16,0},{24,8},{1,17},{9,25},{17,1},{25,9},{2,18},{10... | collective-permute-start | bytes 393224 | tf_op jit(solution)/shard_map/ppermute | solution.py:21
  23.6 1.8 %collective-permute-start.9 = (bf16[8,32,256]{2,1,0:T(8,128)(2,1)S(1)}, bf16[8,32,256]{2,1,0:T(8,128)(2,1)S(1)}, u32[]{:S(2)}, u32[]{:S(2)}) collective-permute-start(bf16[8,32,256]{2,1,0:T(8,128)(2,1)S(1)} %get-tuple-element.47.refs_0_.refs_4_), channel_id=1, source_target_pairs={{0,8},{8,0},{16,24},{24,16},{1,9},{9,1},{17,25},{25,17},{2,10},{10... | collective-permute-start | bytes 393224 | tf_op jit(solution)/shard_map/ppermute | solution.py:21
  25.5 2.2 %collective-permute-start.13 = (bf16[4,8,4,512]{3,2,1,0:T(4,128)(2,1)S(1)}, bf16[4,8,4,512]{3,2,1,0:T(4,128)(2,1)S(1)}, u32[]{:S(2)}, u32[]{:S(2)}) collective-permute-start(bf16[4,8,4,512]{3,2,1,0:T(4,128)(2,1)S(1)} %get-tuple-element.50), channel_id=1, source_target_pairs={{0,1},{1,0},{2,3},{3,2},{4,5},{5,4},{6,7},{7,6},{8,9},{9,8},{10,11... | collective-permute-start | bytes 393224 | tf_op jit(solution)/shard_map/ppermute | solution.py:21
  27.7 1.2 %collective-permute-done.10.refs_1_.refs_2_.refs_6_ = bf16[8,32,256]{2,1,0:T(8,128)(2,1)S(1)} collective-permute-done((bf16[8,32,256]{2,1,0:T(8,128)(2,1)S(1)}, bf16[8,32,256]{2,1,0:T(8,128)(2,1)S(1)}, u32[]{:S(2)}, u32[]{:S(2)}) %collective-permute-start.10) | collective-permute-done | bytes 131104 | tf_op jit(solution)/shard_map/ppermute | solution.py:21
  29.0 0.8 %collective-permute-start = (s32[4,4]{1,0:T(4,128)S(1)}, s32[4,4]{1,0:T(4,128)S(1)}, u32[]{:S(2)}, u32[]{:S(2)}) collective-permute-start(s32[4,4]{1,0:T(4,128)S(1)} %copy-done), channel_id=1, source_target_pairs={{0,4},{4,0},{1,5},{5,1},{2,6},{6,2},{3,7},{7,3},{8,12},{12,8},{9,1... | collective-permute-start | bytes 200 | tf_op jit(solution)/shard_map/ppermute | solution.py:21
  29.8 1.9 %collective-permute-done.refs_3_.refs_1_ = s32[4,4]{1,0:T(4,128)S(1)} collective-permute-done((s32[4,4]{1,0:T(4,128)S(1)}, s32[4,4]{1,0:T(4,128)S(1)}, u32[]{:S(2)}, u32[]{:S(2)}) %collective-permute-start) | collective-permute-done | bytes 96 | tf_op jit(solution)/shard_map/ppermute | solution.py:21
  31.7 1.1 %collective-permute-done.14.refs_5_.refs_6_ = bf16[4,8,4,512]{3,2,1,0:T(4,128)(2,1)S(1)} collective-permute-done((bf16[4,8,4,512]{3,2,1,0:T(4,128)(2,1)S(1)}, bf16[4,8,4,512]{3,2,1,0:T(4,128)(2,1)S(1)}, u32[]{:S(2)}, u32[]{:S(2)}) %collective-permute-start.14) | collective-permute-done | bytes 131104 | tf_op jit(solution)/shard_map/ppermute | solution.py:21
  32.8 0.3 collective-permute-done.11.refs_2_.refs_3_.refs_7_
  33.1 1.1 %collective-permute-start.15 = (bf16[3,8,24,256]{3,2,1,0:T(8,128)(2,1)S(1)}, bf16[3,8,24,256]{3,2,1,0:T(8,128)(2,1)S(1)}, u32[]{:S(2)}, u32[]{:S(2)}) collective-permute-start(bf16[3,8,24,256]{3,2,1,0:T(8,128)(2,1)S(1)} %get-tuple-element.52), channel_id=1, source_target_pairs={{0,4},{4,0},{1,5},{5,1},{2,6},{6,2},{3,7},{7,3},{8,12},{12,8},{9,1... | collective-permute-start | bytes 884744 | tf_op jit(solution)/shard_map/ppermute | solution.py:21
  34.2 0.4 collective-permute-start.12
  34.9 4.7 %collective-permute-start.16 = (bf16[4,8,4,4,256]{4,3,2,1,0:T(4,128)(2,1)S(1)}, bf16[4,8,4,4,256]{4,3,2,1,0:T(4,128)(2,1)S(1)}, u32[]{:S(2)}, u32[]{:S(2)}) collective-permute-start(bf16[4,8,4,4,256]{4,3,2,1,0:T(4,128)(2,1)S(1)} %get-tuple-element.54), channel_id=1, source_target_pairs={{0,1},{1,0},{2,3},{3,2},{4,5},{5,4},{6,7},{7,6},{8,9},{9,8},{10,11... | collective-permute-start | bytes 786440 | tf_op jit(solution)/shard_map/ppermute | solution.py:21
  39.6 2.1 %collective-permute-start.17 = (bf16[4,8,4,4,256]{4,3,2,1,0:T(4,128)(2,1)S(1)}, bf16[4,8,4,4,256]{4,3,2,1,0:T(4,128)(2,1)S(1)}, u32[]{:S(2)}, u32[]{:S(2)}) collective-permute-start(bf16[4,8,4,4,256]{4,3,2,1,0:T(4,128)(2,1)S(1)} %get-tuple-element.55), channel_id=1, source_target_pairs={{1,2},{2,1},{5,6},{6,5},{9,10},{10,9},{13,14},{14,13},{17,18},{18,... | collective-permute-start | bytes 786440 | tf_op jit(solution)/shard_map/ppermute | solution.py:28
  41.8 2.6 %shard_map.98 = (bf16[10,128,256]{2,1,0:T(8,128)(2,1)S(1)}, bf16[2,8,112,256]{3,2,1,0:T(8,128)(2,1)S(1)}, f32[8,128]{1,0:T(8,128)S(1)}) custom-call(f32[64,128]{1,0:T(8,128)S(1)} %get-tuple-element.39.num_ref.refs_2_, bf16[6,512,256]{2,1,0:T(8,128)(2,1)S(1)} %get-tuple-element.56.blocks_ref.refs_16_, bf16[40,512]{1,0:T(8,128)(2,1)S(1)} %get-tuple-element.35.refs_2_.refs_0_, ...), custom_call_target="tpu_custom_call" | custom-call | tf_op jit(solution)/shard_map/pallas_call | solution.py:643
  44.6 0.8 %collective-permute-start.18 = (bf16[4,8,3,4,256]{4,3,2,1,0:T(4,128)(2,1)S(1)}, bf16[4,8,3,4,256]{4,3,2,1,0:T(4,128)(2,1)S(1)}, u32[]{:S(2)}, u32[]{:S(2)}) collective-permute-start(bf16[4,8,3,4,256]{4,3,2,1,0:T(4,128)(2,1)S(1)} %get-tuple-element.59), channel_id=1, source_target_pairs={{0,1},{1,0},{2,3},{3,2},{4,5},{5,4},{6,7},{7,6},{8,9},{9,8},{10,11... | collective-permute-start | bytes 589832 | tf_op jit(solution)/shard_map/ppermute | solution.py:21
  45.3 2.7 %collective-permute-start.19 = (bf16[4,8,3,4,256]{4,3,2,1,0:T(4,128)(2,1)S(1)}, bf16[4,8,3,4,256]{4,3,2,1,0:T(4,128)(2,1)S(1)}, u32[]{:S(2)}, u32[]{:S(2)}) collective-permute-start(bf16[4,8,3,4,256]{4,3,2,1,0:T(4,128)(2,1)S(1)} %get-tuple-element.60), channel_id=1, source_target_pairs={{1,2},{2,1},{5,6},{6,5},{9,10},{10,9},{13,14},{14,13},{17,18},{18,... | collective-permute-start | bytes 589832 | tf_op jit(solution)/shard_map/ppermute | solution.py:28
  48.1 3.1 %shard_map.100 = (bf16[2,8,112,256]{3,2,1,0:T(8,128)(2,1)S(1)}, f32[8,128]{1,0:T(8,128)}) custom-call(f32[64,128]{1,0:T(8,128)S(1)} %get-tuple-element.39.num_ref.refs_2_, bf16[6,512,256]{2,1,0:T(8,128)(2,1)S(1)} %get-tuple-element.56.blocks_ref.refs_16_, bf16[10,128,256]{2,1,0:T(8,128)(2,1)S(1)} %get-tuple-element.62.frame_ref.refs_17_, ...), custom_call_target="tpu_custom_call" | custom-call | tf_op jit(solution)/shard_map/pallas_call | solution.py:643
  51.2 1.1 %collective-permute-done.19.refs_13_ = bf16[4,8,3,4,256]{4,3,2,1,0:T(4,128)(2,1)S(1)} collective-permute-done((bf16[4,8,3,4,256]{4,3,2,1,0:T(4,128)(2,1)S(1)}, bf16[4,8,3,4,256]{4,3,2,1,0:T(4,128)(2,1)S(1)}, u32[]{:S(2)}, u32[]{:S(2)}) %collective-permute-start.19) | collective-permute-done | bytes 196640 | tf_op jit(solution)/shard_map/ppermute | solution.py:28
  52.3 10.8 %shard_map.101 = f32[4,8,512]{2,1,0:T(8,128)} custom-call(f32[4,16]{1,0:T(4,128)} %table_ref.1, s32[4,4]{1,0:T(4,128)S(1)} %copy-done, s32[4,4]{1,0:T(4,128)S(1)} %collective-permute-done.refs_3_.refs_1_, f32[64,128]{1,0:T(8,128)S(1)} %get-tuple-element.39.num_ref.refs_2_, f32[4,8,512]{2,1,0:T(8,128)} %refs_3_.1, ...), custom_call_target="tpu_custom_call" | custom-call | tf_op jit(solution)/shard_map/pallas_call | solution.py:643
  (21 shorter events, 0.9 us)
Async XLA Ops:
  0.0 29.0 %copy-start = (s32[4,4]{1,0:T(4,128)S(1)}, s32[4,4]{1,0:T(4,128)}, u32[]{:S(2)}) copy-start(s32[4,4]{1,0:T(4,128)} %refs_0_.1) | copy-start | bytes 196
  2.3 9.0 %collective-permute-start.4 = (bf16[4,4,8,2048]{3,2,1,0:T(8,128)(2,1)S(1)}, bf16[4,4,8,2048]{3,2,1,0:T(8,128)(2,1)S(1)}, u32[]{:S(2)}, u32[]{:S(2)}) collective-permute-start(bf16[4,4,8,2048]{3,2,1,0:T(8,128)(2,1)S(1)} %get-tuple-element.37), channel_id=1, source_target_pairs={{0,1},{1,0},{2,3},{3,2},{4,5},{5,4},{6,7},{7,6},{8,9},{9,8},{10,11... | collective-permute-start | bytes 1572872 | tf_op jit(solution)/shard_map/ppermute | solution.py:21
  2.5 6.6 %collective-permute-start.3 = (bf16[40,512]{1,0:T(8,128)(2,1)S(1)}, bf16[40,512]{1,0:T(8,128)(2,1)S(1)}, u32[]{:S(2)}, u32[]{:S(2)}) collective-permute-start(bf16[40,512]{1,0:T(8,128)(2,1)S(1)} %get-tuple-element.35.refs_2_.refs_0_), channel_id=1, source_target_pairs={{0,24},{8,16},{16,8},{24,0},{1,25},{9,17},{17,9},{25,1},{2,26},{10... | collective-permute-start | bytes 122888 | tf_op jit(solution)/shard_map/ppermute | solution.py:21
  7.3 4.1 %collective-permute-start.2 = (bf16[40,512]{1,0:T(8,128)(2,1)S(1)}, bf16[40,512]{1,0:T(8,128)(2,1)S(1)}, u32[]{:S(2)}, u32[]{:S(2)}) collective-permute-start(bf16[40,512]{1,0:T(8,128)(2,1)S(1)} %get-tuple-element.35.refs_2_.refs_0_), channel_id=1, source_target_pairs={{0,16},{8,24},{16,0},{24,8},{1,17},{9,25},{17,1},{25,9},{2,18},{10... | collective-permute-start | bytes 122888 | tf_op jit(solution)/shard_map/ppermute | solution.py:21
  7.3 4.1 %collective-permute-start.1 = (bf16[40,512]{1,0:T(8,128)(2,1)S(1)}, bf16[40,512]{1,0:T(8,128)(2,1)S(1)}, u32[]{:S(2)}, u32[]{:S(2)}) collective-permute-start(bf16[40,512]{1,0:T(8,128)(2,1)S(1)} %get-tuple-element.35.refs_2_.refs_0_), channel_id=1, source_target_pairs={{0,8},{8,0},{16,24},{24,16},{1,9},{9,1},{17,25},{25,17},{2,10},{10... | collective-permute-start | bytes 122888 | tf_op jit(solution)/shard_map/ppermute | solution.py:21
  11.5 4.8 %collective-permute-start.8 = (bf16[4,32,512]{2,1,0:T(8,128)(2,1)S(1)}, bf16[4,32,512]{2,1,0:T(8,128)(2,1)S(1)}, u32[]{:S(2)}, u32[]{:S(2)}) collective-permute-start(bf16[4,32,512]{2,1,0:T(8,128)(2,1)S(1)} %get-tuple-element.44), channel_id=1, source_target_pairs={{0,4},{4,0},{1,5},{5,1},{2,6},{6,2},{3,7},{7,3},{8,12},{12,8},{9,1... | collective-permute-start | bytes 393224 | tf_op jit(solution)/shard_map/ppermute | solution.py:21
  12.8 4.1 %collective-permute-start.5 = (bf16[4,8,2048]{2,1,0:T(8,128)(2,1)S(1)}, bf16[4,8,2048]{2,1,0:T(8,128)(2,1)S(1)}, u32[]{:S(2)}, u32[]{:S(2)}) collective-permute-start(bf16[4,8,2048]{2,1,0:T(8,128)(2,1)S(1)} %get-tuple-element.41), channel_id=1, source_target_pairs={{0,2},{1,3},{2,0},{3,1},{4,6},{5,7},{6,4},{7,5},{8,10},{9,11},{10,... | collective-permute-start | bytes 393224 | tf_op jit(solution)/shard_map/ppermute | solution.py:21
  14.0 4.7 %collective-permute-start.6 = (bf16[4,8,2048]{2,1,0:T(8,128)(2,1)S(1)}, bf16[4,8,2048]{2,1,0:T(8,128)(2,1)S(1)}, u32[]{:S(2)}, u32[]{:S(2)}) collective-permute-start(bf16[4,8,2048]{2,1,0:T(8,128)(2,1)S(1)} %get-tuple-element.42), channel_id=1, source_target_pairs={{0,4},{1,5},{2,6},{3,7},{4,0},{5,1},{6,2},{7,3},{8,12},{9,13},{10,... | collective-permute-start | bytes 393224 | tf_op jit(solution)/shard_map/ppermute | solution.py:21
  14.3 7.5 %collective-permute-start.7 = (bf16[4,8,2048]{2,1,0:T(8,128)(2,1)S(1)}, bf16[4,8,2048]{2,1,0:T(8,128)(2,1)S(1)}, u32[]{:S(2)}, u32[]{:S(2)}) collective-permute-start(bf16[4,8,2048]{2,1,0:T(8,128)(2,1)S(1)} %get-tuple-element.43), channel_id=1, source_target_pairs={{0,6},{1,7},{2,4},{3,5},{4,2},{5,3},{6,0},{7,1},{8,14},{9,15},{10,... | collective-permute-start | bytes 393224 | tf_op jit(solution)/shard_map/ppermute | solution.py:21
  22.5 6.5 %collective-permute-start.10 = (bf16[8,32,256]{2,1,0:T(8,128)(2,1)S(1)}, bf16[8,32,256]{2,1,0:T(8,128)(2,1)S(1)}, u32[]{:S(2)}, u32[]{:S(2)}) collective-permute-start(bf16[8,32,256]{2,1,0:T(8,128)(2,1)S(1)} %get-tuple-element.48), channel_id=1, source_target_pairs={{0,16},{8,24},{16,0},{24,8},{1,17},{9,25},{17,1},{25,9},{2,18},{10... | collective-permute-start | bytes 393224 | tf_op jit(solution)/shard_map/ppermute | solution.py:21
  23.6 8.0 %collective-permute-start.9 = (bf16[8,32,256]{2,1,0:T(8,128)(2,1)S(1)}, bf16[8,32,256]{2,1,0:T(8,128)(2,1)S(1)}, u32[]{:S(2)}, u32[]{:S(2)}) collective-permute-start(bf16[8,32,256]{2,1,0:T(8,128)(2,1)S(1)} %get-tuple-element.47.refs_0_.refs_4_), channel_id=1, source_target_pairs={{0,8},{8,0},{16,24},{24,16},{1,9},{9,1},{17,25},{25,17},{2,10},{10... | collective-permute-start | bytes 393224 | tf_op jit(solution)/shard_map/ppermute | solution.py:21
  25.5 6.2 %collective-permute-start.13 = (bf16[4,8,4,512]{3,2,1,0:T(4,128)(2,1)S(1)}, bf16[4,8,4,512]{3,2,1,0:T(4,128)(2,1)S(1)}, u32[]{:S(2)}, u32[]{:S(2)}) collective-permute-start(bf16[4,8,4,512]{3,2,1,0:T(4,128)(2,1)S(1)} %get-tuple-element.50), channel_id=1, source_target_pairs={{0,1},{1,0},{2,3},{3,2},{4,5},{5,4},{6,7},{7,6},{8,9},{9,8},{10,11... | collective-permute-start | bytes 393224 | tf_op jit(solution)/shard_map/ppermute | solution.py:21
  27.7 5.1 %collective-permute-start.14 = (bf16[4,8,4,512]{3,2,1,0:T(4,128)(2,1)S(1)}, bf16[4,8,4,512]{3,2,1,0:T(4,128)(2,1)S(1)}, u32[]{:S(2)}, u32[]{:S(2)}) collective-permute-start(bf16[4,8,4,512]{3,2,1,0:T(4,128)(2,1)S(1)} %get-tuple-element.51), channel_id=1, source_target_pairs={{0,3},{1,2},{2,1},{3,0},{4,7},{5,6},{6,5},{7,4},{8,11},{9,10},{10,... | collective-permute-start | bytes 393224 | tf_op jit(solution)/shard_map/ppermute | solution.py:21
  28.9 4.2 %collective-permute-start.11 = (bf16[8,32,256]{2,1,0:T(8,128)(2,1)S(1)}, bf16[8,32,256]{2,1,0:T(8,128)(2,1)S(1)}, u32[]{:S(2)}, u32[]{:S(2)}) collective-permute-start(bf16[8,32,256]{2,1,0:T(8,128)(2,1)S(1)} %collective-permute-done.10.refs_1_.refs_2_.refs_6_), channel_id=1, source_target_pairs={{0,8},{8,0},{16,24},{24,16},{1,9},{9,1},{17,25},{25,17},{2,10},{10... | collective-permute-start | bytes 393224 | tf_op jit(solution)/shard_map/ppermute | solution.py:21
  29.0 2.7 %collective-permute-start = (s32[4,4]{1,0:T(4,128)S(1)}, s32[4,4]{1,0:T(4,128)S(1)}, u32[]{:S(2)}, u32[]{:S(2)}) collective-permute-start(s32[4,4]{1,0:T(4,128)S(1)} %copy-done), channel_id=1, source_target_pairs={{0,4},{4,0},{1,5},{5,1},{2,6},{6,2},{3,7},{7,3},{8,12},{12,8},{9,1... | collective-permute-start | bytes 200 | tf_op jit(solution)/shard_map/ppermute | solution.py:21
  33.1 11.3 %collective-permute-start.15 = (bf16[3,8,24,256]{3,2,1,0:T(8,128)(2,1)S(1)}, bf16[3,8,24,256]{3,2,1,0:T(8,128)(2,1)S(1)}, u32[]{:S(2)}, u32[]{:S(2)}) collective-permute-start(bf16[3,8,24,256]{3,2,1,0:T(8,128)(2,1)S(1)} %get-tuple-element.52), channel_id=1, source_target_pairs={{0,4},{4,0},{1,5},{5,1},{2,6},{6,2},{3,7},{7,3},{8,12},{12,8},{9,1... | collective-permute-start | bytes 884744 | tf_op jit(solution)/shard_map/ppermute | solution.py:21
  34.2 10.1 %collective-permute-start.12 = (bf16[1,8,24,256]{3,2,1,0:T(8,128)(2,1)S(1)}, bf16[1,8,24,256]{3,2,1,0:T(8,128)(2,1)S(1)}, u32[]{:S(2)}, u32[]{:S(2)}) collective-permute-start(bf16[1,8,24,256]{3,2,1,0:T(8,128)(2,1)S(1)} %get-tuple-element.49), channel_id=1, source_target_pairs={{0,4},{4,0},{1,5},{5,1},{2,6},{6,2},{3,7},{7,3},{8,12},{12,8},{9,1... | collective-permute-start | bytes 294920 | tf_op jit(solution)/shard_map/ppermute | solution.py:21
  34.9 16.3 %collective-permute-start.16 = (bf16[4,8,4,4,256]{4,3,2,1,0:T(4,128)(2,1)S(1)}, bf16[4,8,4,4,256]{4,3,2,1,0:T(4,128)(2,1)S(1)}, u32[]{:S(2)}, u32[]{:S(2)}) collective-permute-start(bf16[4,8,4,4,256]{4,3,2,1,0:T(4,128)(2,1)S(1)} %get-tuple-element.54), channel_id=1, source_target_pairs={{0,1},{1,0},{2,3},{3,2},{4,5},{5,4},{6,7},{7,6},{8,9},{9,8},{10,11... | collective-permute-start | bytes 786440 | tf_op jit(solution)/shard_map/ppermute | solution.py:21
  39.6 11.6 %collective-permute-start.17 = (bf16[4,8,4,4,256]{4,3,2,1,0:T(4,128)(2,1)S(1)}, bf16[4,8,4,4,256]{4,3,2,1,0:T(4,128)(2,1)S(1)}, u32[]{:S(2)}, u32[]{:S(2)}) collective-permute-start(bf16[4,8,4,4,256]{4,3,2,1,0:T(4,128)(2,1)S(1)} %get-tuple-element.55), channel_id=1, source_target_pairs={{1,2},{2,1},{5,6},{6,5},{9,10},{10,9},{13,14},{14,13},{17,18},{18,... | collective-permute-start | bytes 786440 | tf_op jit(solution)/shard_map/ppermute | solution.py:28
  44.6 6.6 %collective-permute-start.18 = (bf16[4,8,3,4,256]{4,3,2,1,0:T(4,128)(2,1)S(1)}, bf16[4,8,3,4,256]{4,3,2,1,0:T(4,128)(2,1)S(1)}, u32[]{:S(2)}, u32[]{:S(2)}) collective-permute-start(bf16[4,8,3,4,256]{4,3,2,1,0:T(4,128)(2,1)S(1)} %get-tuple-element.59), channel_id=1, source_target_pairs={{0,1},{1,0},{2,3},{3,2},{4,5},{5,4},{6,7},{7,6},{8,9},{9,8},{10,11... | collective-permute-start | bytes 589832 | tf_op jit(solution)/shard_map/ppermute | solution.py:21
  45.3 7.0 %collective-permute-start.19 = (bf16[4,8,3,4,256]{4,3,2,1,0:T(4,128)(2,1)S(1)}, bf16[4,8,3,4,256]{4,3,2,1,0:T(4,128)(2,1)S(1)}, u32[]{:S(2)}, u32[]{:S(2)}) collective-permute-start(bf16[4,8,3,4,256]{4,3,2,1,0:T(4,128)(2,1)S(1)} %get-tuple-element.60), channel_id=1, source_target_pairs={{1,2},{2,1},{5,6},{6,5},{9,10},{10,9},{13,14},{14,13},{17,18},{18,... | collective-permute-start | bytes 589832 | tf_op jit(solution)/shard_map/ppermute | solution.py:28

commit v8 on v7

--- a/solution.py
+++ b/solution.py
@@ -169,16 +169,23 @@
     return jnp.broadcast_to(column, (16, 128))
 
 
-def sum_kernel(pairs, parts, *refs):
-    even_ref, other_ref = refs[:2]
-    heard = refs[2:6]
-    sums, stacks, done_ref = refs[6 : 6 + pairs], refs[6 + pairs : -1], refs[-1]
+def sum_kernel(pairs, *refs):
+    even_ref, other_ref, own_ref, near_ref, _ = refs[:5]
+    sums, (pair_ref, done_ref) = refs[5 : 5 + pairs], refs[5 + pairs :]
     done_ref[...] = jnp.zeros(done_ref.shape, F32)
     for k in range(pairs):
         sums[k][...] = (even_ref[k].astype(F32) + other_ref[k].astype(F32)).astype(BF)
-    for rows, ref in zip(parts, stacks):
-        for v in range(4):
-            ref[v] = heard[v][rows, :]
+    pair_ref[0] = own_ref[...]
+    pair_ref[1] = near_ref[...]
+
+
+def views_of(first, second):
+    return [first.at[0], first.at[1], second.at[0], second.at[1]]
+
+
+def est_rows_kernel(rows, first, second, _, out_ref):
+    for v, ref in enumerate(views_of(first, second)):
+        out_ref[v] = ref[rows, :]
 
 
 def stack_kernel(rows, count, *refs):
@@ -188,12 +195,14 @@
         out_ref[v] = ref[..., rows, :]
 
 
-def edges_kernel(height, depth, sides, *refs):
+def edges_kernel(height, depth, sides, paired, *refs):
     out1, out2, done_ref = refs[-3:]
     done_ref[...] = jnp.zeros(done_ref.shape, F32)
     count = out1.shape[0]
     views = refs[:count] if depth else [None] * count
     fars = refs[count if depth else 0 : -4]
+    if paired:
+        views, fars = views_of(*refs[:2]), refs[2:-4]
     half = height // 2
     gy = lax.axis_index("gy")
     even = gy % 2 == 0
@@ -269,7 +278,7 @@
 
 
 def band_kernel(at, *refs):
-    heard, (out_ref, num_ref, done_ref) = refs[:4], refs[5:]
+    heard, (out_ref, num_ref, done_ref) = views_of(*refs[:2]), refs[3:]
     done_ref[...] = jnp.zeros(done_ref.shape, F32)
     for v in range(4):
         num_ref[v * 16 : (v + 1) * 16, :] = numbers_of(heard[v], at)
@@ -311,21 +320,28 @@
     return v + 2
 
 
+def spots(t, h):
+    return t + h, slice((1 - h) * (TILE // 2), (2 - h) * (TILE // 2))
+
+
+def zero_ends(ref):
+    half = TILE // 2
+    ref[0, :, :half] = jnp.zeros((ref.shape[1], half), BF)
+    ref[ref.shape[0] - 1, :, half:] = jnp.zeros((ref.shape[1], half), BF)
+
+
 def conv(src, first, tiles, rows, blocks, dst, step):
-    half = TILE // 2
     s = 0
     while s < tiles:
         n = min(step, tiles - s)
-        lhs = jnp.concatenate(
-            [
-                src[pl.ds(first + s + k, n), :, cut].reshape(n * rows, cut.stop - cut.start)
-                for k, cut in enumerate(
-                    (slice(half, TILE), slice(0, TILE), slice(0, half))
-                )
-            ],
-            axis=1,
-        )
-        out = jnp.dot(lhs, blocks, preferred_element_type=F32).astype(BF)
+        out = sum(
+            jnp.dot(
+                src[pl.ds(first + s + k, n)].reshape(n * rows, TILE),
+                blocks[k * TILE : (k + 1) * TILE, :],
+                preferred_element_type=F32,
+            )
+            for k in range(2)
+        ).astype(BF)
         dst[s : s + n] = out.reshape(n, rows, TILE)
         s += n
 
@@ -350,17 +366,16 @@
 
 
 def write_frame(frame, tiles, sides, *refs):
-    own_refs, refs = refs[:4], refs[4:]
+    own_refs, refs = views_of(*refs[:2]), refs[2:]
     side_refs = dict(zip(sides, refs[: len(sides)]))
     one_ref, two_ref, out_ref = refs[len(sides) :]
     view = lax.axis_index("view")
     even = lax.axis_index("gy") % 2 == 0
-    for e in (0, tiles + 1):
-        out_ref[e] = jnp.zeros(out_ref.shape[1:], BF)
+    zero_ends(out_ref)
     for v in range(4):
-        for s in range(tiles // 4):
-            t = (view ^ v) * (tiles // 4) + s + 1
-            cut = slice(s * TILE, (s + 1) * TILE)
+        for s in range(tiles // 4 * 2):
+            t, lanes = spots((view ^ v) * (tiles // 4) + s // 2, s % 2)
+            cut = slice(s * TILE // 2, (s + 1) * TILE // 2)
             for f in range(frame.size):
                 where, k = frame.source(f)
                 rows = slice(k * 8, (k + 1) * 8)
@@ -369,7 +384,7 @@
                 else:
                     own = side_refs[where][v, rows, cut]
                 n = frame.place(f, frame.depth)
-                out_ref[t, f * 16 : (f + 1) * 16, :] = jnp.concatenate(
+                out_ref[t, f * 16 : (f + 1) * 16, lanes] = jnp.concatenate(
                     [
                         own.astype(F32),
                         beside(even, one_ref[v, n, :, cut], two_ref[v, n, :, cut]),
@@ -380,8 +395,8 @@
 
 def start_kernel(frame, tiles, sides, views, num_ref, blocks_ref, *refs):
     count = len(sides)
-    out_ref, recip_ref, done_ref, c = refs[7 + count :]
-    write_frame(frame, tiles, sides, *refs[: 6 + count], out_ref)
+    out_ref, recip_ref, done_ref, c = refs[5 + count :]
+    write_frame(frame, tiles, sides, *refs[: 4 + count], out_ref)
     forward_views(frame, tiles, views, num_ref, blocks_ref, out_ref, recip_ref, c)
     done_ref[...] = jnp.zeros(done_ref.shape, F32)
 
@@ -395,7 +410,7 @@
     size = frame.size
     zs = frame.need(3)
     for at, v in enumerate(views):
-        conv(frame_ref, 0, tiles, size * 16, blocks_ref[forward_block(v)], c, 2)
+        conv(frame_ref, 0, tiles, size * 16, blocks_ref.at[forward_block(v)], c, 2)
 
         def divide(t, carry, v=v, at=at):
             from_t = t if v < 2 else tiles - 1 - t
@@ -412,7 +427,7 @@
                     ).astype(BF)
             return carry
 
-        lax.fori_loop(0, tiles, divide, 0)
+        lax.fori_loop(0, tiles, divide, 0, unroll=True)
 
 
 def main_kernel(frame, tiles, sides, table_ref, *refs):
@@ -481,10 +496,6 @@
         b = (measured(v + 2, t, z, cut) * recip_b).astype(BF).astype(F32)
         return (0.5 * (a + b)).astype(BF)
 
-    def zero_ends(ref):
-        for e in (0, ref.shape[0] - 1):
-            ref[e] = jnp.zeros(ref.shape[1:], BF)
-
     for ref in (m1, u2, m2):
         zero_ends(ref)
 
@@ -493,9 +504,10 @@
         def ratios(t, carry, v=v):
             for h in range(TILE // 128):
                 cut = slice(h * 128, (h + 1) * 128)
+                to, lanes = spots(t, h)
                 for n, z in enumerate(z3):
                     at = slice(n * 16, (n + 1) * 16)
-                    m1[t + 1, at, cut] = mix(
+                    m1[to, at, lanes] = mix(
                         v,
                         t,
                         z,
@@ -505,9 +517,9 @@
                     )
             return carry
 
-        lax.fori_loop(0, tiles, ratios, 0)
+        lax.fori_loop(0, tiles, ratios, 0, unroll=True)
         for w in (v, v + 2):
-            conv(m1, 0, tiles, m1.shape[1], blocks_ref[backward_block(w)], c[w], 2)
+            conv(m1, 0, tiles, m1.shape[1], blocks_ref.at[backward_block(w)], c[w], 2)
 
     def numerator(slices_of, zs):
         totals = {z: [None, None, None] for z in zs}
@@ -535,23 +547,24 @@
                     for n, z in enumerate(z3)
                 }
 
+            to, lanes = spots(t, h)
             totals = numerator(slices_of, z2)
             for n, z in enumerate(z2):
                 change = along_y(totals[z])
-                before = frame_ref[t + 1, z * 16 : (z + 1) * 16, cut].astype(F32)
-                u2[t + 1, n * 16 : (n + 1) * 16, cut] = (before * change).astype(BF)
+                before = frame_ref[to, z * 16 : (z + 1) * 16, lanes].astype(F32)
+                u2[to, n * 16 : (n + 1) * 16, lanes] = (before * change).astype(BF)
                 if z in z0:
                     k = z - frame.own
                     kept[t, k * 8 : (k + 1) * 8, cut] = change[:8]
         return carry
 
-    lax.fori_loop(0, tiles, update, 0)
+    lax.fori_loop(0, tiles, update, 0, unroll=True)
 
     rows1 = m2.shape[1]
     n2 = u2.shape[1]
     for v in range(2):
         for w in (v, v + 2):
-            conv(u2, 0, tiles, n2, blocks_ref[forward_block(w)], c[w].at[:, :n2, :], 2)
+            conv(u2, 0, tiles, n2, blocks_ref.at[forward_block(w)], c[w].at[:, :n2, :], 2)
 
         def ratios2(t, carry, v=v):
             for h in range(TILE // 128):
@@ -569,17 +582,18 @@
                     recips.append(
                         {z: 1.0 / (along_y(sums[z]) + num_ref[w * 16 + 9 : w * 16 + 10, :]) for z in z1}
                     )
+                to, lanes = spots(t, h)
                 for n, z in enumerate(z1):
-                    m2[t + 1, n * 16 : (n + 1) * 16, cut] = mix(
+                    m2[to, n * 16 : (n + 1) * 16, lanes] = mix(
                         v, t, z, cut, recips[0][z], recips[1][z]
                     )
             return carry
 
-        lax.fori_loop(0, tiles, ratios2, 0)
+        lax.fori_loop(0, tiles, ratios2, 0, unroll=True)
         mine = tiles // 4
         for w in (v, v + 2):
             first = view * mine if w < 2 else tiles - (view + 1) * mine
-            conv(m2, first, mine, rows1, blocks_ref[backward_block(w)], c[w].at[:, :rows1, :], 2)
+            conv(m2, first, mine, rows1, blocks_ref.at[backward_block(w)], c[w].at[:, :rows1, :], 2)
 
     mine = tiles // 4
     for s in range(mine):
@@ -675,25 +689,21 @@
         scratch=[vmem((blocks * depth, height, width), F32), vmem((8, chunk), F32)],
     )
     other = swap(odd, "gy", bands, 1)
-    heard = [payload] + [swap(payload, "view", 4, mask) for mask in (1, 2, 3)]
+    near_payload = swap(payload, "view", 4, 1)
     index_far = exchange_z(frame, lambda s: bleach_index[:, s.start : s.stop], slabs, depth)
-    est_slices = frame.sent(depth)
-    out = call(
-        functools.partial(
-            sum_kernel,
-            pairs,
-            [slice(s.start * height, s.stop * height) for s in est_slices.values()],
-        ),
+    *kept, pair, sums_done = call(
+        functools.partial(sum_kernel, pairs),
         (resident(depth, height, width),) * pairs
-        + tuple(resident(4, len(s) * height, chunk) for s in est_slices.values())
-        + (mark,),
-        [vmem] * 6,
-        [vmem] * (pairs + len(sides) + 1),
+        + (resident(2, area + 8, chunk), mark),
+        [vmem] * 4 + [free],
+        [vmem] * (pairs + 2),
         even,
         other,
-        *heard,
-    )
-    kept, est_stacks, sums_done = out[:pairs], out[pairs:-1], out[-1]
+        payload,
+        near_payload,
+        index_far[sides[0]],
+    )
+    heard = (pair, swap(pair, "view", 4, 2))
     moved = [swap(kept[k], ("gz", "gy"), blocks, 2 * k) for k in range(1, pairs)]
 
     def stack(arrays, slices, *tokens):
@@ -712,7 +722,11 @@
         out = resident(4, *dims[:-2], slices, height // 2, dims[-1])
         return call(
             functools.partial(
-                edges_kernel, height, depth if arrays else 0, len(sides)
+                edges_kernel,
+                height,
+                depth if arrays else 0,
+                len(sides),
+                len(arrays) == 2,
             ),
             (out, out, mark),
             [vmem] * (len(arrays) + len(fars)) + [free],
@@ -722,20 +736,15 @@
             token,
         )
 
-    stacks = dict(zip([(s.start, s.stop) for s in est_slices.values()], est_stacks))
-    far_est = exchange_z(frame, lambda s: stacks[s.start, s.stop], slabs, depth)
-    far_est = [far_est[s] for s in sides]
     table, nums, token = call(
         functools.partial(band_kernel, area),
         (resident(6, 2 * TILE, TILE), resident(64, 128, dtype=F32), mark),
-        [vmem] * 4 + [free],
+        [vmem] * 2 + [free],
         (vmem, vmem, vmem),
         *heard,
         sums_done,
     )
     kept_table, kept_nums = table, nums
-    est_edges = edges(heard, far_est, token, size, payload.shape)
-    one_est, two_est = core_side(est_edges, bands, True)
 
     far_slices = frame.sent(3)
     plain, turned, *own_far, total_done = call(
@@ -751,12 +760,28 @@
         [vmem] * (3 + len(sides)),
         kept[0],
         *moved,
-        est_edges[2],
+        token,
     )
     near = swap(plain, "view", 4, 1)
     opposite = swap(turned, "view", 4, 2)
     last = swap(opposite, "view", 4, 1)
     ready = dict(zip([(s.start, s.stop) for s in far_slices.values()], own_far))
+    def est_rows(slices):
+        return call(
+            functools.partial(
+                est_rows_kernel, slice(slices.start * height, slices.stop * height)
+            ),
+            resident(4, len(slices) * height, chunk),
+            [vmem] * 2 + [free],
+            (vmem,),
+            *heard,
+            total_done,
+        )
+
+    far_est = exchange_z(frame, est_rows, slabs, depth)
+    far_est = [far_est[s] for s in sides]
+    est_edges = edges(heard, far_est, total_done, size, payload.shape)
+    one_est, two_est = core_side(est_edges, bands, True)
     far_own = exchange_z(frame, lambda s: ready[s.start, s.stop], slabs, 3)
     far_own = [far_own[s] for s in sides]
     n3, n2, n1 = (len(frame.need(r)) * 16 for r in (3, 2, 1))
@@ -766,7 +791,7 @@
 
     def others(slices):
         rows, done = stack(
-            (near, opposite, last), slices, index_far[sides[0]], one_est, two_est
+            (near, opposite, last), slices, total_done, one_est, two_est
         )
         tokens.append(done)
         return rows
@@ -778,11 +803,11 @@
     est_frame, recip_a, token = call(
         functools.partial(start_kernel, frame, tiles, sides, (0, 1)),
         (
-            resident(tiles + 2, size * 16, TILE),
+            resident(tiles + 1, size * 16, TILE),
             resident(2, tiles, n3, TILE),
             mark,
         ),
-        [vmem] * (8 + len(sides)) + [free],
+        [vmem] * (6 + len(sides)) + [free],
         (vmem, vmem, vmem),
         kept_nums,
         kept_table,
@@ -831,9 +856,9 @@
         kept_table,
         est_frame,
         scratch=[
-            vmem((tiles + 2, n3, TILE), BF),
-            vmem((tiles + 2, n2, TILE), BF),
-            vmem((tiles + 2, n1, TILE), BF),
+            vmem((tiles + 1, n3, TILE), BF),
+            vmem((tiles + 1, n2, TILE), BF),
+            vmem((tiles + 1, n1, TILE), BF),
         ]
         + [vmem((tiles, n3, TILE), BF)] * 4
         + [vmem((tiles, area, TILE), F32), vmem((4 * size * 16, 128), F32)],

time: 63.3 us -> 62.3 us (0.984)
  Pallas kernels: 20.4 us -> 18.3 us
  starting transfers between devices: 27.1 us -> 28.6 us
    pallas_call x11 -> x12, Pallas kernels: 20.4 us -> 18.3 us  [call(): pl.pallas_call(kernel, out_shape=shapes, in_specs=whole(*ins), out_specs=...]
    ppermute x18 -> x17, starting transfers between devices: 22.2 us -> 24.2 us  [swap(): return lax.ppermute(array, axis, [(i, i ^ mask) for i in range(size)])]
    ppermute x18 -> x17, waiting for transfers between devices: 13.7 us -> 12.3 us  [swap(): return lax.ppermute(array, axis, [(i, i ^ mask) for i in range(size)])]
    ppermute x2, waiting for transfers between devices: 1.11 us -> 2.22 us  [core_side(): return (first, lax.ppermute(own[1], 'gy', [(1, 2), (2, 1)]))]
  transfers between devices with their start and end apart: 20 -> 19, of which waited for: 10 -> 7; matrix products, arithmetic and copies ran while one was open for 0% -> 0% of each run, Pallas kernels for 11% -> 11%
where the time goes in v8:
time: 62.3 us; the launch traced here: 62.1 us
  starting transfers between devices  28.6 us (46%)
  Pallas kernels  18.3 us (29%)
  waiting for transfers between devices  14.5 us (23%)
  between operations  0.79 us (1%)
    ppermute x17, starting transfers between devices, swap(): return lax.ppermute(array, axis, [(i, i ^ mask) for i in range(size)])  24.2 us
    pallas_call x12, Pallas kernels, call(): pl.pallas_call(kernel, out_shape=shapes, in_specs=whole(*ins), out_specs=...  18.3 us
    ppermute x17, waiting for transfers between devices, swap(): return lax.ppermute(array, axis, [(i, i ^ mask) for i in range(size)])  12.3 us
    ppermute x2, starting transfers between devices, core_side(): return (first, lax.ppermute(own[1], 'gy', [(1, 2), (2, 1)]))  4.38 us
    ppermute x2, waiting for transfers between devices, core_side(): return (first, lax.ppermute(own[1], 'gy', [(1, 2), (2, 1)]))  2.22 us
  transfers between devices with their start and end apart: 19, of which 7 were waited for; matrix products, arithmetic and copies ran while one was open for 0% of the time, Pallas kernels for 11%

profile of v8, /device:TPU:1, one launch (start us, length us, event | category | flops | bytes accessed | tf_op | source)
XLA Modules:
  0.0 62.1 jit_solution(18327010649342026888)
XLA Ops:
  0.7 1.7 %shard_map.91 = (bf16[4,4,8,2048]{3,2,1,0:T(8,128)(2,1)S(1)}, bf16[4,4,8,2048]{3,2,1,0:T(8,128)(2,1)S(1)}, bf16[40,512]{1,0:T(8,128)(2,1)S(1)}) custom-call(s32[1,1,16]{2,1,0:T(1,128)} %bitcast.5, s32[1,16]{1,0:T(1,128)} %row_ref.1, f32[1]{0:T(128)S(6)} %copy.10.bg_ref, bf16[16,8,2048]{2,1,0:T(8,128)(2,1)} %bitcast.3, f32[3,1,3]{2,1,0:T(1,128)} %bitcast.4, ...), custom_call_target="tpu_custom_call" | custom-call | tf_op jit(solution)/shard_map/pallas_call | solution.py:657
  2.5 2.8 %collective-permute-start.2 = (bf16[40,512]{1,0:T(8,128)(2,1)S(1)}, bf16[40,512]{1,0:T(8,128)(2,1)S(1)}, u32[]{:S(2)}, u32[]{:S(2)}) collective-permute-start(bf16[40,512]{1,0:T(8,128)(2,1)S(1)} %get-tuple-element.37.refs_2_), channel_id=1, source_target_pairs={{0,8},{8,0},{16,24},{24,16},{1,9},{9,1},{17,25},{25,17},{2,10},{10... | collective-permute-start | bytes 122888 | tf_op jit(solution)/shard_map/ppermute | solution.py:21
  5.2 1.2 %collective-permute-start = (s32[4,4]{1,0:T(4,128)}, s32[4,4]{1,0:T(4,128)S(1)}, u32[]{:S(2)}, u32[]{:S(2)}) collective-permute-start(s32[4,4]{1,0:T(4,128)} %refs_0_.1), channel_id=1, source_target_pairs={{0,4},{4,0},{1,5},{5,1},{2,6},{6,2},{3,7},{7,3},{8,12},{12,8},{9,1... | collective-permute-start | bytes 200 | tf_op jit(solution)/shard_map/ppermute | solution.py:21
  6.4 1.4 %collective-permute-done.refs_4_.refs_1_ = s32[4,4]{1,0:T(4,128)S(1)} collective-permute-done((s32[4,4]{1,0:T(4,128)}, s32[4,4]{1,0:T(4,128)S(1)}, u32[]{:S(2)}, u32[]{:S(2)}) %collective-permute-start) | collective-permute-done | bytes 96 | tf_op jit(solution)/shard_map/ppermute | solution.py:21
  8.0 1.3 %collective-permute-start.4 = (bf16[4,8,2048]{2,1,0:T(8,128)(2,1)S(1)}, bf16[4,8,2048]{2,1,0:T(8,128)(2,1)S(1)}, u32[]{:S(2)}, u32[]{:S(2)}) collective-permute-start(bf16[4,8,2048]{2,1,0:T(8,128)(2,1)S(1)} %get-tuple-element.42), channel_id=1, source_target_pairs={{0,2},{1,3},{2,0},{3,1},{4,6},{5,7},{6,4},{7,5},{8,10},{9,11},{10,... | collective-permute-start | bytes 393224 | tf_op jit(solution)/shard_map/ppermute | solution.py:21
  9.3 1.2 %collective-permute-start.5 = (bf16[4,8,2048]{2,1,0:T(8,128)(2,1)S(1)}, bf16[4,8,2048]{2,1,0:T(8,128)(2,1)S(1)}, u32[]{:S(2)}, u32[]{:S(2)}) collective-permute-start(bf16[4,8,2048]{2,1,0:T(8,128)(2,1)S(1)} %get-tuple-element.43), channel_id=1, source_target_pairs={{0,4},{1,5},{2,6},{3,7},{4,0},{5,1},{6,2},{7,3},{8,12},{9,13},{10,... | collective-permute-start | bytes 393224 | tf_op jit(solution)/shard_map/ppermute | solution.py:21
  10.5 0.2 collective-permute-start.6
  10.7 2.3 %collective-permute-start.3 = (bf16[2,40,512]{2,1,0:T(8,128)(2,1)S(1)}, bf16[2,40,512]{2,1,0:T(8,128)(2,1)S(1)}, u32[]{:S(2)}, u32[]{:S(2)}) collective-permute-start(bf16[2,40,512]{2,1,0:T(8,128)(2,1)S(1)} %get-tuple-element.38.refs_0_.first), channel_id=1, source_target_pairs={{0,16},{8,24},{16,0},{24,8},{1,17},{9,25},{17,1},{25,9},{2,18},{10... | collective-permute-start | bytes 245768 | tf_op jit(solution)/shard_map/ppermute | solution.py:21
  13.0 2.7 %collective-permute-done.3.refs_1_.second = bf16[2,40,512]{2,1,0:T(8,128)(2,1)S(1)} collective-permute-done((bf16[2,40,512]{2,1,0:T(8,128)(2,1)S(1)}, bf16[2,40,512]{2,1,0:T(8,128)(2,1)S(1)}, u32[]{:S(2)}, u32[]{:S(2)}) %collective-permute-start.3) | collective-permute-done | bytes 81952 | tf_op jit(solution)/shard_map/ppermute | solution.py:21
  15.7 0.9 %shard_map.93 = (bf16[6,512,256]{2,1,0:T(8,128)(2,1)S(1)}, f32[64,128]{1,0:T(8,128)S(1)}, f32[8,128]{1,0:T(8,128)S(1)}) custom-call(bf16[2,40,512]{2,1,0:T(8,128)(2,1)S(1)} %get-tuple-element.38.refs_0_.first, bf16[2,40,512]{2,1,0:T(8,128)(2,1)S(1)} %collective-permute-done.3.refs_1_.second, f32[8,128]{1,0:T(8,128)S(1)} %get-tuple-element.39.refs_2_), custom_call_target="tpu_custom_call" | custom-call | tf_op jit(solution)/shard_map/pallas_call | solution.py:657
  16.7 0.2 shard_map.94
  16.9 1.3 %collective-permute-start.11 = (bf16[4,32,512]{2,1,0:T(8,128)(2,1)S(1)}, bf16[4,32,512]{2,1,0:T(8,128)(2,1)S(1)}, u32[]{:S(2)}, u32[]{:S(2)}) collective-permute-start(bf16[4,32,512]{2,1,0:T(8,128)(2,1)S(1)} %shard_map.95), channel_id=1, source_target_pairs={{0,4},{4,0},{1,5},{5,1},{2,6},{6,2},{3,7},{7,3},{8,12},{12,8},{9,1... | collective-permute-start | bytes 393224 | tf_op jit(solution)/shard_map/ppermute | solution.py:21
  18.2 1.5 %collective-permute-start.8 = (bf16[8,32,256]{2,1,0:T(8,128)(2,1)S(1)}, bf16[8,32,256]{2,1,0:T(8,128)(2,1)S(1)}, u32[]{:S(2)}, u32[]{:S(2)}) collective-permute-start(bf16[8,32,256]{2,1,0:T(8,128)(2,1)S(1)} %get-tuple-element.47), channel_id=1, source_target_pairs={{0,16},{8,24},{16,0},{24,8},{1,17},{9,25},{17,1},{25,9},{2,18},{10... | collective-permute-start | bytes 393224 | tf_op jit(solution)/shard_map/ppermute | solution.py:21
  19.7 0.2 collective-permute-start.7
  19.9 0.9 %collective-permute-done.11.refs_2_ = bf16[4,32,512]{2,1,0:T(8,128)(2,1)S(1)} collective-permute-done((bf16[4,32,512]{2,1,0:T(8,128)(2,1)S(1)}, bf16[4,32,512]{2,1,0:T(8,128)(2,1)S(1)}, u32[]{:S(2)}, u32[]{:S(2)}) %collective-permute-start.11) | collective-permute-done | bytes 131104 | tf_op jit(solution)/shard_map/ppermute | solution.py:21
  20.8 0.6 shard_map.96
  21.4 4.4 %collective-permute-start.12 = (bf16[4,8,4,512]{3,2,1,0:T(4,128)(2,1)S(1)}, bf16[4,8,4,512]{3,2,1,0:T(4,128)(2,1)S(1)}, u32[]{:S(2)}, u32[]{:S(2)}) collective-permute-start(bf16[4,8,4,512]{3,2,1,0:T(4,128)(2,1)S(1)} %get-tuple-element.50), channel_id=1, source_target_pairs={{0,1},{1,0},{2,3},{3,2},{4,5},{5,4},{6,7},{7,6},{8,9},{9,8},{10,11... | collective-permute-start | bytes 393224 | tf_op jit(solution)/shard_map/ppermute | solution.py:21
  25.7 0.3 collective-permute-start.9
  26.1 3.5 %collective-permute-start.13 = (bf16[4,8,4,512]{3,2,1,0:T(4,128)(2,1)S(1)}, bf16[4,8,4,512]{3,2,1,0:T(4,128)(2,1)S(1)}, u32[]{:S(2)}, u32[]{:S(2)}) collective-permute-start(bf16[4,8,4,512]{3,2,1,0:T(4,128)(2,1)S(1)} %get-tuple-element.51), channel_id=1, source_target_pairs={{0,3},{1,2},{2,1},{3,0},{4,7},{5,6},{6,5},{7,4},{8,11},{9,10},{10,... | collective-permute-start | bytes 393224 | tf_op jit(solution)/shard_map/ppermute | solution.py:21
  29.6 0.9 %collective-permute-done.9.refs_2_.refs_3_.refs_7_ = bf16[8,32,256]{2,1,0:T(8,128)(2,1)S(1)} collective-permute-done((bf16[8,32,256]{2,1,0:T(8,128)(2,1)S(1)}, bf16[8,32,256]{2,1,0:T(8,128)(2,1)S(1)}, u32[]{:S(2)}, u32[]{:S(2)}) %collective-permute-start.9) | collective-permute-done | bytes 131104 | tf_op jit(solution)/shard_map/ppermute | solution.py:21
  30.5 3.3 %collective-permute-done.13.refs_5_.refs_4_ = bf16[4,8,4,512]{3,2,1,0:T(4,128)(2,1)S(1)} collective-permute-done((bf16[4,8,4,512]{3,2,1,0:T(4,128)(2,1)S(1)}, bf16[4,8,4,512]{3,2,1,0:T(4,128)(2,1)S(1)}, u32[]{:S(2)}, u32[]{:S(2)}) %collective-permute-start.13) | collective-permute-done | bytes 131104 | tf_op jit(solution)/shard_map/ppermute | solution.py:21
  33.9 1.5 %collective-permute-start.10 = (bf16[1,8,24,256]{3,2,1,0:T(8,128)(2,1)S(1)}, bf16[1,8,24,256]{3,2,1,0:T(8,128)(2,1)S(1)}, u32[]{:S(2)}, u32[]{:S(2)}) collective-permute-start(bf16[1,8,24,256]{3,2,1,0:T(8,128)(2,1)S(1)} %get-tuple-element.48), channel_id=1, source_target_pairs={{0,4},{4,0},{1,5},{5,1},{2,6},{6,2},{3,7},{7,3},{8,12},{12,8},{9,1... | collective-permute-start | bytes 294920 | tf_op jit(solution)/shard_map/ppermute | solution.py:21
  35.4 0.2 shard_map.98
  35.6 1.0 %collective-permute-start.15 = (bf16[4,8,4,4,256]{4,3,2,1,0:T(4,128)(2,1)S(1)}, bf16[4,8,4,4,256]{4,3,2,1,0:T(4,128)(2,1)S(1)}, u32[]{:S(2)}, u32[]{:S(2)}) collective-permute-start(bf16[4,8,4,4,256]{4,3,2,1,0:T(4,128)(2,1)S(1)} %get-tuple-element.54), channel_id=1, source_target_pairs={{0,1},{1,0},{2,3},{3,2},{4,5},{5,4},{6,7},{7,6},{8,9},{9,8},{10,11... | collective-permute-start | bytes 786440 | tf_op jit(solution)/shard_map/ppermute | solution.py:21
  36.6 2.3 %collective-permute-start.16 = (bf16[4,8,4,4,256]{4,3,2,1,0:T(4,128)(2,1)S(1)}, bf16[4,8,4,4,256]{4,3,2,1,0:T(4,128)(2,1)S(1)}, u32[]{:S(2)}, u32[]{:S(2)}) collective-permute-start(bf16[4,8,4,4,256]{4,3,2,1,0:T(4,128)(2,1)S(1)} %get-tuple-element.55), channel_id=1, source_target_pairs={{1,2},{2,1},{5,6},{6,5},{9,10},{10,9},{13,14},{14,13},{17,18},{18,... | collective-permute-start | bytes 786440 | tf_op jit(solution)/shard_map/ppermute | solution.py:28
  38.9 2.2 %shard_map.99 = (bf16[9,128,256]{2,1,0:T(8,128)(2,1)S(1)}, bf16[2,8,112,256]{3,2,1,0:T(8,128)(2,1)S(1)}, f32[8,128]{1,0:T(8,128)S(1)}) custom-call(f32[64,128]{1,0:T(8,128)S(1)} %get-tuple-element.40.num_ref.refs_2_, bf16[6,512,256]{2,1,0:T(8,128)(2,1)S(1)} %get-tuple-element.56.blocks_ref.refs_16_, bf16[2,40,512]{2,1,0:T(8,128)(2,1)S(1)} %get-tuple-element.38.refs_0_.first, ...), custom_call_target="tpu_custom_call" | custom-call | tf_op jit(solution)/shard_map/pallas_call | solution.py:657
  41.2 3.1 %collective-permute-done.10.refs_0_.refs_8_ = bf16[1,8,24,256]{3,2,1,0:T(8,128)(2,1)S(1)} collective-permute-done((bf16[1,8,24,256]{3,2,1,0:T(8,128)(2,1)S(1)}, bf16[1,8,24,256]{3,2,1,0:T(8,128)(2,1)S(1)}, u32[]{:S(2)}, u32[]{:S(2)}) %collective-permute-start.10) | collective-permute-done | bytes 98336 | tf_op jit(solution)/shard_map/ppermute | solution.py:21
  44.4 1.3 %collective-permute-start.17 = (bf16[4,8,3,4,256]{4,3,2,1,0:T(4,128)(2,1)S(1)}, bf16[4,8,3,4,256]{4,3,2,1,0:T(4,128)(2,1)S(1)}, u32[]{:S(2)}, u32[]{:S(2)}) collective-permute-start(bf16[4,8,3,4,256]{4,3,2,1,0:T(4,128)(2,1)S(1)} %get-tuple-element.59), channel_id=1, source_target_pairs={{0,1},{1,0},{2,3},{3,2},{4,5},{5,4},{6,7},{7,6},{8,9},{9,8},{10,11... | collective-permute-start | bytes 589832 | tf_op jit(solution)/shard_map/ppermute | solution.py:21
  45.7 2.1 %collective-permute-start.18 = (bf16[4,8,3,4,256]{4,3,2,1,0:T(4,128)(2,1)S(1)}, bf16[4,8,3,4,256]{4,3,2,1,0:T(4,128)(2,1)S(1)}, u32[]{:S(2)}, u32[]{:S(2)}) collective-permute-start(bf16[4,8,3,4,256]{4,3,2,1,0:T(4,128)(2,1)S(1)} %get-tuple-element.60), channel_id=1, source_target_pairs={{1,2},{2,1},{5,6},{6,5},{9,10},{10,9},{13,14},{14,13},{17,18},{18,... | collective-permute-start | bytes 589832 | tf_op jit(solution)/shard_map/ppermute | solution.py:28
  47.8 2.7 %shard_map.101 = (bf16[2,8,112,256]{3,2,1,0:T(8,128)(2,1)S(1)}, f32[8,128]{1,0:T(8,128)}) custom-call(f32[64,128]{1,0:T(8,128)S(1)} %get-tuple-element.40.num_ref.refs_2_, bf16[6,512,256]{2,1,0:T(8,128)(2,1)S(1)} %get-tuple-element.56.blocks_ref.refs_16_, bf16[9,128,256]{2,1,0:T(8,128)(2,1)S(1)} %get-tuple-element.62.frame_ref.refs_17_, ...), custom_call_target="tpu_custom_call" | custom-call | tf_op jit(solution)/shard_map/pallas_call | solution.py:657
  50.4 2.2 %collective-permute-done.18.refs_13_ = bf16[4,8,3,4,256]{4,3,2,1,0:T(4,128)(2,1)S(1)} collective-permute-done((bf16[4,8,3,4,256]{4,3,2,1,0:T(4,128)(2,1)S(1)}, bf16[4,8,3,4,256]{4,3,2,1,0:T(4,128)(2,1)S(1)}, u32[]{:S(2)}, u32[]{:S(2)}) %collective-permute-start.18) | collective-permute-done | bytes 196640 | tf_op jit(solution)/shard_map/ppermute | solution.py:28
  52.7 9.5 %shard_map.102 = f32[4,8,512]{2,1,0:T(8,128)} custom-call(f32[4,16]{1,0:T(4,128)} %table_ref.1, s32[4,4]{1,0:T(4,128)S(1)} %copy-done, s32[4,4]{1,0:T(4,128)S(1)} %collective-permute-done.refs_4_.refs_1_, f32[64,128]{1,0:T(8,128)S(1)} %get-tuple-element.40.num_ref.refs_2_, f32[4,8,512]{2,1,0:T(8,128)} %refs_3_.1, ...), custom_call_target="tpu_custom_call" | custom-call | tf_op jit(solution)/shard_map/pallas_call | solution.py:657
  (20 shorter events, 0.6 us)
Async XLA Ops:
  2.3 5.5 %collective-permute-start.1 = (bf16[4,4,8,2048]{3,2,1,0:T(8,128)(2,1)S(1)}, bf16[4,4,8,2048]{3,2,1,0:T(8,128)(2,1)S(1)}, u32[]{:S(2)}, u32[]{:S(2)}) collective-permute-start(bf16[4,4,8,2048]{3,2,1,0:T(8,128)(2,1)S(1)} %get-tuple-element.36), channel_id=1, source_target_pairs={{0,1},{1,0},{2,3},{3,2},{4,5},{5,4},{6,7},{7,6},{8,9},{9,8},{10,11... | collective-permute-start | bytes 1572872 | tf_op jit(solution)/shard_map/ppermute | solution.py:21
  2.5 5.4 %collective-permute-start.2 = (bf16[40,512]{1,0:T(8,128)(2,1)S(1)}, bf16[40,512]{1,0:T(8,128)(2,1)S(1)}, u32[]{:S(2)}, u32[]{:S(2)}) collective-permute-start(bf16[40,512]{1,0:T(8,128)(2,1)S(1)} %get-tuple-element.37.refs_2_), channel_id=1, source_target_pairs={{0,8},{8,0},{16,24},{24,16},{1,9},{9,1},{17,25},{25,17},{2,10},{10... | collective-permute-start | bytes 122888 | tf_op jit(solution)/shard_map/ppermute | solution.py:21
  5.2 2.6 %collective-permute-start = (s32[4,4]{1,0:T(4,128)}, s32[4,4]{1,0:T(4,128)S(1)}, u32[]{:S(2)}, u32[]{:S(2)}) collective-permute-start(s32[4,4]{1,0:T(4,128)} %refs_0_.1), channel_id=1, source_target_pairs={{0,4},{4,0},{1,5},{5,1},{2,6},{6,2},{3,7},{7,3},{8,12},{12,8},{9,1... | collective-permute-start | bytes 200 | tf_op jit(solution)/shard_map/ppermute | solution.py:21
  8.0 8.6 %collective-permute-start.4 = (bf16[4,8,2048]{2,1,0:T(8,128)(2,1)S(1)}, bf16[4,8,2048]{2,1,0:T(8,128)(2,1)S(1)}, u32[]{:S(2)}, u32[]{:S(2)}) collective-permute-start(bf16[4,8,2048]{2,1,0:T(8,128)(2,1)S(1)} %get-tuple-element.42), channel_id=1, source_target_pairs={{0,2},{1,3},{2,0},{3,1},{4,6},{5,7},{6,4},{7,5},{8,10},{9,11},{10,... | collective-permute-start | bytes 393224 | tf_op jit(solution)/shard_map/ppermute | solution.py:21
  9.3 7.3 %collective-permute-start.5 = (bf16[4,8,2048]{2,1,0:T(8,128)(2,1)S(1)}, bf16[4,8,2048]{2,1,0:T(8,128)(2,1)S(1)}, u32[]{:S(2)}, u32[]{:S(2)}) collective-permute-start(bf16[4,8,2048]{2,1,0:T(8,128)(2,1)S(1)} %get-tuple-element.43), channel_id=1, source_target_pairs={{0,4},{1,5},{2,6},{3,7},{4,0},{5,1},{6,2},{7,3},{8,12},{9,13},{10,... | collective-permute-start | bytes 393224 | tf_op jit(solution)/shard_map/ppermute | solution.py:21
  10.5 6.1 %collective-permute-start.6 = (bf16[4,8,2048]{2,1,0:T(8,128)(2,1)S(1)}, bf16[4,8,2048]{2,1,0:T(8,128)(2,1)S(1)}, u32[]{:S(2)}, u32[]{:S(2)}) collective-permute-start(bf16[4,8,2048]{2,1,0:T(8,128)(2,1)S(1)} %get-tuple-element.44), channel_id=1, source_target_pairs={{0,6},{1,7},{2,4},{3,5},{4,2},{5,3},{6,0},{7,1},{8,14},{9,15},{10,... | collective-permute-start | bytes 393224 | tf_op jit(solution)/shard_map/ppermute | solution.py:21
  10.7 5.0 %collective-permute-start.3 = (bf16[2,40,512]{2,1,0:T(8,128)(2,1)S(1)}, bf16[2,40,512]{2,1,0:T(8,128)(2,1)S(1)}, u32[]{:S(2)}, u32[]{:S(2)}) collective-permute-start(bf16[2,40,512]{2,1,0:T(8,128)(2,1)S(1)} %get-tuple-element.38.refs_0_.first), channel_id=1, source_target_pairs={{0,16},{8,24},{16,0},{24,8},{1,17},{9,25},{17,1},{25,9},{2,18},{10... | collective-permute-start | bytes 245768 | tf_op jit(solution)/shard_map/ppermute | solution.py:21
  16.9 3.9 %collective-permute-start.11 = (bf16[4,32,512]{2,1,0:T(8,128)(2,1)S(1)}, bf16[4,32,512]{2,1,0:T(8,128)(2,1)S(1)}, u32[]{:S(2)}, u32[]{:S(2)}) collective-permute-start(bf16[4,32,512]{2,1,0:T(8,128)(2,1)S(1)} %shard_map.95), channel_id=1, source_target_pairs={{0,4},{4,0},{1,5},{5,1},{2,6},{6,2},{3,7},{7,3},{8,12},{12,8},{9,1... | collective-permute-start | bytes 393224 | tf_op jit(solution)/shard_map/ppermute | solution.py:21
  18.2 7.6 %collective-permute-start.8 = (bf16[8,32,256]{2,1,0:T(8,128)(2,1)S(1)}, bf16[8,32,256]{2,1,0:T(8,128)(2,1)S(1)}, u32[]{:S(2)}, u32[]{:S(2)}) collective-permute-start(bf16[8,32,256]{2,1,0:T(8,128)(2,1)S(1)} %get-tuple-element.47), channel_id=1, source_target_pairs={{0,16},{8,24},{16,0},{24,8},{1,17},{9,25},{17,1},{25,9},{2,18},{10... | collective-permute-start | bytes 393224 | tf_op jit(solution)/shard_map/ppermute | solution.py:21
  19.7 9.9 %collective-permute-start.7 = (bf16[8,32,256]{2,1,0:T(8,128)(2,1)S(1)}, bf16[8,32,256]{2,1,0:T(8,128)(2,1)S(1)}, u32[]{:S(2)}, u32[]{:S(2)}) collective-permute-start(bf16[8,32,256]{2,1,0:T(8,128)(2,1)S(1)} %get-tuple-element.46.refs_0_.refs_4_), channel_id=1, source_target_pairs={{0,8},{8,0},{16,24},{24,16},{1,9},{9,1},{17,25},{25,17},{2,10},{10... | collective-permute-start | bytes 393224 | tf_op jit(solution)/shard_map/ppermute | solution.py:21
  21.4 9.1 %collective-permute-start.12 = (bf16[4,8,4,512]{3,2,1,0:T(4,128)(2,1)S(1)}, bf16[4,8,4,512]{3,2,1,0:T(4,128)(2,1)S(1)}, u32[]{:S(2)}, u32[]{:S(2)}) collective-permute-start(bf16[4,8,4,512]{3,2,1,0:T(4,128)(2,1)S(1)} %get-tuple-element.50), channel_id=1, source_target_pairs={{0,1},{1,0},{2,3},{3,2},{4,5},{5,4},{6,7},{7,6},{8,9},{9,8},{10,11... | collective-permute-start | bytes 393224 | tf_op jit(solution)/shard_map/ppermute | solution.py:21
  25.7 4.8 %collective-permute-start.9 = (bf16[8,32,256]{2,1,0:T(8,128)(2,1)S(1)}, bf16[8,32,256]{2,1,0:T(8,128)(2,1)S(1)}, u32[]{:S(2)}, u32[]{:S(2)}) collective-permute-start(bf16[8,32,256]{2,1,0:T(8,128)(2,1)S(1)} %collective-permute-done.8.refs_1_.refs_2_.refs_6_), channel_id=1, source_target_pairs={{0,8},{8,0},{16,24},{24,16},{1,9},{9,1},{17,25},{25,17},{2,10},{10... | collective-permute-start | bytes 393224 | tf_op jit(solution)/shard_map/ppermute | solution.py:21
  26.1 7.7 %collective-permute-start.13 = (bf16[4,8,4,512]{3,2,1,0:T(4,128)(2,1)S(1)}, bf16[4,8,4,512]{3,2,1,0:T(4,128)(2,1)S(1)}, u32[]{:S(2)}, u32[]{:S(2)}) collective-permute-start(bf16[4,8,4,512]{3,2,1,0:T(4,128)(2,1)S(1)} %get-tuple-element.51), channel_id=1, source_target_pairs={{0,3},{1,2},{2,1},{3,0},{4,7},{5,6},{6,5},{7,4},{8,11},{9,10},{10,... | collective-permute-start | bytes 393224 | tf_op jit(solution)/shard_map/ppermute | solution.py:21
  33.8 10.4 %collective-permute-start.14 = (bf16[3,8,24,256]{3,2,1,0:T(8,128)(2,1)S(1)}, bf16[3,8,24,256]{3,2,1,0:T(8,128)(2,1)S(1)}, u32[]{:S(2)}, u32[]{:S(2)}) collective-permute-start(bf16[3,8,24,256]{3,2,1,0:T(8,128)(2,1)S(1)} %get-tuple-element.52), channel_id=1, source_target_pairs={{0,4},{4,0},{1,5},{5,1},{2,6},{6,2},{3,7},{7,3},{8,12},{12,8},{9,1... | collective-permute-start | bytes 884744 | tf_op jit(solution)/shard_map/ppermute | solution.py:21
  33.9 10.3 %collective-permute-start.10 = (bf16[1,8,24,256]{3,2,1,0:T(8,128)(2,1)S(1)}, bf16[1,8,24,256]{3,2,1,0:T(8,128)(2,1)S(1)}, u32[]{:S(2)}, u32[]{:S(2)}) collective-permute-start(bf16[1,8,24,256]{3,2,1,0:T(8,128)(2,1)S(1)} %get-tuple-element.48), channel_id=1, source_target_pairs={{0,4},{4,0},{1,5},{5,1},{2,6},{6,2},{3,7},{7,3},{8,12},{12,8},{9,1... | collective-permute-start | bytes 294920 | tf_op jit(solution)/shard_map/ppermute | solution.py:21
  35.6 14.8 %collective-permute-start.15 = (bf16[4,8,4,4,256]{4,3,2,1,0:T(4,128)(2,1)S(1)}, bf16[4,8,4,4,256]{4,3,2,1,0:T(4,128)(2,1)S(1)}, u32[]{:S(2)}, u32[]{:S(2)}) collective-permute-start(bf16[4,8,4,4,256]{4,3,2,1,0:T(4,128)(2,1)S(1)} %get-tuple-element.54), channel_id=1, source_target_pairs={{0,1},{1,0},{2,3},{3,2},{4,5},{5,4},{6,7},{7,6},{8,9},{9,8},{10,11... | collective-permute-start | bytes 786440 | tf_op jit(solution)/shard_map/ppermute | solution.py:21
  36.6 13.8 %collective-permute-start.16 = (bf16[4,8,4,4,256]{4,3,2,1,0:T(4,128)(2,1)S(1)}, bf16[4,8,4,4,256]{4,3,2,1,0:T(4,128)(2,1)S(1)}, u32[]{:S(2)}, u32[]{:S(2)}) collective-permute-start(bf16[4,8,4,4,256]{4,3,2,1,0:T(4,128)(2,1)S(1)} %get-tuple-element.55), channel_id=1, source_target_pairs={{1,2},{2,1},{5,6},{6,5},{9,10},{10,9},{13,14},{14,13},{17,18},{18,... | collective-permute-start | bytes 786440 | tf_op jit(solution)/shard_map/ppermute | solution.py:28
  41.1 11.5 %copy-start = (s32[4,4]{1,0:T(4,128)S(1)}, s32[4,4]{1,0:T(4,128)}, u32[]{:S(2)}) copy-start(s32[4,4]{1,0:T(4,128)} %refs_0_.1) | copy-start | bytes 196
  44.4 6.1 %collective-permute-start.17 = (bf16[4,8,3,4,256]{4,3,2,1,0:T(4,128)(2,1)S(1)}, bf16[4,8,3,4,256]{4,3,2,1,0:T(4,128)(2,1)S(1)}, u32[]{:S(2)}, u32[]{:S(2)}) collective-permute-start(bf16[4,8,3,4,256]{4,3,2,1,0:T(4,128)(2,1)S(1)} %get-tuple-element.59), channel_id=1, source_target_pairs={{0,1},{1,0},{2,3},{3,2},{4,5},{5,4},{6,7},{7,6},{8,9},{9,8},{10,11... | collective-permute-start | bytes 589832 | tf_op jit(solution)/shard_map/ppermute | solution.py:21
  45.7 7.0 %collective-permute-start.18 = (bf16[4,8,3,4,256]{4,3,2,1,0:T(4,128)(2,1)S(1)}, bf16[4,8,3,4,256]{4,3,2,1,0:T(4,128)(2,1)S(1)}, u32[]{:S(2)}, u32[]{:S(2)}) collective-permute-start(bf16[4,8,3,4,256]{4,3,2,1,0:T(4,128)(2,1)S(1)} %get-tuple-element.60), channel_id=1, source_target_pairs={{1,2},{2,1},{5,6},{6,5},{9,10},{10,9},{13,14},{14,13},{17,18},{18,... | collective-permute-start | bytes 589832 | tf_op jit(solution)/shard_map/ppermute | solution.py:28

commit v9 on v8

--- a/solution.py
+++ b/solution.py
@@ -97,6 +97,7 @@
     owner_ref,
     row_ref,
     bg_ref,
+    index_ref,
     pieces_ref,
     taps_ref,
     est_ref,
@@ -107,7 +108,7 @@
     acc,
     tail,
 ):
-    write_payload(mirrored, bg_ref, taps_ref, est_ref, psf_ref, payload_ref, tail)
+    write_payload(mirrored, bg_ref, index_ref, taps_ref, est_ref, psf_ref, payload_ref, tail)
     count = pieces_ref.shape[0]
     depth = even_ref.shape[1]
     me = lax.axis_index("gz") * bands + lax.axis_index("gy")
@@ -138,7 +139,7 @@
     lax.fori_loop(0, pairs, put, 0)
 
 
-def write_payload(mirrored, bg_ref, taps_ref, est_ref, psf_ref, out_ref, tail):
+def write_payload(mirrored, bg_ref, index_ref, taps_ref, est_ref, psf_ref, out_ref, tail):
     depth, height = est_ref.shape[:2]
     upside = lax.axis_index("gz") if mirrored else 0
     for k in range(depth):
@@ -154,8 +155,27 @@
         part = exact.astype(BF).astype(F32)
         tail[n + 1 : n + 2, :128] = part
         exact = exact - part
+    levels = jnp.zeros((1, 128), F32)
+    for v in range(4):
+        for k in range(depth):
+            level = jnp.full((1, 128), index_ref[v, k], jnp.int32).astype(F32)
+            levels = jnp.where(lanes == v * depth + k, level, levels)
+    tail[4:5, :128] = levels
     tail[0:1, : psf_ref.shape[1]] = psf_ref[...]
     out_ref[depth * height :, :] = tail[...].astype(BF)
+
+
+def bleach_weights(rows, table):
+    wide = jnp.broadcast_to(rows[4:5], (16, 128))
+    down = lax.broadcasted_iota(jnp.int32, (16, 128), 0)
+    across = lax.broadcasted_iota(jnp.int32, (16, 128), 1)
+    level = jnp.sum(jnp.where(down == across, wide, 0.0), axis=1, keepdims=True)
+    listed = jnp.broadcast_to(table[0:1], (16, 128))
+    for v in range(1, 4):
+        listed = jnp.where(down // 4 == v, jnp.broadcast_to(table[v : v + 1], (16, 128)), listed)
+    hit = across.astype(F32) == level
+    weight = jnp.sum(jnp.where(hit, listed, 0.0), axis=1, keepdims=True)
+    return jnp.broadcast_to(weight, (16, 128))
 
 
 def numbers_of(heard, at):
@@ -170,8 +190,8 @@
 
 
 def sum_kernel(pairs, *refs):
-    even_ref, other_ref, own_ref, near_ref, _ = refs[:5]
-    sums, (pair_ref, done_ref) = refs[5 : 5 + pairs], refs[5 + pairs :]
+    even_ref, other_ref, own_ref, near_ref = refs[:4]
+    sums, (pair_ref, done_ref) = refs[4 : 4 + pairs], refs[4 + pairs :]
     done_ref[...] = jnp.zeros(done_ref.shape, F32)
     for k in range(pairs):
         sums[k][...] = (even_ref[k].astype(F32) + other_ref[k].astype(F32)).astype(BF)
@@ -183,9 +203,9 @@
     return [first.at[0], first.at[1], second.at[0], second.at[1]]
 
 
-def est_rows_kernel(rows, first, second, _, out_ref):
+def est_rows_kernel(first, second, _, out_ref):
     for v, ref in enumerate(views_of(first, second)):
-        out_ref[v] = ref[rows, :]
+        out_ref[v] = ref[...]
 
 
 def stack_kernel(rows, count, *refs):
@@ -227,7 +247,7 @@
         sources = [(depth, own)] if depth else []
         if fars:
             sources += [
-                (fars[side].shape[-2] // height, far_of(v, side)) for side in range(sides)
+                (min(4, fars[side].shape[-2] // height), far_of(v, side)) for side in range(sides)
             ]
         for number, source in sources:
             for k in range(number):
@@ -430,7 +450,7 @@
         lax.fori_loop(0, tiles, divide, 0, unroll=True)
 
 
-def main_kernel(frame, tiles, sides, table_ref, *refs):
+def main_kernel(frame, tiles, sides, at, table_ref, *refs):
     count = len(sides)
     index_refs, refs = refs[: count + 1], refs[count + 1 :]
     num_ref, est_ref, refs = refs[0], refs[1], refs[2:]
@@ -439,7 +459,7 @@
     near_refs, beyond_refs = refs[:2], refs[2:4]
     recip_refs = refs[4:6]
     blocks_ref, frame_ref, out_ref = refs[6:9]
-    m1, u2, m2, c0, c1, c2, c3, kept, wt = refs[9:]
+    m1, u2, m2, c0, c1, c2, c3, kept, wt, listed, bleach = refs[9:]
     even = lax.axis_index("gy") % 2 == 0
     c = [c0, c1, c2, c3]
     view = lax.axis_index("view")
@@ -448,21 +468,23 @@
     z3, z2, z1, z0 = (frame.need(r) for r in (3, 2, 1, 0))
     sent = frame.sent(3)
 
+    listed[...] = jnp.zeros(listed.shape, F32)
+    listed[0:4, : table_ref.shape[1]] = table_ref[...]
+    for n, ref in enumerate(index_refs):
+        bleach[n * 16 : (n + 1) * 16, :] = bleach_weights(
+            ref[0, at : at + 8, :128].astype(F32), listed[...]
+        )
     for f in z2:
         where, k = frame.source(f)
-        index_ref = index_refs[0 if where == "own" else 1 + sides.index(where)]
+        n = 0 if where == "own" else 1 + sides.index(where)
         over = upside if where == "own" else 1 - upside
-        raw = k + over * (depth - 1 - 2 * k) if frame.mirrored else k
-        weights = [
-            jnp.full((16, 128), table_ref[v, index_ref[v, raw]], F32) for v in range(4)
-        ]
+        raw = n * 16 + (k + over * (depth - 1 - 2 * k) if frame.mirrored else k)
+        weights = [bleach[pl.ds(raw + v * depth, 1), :] for v in range(4)]
         total = (weights[0] + weights[1]) + (weights[2] + weights[3])
         for v in range(4):
-            mine = jnp.full(
-                (16, 128), table_ref[view ^ v, index_ref[view ^ v, raw]], F32
-            )
-            at = (v * frame.size + f) * 16
-            wt[at : at + 16, :] = num_ref[v * 16 : (v + 1) * 16, :] * (mine / total)
+            mine = bleach[pl.ds(raw + (view ^ v) * depth, 1), :]
+            to = (v * frame.size + f) * 16
+            wt[to : to + 16, :] = num_ref[v * 16 : (v + 1) * 16, :] * (mine / total)
 
     def weighted(v, z, n):
         at = (v * frame.size + z) * 16 + 8 - n
@@ -677,11 +699,12 @@
     even, odd, payload = call(
         functools.partial(first_kernel, pairs, bands, frame.mirrored),
         (half_cells, half_cells, resident(area + 8, chunk)),
-        (smem, smem, smem, vmem, vmem, vmem, vmem),
+        (smem, smem, smem, smem, vmem, vmem, vmem, vmem),
         (vmem, vmem, vmem),
         first_owner,
         piece_row,
         background,
+        bleach_index,
         first_pieces,
         first_taps,
         estimate,
@@ -690,18 +713,16 @@
     )
     other = swap(odd, "gy", bands, 1)
     near_payload = swap(payload, "view", 4, 1)
-    index_far = exchange_z(frame, lambda s: bleach_index[:, s.start : s.stop], slabs, depth)
     *kept, pair, sums_done = call(
         functools.partial(sum_kernel, pairs),
         (resident(depth, height, width),) * pairs
         + (resident(2, area + 8, chunk), mark),
-        [vmem] * 4 + [free],
+        [vmem] * 4,
         [vmem] * (pairs + 2),
         even,
         other,
         payload,
         near_payload,
-        index_far[sides[0]],
     )
     heard = (pair, swap(pair, "view", 4, 2))
     moved = [swap(kept[k], ("gz", "gy"), blocks, 2 * k) for k in range(1, pairs)]
@@ -736,16 +757,6 @@
             token,
         )
 
-    table, nums, token = call(
-        functools.partial(band_kernel, area),
-        (resident(6, 2 * TILE, TILE), resident(64, 128, dtype=F32), mark),
-        [vmem] * 2 + [free],
-        (vmem, vmem, vmem),
-        *heard,
-        sums_done,
-    )
-    kept_table, kept_nums = table, nums
-
     far_slices = frame.sent(3)
     plain, turned, *own_far, total_done = call(
         functools.partial(
@@ -760,18 +771,26 @@
         [vmem] * (3 + len(sides)),
         kept[0],
         *moved,
-        token,
+        sums_done,
     )
     near = swap(plain, "view", 4, 1)
     opposite = swap(turned, "view", 4, 2)
     last = swap(opposite, "view", 4, 1)
     ready = dict(zip([(s.start, s.stop) for s in far_slices.values()], own_far))
+    table, nums, token = call(
+        functools.partial(band_kernel, area),
+        (resident(6, 2 * TILE, TILE), resident(64, 128, dtype=F32), mark),
+        [vmem] * 3,
+        (vmem, vmem, vmem),
+        *heard,
+        near,
+    )
+    kept_table, kept_nums = table, nums
+
     def est_rows(slices):
         return call(
-            functools.partial(
-                est_rows_kernel, slice(slices.start * height, slices.stop * height)
-            ),
-            resident(4, len(slices) * height, chunk),
+            est_rows_kernel,
+            resident(4, area + 8, chunk),
             [vmem] * 2 + [free],
             (vmem,),
             *heard,
@@ -834,13 +853,13 @@
         scratch=scratch,
     )
     return call(
-        functools.partial(main_kernel, frame, tiles, sides),
+        functools.partial(main_kernel, frame, tiles, sides, area),
         jax.ShapeDtypeStruct(estimate.shape, F32),
-        [smem] * (2 + len(sides)) + [vmem] * (14 + 2 * len(sides)),
+        [vmem] * (16 + 3 * len(sides)),
         (vmem,),
         bleach_table,
-        bleach_index,
-        *[index_far[s] for s in sides],
+        pair,
+        *far_est,
         kept_nums,
         estimate,
         plain,
@@ -861,7 +880,8 @@
             vmem((tiles + 1, n1, TILE), BF),
         ]
         + [vmem((tiles, n3, TILE), BF)] * 4
-        + [vmem((tiles, area, TILE), F32), vmem((4 * size * 16, 128), F32)],
+        + [vmem((tiles, area, TILE), F32), vmem((4 * size * 16, 128), F32)]
+        + [vmem((8, 128), F32), vmem(((1 + len(sides)) * 16, 128), F32)],
     )
 
 

time: 62.3 us -> 61.4 us (0.986)
  starting transfers between devices: 28.6 us -> 26.5 us
  waiting for transfers between devices: 14.5 us -> 15.2 us
  local copies, waits for them, and re-layouts: 0.01 us -> 0.67 us
    ppermute x17 -> x16, starting transfers between devices: 24.2 us -> 20.2 us  [swap(): return lax.ppermute(array, axis, [(i, i ^ mask) for i in range(size)])]
    ppermute x2, starting transfers between devices: 4.38 us -> 6.27 us  [core_side(): return (first, lax.ppermute(own[1], 'gy', [(1, 2), (2, 1)]))]
    ppermute x17 -> x16, waiting for transfers between devices: 12.3 us -> 14.1 us  [swap(): return lax.ppermute(array, axis, [(i, i ^ mask) for i in range(size)])]
    ppermute x2, waiting for transfers between devices: 2.22 us -> 1.11 us  [core_side(): return (first, lax.ppermute(own[1], 'gy', [(1, 2), (2, 1)]))]
    unnamed x2, local copies, waits for them, and re-layouts: 0.01 us -> 0.67 us
  transfers between devices with their start and end apart: 19 -> 18, of which waited for: 7 -> 7; matrix products, arithmetic and copies ran while one was open for 0% -> 0% of each run, Pallas kernels for 11% -> 11%
where the time goes in v9:
time: 61.4 us; the launch traced here: 61.2 us
  starting transfers between devices  26.5 us (43%)
  Pallas kernels  18.1 us (29%)
  waiting for transfers between devices  15.2 us (25%)
  between operations  0.77 us (1%)
  local copies, waits for them, and re-layouts  0.67 us (1%)
    ppermute x16, starting transfers between devices, swap(): return lax.ppermute(array, axis, [(i, i ^ mask) for i in range(size)])  20.2 us
    pallas_call x12, Pallas kernels, call(): pl.pallas_call(kernel, out_shape=shapes, in_specs=whole(*ins), out_specs=...  18.1 us
    ppermute x16, waiting for transfers between devices, swap(): return lax.ppermute(array, axis, [(i, i ^ mask) for i in range(size)])  14.1 us
    ppermute x2, starting transfers between devices, core_side(): return (first, lax.ppermute(own[1], 'gy', [(1, 2), (2, 1)]))  6.27 us
  transfers between devices with their start and end apart: 18, of which 7 were waited for; matrix products, arithmetic and copies ran while one was open for 0% of the time, Pallas kernels for 11%

profile of v9, /device:TPU:1, one launch (start us, length us, event | category | flops | bytes accessed | tf_op | source)
XLA Modules:
  0.0 61.2 jit_solution(15133989789198323007)
XLA Ops:
  0.7 0.7 %copy-done = s32[4,4]{1,0:T(4,128)S(1)} copy-done((s32[4,4]{1,0:T(4,128)S(1)}, s32[4,4]{1,0:T(4,128)}, u32[]{:S(2)}) %copy-start) | copy-done | bytes 88
  1.3 1.7 %shard_map.91 = (bf16[4,4,8,2048]{3,2,1,0:T(8,128)(2,1)S(1)}, bf16[4,4,8,2048]{3,2,1,0:T(8,128)(2,1)S(1)}, bf16[40,512]{1,0:T(8,128)(2,1)S(1)}) custom-call(s32[1,1,16]{2,1,0:T(1,128)} %bitcast.5, s32[1,16]{1,0:T(1,128)} %row_ref.1, f32[1]{0:T(128)S(6)} %copy.10.bg_ref, s32[4,4]{1,0:T(4,128)S(1)} %copy-done, bf16[16,8,2048]{2,1,0:T(8,128)(2,1)} %bitcast.3, ...), custom_call_target="tpu_custom_call" | custom-call | tf_op jit(solution)/shard_map/pallas_call | solution.py:679
  3.1 2.8 %collective-permute-start.1 = (bf16[40,512]{1,0:T(8,128)(2,1)S(1)}, bf16[40,512]{1,0:T(8,128)(2,1)S(1)}, u32[]{:S(2)}, u32[]{:S(2)}) collective-permute-start(bf16[40,512]{1,0:T(8,128)(2,1)S(1)} %get-tuple-element.36.refs_2_), channel_id=1, source_target_pairs={{0,8},{8,0},{16,24},{24,16},{1,9},{9,1},{17,25},{25,17},{2,10},{10... | collective-permute-start | bytes 122888 | tf_op jit(solution)/shard_map/ppermute | solution.py:21
  5.9 1.8 %collective-permute-done.1.refs_3_ = bf16[40,512]{1,0:T(8,128)(2,1)S(1)} collective-permute-done((bf16[40,512]{1,0:T(8,128)(2,1)S(1)}, bf16[40,512]{1,0:T(8,128)(2,1)S(1)}, u32[]{:S(2)}, u32[]{:S(2)}) %collective-permute-start.1) | collective-permute-done | bytes 40992 | tf_op jit(solution)/shard_map/ppermute | solution.py:21
  7.9 1.0 %collective-permute-start.3 = (bf16[4,8,2048]{2,1,0:T(8,128)(2,1)S(1)}, bf16[4,8,2048]{2,1,0:T(8,128)(2,1)S(1)}, u32[]{:S(2)}, u32[]{:S(2)}) collective-permute-start(bf16[4,8,2048]{2,1,0:T(8,128)(2,1)S(1)} %get-tuple-element.39), channel_id=1, source_target_pairs={{0,2},{1,3},{2,0},{3,1},{4,6},{5,7},{6,4},{7,5},{8,10},{9,11},{10,... | collective-permute-start | bytes 393224 | tf_op jit(solution)/shard_map/ppermute | solution.py:21
  8.9 1.2 %collective-permute-start.4 = (bf16[4,8,2048]{2,1,0:T(8,128)(2,1)S(1)}, bf16[4,8,2048]{2,1,0:T(8,128)(2,1)S(1)}, u32[]{:S(2)}, u32[]{:S(2)}) collective-permute-start(bf16[4,8,2048]{2,1,0:T(8,128)(2,1)S(1)} %get-tuple-element.40), channel_id=1, source_target_pairs={{0,4},{1,5},{2,6},{3,7},{4,0},{5,1},{6,2},{7,3},{8,12},{9,13},{10,... | collective-permute-start | bytes 393224 | tf_op jit(solution)/shard_map/ppermute | solution.py:21
  10.1 0.5 collective-permute-start.5
  10.6 2.0 %collective-permute-start.2 = (bf16[2,40,512]{2,1,0:T(8,128)(2,1)S(1)}, bf16[2,40,512]{2,1,0:T(8,128)(2,1)S(1)}, u32[]{:S(2)}, u32[]{:S(2)}) collective-permute-start(bf16[2,40,512]{2,1,0:T(8,128)(2,1)S(1)} %get-tuple-element.37.first.refs_0_), channel_id=1, source_target_pairs={{0,16},{8,24},{16,0},{24,8},{1,17},{9,25},{17,1},{25,9},{2,18},{10... | collective-permute-start | bytes 245768 | tf_op jit(solution)/shard_map/ppermute | solution.py:21
  12.6 0.4 collective-permute-done.4.refs_2_
  13.0 3.1 %collective-permute-done.5.refs_3_ = bf16[4,8,2048]{2,1,0:T(8,128)(2,1)S(1)} collective-permute-done((bf16[4,8,2048]{2,1,0:T(8,128)(2,1)S(1)}, bf16[4,8,2048]{2,1,0:T(8,128)(2,1)S(1)}, u32[]{:S(2)}, u32[]{:S(2)}) %collective-permute-start.5) | collective-permute-done | bytes 131104 | tf_op jit(solution)/shard_map/ppermute | solution.py:21
  16.1 0.2 shard_map.93
  16.4 2.8 %collective-permute-start.8 = (bf16[8,32,256]{2,1,0:T(8,128)(2,1)S(1)}, bf16[8,32,256]{2,1,0:T(8,128)(2,1)S(1)}, u32[]{:S(2)}, u32[]{:S(2)}) collective-permute-start(bf16[8,32,256]{2,1,0:T(8,128)(2,1)S(1)} %get-tuple-element.46), channel_id=1, source_target_pairs={{0,16},{8,24},{16,0},{24,8},{1,17},{9,25},{17,1},{25,9},{2,18},{10... | collective-permute-start | bytes 393224 | tf_op jit(solution)/shard_map/ppermute | solution.py:21
  19.2 1.3 %collective-permute-start.7 = (bf16[8,32,256]{2,1,0:T(8,128)(2,1)S(1)}, bf16[8,32,256]{2,1,0:T(8,128)(2,1)S(1)}, u32[]{:S(2)}, u32[]{:S(2)}) collective-permute-start(bf16[8,32,256]{2,1,0:T(8,128)(2,1)S(1)} %get-tuple-element.44.refs_0_.refs_4_), channel_id=1, source_target_pairs={{0,8},{8,0},{16,24},{24,16},{1,9},{9,1},{17,25},{25,17},{2,10},{10... | collective-permute-start | bytes 393224 | tf_op jit(solution)/shard_map/ppermute | solution.py:21
  20.5 2.6 %collective-permute-done.8.refs_1_.refs_2_.refs_6_ = bf16[8,32,256]{2,1,0:T(8,128)(2,1)S(1)} collective-permute-done((bf16[8,32,256]{2,1,0:T(8,128)(2,1)S(1)}, bf16[8,32,256]{2,1,0:T(8,128)(2,1)S(1)}, u32[]{:S(2)}, u32[]{:S(2)}) %collective-permute-start.8) | collective-permute-done | bytes 131104 | tf_op jit(solution)/shard_map/ppermute | solution.py:21
  23.1 0.6 %collective-permute-start.9 = (bf16[8,32,256]{2,1,0:T(8,128)(2,1)S(1)}, bf16[8,32,256]{2,1,0:T(8,128)(2,1)S(1)}, u32[]{:S(2)}, u32[]{:S(2)}) collective-permute-start(bf16[8,32,256]{2,1,0:T(8,128)(2,1)S(1)} %collective-permute-done.8.refs_1_.refs_2_.refs_6_), channel_id=1, source_target_pairs={{0,8},{8,0},{16,24},{24,16},{1,9},{9,1},{17,25},{25,17},{2,10},{10... | collective-permute-start | bytes 393224 | tf_op jit(solution)/shard_map/ppermute | solution.py:21
  23.7 0.6 shard_map.96
  24.3 3.6 %collective-permute-start.11 = (bf16[4,8,4,512]{3,2,1,0:T(4,128)(2,1)S(1)}, bf16[4,8,4,512]{3,2,1,0:T(4,128)(2,1)S(1)}, u32[]{:S(2)}, u32[]{:S(2)}) collective-permute-start(bf16[4,8,4,512]{3,2,1,0:T(4,128)(2,1)S(1)} %get-tuple-element.48), channel_id=1, source_target_pairs={{0,1},{1,0},{2,3},{3,2},{4,5},{5,4},{6,7},{7,6},{8,9},{9,8},{10,11... | collective-permute-start | bytes 393224 | tf_op jit(solution)/shard_map/ppermute | solution.py:21
  27.9 1.1 %collective-permute-start.12 = (bf16[4,8,4,512]{3,2,1,0:T(4,128)(2,1)S(1)}, bf16[4,8,4,512]{3,2,1,0:T(4,128)(2,1)S(1)}, u32[]{:S(2)}, u32[]{:S(2)}) collective-permute-start(bf16[4,8,4,512]{3,2,1,0:T(4,128)(2,1)S(1)} %get-tuple-element.49), channel_id=1, source_target_pairs={{0,3},{1,2},{2,1},{3,0},{4,7},{5,6},{6,5},{7,4},{8,11},{9,10},{10,... | collective-permute-start | bytes 393224 | tf_op jit(solution)/shard_map/ppermute | solution.py:21
  29.0 4.0 %collective-permute-done.12.refs_5_.refs_4_ = bf16[4,8,4,512]{3,2,1,0:T(4,128)(2,1)S(1)} collective-permute-done((bf16[4,8,4,512]{3,2,1,0:T(4,128)(2,1)S(1)}, bf16[4,8,4,512]{3,2,1,0:T(4,128)(2,1)S(1)}, u32[]{:S(2)}, u32[]{:S(2)}) %collective-permute-start.12) | collective-permute-done | bytes 131104 | tf_op jit(solution)/shard_map/ppermute | solution.py:21
  33.0 1.4 %collective-permute-start.13 = (bf16[3,8,24,256]{3,2,1,0:T(8,128)(2,1)S(1)}, bf16[3,8,24,256]{3,2,1,0:T(8,128)(2,1)S(1)}, u32[]{:S(2)}, u32[]{:S(2)}) collective-permute-start(bf16[3,8,24,256]{3,2,1,0:T(8,128)(2,1)S(1)} %get-tuple-element.50), channel_id=1, source_target_pairs={{0,4},{4,0},{1,5},{5,1},{2,6},{6,2},{3,7},{7,3},{8,12},{12,8},{9,1... | collective-permute-start | bytes 884744 | tf_op jit(solution)/shard_map/ppermute | solution.py:21
  34.4 0.2 collective-permute-start.10
  34.6 0.2 shard_map.98
  34.8 0.7 %collective-permute-start.14 = (bf16[4,8,4,4,256]{4,3,2,1,0:T(4,128)(2,1)S(1)}, bf16[4,8,4,4,256]{4,3,2,1,0:T(4,128)(2,1)S(1)}, u32[]{:S(2)}, u32[]{:S(2)}) collective-permute-start(bf16[4,8,4,4,256]{4,3,2,1,0:T(4,128)(2,1)S(1)} %get-tuple-element.52), channel_id=1, source_target_pairs={{0,1},{1,0},{2,3},{3,2},{4,5},{5,4},{6,7},{7,6},{8,9},{9,8},{10,11... | collective-permute-start | bytes 786440 | tf_op jit(solution)/shard_map/ppermute | solution.py:21
  35.5 3.0 %collective-permute-start.15 = (bf16[4,8,4,4,256]{4,3,2,1,0:T(4,128)(2,1)S(1)}, bf16[4,8,4,4,256]{4,3,2,1,0:T(4,128)(2,1)S(1)}, u32[]{:S(2)}, u32[]{:S(2)}) collective-permute-start(bf16[4,8,4,4,256]{4,3,2,1,0:T(4,128)(2,1)S(1)} %get-tuple-element.53), channel_id=1, source_target_pairs={{1,2},{2,1},{5,6},{6,5},{9,10},{10,9},{13,14},{14,13},{17,18},{18,... | collective-permute-start | bytes 786440 | tf_op jit(solution)/shard_map/ppermute | solution.py:28
  38.5 0.9 %shard_map.95 = (bf16[6,512,256]{2,1,0:T(8,128)(2,1)S(1)}, f32[64,128]{1,0:T(8,128)S(1)}, f32[8,128]{1,0:T(8,128)}) custom-call(bf16[2,40,512]{2,1,0:T(8,128)(2,1)S(1)} %get-tuple-element.37.first.refs_0_, bf16[2,40,512]{2,1,0:T(8,128)(2,1)S(1)} %collective-permute-done.2.second.refs_1_, ...), custom_call_target="tpu_custom_call" | custom-call | tf_op jit(solution)/shard_map/pallas_call | solution.py:679
  39.4 2.2 %shard_map.99 = (bf16[9,128,256]{2,1,0:T(8,128)(2,1)S(1)}, bf16[2,8,112,256]{3,2,1,0:T(8,128)(2,1)S(1)}, f32[8,128]{1,0:T(8,128)S(1)}) custom-call(f32[64,128]{1,0:T(8,128)S(1)} %get-tuple-element.45.num_ref.refs_2_, bf16[6,512,256]{2,1,0:T(8,128)(2,1)S(1)} %get-tuple-element.54.blocks_ref.refs_16_, bf16[2,40,512]{2,1,0:T(8,128)(2,1)S(1)} %get-tuple-element.37.first.refs_0_, ...), custom_call_target="tpu_custom_call" | custom-call | tf_op jit(solution)/shard_map/pallas_call | solution.py:679
  41.6 2.2 %collective-permute-done.10.refs_0_.refs_8_ = bf16[1,8,24,256]{3,2,1,0:T(8,128)(2,1)S(1)} collective-permute-done((bf16[1,8,24,256]{3,2,1,0:T(8,128)(2,1)S(1)}, bf16[1,8,24,256]{3,2,1,0:T(8,128)(2,1)S(1)}, u32[]{:S(2)}, u32[]{:S(2)}) %collective-permute-start.10) | collective-permute-done | bytes 98336 | tf_op jit(solution)/shard_map/ppermute | solution.py:21
  44.0 0.9 %collective-permute-start.16 = (bf16[4,8,3,4,256]{4,3,2,1,0:T(4,128)(2,1)S(1)}, bf16[4,8,3,4,256]{4,3,2,1,0:T(4,128)(2,1)S(1)}, u32[]{:S(2)}, u32[]{:S(2)}) collective-permute-start(bf16[4,8,3,4,256]{4,3,2,1,0:T(4,128)(2,1)S(1)} %get-tuple-element.57), channel_id=1, source_target_pairs={{0,1},{1,0},{2,3},{3,2},{4,5},{5,4},{6,7},{7,6},{8,9},{9,8},{10,11... | collective-permute-start | bytes 589832 | tf_op jit(solution)/shard_map/ppermute | solution.py:21
  44.9 3.2 %collective-permute-start.17 = (bf16[4,8,3,4,256]{4,3,2,1,0:T(4,128)(2,1)S(1)}, bf16[4,8,3,4,256]{4,3,2,1,0:T(4,128)(2,1)S(1)}, u32[]{:S(2)}, u32[]{:S(2)}) collective-permute-start(bf16[4,8,3,4,256]{4,3,2,1,0:T(4,128)(2,1)S(1)} %get-tuple-element.58), channel_id=1, source_target_pairs={{1,2},{2,1},{5,6},{6,5},{9,10},{10,9},{13,14},{14,13},{17,18},{18,... | collective-permute-start | bytes 589832 | tf_op jit(solution)/shard_map/ppermute | solution.py:28
  48.1 2.6 %shard_map.101 = (bf16[2,8,112,256]{3,2,1,0:T(8,128)(2,1)S(1)}, f32[8,128]{1,0:T(8,128)}) custom-call(f32[64,128]{1,0:T(8,128)S(1)} %get-tuple-element.45.num_ref.refs_2_, bf16[6,512,256]{2,1,0:T(8,128)(2,1)S(1)} %get-tuple-element.54.blocks_ref.refs_16_, bf16[9,128,256]{2,1,0:T(8,128)(2,1)S(1)} %get-tuple-element.60.frame_ref.refs_17_, ...), custom_call_target="tpu_custom_call" | custom-call | tf_op jit(solution)/shard_map/pallas_call | solution.py:679
  50.7 1.1 %collective-permute-done.17.refs_13_ = bf16[4,8,3,4,256]{4,3,2,1,0:T(4,128)(2,1)S(1)} collective-permute-done((bf16[4,8,3,4,256]{4,3,2,1,0:T(4,128)(2,1)S(1)}, bf16[4,8,3,4,256]{4,3,2,1,0:T(4,128)(2,1)S(1)}, u32[]{:S(2)}, u32[]{:S(2)}) %collective-permute-start.17) | collective-permute-done | bytes 196640 | tf_op jit(solution)/shard_map/ppermute | solution.py:28
  51.9 9.3 %shard_map.102 = f32[4,8,512]{2,1,0:T(8,128)} custom-call(f32[4,16]{1,0:T(4,128)} %table_ref.1, bf16[2,40,512]{2,1,0:T(8,128)(2,1)S(1)} %get-tuple-element.37.first.refs_0_, bf16[4,40,512]{2,1,0:T(8,128)(2,1)S(1)} %collective-permute-done.6.refs_2_.refs_1_, f32[64,128]{1,0:T(8,128)S(1)} %get-tuple-element.45.num_ref.refs_2_, f32[4,8,512]{2,1,0:T(8,128)} %refs_3_.1, ...), custom_call_target="tpu_custom_call" | custom-call | tf_op jit(solution)/shard_map/pallas_call | solution.py:679
  (18 shorter events, 0.5 us)
Async XLA Ops:
  0.7 0.7 %copy-start = (s32[4,4]{1,0:T(4,128)S(1)}, s32[4,4]{1,0:T(4,128)}, u32[]{:S(2)}) copy-start(s32[4,4]{1,0:T(4,128)} %index_ref.1) | copy-start | bytes 196
  3.0 4.7 %collective-permute-start = (bf16[4,4,8,2048]{3,2,1,0:T(8,128)(2,1)S(1)}, bf16[4,4,8,2048]{3,2,1,0:T(8,128)(2,1)S(1)}, u32[]{:S(2)}, u32[]{:S(2)}) collective-permute-start(bf16[4,4,8,2048]{3,2,1,0:T(8,128)(2,1)S(1)} %get-tuple-element.35), channel_id=1, source_target_pairs={{0,1},{1,0},{2,3},{3,2},{4,5},{5,4},{6,7},{7,6},{8,9},{9,8},{10,11... | collective-permute-start | bytes 1572872 | tf_op jit(solution)/shard_map/ppermute | solution.py:21
  3.1 4.6 %collective-permute-start.1 = (bf16[40,512]{1,0:T(8,128)(2,1)S(1)}, bf16[40,512]{1,0:T(8,128)(2,1)S(1)}, u32[]{:S(2)}, u32[]{:S(2)}) collective-permute-start(bf16[40,512]{1,0:T(8,128)(2,1)S(1)} %get-tuple-element.36.refs_2_), channel_id=1, source_target_pairs={{0,8},{8,0},{16,24},{24,16},{1,9},{9,1},{17,25},{25,17},{2,10},{10... | collective-permute-start | bytes 122888 | tf_op jit(solution)/shard_map/ppermute | solution.py:21
  7.9 4.7 %collective-permute-start.3 = (bf16[4,8,2048]{2,1,0:T(8,128)(2,1)S(1)}, bf16[4,8,2048]{2,1,0:T(8,128)(2,1)S(1)}, u32[]{:S(2)}, u32[]{:S(2)}) collective-permute-start(bf16[4,8,2048]{2,1,0:T(8,128)(2,1)S(1)} %get-tuple-element.39), channel_id=1, source_target_pairs={{0,2},{1,3},{2,0},{3,1},{4,6},{5,7},{6,4},{7,5},{8,10},{9,11},{10,... | collective-permute-start | bytes 393224 | tf_op jit(solution)/shard_map/ppermute | solution.py:21
  8.9 4.1 %collective-permute-start.4 = (bf16[4,8,2048]{2,1,0:T(8,128)(2,1)S(1)}, bf16[4,8,2048]{2,1,0:T(8,128)(2,1)S(1)}, u32[]{:S(2)}, u32[]{:S(2)}) collective-permute-start(bf16[4,8,2048]{2,1,0:T(8,128)(2,1)S(1)} %get-tuple-element.40), channel_id=1, source_target_pairs={{0,4},{1,5},{2,6},{3,7},{4,0},{5,1},{6,2},{7,3},{8,12},{9,13},{10,... | collective-permute-start | bytes 393224 | tf_op jit(solution)/shard_map/ppermute | solution.py:21
  10.1 6.0 %collective-permute-start.5 = (bf16[4,8,2048]{2,1,0:T(8,128)(2,1)S(1)}, bf16[4,8,2048]{2,1,0:T(8,128)(2,1)S(1)}, u32[]{:S(2)}, u32[]{:S(2)}) collective-permute-start(bf16[4,8,2048]{2,1,0:T(8,128)(2,1)S(1)} %get-tuple-element.41), channel_id=1, source_target_pairs={{0,6},{1,7},{2,4},{3,5},{4,2},{5,3},{6,0},{7,1},{8,14},{9,15},{10,... | collective-permute-start | bytes 393224 | tf_op jit(solution)/shard_map/ppermute | solution.py:21
  10.6 5.7 %collective-permute-start.2 = (bf16[2,40,512]{2,1,0:T(8,128)(2,1)S(1)}, bf16[2,40,512]{2,1,0:T(8,128)(2,1)S(1)}, u32[]{:S(2)}, u32[]{:S(2)}) collective-permute-start(bf16[2,40,512]{2,1,0:T(8,128)(2,1)S(1)} %get-tuple-element.37.first.refs_0_), channel_id=1, source_target_pairs={{0,16},{8,24},{16,0},{24,8},{1,17},{9,25},{17,1},{25,9},{2,18},{10... | collective-permute-start | bytes 245768 | tf_op jit(solution)/shard_map/ppermute | solution.py:21
  16.3 7.4 %collective-permute-start.6 = (bf16[4,40,512]{2,1,0:T(8,128)(2,1)S(1)}, bf16[4,40,512]{2,1,0:T(8,128)(2,1)S(1)}, u32[]{:S(2)}, u32[]{:S(2)}) collective-permute-start(bf16[4,40,512]{2,1,0:T(8,128)(2,1)S(1)} %shard_map.94), channel_id=1, source_target_pairs={{0,4},{4,0},{1,5},{5,1},{2,6},{6,2},{3,7},{7,3},{8,12},{12,8},{9,1... | collective-permute-start | bytes 491528 | tf_op jit(solution)/shard_map/ppermute | solution.py:21
  16.4 6.7 %collective-permute-start.8 = (bf16[8,32,256]{2,1,0:T(8,128)(2,1)S(1)}, bf16[8,32,256]{2,1,0:T(8,128)(2,1)S(1)}, u32[]{:S(2)}, u32[]{:S(2)}) collective-permute-start(bf16[8,32,256]{2,1,0:T(8,128)(2,1)S(1)} %get-tuple-element.46), channel_id=1, source_target_pairs={{0,16},{8,24},{16,0},{24,8},{1,17},{9,25},{17,1},{25,9},{2,18},{10... | collective-permute-start | bytes 393224 | tf_op jit(solution)/shard_map/ppermute | solution.py:21
  19.2 9.8 %collective-permute-start.7 = (bf16[8,32,256]{2,1,0:T(8,128)(2,1)S(1)}, bf16[8,32,256]{2,1,0:T(8,128)(2,1)S(1)}, u32[]{:S(2)}, u32[]{:S(2)}) collective-permute-start(bf16[8,32,256]{2,1,0:T(8,128)(2,1)S(1)} %get-tuple-element.44.refs_0_.refs_4_), channel_id=1, source_target_pairs={{0,8},{8,0},{16,24},{24,16},{1,9},{9,1},{17,25},{25,17},{2,10},{10... | collective-permute-start | bytes 393224 | tf_op jit(solution)/shard_map/ppermute | solution.py:21
  23.1 6.0 %collective-permute-start.9 = (bf16[8,32,256]{2,1,0:T(8,128)(2,1)S(1)}, bf16[8,32,256]{2,1,0:T(8,128)(2,1)S(1)}, u32[]{:S(2)}, u32[]{:S(2)}) collective-permute-start(bf16[8,32,256]{2,1,0:T(8,128)(2,1)S(1)} %collective-permute-done.8.refs_1_.refs_2_.refs_6_), channel_id=1, source_target_pairs={{0,8},{8,0},{16,24},{24,16},{1,9},{9,1},{17,25},{25,17},{2,10},{10... | collective-permute-start | bytes 393224 | tf_op jit(solution)/shard_map/ppermute | solution.py:21
  24.3 4.7 %collective-permute-start.11 = (bf16[4,8,4,512]{3,2,1,0:T(4,128)(2,1)S(1)}, bf16[4,8,4,512]{3,2,1,0:T(4,128)(2,1)S(1)}, u32[]{:S(2)}, u32[]{:S(2)}) collective-permute-start(bf16[4,8,4,512]{3,2,1,0:T(4,128)(2,1)S(1)} %get-tuple-element.48), channel_id=1, source_target_pairs={{0,1},{1,0},{2,3},{3,2},{4,5},{5,4},{6,7},{7,6},{8,9},{9,8},{10,11... | collective-permute-start | bytes 393224 | tf_op jit(solution)/shard_map/ppermute | solution.py:21
  27.9 5.1 %collective-permute-start.12 = (bf16[4,8,4,512]{3,2,1,0:T(4,128)(2,1)S(1)}, bf16[4,8,4,512]{3,2,1,0:T(4,128)(2,1)S(1)}, u32[]{:S(2)}, u32[]{:S(2)}) collective-permute-start(bf16[4,8,4,512]{3,2,1,0:T(4,128)(2,1)S(1)} %get-tuple-element.49), channel_id=1, source_target_pairs={{0,3},{1,2},{2,1},{3,0},{4,7},{5,6},{6,5},{7,4},{8,11},{9,10},{10,... | collective-permute-start | bytes 393224 | tf_op jit(solution)/shard_map/ppermute | solution.py:21
  33.0 10.8 %collective-permute-start.13 = (bf16[3,8,24,256]{3,2,1,0:T(8,128)(2,1)S(1)}, bf16[3,8,24,256]{3,2,1,0:T(8,128)(2,1)S(1)}, u32[]{:S(2)}, u32[]{:S(2)}) collective-permute-start(bf16[3,8,24,256]{3,2,1,0:T(8,128)(2,1)S(1)} %get-tuple-element.50), channel_id=1, source_target_pairs={{0,4},{4,0},{1,5},{5,1},{2,6},{6,2},{3,7},{7,3},{8,12},{12,8},{9,1... | collective-permute-start | bytes 884744 | tf_op jit(solution)/shard_map/ppermute | solution.py:21
  34.4 9.4 %collective-permute-start.10 = (bf16[1,8,24,256]{3,2,1,0:T(8,128)(2,1)S(1)}, bf16[1,8,24,256]{3,2,1,0:T(8,128)(2,1)S(1)}, u32[]{:S(2)}, u32[]{:S(2)}) collective-permute-start(bf16[1,8,24,256]{3,2,1,0:T(8,128)(2,1)S(1)} %get-tuple-element.47), channel_id=1, source_target_pairs={{0,4},{4,0},{1,5},{5,1},{2,6},{6,2},{3,7},{7,3},{8,12},{12,8},{9,1... | collective-permute-start | bytes 294920 | tf_op jit(solution)/shard_map/ppermute | solution.py:21
  34.8 15.9 %collective-permute-start.14 = (bf16[4,8,4,4,256]{4,3,2,1,0:T(4,128)(2,1)S(1)}, bf16[4,8,4,4,256]{4,3,2,1,0:T(4,128)(2,1)S(1)}, u32[]{:S(2)}, u32[]{:S(2)}) collective-permute-start(bf16[4,8,4,4,256]{4,3,2,1,0:T(4,128)(2,1)S(1)} %get-tuple-element.52), channel_id=1, source_target_pairs={{0,1},{1,0},{2,3},{3,2},{4,5},{5,4},{6,7},{7,6},{8,9},{9,8},{10,11... | collective-permute-start | bytes 786440 | tf_op jit(solution)/shard_map/ppermute | solution.py:21
  35.5 15.3 %collective-permute-start.15 = (bf16[4,8,4,4,256]{4,3,2,1,0:T(4,128)(2,1)S(1)}, bf16[4,8,4,4,256]{4,3,2,1,0:T(4,128)(2,1)S(1)}, u32[]{:S(2)}, u32[]{:S(2)}) collective-permute-start(bf16[4,8,4,4,256]{4,3,2,1,0:T(4,128)(2,1)S(1)} %get-tuple-element.53), channel_id=1, source_target_pairs={{1,2},{2,1},{5,6},{6,5},{9,10},{10,9},{13,14},{14,13},{17,18},{18,... | collective-permute-start | bytes 786440 | tf_op jit(solution)/shard_map/ppermute | solution.py:28
  44.0 6.8 %collective-permute-start.16 = (bf16[4,8,3,4,256]{4,3,2,1,0:T(4,128)(2,1)S(1)}, bf16[4,8,3,4,256]{4,3,2,1,0:T(4,128)(2,1)S(1)}, u32[]{:S(2)}, u32[]{:S(2)}) collective-permute-start(bf16[4,8,3,4,256]{4,3,2,1,0:T(4,128)(2,1)S(1)} %get-tuple-element.57), channel_id=1, source_target_pairs={{0,1},{1,0},{2,3},{3,2},{4,5},{5,4},{6,7},{7,6},{8,9},{9,8},{10,11... | collective-permute-start | bytes 589832 | tf_op jit(solution)/shard_map/ppermute | solution.py:21
  44.9 7.0 %collective-permute-start.17 = (bf16[4,8,3,4,256]{4,3,2,1,0:T(4,128)(2,1)S(1)}, bf16[4,8,3,4,256]{4,3,2,1,0:T(4,128)(2,1)S(1)}, u32[]{:S(2)}, u32[]{:S(2)}) collective-permute-start(bf16[4,8,3,4,256]{4,3,2,1,0:T(4,128)(2,1)S(1)} %get-tuple-element.58), channel_id=1, source_target_pairs={{1,2},{2,1},{5,6},{6,5},{9,10},{10,9},{13,14},{14,13},{17,18},{18,... | collective-permute-start | bytes 589832 | tf_op jit(solution)/shard_map/ppermute | solution.py:28

commit v10 on v9

--- a/solution.py
+++ b/solution.py
@@ -459,7 +459,8 @@
     near_refs, beyond_refs = refs[:2], refs[2:4]
     recip_refs = refs[4:6]
     blocks_ref, frame_ref, out_ref = refs[6:9]
-    m1, u2, m2, c0, c1, c2, c3, kept, wt, listed, bleach = refs[9:]
+    m1a, m1b, u2, m2a, m2b, c0, c1, c2, c3, kept, wt, listed, bleach = refs[9:]
+    m1s, m2s = (m1a, m1b), (m2a, m2b)
     even = lax.axis_index("gy") % 2 == 0
     c = [c0, c1, c2, c3]
     view = lax.axis_index("view")
@@ -518,7 +519,7 @@
         b = (measured(v + 2, t, z, cut) * recip_b).astype(BF).astype(F32)
         return (0.5 * (a + b)).astype(BF)
 
-    for ref in (m1, u2, m2):
+    for ref in (m1a, m1b, u2, m2a, m2b):
         zero_ends(ref)
 
     for v in range(2):
@@ -529,7 +530,7 @@
                 to, lanes = spots(t, h)
                 for n, z in enumerate(z3):
                     at = slice(n * 16, (n + 1) * 16)
-                    m1[to, at, lanes] = mix(
+                    m1s[v][to, at, lanes] = mix(
                         v,
                         t,
                         z,
@@ -541,7 +542,7 @@
 
         lax.fori_loop(0, tiles, ratios, 0, unroll=True)
         for w in (v, v + 2):
-            conv(m1, 0, tiles, m1.shape[1], blocks_ref.at[backward_block(w)], c[w], 2)
+            conv(m1s[v], 0, tiles, m1a.shape[1], blocks_ref.at[backward_block(w)], c[w], 2)
 
     def numerator(slices_of, zs):
         totals = {z: [None, None, None] for z in zs}
@@ -582,11 +583,11 @@
 
     lax.fori_loop(0, tiles, update, 0, unroll=True)
 
-    rows1 = m2.shape[1]
+    rows1 = m2a.shape[1]
     n2 = u2.shape[1]
+    for w in (0, 2, 1, 3):
+        conv(u2, 0, tiles, n2, blocks_ref.at[forward_block(w)], c[w].at[:, :n2, :], 2)
     for v in range(2):
-        for w in (v, v + 2):
-            conv(u2, 0, tiles, n2, blocks_ref.at[forward_block(w)], c[w].at[:, :n2, :], 2)
 
         def ratios2(t, carry, v=v):
             for h in range(TILE // 128):
@@ -606,7 +607,7 @@
                     )
                 to, lanes = spots(t, h)
                 for n, z in enumerate(z1):
-                    m2[to, n * 16 : (n + 1) * 16, lanes] = mix(
+                    m2s[v][to, n * 16 : (n + 1) * 16, lanes] = mix(
                         v, t, z, cut, recips[0][z], recips[1][z]
                     )
             return carry
@@ -615,7 +616,7 @@
         mine = tiles // 4
         for w in (v, v + 2):
             first = view * mine if w < 2 else tiles - (view + 1) * mine
-            conv(m2, first, mine, rows1, blocks_ref.at[backward_block(w)], c[w].at[:, :rows1, :], 2)
+            conv(m2s[v], first, mine, rows1, blocks_ref.at[backward_block(w)], c[w].at[:, :rows1, :], 2)
 
     mine = tiles // 4
     for s in range(mine):
@@ -658,7 +659,7 @@
     def stay(array):
         return pltpu.with_memory_space_constraint(array, pltpu.VMEM)
 
-    given = [piece_row, estimate, psf_x, bleach_table]
+    given = [piece_row, estimate, psf_x, bleach_table, bleach_index]
     given += [pieces[0], stencil.transpose(1, 0, 2), piece_owner.transpose(0, 2, 1)]
     first_pieces, first_taps, first_owner = given[-3:]
 
@@ -857,11 +858,11 @@
         jax.ShapeDtypeStruct(estimate.shape, F32),
         [vmem] * (16 + 3 * len(sides)),
         (vmem,),
-        bleach_table,
+        stay(bleach_table),
         pair,
         *far_est,
         kept_nums,
-        estimate,
+        stay(estimate),
         plain,
         near,
         opposite,
@@ -876,7 +877,9 @@
         est_frame,
         scratch=[
             vmem((tiles + 1, n3, TILE), BF),
+            vmem((tiles + 1, n3, TILE), BF),
             vmem((tiles + 1, n2, TILE), BF),
+            vmem((tiles + 1, n1, TILE), BF),
             vmem((tiles + 1, n1, TILE), BF),
         ]
         + [vmem((tiles, n3, TILE), BF)] * 4

time: 61.4 us -> 59.8 us (0.974)
  Pallas kernels: 18.1 us -> 17.2 us
  local copies, waits for them, and re-layouts: 0.67 us -> 0.01 us
    pallas_call x12, Pallas kernels: 18.1 us -> 17.2 us  [call(): pl.pallas_call(kernel, out_shape=shapes, in_specs=whole(*ins), out_specs=...]
    unnamed x2 -> x4, local copies, waits for them, and re-layouts: 0.67 us -> 0.01 us
  transfers between devices with their start and end apart: 18 -> 18, of which waited for: 7 -> 7; matrix products, arithmetic and copies ran while one was open for 0% -> 0% of each run, Pallas kernels for 11% -> 12%
where the time goes in v10:
time: 59.8 us; the launch traced here: 59.6 us
  starting transfers between devices  26.5 us (44%)
  Pallas kernels  17.2 us (29%)
  waiting for transfers between devices  15.1 us (25%)
  between operations  0.78 us (1%)
    ppermute x16, starting transfers between devices, swap(): return lax.ppermute(array, axis, [(i, i ^ mask) for i in range(size)])  20.2 us
    pallas_call x12, Pallas kernels, call(): pl.pallas_call(kernel, out_shape=shapes, in_specs=whole(*ins), out_specs=...  17.2 us
    ppermute x16, waiting for transfers between devices, swap(): return lax.ppermute(array, axis, [(i, i ^ mask) for i in range(size)])  14 us
    ppermute x2, starting transfers between devices, core_side(): return (first, lax.ppermute(own[1], 'gy', [(1, 2), (2, 1)]))  6.27 us
  transfers between devices with their start and end apart: 18, of which 7 were waited for; matrix products, arithmetic and copies ran while one was open for 0% of the time, Pallas kernels for 12%

profile of v10, /device:TPU:1, one launch (start us, length us, event | category | flops | bytes accessed | tf_op | source)
XLA Modules:
  0.0 59.6 jit_solution(10422460319028536461)
XLA Ops:
  0.7 1.7 %shard_map.91 = (bf16[4,4,8,2048]{3,2,1,0:T(8,128)(2,1)S(1)}, bf16[4,4,8,2048]{3,2,1,0:T(8,128)(2,1)S(1)}, bf16[40,512]{1,0:T(8,128)(2,1)S(1)}) custom-call(s32[1,1,16]{2,1,0:T(1,128)} %bitcast.5, s32[1,16]{1,0:T(1,128)} %row_ref.1, f32[1]{0:T(128)S(6)} %copy.10.bg_ref, s32[4,4]{1,0:T(4,128)} %index_ref.1, bf16[16,8,2048]{2,1,0:T(8,128)(2,1)} %bitcast.3, ...), custom_call_target="tpu_custom_call" | custom-call | tf_op jit(solution)/shard_map/pallas_call | solution.py:680
  2.5 2.8 %collective-permute-start.1 = (bf16[40,512]{1,0:T(8,128)(2,1)S(1)}, bf16[40,512]{1,0:T(8,128)(2,1)S(1)}, u32[]{:S(2)}, u32[]{:S(2)}) collective-permute-start(bf16[40,512]{1,0:T(8,128)(2,1)S(1)} %get-tuple-element.36.refs_2_), channel_id=1, source_target_pairs={{0,8},{8,0},{16,24},{24,16},{1,9},{9,1},{17,25},{25,17},{2,10},{10... | collective-permute-start | bytes 122888 | tf_op jit(solution)/shard_map/ppermute | solution.py:21
  5.2 1.8 %collective-permute-done.1.refs_3_ = bf16[40,512]{1,0:T(8,128)(2,1)S(1)} collective-permute-done((bf16[40,512]{1,0:T(8,128)(2,1)S(1)}, bf16[40,512]{1,0:T(8,128)(2,1)S(1)}, u32[]{:S(2)}, u32[]{:S(2)}) %collective-permute-start.1) | collective-permute-done | bytes 40992 | tf_op jit(solution)/shard_map/ppermute | solution.py:21
  7.2 1.0 %collective-permute-start.3 = (bf16[4,8,2048]{2,1,0:T(8,128)(2,1)S(1)}, bf16[4,8,2048]{2,1,0:T(8,128)(2,1)S(1)}, u32[]{:S(2)}, u32[]{:S(2)}) collective-permute-start(bf16[4,8,2048]{2,1,0:T(8,128)(2,1)S(1)} %get-tuple-element.39), channel_id=1, source_target_pairs={{0,2},{1,3},{2,0},{3,1},{4,6},{5,7},{6,4},{7,5},{8,10},{9,11},{10,... | collective-permute-start | bytes 393224 | tf_op jit(solution)/shard_map/ppermute | solution.py:21
  8.2 1.2 %collective-permute-start.4 = (bf16[4,8,2048]{2,1,0:T(8,128)(2,1)S(1)}, bf16[4,8,2048]{2,1,0:T(8,128)(2,1)S(1)}, u32[]{:S(2)}, u32[]{:S(2)}) collective-permute-start(bf16[4,8,2048]{2,1,0:T(8,128)(2,1)S(1)} %get-tuple-element.40), channel_id=1, source_target_pairs={{0,4},{1,5},{2,6},{3,7},{4,0},{5,1},{6,2},{7,3},{8,12},{9,13},{10,... | collective-permute-start | bytes 393224 | tf_op jit(solution)/shard_map/ppermute | solution.py:21
  9.4 0.5 collective-permute-start.5
  9.9 2.0 %collective-permute-start.2 = (bf16[2,40,512]{2,1,0:T(8,128)(2,1)S(1)}, bf16[2,40,512]{2,1,0:T(8,128)(2,1)S(1)}, u32[]{:S(2)}, u32[]{:S(2)}) collective-permute-start(bf16[2,40,512]{2,1,0:T(8,128)(2,1)S(1)} %get-tuple-element.37.first.refs_0_), channel_id=1, source_target_pairs={{0,16},{8,24},{16,0},{24,8},{1,17},{9,25},{17,1},{25,9},{2,18},{10... | collective-permute-start | bytes 245768 | tf_op jit(solution)/shard_map/ppermute | solution.py:21
  11.9 0.4 collective-permute-done.4.refs_2_
  12.3 3.1 %collective-permute-done.5.refs_3_ = bf16[4,8,2048]{2,1,0:T(8,128)(2,1)S(1)} collective-permute-done((bf16[4,8,2048]{2,1,0:T(8,128)(2,1)S(1)}, bf16[4,8,2048]{2,1,0:T(8,128)(2,1)S(1)}, u32[]{:S(2)}, u32[]{:S(2)}) %collective-permute-start.5) | collective-permute-done | bytes 131104 | tf_op jit(solution)/shard_map/ppermute | solution.py:21
  15.4 0.2 shard_map.93
  15.7 2.8 %collective-permute-start.8 = (bf16[8,32,256]{2,1,0:T(8,128)(2,1)S(1)}, bf16[8,32,256]{2,1,0:T(8,128)(2,1)S(1)}, u32[]{:S(2)}, u32[]{:S(2)}) collective-permute-start(bf16[8,32,256]{2,1,0:T(8,128)(2,1)S(1)} %get-tuple-element.46), channel_id=1, source_target_pairs={{0,16},{8,24},{16,0},{24,8},{1,17},{9,25},{17,1},{25,9},{2,18},{10... | collective-permute-start | bytes 393224 | tf_op jit(solution)/shard_map/ppermute | solution.py:21
  18.6 1.3 %collective-permute-start.7 = (bf16[8,32,256]{2,1,0:T(8,128)(2,1)S(1)}, bf16[8,32,256]{2,1,0:T(8,128)(2,1)S(1)}, u32[]{:S(2)}, u32[]{:S(2)}) collective-permute-start(bf16[8,32,256]{2,1,0:T(8,128)(2,1)S(1)} %get-tuple-element.44.refs_0_.refs_4_), channel_id=1, source_target_pairs={{0,8},{8,0},{16,24},{24,16},{1,9},{9,1},{17,25},{25,17},{2,10},{10... | collective-permute-start | bytes 393224 | tf_op jit(solution)/shard_map/ppermute | solution.py:21
  19.8 2.6 %collective-permute-done.8.refs_1_.refs_2_.refs_6_ = bf16[8,32,256]{2,1,0:T(8,128)(2,1)S(1)} collective-permute-done((bf16[8,32,256]{2,1,0:T(8,128)(2,1)S(1)}, bf16[8,32,256]{2,1,0:T(8,128)(2,1)S(1)}, u32[]{:S(2)}, u32[]{:S(2)}) %collective-permute-start.8) | collective-permute-done | bytes 131104 | tf_op jit(solution)/shard_map/ppermute | solution.py:21
  22.4 0.6 %collective-permute-start.9 = (bf16[8,32,256]{2,1,0:T(8,128)(2,1)S(1)}, bf16[8,32,256]{2,1,0:T(8,128)(2,1)S(1)}, u32[]{:S(2)}, u32[]{:S(2)}) collective-permute-start(bf16[8,32,256]{2,1,0:T(8,128)(2,1)S(1)} %collective-permute-done.8.refs_1_.refs_2_.refs_6_), channel_id=1, source_target_pairs={{0,8},{8,0},{16,24},{24,16},{1,9},{9,1},{17,25},{25,17},{2,10},{10... | collective-permute-start | bytes 393224 | tf_op jit(solution)/shard_map/ppermute | solution.py:21
  23.1 0.6 %shard_map.96 = (bf16[4,8,4,512]{3,2,1,0:T(4,128)(2,1)S(1)}, bf16[4,8,4,512]{3,2,1,0:T(4,128)(2,1)S(1)}, f32[8,128]{1,0:T(8,128)}) custom-call(bf16[2,40,512]{2,1,0:T(8,128)(2,1)S(1)} %get-tuple-element.37.first.refs_0_, bf16[2,40,512]{2,1,0:T(8,128)(2,1)S(1)} %collective-permute-done.2.second.refs_1_, ...), custom_call_target="tpu_custom_call" | custom-call | tf_op jit(solution)/shard_map/pallas_call | solution.py:680
  23.7 3.6 %collective-permute-start.11 = (bf16[4,8,4,512]{3,2,1,0:T(4,128)(2,1)S(1)}, bf16[4,8,4,512]{3,2,1,0:T(4,128)(2,1)S(1)}, u32[]{:S(2)}, u32[]{:S(2)}) collective-permute-start(bf16[4,8,4,512]{3,2,1,0:T(4,128)(2,1)S(1)} %get-tuple-element.48), channel_id=1, source_target_pairs={{0,1},{1,0},{2,3},{3,2},{4,5},{5,4},{6,7},{7,6},{8,9},{9,8},{10,11... | collective-permute-start | bytes 393224 | tf_op jit(solution)/shard_map/ppermute | solution.py:21
  27.2 1.1 %collective-permute-start.12 = (bf16[4,8,4,512]{3,2,1,0:T(4,128)(2,1)S(1)}, bf16[4,8,4,512]{3,2,1,0:T(4,128)(2,1)S(1)}, u32[]{:S(2)}, u32[]{:S(2)}) collective-permute-start(bf16[4,8,4,512]{3,2,1,0:T(4,128)(2,1)S(1)} %get-tuple-element.49), channel_id=1, source_target_pairs={{0,3},{1,2},{2,1},{3,0},{4,7},{5,6},{6,5},{7,4},{8,11},{9,10},{10,... | collective-permute-start | bytes 393224 | tf_op jit(solution)/shard_map/ppermute | solution.py:21
  28.4 4.0 %collective-permute-done.12.refs_5_.refs_4_ = bf16[4,8,4,512]{3,2,1,0:T(4,128)(2,1)S(1)} collective-permute-done((bf16[4,8,4,512]{3,2,1,0:T(4,128)(2,1)S(1)}, bf16[4,8,4,512]{3,2,1,0:T(4,128)(2,1)S(1)}, u32[]{:S(2)}, u32[]{:S(2)}) %collective-permute-start.12) | collective-permute-done | bytes 131104 | tf_op jit(solution)/shard_map/ppermute | solution.py:21
  32.4 1.4 %collective-permute-start.13 = (bf16[3,8,24,256]{3,2,1,0:T(8,128)(2,1)S(1)}, bf16[3,8,24,256]{3,2,1,0:T(8,128)(2,1)S(1)}, u32[]{:S(2)}, u32[]{:S(2)}) collective-permute-start(bf16[3,8,24,256]{3,2,1,0:T(8,128)(2,1)S(1)} %get-tuple-element.50), channel_id=1, source_target_pairs={{0,4},{4,0},{1,5},{5,1},{2,6},{6,2},{3,7},{7,3},{8,12},{12,8},{9,1... | collective-permute-start | bytes 884744 | tf_op jit(solution)/shard_map/ppermute | solution.py:21
  33.7 0.2 collective-permute-start.10
  33.9 0.2 shard_map.98
  34.1 0.7 %collective-permute-start.14 = (bf16[4,8,4,4,256]{4,3,2,1,0:T(4,128)(2,1)S(1)}, bf16[4,8,4,4,256]{4,3,2,1,0:T(4,128)(2,1)S(1)}, u32[]{:S(2)}, u32[]{:S(2)}) collective-permute-start(bf16[4,8,4,4,256]{4,3,2,1,0:T(4,128)(2,1)S(1)} %get-tuple-element.52), channel_id=1, source_target_pairs={{0,1},{1,0},{2,3},{3,2},{4,5},{5,4},{6,7},{7,6},{8,9},{9,8},{10,11... | collective-permute-start | bytes 786440 | tf_op jit(solution)/shard_map/ppermute | solution.py:21
  34.8 3.0 %collective-permute-start.15 = (bf16[4,8,4,4,256]{4,3,2,1,0:T(4,128)(2,1)S(1)}, bf16[4,8,4,4,256]{4,3,2,1,0:T(4,128)(2,1)S(1)}, u32[]{:S(2)}, u32[]{:S(2)}) collective-permute-start(bf16[4,8,4,4,256]{4,3,2,1,0:T(4,128)(2,1)S(1)} %get-tuple-element.53), channel_id=1, source_target_pairs={{1,2},{2,1},{5,6},{6,5},{9,10},{10,9},{13,14},{14,13},{17,18},{18,... | collective-permute-start | bytes 786440 | tf_op jit(solution)/shard_map/ppermute | solution.py:28
  37.9 0.9 %shard_map.95 = (bf16[6,512,256]{2,1,0:T(8,128)(2,1)S(1)}, f32[64,128]{1,0:T(8,128)S(1)}, f32[8,128]{1,0:T(8,128)}) custom-call(bf16[2,40,512]{2,1,0:T(8,128)(2,1)S(1)} %get-tuple-element.37.first.refs_0_, bf16[2,40,512]{2,1,0:T(8,128)(2,1)S(1)} %collective-permute-done.2.second.refs_1_, ...), custom_call_target="tpu_custom_call" | custom-call | tf_op jit(solution)/shard_map/pallas_call | solution.py:680
  38.8 2.2 %shard_map.99 = (bf16[9,128,256]{2,1,0:T(8,128)(2,1)S(1)}, bf16[2,8,112,256]{3,2,1,0:T(8,128)(2,1)S(1)}, f32[8,128]{1,0:T(8,128)S(1)}) custom-call(f32[64,128]{1,0:T(8,128)S(1)} %get-tuple-element.45.num_ref.refs_2_, bf16[6,512,256]{2,1,0:T(8,128)(2,1)S(1)} %get-tuple-element.54.blocks_ref.refs_16_, bf16[2,40,512]{2,1,0:T(8,128)(2,1)S(1)} %get-tuple-element.37.first.refs_0_, ...), custom_call_target="tpu_custom_call" | custom-call | tf_op jit(solution)/shard_map/pallas_call | solution.py:680
  41.0 2.1 %collective-permute-done.10.refs_0_.refs_8_ = bf16[1,8,24,256]{3,2,1,0:T(8,128)(2,1)S(1)} collective-permute-done((bf16[1,8,24,256]{3,2,1,0:T(8,128)(2,1)S(1)}, bf16[1,8,24,256]{3,2,1,0:T(8,128)(2,1)S(1)}, u32[]{:S(2)}, u32[]{:S(2)}) %collective-permute-start.10) | collective-permute-done | bytes 98336 | tf_op jit(solution)/shard_map/ppermute | solution.py:21
  43.1 0.2 shard_map.100
  43.3 0.9 %collective-permute-start.16 = (bf16[4,8,3,4,256]{4,3,2,1,0:T(4,128)(2,1)S(1)}, bf16[4,8,3,4,256]{4,3,2,1,0:T(4,128)(2,1)S(1)}, u32[]{:S(2)}, u32[]{:S(2)}) collective-permute-start(bf16[4,8,3,4,256]{4,3,2,1,0:T(4,128)(2,1)S(1)} %get-tuple-element.57), channel_id=1, source_target_pairs={{0,1},{1,0},{2,3},{3,2},{4,5},{5,4},{6,7},{7,6},{8,9},{9,8},{10,11... | collective-permute-start | bytes 589832 | tf_op jit(solution)/shard_map/ppermute | solution.py:21
  44.2 3.2 %collective-permute-start.17 = (bf16[4,8,3,4,256]{4,3,2,1,0:T(4,128)(2,1)S(1)}, bf16[4,8,3,4,256]{4,3,2,1,0:T(4,128)(2,1)S(1)}, u32[]{:S(2)}, u32[]{:S(2)}) collective-permute-start(bf16[4,8,3,4,256]{4,3,2,1,0:T(4,128)(2,1)S(1)} %get-tuple-element.58), channel_id=1, source_target_pairs={{1,2},{2,1},{5,6},{6,5},{9,10},{10,9},{13,14},{14,13},{17,18},{18,... | collective-permute-start | bytes 589832 | tf_op jit(solution)/shard_map/ppermute | solution.py:28
  47.5 2.6 %shard_map.101 = (bf16[2,8,112,256]{3,2,1,0:T(8,128)(2,1)S(1)}, f32[8,128]{1,0:T(8,128)}) custom-call(f32[64,128]{1,0:T(8,128)S(1)} %get-tuple-element.45.num_ref.refs_2_, bf16[6,512,256]{2,1,0:T(8,128)(2,1)S(1)} %get-tuple-element.54.blocks_ref.refs_16_, bf16[9,128,256]{2,1,0:T(8,128)(2,1)S(1)} %get-tuple-element.60.frame_ref.refs_17_, ...), custom_call_target="tpu_custom_call" | custom-call | tf_op jit(solution)/shard_map/pallas_call | solution.py:680
  50.1 1.1 %collective-permute-done.17.refs_13_ = bf16[4,8,3,4,256]{4,3,2,1,0:T(4,128)(2,1)S(1)} collective-permute-done((bf16[4,8,3,4,256]{4,3,2,1,0:T(4,128)(2,1)S(1)}, bf16[4,8,3,4,256]{4,3,2,1,0:T(4,128)(2,1)S(1)}, u32[]{:S(2)}, u32[]{:S(2)}) %collective-permute-start.17) | collective-permute-done | bytes 196640 | tf_op jit(solution)/shard_map/ppermute | solution.py:28
  51.2 8.4 %shard_map.102 = f32[4,8,512]{2,1,0:T(8,128)} custom-call(f32[4,16]{1,0:T(4,128)S(1)} %copy-done.1, bf16[2,40,512]{2,1,0:T(8,128)(2,1)S(1)} %get-tuple-element.37.first.refs_0_, bf16[4,40,512]{2,1,0:T(8,128)(2,1)S(1)} %collective-permute-done.6.refs_2_.refs_1_, f32[64,128]{1,0:T(8,128)S(1)} %get-tuple-element.45.num_ref.refs_2_, f32[4,8,512]{2,1,0:T(8,128)S(1)} %copy-done, ...), custom_call_target="tpu_custom_call" | custom-call | tf_op jit(solution)/shard_map/pallas_call | solution.py:680
  (20 shorter events, 0.4 us)
Async XLA Ops:
  2.3 4.7 %collective-permute-start = (bf16[4,4,8,2048]{3,2,1,0:T(8,128)(2,1)S(1)}, bf16[4,4,8,2048]{3,2,1,0:T(8,128)(2,1)S(1)}, u32[]{:S(2)}, u32[]{:S(2)}) collective-permute-start(bf16[4,4,8,2048]{3,2,1,0:T(8,128)(2,1)S(1)} %get-tuple-element.35), channel_id=1, source_target_pairs={{0,1},{1,0},{2,3},{3,2},{4,5},{5,4},{6,7},{7,6},{8,9},{9,8},{10,11... | collective-permute-start | bytes 1572872 | tf_op jit(solution)/shard_map/ppermute | solution.py:21
  2.5 4.6 %collective-permute-start.1 = (bf16[40,512]{1,0:T(8,128)(2,1)S(1)}, bf16[40,512]{1,0:T(8,128)(2,1)S(1)}, u32[]{:S(2)}, u32[]{:S(2)}) collective-permute-start(bf16[40,512]{1,0:T(8,128)(2,1)S(1)} %get-tuple-element.36.refs_2_), channel_id=1, source_target_pairs={{0,8},{8,0},{16,24},{24,16},{1,9},{9,1},{17,25},{25,17},{2,10},{10... | collective-permute-start | bytes 122888 | tf_op jit(solution)/shard_map/ppermute | solution.py:21
  7.2 4.7 %collective-permute-start.3 = (bf16[4,8,2048]{2,1,0:T(8,128)(2,1)S(1)}, bf16[4,8,2048]{2,1,0:T(8,128)(2,1)S(1)}, u32[]{:S(2)}, u32[]{:S(2)}) collective-permute-start(bf16[4,8,2048]{2,1,0:T(8,128)(2,1)S(1)} %get-tuple-element.39), channel_id=1, source_target_pairs={{0,2},{1,3},{2,0},{3,1},{4,6},{5,7},{6,4},{7,5},{8,10},{9,11},{10,... | collective-permute-start | bytes 393224 | tf_op jit(solution)/shard_map/ppermute | solution.py:21
  8.2 4.1 %collective-permute-start.4 = (bf16[4,8,2048]{2,1,0:T(8,128)(2,1)S(1)}, bf16[4,8,2048]{2,1,0:T(8,128)(2,1)S(1)}, u32[]{:S(2)}, u32[]{:S(2)}) collective-permute-start(bf16[4,8,2048]{2,1,0:T(8,128)(2,1)S(1)} %get-tuple-element.40), channel_id=1, source_target_pairs={{0,4},{1,5},{2,6},{3,7},{4,0},{5,1},{6,2},{7,3},{8,12},{9,13},{10,... | collective-permute-start | bytes 393224 | tf_op jit(solution)/shard_map/ppermute | solution.py:21
  9.4 6.0 %collective-permute-start.5 = (bf16[4,8,2048]{2,1,0:T(8,128)(2,1)S(1)}, bf16[4,8,2048]{2,1,0:T(8,128)(2,1)S(1)}, u32[]{:S(2)}, u32[]{:S(2)}) collective-permute-start(bf16[4,8,2048]{2,1,0:T(8,128)(2,1)S(1)} %get-tuple-element.41), channel_id=1, source_target_pairs={{0,6},{1,7},{2,4},{3,5},{4,2},{5,3},{6,0},{7,1},{8,14},{9,15},{10,... | collective-permute-start | bytes 393224 | tf_op jit(solution)/shard_map/ppermute | solution.py:21
  9.9 5.7 %collective-permute-start.2 = (bf16[2,40,512]{2,1,0:T(8,128)(2,1)S(1)}, bf16[2,40,512]{2,1,0:T(8,128)(2,1)S(1)}, u32[]{:S(2)}, u32[]{:S(2)}) collective-permute-start(bf16[2,40,512]{2,1,0:T(8,128)(2,1)S(1)} %get-tuple-element.37.first.refs_0_), channel_id=1, source_target_pairs={{0,16},{8,24},{16,0},{24,8},{1,17},{9,25},{17,1},{25,9},{2,18},{10... | collective-permute-start | bytes 245768 | tf_op jit(solution)/shard_map/ppermute | solution.py:21
  15.7 7.4 %collective-permute-start.6 = (bf16[4,40,512]{2,1,0:T(8,128)(2,1)S(1)}, bf16[4,40,512]{2,1,0:T(8,128)(2,1)S(1)}, u32[]{:S(2)}, u32[]{:S(2)}) collective-permute-start(bf16[4,40,512]{2,1,0:T(8,128)(2,1)S(1)} %shard_map.94), channel_id=1, source_target_pairs={{0,4},{4,0},{1,5},{5,1},{2,6},{6,2},{3,7},{7,3},{8,12},{12,8},{9,1... | collective-permute-start | bytes 491528 | tf_op jit(solution)/shard_map/ppermute | solution.py:21
  15.7 6.7 %collective-permute-start.8 = (bf16[8,32,256]{2,1,0:T(8,128)(2,1)S(1)}, bf16[8,32,256]{2,1,0:T(8,128)(2,1)S(1)}, u32[]{:S(2)}, u32[]{:S(2)}) collective-permute-start(bf16[8,32,256]{2,1,0:T(8,128)(2,1)S(1)} %get-tuple-element.46), channel_id=1, source_target_pairs={{0,16},{8,24},{16,0},{24,8},{1,17},{9,25},{17,1},{25,9},{2,18},{10... | collective-permute-start | bytes 393224 | tf_op jit(solution)/shard_map/ppermute | solution.py:21
  18.6 9.8 %collective-permute-start.7 = (bf16[8,32,256]{2,1,0:T(8,128)(2,1)S(1)}, bf16[8,32,256]{2,1,0:T(8,128)(2,1)S(1)}, u32[]{:S(2)}, u32[]{:S(2)}) collective-permute-start(bf16[8,32,256]{2,1,0:T(8,128)(2,1)S(1)} %get-tuple-element.44.refs_0_.refs_4_), channel_id=1, source_target_pairs={{0,8},{8,0},{16,24},{24,16},{1,9},{9,1},{17,25},{25,17},{2,10},{10... | collective-permute-start | bytes 393224 | tf_op jit(solution)/shard_map/ppermute | solution.py:21
  22.4 6.0 %collective-permute-start.9 = (bf16[8,32,256]{2,1,0:T(8,128)(2,1)S(1)}, bf16[8,32,256]{2,1,0:T(8,128)(2,1)S(1)}, u32[]{:S(2)}, u32[]{:S(2)}) collective-permute-start(bf16[8,32,256]{2,1,0:T(8,128)(2,1)S(1)} %collective-permute-done.8.refs_1_.refs_2_.refs_6_), channel_id=1, source_target_pairs={{0,8},{8,0},{16,24},{24,16},{1,9},{9,1},{17,25},{25,17},{2,10},{10... | collective-permute-start | bytes 393224 | tf_op jit(solution)/shard_map/ppermute | solution.py:21
  23.7 4.7 %collective-permute-start.11 = (bf16[4,8,4,512]{3,2,1,0:T(4,128)(2,1)S(1)}, bf16[4,8,4,512]{3,2,1,0:T(4,128)(2,1)S(1)}, u32[]{:S(2)}, u32[]{:S(2)}) collective-permute-start(bf16[4,8,4,512]{3,2,1,0:T(4,128)(2,1)S(1)} %get-tuple-element.48), channel_id=1, source_target_pairs={{0,1},{1,0},{2,3},{3,2},{4,5},{5,4},{6,7},{7,6},{8,9},{9,8},{10,11... | collective-permute-start | bytes 393224 | tf_op jit(solution)/shard_map/ppermute | solution.py:21
  27.2 5.1 %collective-permute-start.12 = (bf16[4,8,4,512]{3,2,1,0:T(4,128)(2,1)S(1)}, bf16[4,8,4,512]{3,2,1,0:T(4,128)(2,1)S(1)}, u32[]{:S(2)}, u32[]{:S(2)}) collective-permute-start(bf16[4,8,4,512]{3,2,1,0:T(4,128)(2,1)S(1)} %get-tuple-element.49), channel_id=1, source_target_pairs={{0,3},{1,2},{2,1},{3,0},{4,7},{5,6},{6,5},{7,4},{8,11},{9,10},{10,... | collective-permute-start | bytes 393224 | tf_op jit(solution)/shard_map/ppermute | solution.py:21
  32.4 10.8 %collective-permute-start.13 = (bf16[3,8,24,256]{3,2,1,0:T(8,128)(2,1)S(1)}, bf16[3,8,24,256]{3,2,1,0:T(8,128)(2,1)S(1)}, u32[]{:S(2)}, u32[]{:S(2)}) collective-permute-start(bf16[3,8,24,256]{3,2,1,0:T(8,128)(2,1)S(1)} %get-tuple-element.50), channel_id=1, source_target_pairs={{0,4},{4,0},{1,5},{5,1},{2,6},{6,2},{3,7},{7,3},{8,12},{12,8},{9,1... | collective-permute-start | bytes 884744 | tf_op jit(solution)/shard_map/ppermute | solution.py:21
  33.7 9.4 %collective-permute-start.10 = (bf16[1,8,24,256]{3,2,1,0:T(8,128)(2,1)S(1)}, bf16[1,8,24,256]{3,2,1,0:T(8,128)(2,1)S(1)}, u32[]{:S(2)}, u32[]{:S(2)}) collective-permute-start(bf16[1,8,24,256]{3,2,1,0:T(8,128)(2,1)S(1)} %get-tuple-element.47), channel_id=1, source_target_pairs={{0,4},{4,0},{1,5},{5,1},{2,6},{6,2},{3,7},{7,3},{8,12},{12,8},{9,1... | collective-permute-start | bytes 294920 | tf_op jit(solution)/shard_map/ppermute | solution.py:21
  34.1 16.0 %collective-permute-start.14 = (bf16[4,8,4,4,256]{4,3,2,1,0:T(4,128)(2,1)S(1)}, bf16[4,8,4,4,256]{4,3,2,1,0:T(4,128)(2,1)S(1)}, u32[]{:S(2)}, u32[]{:S(2)}) collective-permute-start(bf16[4,8,4,4,256]{4,3,2,1,0:T(4,128)(2,1)S(1)} %get-tuple-element.52), channel_id=1, source_target_pairs={{0,1},{1,0},{2,3},{3,2},{4,5},{5,4},{6,7},{7,6},{8,9},{9,8},{10,11... | collective-permute-start | bytes 786440 | tf_op jit(solution)/shard_map/ppermute | solution.py:21
  34.8 15.3 %collective-permute-start.15 = (bf16[4,8,4,4,256]{4,3,2,1,0:T(4,128)(2,1)S(1)}, bf16[4,8,4,4,256]{4,3,2,1,0:T(4,128)(2,1)S(1)}, u32[]{:S(2)}, u32[]{:S(2)}) collective-permute-start(bf16[4,8,4,4,256]{4,3,2,1,0:T(4,128)(2,1)S(1)} %get-tuple-element.53), channel_id=1, source_target_pairs={{1,2},{2,1},{5,6},{6,5},{9,10},{10,9},{13,14},{14,13},{17,18},{18,... | collective-permute-start | bytes 786440 | tf_op jit(solution)/shard_map/ppermute | solution.py:28
  41.0 10.2 %copy-start = (f32[4,8,512]{2,1,0:T(8,128)S(1)}, f32[4,8,512]{2,1,0:T(8,128)}, u32[]{:S(2)}) copy-start(f32[4,8,512]{2,1,0:T(8,128)} %refs_3_.1) | copy-start | bytes 196612
  41.0 10.2 %copy-start.1 = (f32[4,16]{1,0:T(4,128)S(1)}, f32[4,16]{1,0:T(4,128)}, u32[]{:S(2)}) copy-start(f32[4,16]{1,0:T(4,128)} %table_ref.1) | copy-start | bytes 772
  43.3 6.8 %collective-permute-start.16 = (bf16[4,8,3,4,256]{4,3,2,1,0:T(4,128)(2,1)S(1)}, bf16[4,8,3,4,256]{4,3,2,1,0:T(4,128)(2,1)S(1)}, u32[]{:S(2)}, u32[]{:S(2)}) collective-permute-start(bf16[4,8,3,4,256]{4,3,2,1,0:T(4,128)(2,1)S(1)} %get-tuple-element.57), channel_id=1, source_target_pairs={{0,1},{1,0},{2,3},{3,2},{4,5},{5,4},{6,7},{7,6},{8,9},{9,8},{10,11... | collective-permute-start | bytes 589832 | tf_op jit(solution)/shard_map/ppermute | solution.py:21
  44.2 7.0 %collective-permute-start.17 = (bf16[4,8,3,4,256]{4,3,2,1,0:T(4,128)(2,1)S(1)}, bf16[4,8,3,4,256]{4,3,2,1,0:T(4,128)(2,1)S(1)}, u32[]{:S(2)}, u32[]{:S(2)}) collective-permute-start(bf16[4,8,3,4,256]{4,3,2,1,0:T(4,128)(2,1)S(1)} %get-tuple-element.58), channel_id=1, source_target_pairs={{1,2},{2,1},{5,6},{6,5},{9,10},{10,9},{13,14},{14,13},{17,18},{18,... | collective-permute-start | bytes 589832 | tf_op jit(solution)/shard_map/ppermute | solution.py:28

commit v11 on v10

--- a/solution.py
+++ b/solution.py
@@ -215,14 +215,14 @@
         out_ref[v] = ref[..., rows, :]
 
 
-def edges_kernel(height, depth, sides, paired, *refs):
+def edges_kernel(height, depth, sides, paired, unread, *refs):
     out1, out2, done_ref = refs[-3:]
     done_ref[...] = jnp.zeros(done_ref.shape, F32)
     count = out1.shape[0]
     views = refs[:count] if depth else [None] * count
-    fars = refs[count if depth else 0 : -4]
+    fars = refs[count if depth else 0 : -4 - unread]
     if paired:
-        views, fars = views_of(*refs[:2]), refs[2:-4]
+        views, fars = views_of(*refs[:2]), refs[2 : -4 - unread]
     half = height // 2
     gy = lax.axis_index("gy")
     even = gy % 2 == 0
@@ -740,7 +740,7 @@
             *tokens,
         )
 
-    def edges(arrays, fars, token, slices, dims):
+    def edges(arrays, fars, token, slices, dims, unread=()):
         out = resident(4, *dims[:-2], slices, height // 2, dims[-1])
         return call(
             functools.partial(
@@ -749,12 +749,14 @@
                 depth if arrays else 0,
                 len(sides),
                 len(arrays) == 2,
+                len(unread),
             ),
             (out, out, mark),
-            [vmem] * (len(arrays) + len(fars)) + [free],
+            [vmem] * (len(arrays) + len(fars) + len(unread)) + [free],
             (vmem, vmem, vmem),
             *arrays,
             *fars,
+            *unread,
             token,
         )
 
@@ -811,14 +813,21 @@
 
     def others(slices):
         rows, done = stack(
-            (near, opposite, last), slices, total_done, one_est, two_est
+            (near, opposite, last), slices, total_done
         )
         tokens.append(done)
         return rows
 
     far_others = exchange_z(frame, others, slabs, 3)
     far_others = [far_others[s] for s in sides]
-    own_edges = edges((plain, near, opposite, last), (), tokens[-1], depth, plain.shape)
+    own_edges = edges(
+        (plain, near, opposite, last),
+        (),
+        tokens[-1],
+        depth,
+        plain.shape,
+        (one_est, two_est),
+    )
     near_halo = core_side(own_edges, bands, False)
     est_frame, recip_a, token = call(
         functools.partial(start_kernel, frame, tiles, sides, (0, 1)),

time: 59.8 us -> 63.8 us (1.067)
  waiting for transfers between devices: 15.1 us -> 20 us
  starting transfers between devices: 26.5 us -> 25.6 us
    ppermute x16, waiting for transfers between devices: 14 us -> 19 us  [swap(): return lax.ppermute(array, axis, [(i, i ^ mask) for i in range(size)])]
  transfers between devices with their start and end apart: 18 -> 18, of which waited for: 7 -> 10; matrix products, arithmetic and copies ran while one was open for 0% -> 0% of each run, Pallas kernels for 12% -> 11%
where the time goes in v11:
time: 63.8 us; the launch traced here: 63.7 us
  starting transfers between devices  25.6 us (40%)
  waiting for transfers between devices  20 us (31%)
  Pallas kernels  17.2 us (27%)
  between operations  0.81 us (1%)
    ppermute x16, starting transfers between devices, swap(): return lax.ppermute(array, axis, [(i, i ^ mask) for i in range(size)])  19.9 us
    ppermute x16, waiting for transfers between devices, swap(): return lax.ppermute(array, axis, [(i, i ^ mask) for i in range(size)])  19 us
    pallas_call x12, Pallas kernels, call(): pl.pallas_call(kernel, out_shape=shapes, in_specs=whole(*ins), out_specs=...  17.2 us
    ppermute x2, starting transfers between devices, core_side(): return (first, lax.ppermute(own[1], 'gy', [(1, 2), (2, 1)]))  5.74 us
  transfers between devices with their start and end apart: 18, of which 10 were waited for; matrix products, arithmetic and copies ran while one was open for 0% of the time, Pallas kernels for 11%

profile of v11, /device:TPU:1, one launch (start us, length us, event | category | flops | bytes accessed | tf_op | source)
XLA Modules:
  0.0 63.7 jit_solution(9814260510342189571)
XLA Ops:
  0.7 1.7 %shard_map.91 = (bf16[4,4,8,2048]{3,2,1,0:T(8,128)(2,1)S(1)}, bf16[4,4,8,2048]{3,2,1,0:T(8,128)(2,1)S(1)}, bf16[40,512]{1,0:T(8,128)(2,1)S(1)}) custom-call(s32[1,1,16]{2,1,0:T(1,128)} %bitcast.5, s32[1,16]{1,0:T(1,128)} %row_ref.1, f32[1]{0:T(128)S(6)} %copy.10.bg_ref, s32[4,4]{1,0:T(4,128)} %index_ref.1, bf16[16,8,2048]{2,1,0:T(8,128)(2,1)} %bitcast.3, ...), custom_call_target="tpu_custom_call" | custom-call | tf_op jit(solution)/shard_map/pallas_call | solution.py:680
  2.3 0.1 collective-permute-start
  2.5 2.8 %collective-permute-start.1 = (bf16[40,512]{1,0:T(8,128)(2,1)S(1)}, bf16[40,512]{1,0:T(8,128)(2,1)S(1)}, u32[]{:S(2)}, u32[]{:S(2)}) collective-permute-start(bf16[40,512]{1,0:T(8,128)(2,1)S(1)} %get-tuple-element.36.refs_2_), channel_id=1, source_target_pairs={{0,8},{8,0},{16,24},{24,16},{1,9},{9,1},{17,25},{25,17},{2,10},{10... | collective-permute-start | bytes 122888 | tf_op jit(solution)/shard_map/ppermute | solution.py:21
  5.2 1.8 %collective-permute-done.1.refs_3_ = bf16[40,512]{1,0:T(8,128)(2,1)S(1)} collective-permute-done((bf16[40,512]{1,0:T(8,128)(2,1)S(1)}, bf16[40,512]{1,0:T(8,128)(2,1)S(1)}, u32[]{:S(2)}, u32[]{:S(2)}) %collective-permute-start.1) | collective-permute-done | bytes 40992 | tf_op jit(solution)/shard_map/ppermute | solution.py:21
  7.1 0.1 shard_map.92
  7.2 1.0 %collective-permute-start.3 = (bf16[4,8,2048]{2,1,0:T(8,128)(2,1)S(1)}, bf16[4,8,2048]{2,1,0:T(8,128)(2,1)S(1)}, u32[]{:S(2)}, u32[]{:S(2)}) collective-permute-start(bf16[4,8,2048]{2,1,0:T(8,128)(2,1)S(1)} %get-tuple-element.39), channel_id=1, source_target_pairs={{0,2},{1,3},{2,0},{3,1},{4,6},{5,7},{6,4},{7,5},{8,10},{9,11},{10,... | collective-permute-start | bytes 393224 | tf_op jit(solution)/shard_map/ppermute | solution.py:21
  8.2 1.2 %collective-permute-start.4 = (bf16[4,8,2048]{2,1,0:T(8,128)(2,1)S(1)}, bf16[4,8,2048]{2,1,0:T(8,128)(2,1)S(1)}, u32[]{:S(2)}, u32[]{:S(2)}) collective-permute-start(bf16[4,8,2048]{2,1,0:T(8,128)(2,1)S(1)} %get-tuple-element.40), channel_id=1, source_target_pairs={{0,4},{1,5},{2,6},{3,7},{4,0},{5,1},{6,2},{7,3},{8,12},{9,13},{10,... | collective-permute-start | bytes 393224 | tf_op jit(solution)/shard_map/ppermute | solution.py:21
  9.4 0.5 collective-permute-start.5
  9.9 1.7 %collective-permute-done.3.refs_1_ = bf16[4,8,2048]{2,1,0:T(8,128)(2,1)S(1)} collective-permute-done((bf16[4,8,2048]{2,1,0:T(8,128)(2,1)S(1)}, bf16[4,8,2048]{2,1,0:T(8,128)(2,1)S(1)}, u32[]{:S(2)}, u32[]{:S(2)}) %collective-permute-start.3) | collective-permute-done | bytes 131104 | tf_op jit(solution)/shard_map/ppermute | solution.py:21
  11.7 0.7 %collective-permute-done.4.refs_2_ = bf16[4,8,2048]{2,1,0:T(8,128)(2,1)S(1)} collective-permute-done((bf16[4,8,2048]{2,1,0:T(8,128)(2,1)S(1)}, bf16[4,8,2048]{2,1,0:T(8,128)(2,1)S(1)}, u32[]{:S(2)}, u32[]{:S(2)}) %collective-permute-start.4) | collective-permute-done | bytes 131104 | tf_op jit(solution)/shard_map/ppermute | solution.py:21
  12.3 3.1 %collective-permute-done.5.refs_3_ = bf16[4,8,2048]{2,1,0:T(8,128)(2,1)S(1)} collective-permute-done((bf16[4,8,2048]{2,1,0:T(8,128)(2,1)S(1)}, bf16[4,8,2048]{2,1,0:T(8,128)(2,1)S(1)}, u32[]{:S(2)}, u32[]{:S(2)}) %collective-permute-start.5) | collective-permute-done | bytes 131104 | tf_op jit(solution)/shard_map/ppermute | solution.py:21
  15.4 0.2 shard_map.93
  15.6 2.8 %collective-permute-start.8 = (bf16[8,32,256]{2,1,0:T(8,128)(2,1)S(1)}, bf16[8,32,256]{2,1,0:T(8,128)(2,1)S(1)}, u32[]{:S(2)}, u32[]{:S(2)}) collective-permute-start(bf16[8,32,256]{2,1,0:T(8,128)(2,1)S(1)} %get-tuple-element.46), channel_id=1, source_target_pairs={{0,16},{8,24},{16,0},{24,8},{1,17},{9,25},{17,1},{25,9},{2,18},{10... | collective-permute-start | bytes 393224 | tf_op jit(solution)/shard_map/ppermute | solution.py:21
  18.5 1.3 %collective-permute-start.7 = (bf16[8,32,256]{2,1,0:T(8,128)(2,1)S(1)}, bf16[8,32,256]{2,1,0:T(8,128)(2,1)S(1)}, u32[]{:S(2)}, u32[]{:S(2)}) collective-permute-start(bf16[8,32,256]{2,1,0:T(8,128)(2,1)S(1)} %get-tuple-element.44.refs_0_.refs_4_), channel_id=1, source_target_pairs={{0,8},{8,0},{16,24},{24,16},{1,9},{9,1},{17,25},{25,17},{2,10},{10... | collective-permute-start | bytes 393224 | tf_op jit(solution)/shard_map/ppermute | solution.py:21
  19.8 2.9 %collective-permute-done.8.refs_1_.refs_2_.refs_6_ = bf16[8,32,256]{2,1,0:T(8,128)(2,1)S(1)} collective-permute-done((bf16[8,32,256]{2,1,0:T(8,128)(2,1)S(1)}, bf16[8,32,256]{2,1,0:T(8,128)(2,1)S(1)}, u32[]{:S(2)}, u32[]{:S(2)}) %collective-permute-start.8) | collective-permute-done | bytes 131104 | tf_op jit(solution)/shard_map/ppermute | solution.py:21
  22.7 4.8 %collective-permute-start.9 = (bf16[8,32,256]{2,1,0:T(8,128)(2,1)S(1)}, bf16[8,32,256]{2,1,0:T(8,128)(2,1)S(1)}, u32[]{:S(2)}, u32[]{:S(2)}) collective-permute-start(bf16[8,32,256]{2,1,0:T(8,128)(2,1)S(1)} %collective-permute-done.8.refs_1_.refs_2_.refs_6_), channel_id=1, source_target_pairs={{0,8},{8,0},{16,24},{24,16},{1,9},{9,1},{17,25},{25,17},{2,10},{10... | collective-permute-start | bytes 393224 | tf_op jit(solution)/shard_map/ppermute | solution.py:21
  27.5 0.1 collective-permute-done.2.second.refs_1_
  27.7 2.2 %collective-permute-done.9.refs_2_.refs_3_.refs_7_ = bf16[8,32,256]{2,1,0:T(8,128)(2,1)S(1)} collective-permute-done((bf16[8,32,256]{2,1,0:T(8,128)(2,1)S(1)}, bf16[8,32,256]{2,1,0:T(8,128)(2,1)S(1)}, u32[]{:S(2)}, u32[]{:S(2)}) %collective-permute-start.9) | collective-permute-done | bytes 131104 | tf_op jit(solution)/shard_map/ppermute | solution.py:21
  30.0 2.1 %collective-permute-done.6.refs_2_.refs_1_ = bf16[4,40,512]{2,1,0:T(8,128)(2,1)S(1)} collective-permute-done((bf16[4,40,512]{2,1,0:T(8,128)(2,1)S(1)}, bf16[4,40,512]{2,1,0:T(8,128)(2,1)S(1)}, u32[]{:S(2)}, u32[]{:S(2)}) %collective-permute-start.6) | collective-permute-done | bytes 163872 | tf_op jit(solution)/shard_map/ppermute | solution.py:21
  32.1 0.6 shard_map.97
  32.7 4.0 %collective-permute-start.12 = (bf16[4,8,4,512]{3,2,1,0:T(4,128)(2,1)S(1)}, bf16[4,8,4,512]{3,2,1,0:T(4,128)(2,1)S(1)}, u32[]{:S(2)}, u32[]{:S(2)}) collective-permute-start(bf16[4,8,4,512]{3,2,1,0:T(4,128)(2,1)S(1)} %get-tuple-element.49), channel_id=1, source_target_pairs={{0,1},{1,0},{2,3},{3,2},{4,5},{5,4},{6,7},{7,6},{8,9},{9,8},{10,11... | collective-permute-start | bytes 393224 | tf_op jit(solution)/shard_map/ppermute | solution.py:21
  36.7 1.1 %collective-permute-start.10 = (bf16[1,8,24,256]{3,2,1,0:T(8,128)(2,1)S(1)}, bf16[1,8,24,256]{3,2,1,0:T(8,128)(2,1)S(1)}, u32[]{:S(2)}, u32[]{:S(2)}) collective-permute-start(bf16[1,8,24,256]{3,2,1,0:T(8,128)(2,1)S(1)} %get-tuple-element.47), channel_id=1, source_target_pairs={{0,4},{4,0},{1,5},{5,1},{2,6},{6,2},{3,7},{7,3},{8,12},{12,8},{9,1... | collective-permute-start | bytes 294920 | tf_op jit(solution)/shard_map/ppermute | solution.py:21
  37.8 4.3 %collective-permute-done.13.refs_5_.refs_4_ = bf16[4,8,4,512]{3,2,1,0:T(4,128)(2,1)S(1)} collective-permute-done((bf16[4,8,4,512]{3,2,1,0:T(4,128)(2,1)S(1)}, bf16[4,8,4,512]{3,2,1,0:T(4,128)(2,1)S(1)}, u32[]{:S(2)}, u32[]{:S(2)}) %collective-permute-start.13) | collective-permute-done | bytes 131104 | tf_op jit(solution)/shard_map/ppermute | solution.py:21
  42.1 0.2 shard_map.98
  42.4 2.4 %collective-permute-start.15 = (bf16[4,8,4,4,256]{4,3,2,1,0:T(4,128)(2,1)S(1)}, bf16[4,8,4,4,256]{4,3,2,1,0:T(4,128)(2,1)S(1)}, u32[]{:S(2)}, u32[]{:S(2)}) collective-permute-start(bf16[4,8,4,4,256]{4,3,2,1,0:T(4,128)(2,1)S(1)} %get-tuple-element.53), channel_id=1, source_target_pairs={{1,2},{2,1},{5,6},{6,5},{9,10},{10,9},{13,14},{14,13},{17,18},{18,... | collective-permute-start | bytes 786440 | tf_op jit(solution)/shard_map/ppermute | solution.py:28
  44.8 0.9 %shard_map.95 = (bf16[6,512,256]{2,1,0:T(8,128)(2,1)S(1)}, f32[64,128]{1,0:T(8,128)S(1)}, f32[8,128]{1,0:T(8,128)}) custom-call(bf16[2,40,512]{2,1,0:T(8,128)(2,1)S(1)} %get-tuple-element.37.first.refs_0_, bf16[2,40,512]{2,1,0:T(8,128)(2,1)S(1)} %collective-permute-done.2.second.refs_1_, ...), custom_call_target="tpu_custom_call" | custom-call | tf_op jit(solution)/shard_map/pallas_call | solution.py:680
  45.8 2.2 %shard_map.99 = (bf16[9,128,256]{2,1,0:T(8,128)(2,1)S(1)}, bf16[2,8,112,256]{3,2,1,0:T(8,128)(2,1)S(1)}, f32[8,128]{1,0:T(8,128)S(1)}) custom-call(f32[64,128]{1,0:T(8,128)S(1)} %get-tuple-element.45.num_ref.refs_2_, bf16[6,512,256]{2,1,0:T(8,128)(2,1)S(1)} %get-tuple-element.54.blocks_ref.refs_16_, bf16[2,40,512]{2,1,0:T(8,128)(2,1)S(1)} %get-tuple-element.37.first.refs_0_, ...), custom_call_target="tpu_custom_call" | custom-call | tf_op jit(solution)/shard_map/pallas_call | solution.py:680
  48.0 0.2 shard_map.100
  48.3 3.4 %collective-permute-start.17 = (bf16[4,8,3,4,256]{4,3,2,1,0:T(4,128)(2,1)S(1)}, bf16[4,8,3,4,256]{4,3,2,1,0:T(4,128)(2,1)S(1)}, u32[]{:S(2)}, u32[]{:S(2)}) collective-permute-start(bf16[4,8,3,4,256]{4,3,2,1,0:T(4,128)(2,1)S(1)} %get-tuple-element.58), channel_id=1, source_target_pairs={{1,2},{2,1},{5,6},{6,5},{9,10},{10,9},{13,14},{14,13},{17,18},{18,... | collective-permute-start | bytes 589832 | tf_op jit(solution)/shard_map/ppermute | solution.py:28
  51.6 2.6 %shard_map.101 = (bf16[2,8,112,256]{3,2,1,0:T(8,128)(2,1)S(1)}, f32[8,128]{1,0:T(8,128)}) custom-call(f32[64,128]{1,0:T(8,128)S(1)} %get-tuple-element.45.num_ref.refs_2_, bf16[6,512,256]{2,1,0:T(8,128)(2,1)S(1)} %get-tuple-element.54.blocks_ref.refs_16_, bf16[9,128,256]{2,1,0:T(8,128)(2,1)S(1)} %get-tuple-element.60.frame_ref.refs_17_, ...), custom_call_target="tpu_custom_call" | custom-call | tf_op jit(solution)/shard_map/pallas_call | solution.py:680
  54.3 1.0 %collective-permute-done.17.refs_13_ = bf16[4,8,3,4,256]{4,3,2,1,0:T(4,128)(2,1)S(1)} collective-permute-done((bf16[4,8,3,4,256]{4,3,2,1,0:T(4,128)(2,1)S(1)}, bf16[4,8,3,4,256]{4,3,2,1,0:T(4,128)(2,1)S(1)}, u32[]{:S(2)}, u32[]{:S(2)}) %collective-permute-start.17) | collective-permute-done | bytes 196640 | tf_op jit(solution)/shard_map/ppermute | solution.py:28
  55.2 8.4 %shard_map.102 = f32[4,8,512]{2,1,0:T(8,128)} custom-call(f32[4,16]{1,0:T(4,128)S(1)} %copy-done.1, bf16[2,40,512]{2,1,0:T(8,128)(2,1)S(1)} %get-tuple-element.37.first.refs_0_, bf16[4,40,512]{2,1,0:T(8,128)(2,1)S(1)} %collective-permute-done.6.refs_2_.refs_1_, f32[64,128]{1,0:T(8,128)S(1)} %get-tuple-element.45.num_ref.refs_2_, f32[4,8,512]{2,1,0:T(8,128)S(1)} %copy-done, ...), custom_call_target="tpu_custom_call" | custom-call | tf_op jit(solution)/shard_map/pallas_call | solution.py:680
  (20 shorter events, 0.4 us)
Async XLA Ops:
  2.3 4.7 %collective-permute-start = (bf16[4,4,8,2048]{3,2,1,0:T(8,128)(2,1)S(1)}, bf16[4,4,8,2048]{3,2,1,0:T(8,128)(2,1)S(1)}, u32[]{:S(2)}, u32[]{:S(2)}) collective-permute-start(bf16[4,4,8,2048]{3,2,1,0:T(8,128)(2,1)S(1)} %get-tuple-element.35), channel_id=1, source_target_pairs={{0,1},{1,0},{2,3},{3,2},{4,5},{5,4},{6,7},{7,6},{8,9},{9,8},{10,11... | collective-permute-start | bytes 1572872 | tf_op jit(solution)/shard_map/ppermute | solution.py:21
  2.5 4.6 %collective-permute-start.1 = (bf16[40,512]{1,0:T(8,128)(2,1)S(1)}, bf16[40,512]{1,0:T(8,128)(2,1)S(1)}, u32[]{:S(2)}, u32[]{:S(2)}) collective-permute-start(bf16[40,512]{1,0:T(8,128)(2,1)S(1)} %get-tuple-element.36.refs_2_), channel_id=1, source_target_pairs={{0,8},{8,0},{16,24},{24,16},{1,9},{9,1},{17,25},{25,17},{2,10},{10... | collective-permute-start | bytes 122888 | tf_op jit(solution)/shard_map/ppermute | solution.py:21
  7.2 4.4 %collective-permute-start.3 = (bf16[4,8,2048]{2,1,0:T(8,128)(2,1)S(1)}, bf16[4,8,2048]{2,1,0:T(8,128)(2,1)S(1)}, u32[]{:S(2)}, u32[]{:S(2)}) collective-permute-start(bf16[4,8,2048]{2,1,0:T(8,128)(2,1)S(1)} %get-tuple-element.39), channel_id=1, source_target_pairs={{0,2},{1,3},{2,0},{3,1},{4,6},{5,7},{6,4},{7,5},{8,10},{9,11},{10,... | collective-permute-start | bytes 393224 | tf_op jit(solution)/shard_map/ppermute | solution.py:21
  8.2 4.1 %collective-permute-start.4 = (bf16[4,8,2048]{2,1,0:T(8,128)(2,1)S(1)}, bf16[4,8,2048]{2,1,0:T(8,128)(2,1)S(1)}, u32[]{:S(2)}, u32[]{:S(2)}) collective-permute-start(bf16[4,8,2048]{2,1,0:T(8,128)(2,1)S(1)} %get-tuple-element.40), channel_id=1, source_target_pairs={{0,4},{1,5},{2,6},{3,7},{4,0},{5,1},{6,2},{7,3},{8,12},{9,13},{10,... | collective-permute-start | bytes 393224 | tf_op jit(solution)/shard_map/ppermute | solution.py:21
  9.4 6.0 %collective-permute-start.5 = (bf16[4,8,2048]{2,1,0:T(8,128)(2,1)S(1)}, bf16[4,8,2048]{2,1,0:T(8,128)(2,1)S(1)}, u32[]{:S(2)}, u32[]{:S(2)}) collective-permute-start(bf16[4,8,2048]{2,1,0:T(8,128)(2,1)S(1)} %get-tuple-element.41), channel_id=1, source_target_pairs={{0,6},{1,7},{2,4},{3,5},{4,2},{5,3},{6,0},{7,1},{8,14},{9,15},{10,... | collective-permute-start | bytes 393224 | tf_op jit(solution)/shard_map/ppermute | solution.py:21
  15.6 7.0 %collective-permute-start.8 = (bf16[8,32,256]{2,1,0:T(8,128)(2,1)S(1)}, bf16[8,32,256]{2,1,0:T(8,128)(2,1)S(1)}, u32[]{:S(2)}, u32[]{:S(2)}) collective-permute-start(bf16[8,32,256]{2,1,0:T(8,128)(2,1)S(1)} %get-tuple-element.46), channel_id=1, source_target_pairs={{0,16},{8,24},{16,0},{24,8},{1,17},{9,25},{17,1},{25,9},{2,18},{10... | collective-permute-start | bytes 393224 | tf_op jit(solution)/shard_map/ppermute | solution.py:21
  18.4 9.1 %collective-permute-start.2 = (bf16[2,40,512]{2,1,0:T(8,128)(2,1)S(1)}, bf16[2,40,512]{2,1,0:T(8,128)(2,1)S(1)}, u32[]{:S(2)}, u32[]{:S(2)}) collective-permute-start(bf16[2,40,512]{2,1,0:T(8,128)(2,1)S(1)} %get-tuple-element.37.first.refs_0_), channel_id=1, source_target_pairs={{0,16},{8,24},{16,0},{24,8},{1,17},{9,25},{17,1},{25,9},{2,18},{10... | collective-permute-start | bytes 245768 | tf_op jit(solution)/shard_map/ppermute | solution.py:21
  18.5 9.2 %collective-permute-start.7 = (bf16[8,32,256]{2,1,0:T(8,128)(2,1)S(1)}, bf16[8,32,256]{2,1,0:T(8,128)(2,1)S(1)}, u32[]{:S(2)}, u32[]{:S(2)}) collective-permute-start(bf16[8,32,256]{2,1,0:T(8,128)(2,1)S(1)} %get-tuple-element.44.refs_0_.refs_4_), channel_id=1, source_target_pairs={{0,8},{8,0},{16,24},{24,16},{1,9},{9,1},{17,25},{25,17},{2,10},{10... | collective-permute-start | bytes 393224 | tf_op jit(solution)/shard_map/ppermute | solution.py:21
  22.7 7.3 %collective-permute-start.9 = (bf16[8,32,256]{2,1,0:T(8,128)(2,1)S(1)}, bf16[8,32,256]{2,1,0:T(8,128)(2,1)S(1)}, u32[]{:S(2)}, u32[]{:S(2)}) collective-permute-start(bf16[8,32,256]{2,1,0:T(8,128)(2,1)S(1)} %collective-permute-done.8.refs_1_.refs_2_.refs_6_), channel_id=1, source_target_pairs={{0,8},{8,0},{16,24},{24,16},{1,9},{9,1},{17,25},{25,17},{2,10},{10... | collective-permute-start | bytes 393224 | tf_op jit(solution)/shard_map/ppermute | solution.py:21
  27.6 4.5 %collective-permute-start.6 = (bf16[4,40,512]{2,1,0:T(8,128)(2,1)S(1)}, bf16[4,40,512]{2,1,0:T(8,128)(2,1)S(1)}, u32[]{:S(2)}, u32[]{:S(2)}) collective-permute-start(bf16[4,40,512]{2,1,0:T(8,128)(2,1)S(1)} %shard_map.94), channel_id=1, source_target_pairs={{0,4},{4,0},{1,5},{5,1},{2,6},{6,2},{3,7},{7,3},{8,12},{12,8},{9,1... | collective-permute-start | bytes 491528 | tf_op jit(solution)/shard_map/ppermute | solution.py:21
  30.0 18.0 %collective-permute-start.11 = (bf16[3,8,24,256]{3,2,1,0:T(8,128)(2,1)S(1)}, bf16[3,8,24,256]{3,2,1,0:T(8,128)(2,1)S(1)}, u32[]{:S(2)}, u32[]{:S(2)}) collective-permute-start(bf16[3,8,24,256]{3,2,1,0:T(8,128)(2,1)S(1)} %get-tuple-element.48), channel_id=1, source_target_pairs={{0,4},{4,0},{1,5},{5,1},{2,6},{6,2},{3,7},{7,3},{8,12},{12,8},{9,1... | collective-permute-start | bytes 884744 | tf_op jit(solution)/shard_map/ppermute | solution.py:21
  32.7 5.0 %collective-permute-start.12 = (bf16[4,8,4,512]{3,2,1,0:T(4,128)(2,1)S(1)}, bf16[4,8,4,512]{3,2,1,0:T(4,128)(2,1)S(1)}, u32[]{:S(2)}, u32[]{:S(2)}) collective-permute-start(bf16[4,8,4,512]{3,2,1,0:T(4,128)(2,1)S(1)} %get-tuple-element.49), channel_id=1, source_target_pairs={{0,1},{1,0},{2,3},{3,2},{4,5},{5,4},{6,7},{7,6},{8,9},{9,8},{10,11... | collective-permute-start | bytes 393224 | tf_op jit(solution)/shard_map/ppermute | solution.py:21
  36.7 5.4 %collective-permute-start.13 = (bf16[4,8,4,512]{3,2,1,0:T(4,128)(2,1)S(1)}, bf16[4,8,4,512]{3,2,1,0:T(4,128)(2,1)S(1)}, u32[]{:S(2)}, u32[]{:S(2)}) collective-permute-start(bf16[4,8,4,512]{3,2,1,0:T(4,128)(2,1)S(1)} %get-tuple-element.50), channel_id=1, source_target_pairs={{0,3},{1,2},{2,1},{3,0},{4,7},{5,6},{6,5},{7,4},{8,11},{9,10},{10,... | collective-permute-start | bytes 393224 | tf_op jit(solution)/shard_map/ppermute | solution.py:21
  36.7 11.3 %collective-permute-start.10 = (bf16[1,8,24,256]{3,2,1,0:T(8,128)(2,1)S(1)}, bf16[1,8,24,256]{3,2,1,0:T(8,128)(2,1)S(1)}, u32[]{:S(2)}, u32[]{:S(2)}) collective-permute-start(bf16[1,8,24,256]{3,2,1,0:T(8,128)(2,1)S(1)} %get-tuple-element.47), channel_id=1, source_target_pairs={{0,4},{4,0},{1,5},{5,1},{2,6},{6,2},{3,7},{7,3},{8,12},{12,8},{9,1... | collective-permute-start | bytes 294920 | tf_op jit(solution)/shard_map/ppermute | solution.py:21
  42.4 11.9 %collective-permute-start.14 = (bf16[4,8,4,4,256]{4,3,2,1,0:T(4,128)(2,1)S(1)}, bf16[4,8,4,4,256]{4,3,2,1,0:T(4,128)(2,1)S(1)}, u32[]{:S(2)}, u32[]{:S(2)}) collective-permute-start(bf16[4,8,4,4,256]{4,3,2,1,0:T(4,128)(2,1)S(1)} %get-tuple-element.52), channel_id=1, source_target_pairs={{0,1},{1,0},{2,3},{3,2},{4,5},{5,4},{6,7},{7,6},{8,9},{9,8},{10,11... | collective-permute-start | bytes 786440 | tf_op jit(solution)/shard_map/ppermute | solution.py:21
  42.4 11.8 %collective-permute-start.15 = (bf16[4,8,4,4,256]{4,3,2,1,0:T(4,128)(2,1)S(1)}, bf16[4,8,4,4,256]{4,3,2,1,0:T(4,128)(2,1)S(1)}, u32[]{:S(2)}, u32[]{:S(2)}) collective-permute-start(bf16[4,8,4,4,256]{4,3,2,1,0:T(4,128)(2,1)S(1)} %get-tuple-element.53), channel_id=1, source_target_pairs={{1,2},{2,1},{5,6},{6,5},{9,10},{10,9},{13,14},{14,13},{17,18},{18,... | collective-permute-start | bytes 786440 | tf_op jit(solution)/shard_map/ppermute | solution.py:28
  48.0 7.3 %copy-start = (f32[4,8,512]{2,1,0:T(8,128)S(1)}, f32[4,8,512]{2,1,0:T(8,128)}, u32[]{:S(2)}) copy-start(f32[4,8,512]{2,1,0:T(8,128)} %refs_3_.1) | copy-start | bytes 196612
  48.0 7.3 %copy-start.1 = (f32[4,16]{1,0:T(4,128)S(1)}, f32[4,16]{1,0:T(4,128)}, u32[]{:S(2)}) copy-start(f32[4,16]{1,0:T(4,128)} %table_ref.1) | copy-start | bytes 772
  48.2 6.1 %collective-permute-start.16 = (bf16[4,8,3,4,256]{4,3,2,1,0:T(4,128)(2,1)S(1)}, bf16[4,8,3,4,256]{4,3,2,1,0:T(4,128)(2,1)S(1)}, u32[]{:S(2)}, u32[]{:S(2)}) collective-permute-start(bf16[4,8,3,4,256]{4,3,2,1,0:T(4,128)(2,1)S(1)} %get-tuple-element.57), channel_id=1, source_target_pairs={{0,1},{1,0},{2,3},{3,2},{4,5},{5,4},{6,7},{7,6},{8,9},{9,8},{10,11... | collective-permute-start | bytes 589832 | tf_op jit(solution)/shard_map/ppermute | solution.py:21
  48.3 7.0 %collective-permute-start.17 = (bf16[4,8,3,4,256]{4,3,2,1,0:T(4,128)(2,1)S(1)}, bf16[4,8,3,4,256]{4,3,2,1,0:T(4,128)(2,1)S(1)}, u32[]{:S(2)}, u32[]{:S(2)}) collective-permute-start(bf16[4,8,3,4,256]{4,3,2,1,0:T(4,128)(2,1)S(1)} %get-tuple-element.58), channel_id=1, source_target_pairs={{1,2},{2,1},{5,6},{6,5},{9,10},{10,9},{13,14},{14,13},{17,18},{18,... | collective-permute-start | bytes 589832 | tf_op jit(solution)/shard_map/ppermute | solution.py:28
